TPU v7x, 32 devices: a whole 2x2x4 slice. The times are simulated.
32 devices in a mesh: dp: 8 (over y, x, core), mp: 4 (over z).
Axes of the slice: x: 2, y: 2, z: 4, core: 2. Of those that a mesh axis runs over, the one named last changes fastest.
Arguments:
- patches: bfloat16 [16384, 1024], P(('dp', 'mp')), may hold values from -6 to 6
- cotangent: bfloat16 [16384, 1024], P(('dp', 'mp')), may hold values from -6 to 6
- lengths: int32 [16384], P(('dp', 'mp')), may hold values from 1 to 64, as said below
- hashes: int32 [16384], P(('dp', 'mp')), may hold values from 0 to 500001
- segments: int32 [8, 2048], P('dp'), may hold values from 0 to 3, never falling along the last dimension, each value on 1 to 1024 neighbouring positions
- attend_master: float32 [3, 256, 64, 64], P(None, ('dp', 'mp')), may hold values from -0.1875 to 0.1875
- output_master: float32 [256, 64, 64], P(('dp', 'mp')), may hold values from -2 to 2
- expand_master: float32 [2, 256, 64, 176], P(None, ('dp', 'mp')), may hold values from -0.1875 to 0.1875
- reduce_master: float32 [256, 176, 64], P(('dp', 'mp')), may hold values from -0.109375 to 0.109375
- gains: float32 [2, 1024], replicated, may hold values from 0.5 to 1.5
- attend_left: float32 [3, 256, 64, 64], P(None, ('dp', 'mp')), as said below
- attend_right: float32 [3, 256, 64, 64], P(None, ('dp', 'mp')), as said below
- output_left: float32 [256, 64, 64], P(('dp', 'mp')), as said below
- output_right: float32 [256, 64, 64], P(('dp', 'mp')), as said below
- expand_left: float32 [2, 256, 64, 64], P(None, ('dp', 'mp')), as said below
- expand_right: float32 [2, 256, 176, 176], P(None, ('dp', 'mp')), as said below
- reduce_left: float32 [256, 176, 176], P(('dp', 'mp')), as said below
- reduce_right: float32 [256, 64, 64], P(('dp', 'mp')), as said below
- gains_left: float32 [2, 2], replicated, as said below
- gains_right: float32 [1024], replicated, may hold values from 2 to 8
Outputs:
- activations: bfloat16 [16384, 1024], P(('dp', 'mp'))
- input_grad: float32 [16384, 1024], P(('dp', 'mp'))
- attend_grad: float32 [3, 256, 64, 64], P(None, ('dp', 'mp'))
- attend_weight: float32 [3, 256, 64, 64], P(None, ('dp', 'mp'))
- left_attend: float32 [3, 256, 64, 64], P(None, ('dp', 'mp'))
- right_attend: float32 [3, 256, 64, 64], P(None, ('dp', 'mp'))
- output_grad: float32 [256, 64, 64], P(('dp', 'mp'))
- output_weight: float32 [256, 64, 64], P(('dp', 'mp'))
- left_output: float32 [256, 64, 64], P(('dp', 'mp'))
- right_output: float32 [256, 64, 64], P(('dp', 'mp'))
- expand_grad: float32 [2, 256, 64, 176], P(None, ('dp', 'mp'))
- expand_weight: float32 [2, 256, 64, 176], P(None, ('dp', 'mp'))
- left_expand: float32 [2, 256, 64, 64], P(None, ('dp', 'mp'))
- right_expand: float32 [2, 256, 176, 176], P(None, ('dp', 'mp'))
- reduce_grad: float32 [256, 176, 64], P(('dp', 'mp'))
- reduce_weight: float32 [256, 176, 64], P(('dp', 'mp'))
- left_reduce: float32 [256, 176, 176], P(('dp', 'mp'))
- right_reduce: float32 [256, 64, 64], P(('dp', 'mp'))
- gains_grad: float32 [2, 1024], replicated
- gains_weight: float32 [2, 1024], replicated
- left_gains: float32 [2, 2], replicated
- right_gains: float32 [1024], replicated
Inputs may be any that keep to these rules, and one draw needn't show every extreme that they name: `lengths`: the last patch has 64 bytes. `attend_left`: each matrix is symmetric; every diagonal entry is positive and larger than the sum of the magnitudes of the other entries of its row. `attend_right`: each matrix is symmetric; every diagonal entry is positive and larger than the sum of the magnitudes of the other entries of its row. `output_left`: each matrix is symmetric; every diagonal entry is positive and larger than the sum of the magnitudes of the other entries of its row. `output_right`: each matrix is symmetric; every diagonal entry is positive and larger than the sum of the magnitudes of the other entries of its row. `expand_left`: each matrix is symmetric; every diagonal entry is positive and larger than the sum of the magnitudes of the other entries of its row. `expand_right`: each matrix is symmetric; every diagonal entry is positive and larger than the sum of the magnitudes of the other entries of its row. `reduce_left`: each matrix is symmetric; every diagonal entry is positive and larger than the sum of the magnitudes of the other entries of its row. `reduce_right`: each matrix is symmetric; every diagonal entry is positive and larger than the sum of the magnitudes of the other entries of its row. `gains_left`: symmetric; each diagonal entry is positive and larger than the magnitude of the other entry of its row.
All inputs are finite; a program needn't handle non-finite values.
Results may differ from a plain program's by a relative error of at most 0.015.
The roundings to bfloat16 on the way count: a program that leaves them out, or rounds other values in their place, can miss the bound.
Values may be sent and summed in bfloat16 or wider, within the bound.
No kernel may reach another device: no remote copies, remote signals or barrier semaphores. Data moves between devices by JAX's collectives and lax.ppermute only.
A program may use at most 192 MiB of HBM per device.

v0:
```python
import jax
import jax.numpy as jnp
from jax import lax
from jax.sharding import PartitionSpec as P

D = 1024
HEADS = 16
HD = 64
FF = 2816
L = 2048
BLK = 64
FBLK = 176
HASH_B = 500002
ROOTS = 6
OUT_FAN = 8


EPSILON = 1e-05
STEP_RATE = 16.0
GAIN_RATE = 2.0
HIGHEST = lax.Precision.HIGHEST
MASKED = -1e30


def to_matrix(blocked, row_count):
    leading = blocked.shape[:-3]
    block_count, height, width = blocked.shape[-3:]
    row_blocks = row_count // height
    column_blocks = block_count // row_blocks
    grid = blocked.reshape(leading + (row_blocks, column_blocks, height, width))
    grid = jnp.swapaxes(grid, -3, -2)
    return grid.reshape(leading + (row_blocks * height, column_blocks * width))


def to_blocks(matrix, height, width):
    leading = matrix.shape[:-2]
    row_count, column_count = matrix.shape[-2:]
    grid = matrix.reshape(leading + (row_count // height, height, column_count // width, width))
    grid = jnp.swapaxes(grid, -3, -2)
    return grid.reshape(leading + (row_count // height * (column_count // width), height, width))


def product(first, second):
    return jnp.einsum("...ij,...jk->...ik", first, second, precision=HIGHEST)


def quarter_root(statistic):
    matrix_size = statistic.shape[-1]
    identity = jnp.eye(matrix_size, dtype=jnp.float32)
    frobenius = jnp.sqrt(jnp.sum(statistic * statistic, axis=(-2, -1), keepdims=True) + 1e-06)
    matrix = statistic / frobenius
    estimate = jnp.broadcast_to(identity, statistic.shape)
    for iteration in range(ROOTS):
        update = (5.0 * identity - matrix) * 0.25
        estimate = product(estimate, update)
        squared = product(update, update)
        matrix = product(product(squared, squared), matrix)
    return estimate * lax.rsqrt(jnp.sqrt(frobenius))


def shampoo(gradient, master, left_old, right_old, step_size):
    left_new = 0.5 * left_old + 0.5 * jnp.einsum(
        "...ij,...kj->...ik", gradient, gradient, precision=HIGHEST
    )
    right_new = 0.5 * right_old + 0.5 * jnp.einsum(
        "...ji,...jk->...ik", gradient, gradient, precision=HIGHEST
    )
    direction = product(product(quarter_root(left_new), gradient), quarter_root(right_new))
    return (master - step_size * direction, left_new, right_new)


def gain_update(gradient, gain_rows, left_old, right_old):
    left_new = 0.5 * left_old + 0.5 * jnp.einsum("id,jd->ij", gradient, gradient, precision=HIGHEST)
    right_new = 0.5 * right_old + 0.5 * jnp.sum(gradient * gradient, axis=0)
    direction = jnp.einsum(
        "ij,jd->id", quarter_root(left_new), gradient, precision=HIGHEST
    ) * lax.rsqrt(jnp.sqrt(right_new))
    return (gain_rows - GAIN_RATE * direction, left_new, right_new)


def masked_scores(query_part, key_rows, label_part, labels, query_pos, positions, scaling):
    raw_scores = (
        jnp.einsum("qhd,khd->hqk", query_part, key_rows, preferred_element_type=jnp.float32)
        * scaling
    )
    allowed = (label_part[:, None] == labels[None, :]) & (query_pos[:, None] >= positions[None, :])
    return jnp.where(allowed[None], raw_scores, MASKED)


def attend_row(queries, key_rows, values, labels, block_rows, scaling):
    length = key_rows.shape[0]
    positions = jnp.arange(length, dtype=jnp.int32)

    def one_block(block_index):
        offset = block_index * block_rows
        query_part = lax.dynamic_slice_in_dim(queries, offset, block_rows, 0)
        label_part = lax.dynamic_slice_in_dim(labels, offset, block_rows, 0)
        query_pos = offset + jnp.arange(block_rows, dtype=jnp.int32)
        scores = masked_scores(
            query_part, key_rows, label_part, labels, query_pos, positions, scaling
        )
        maximum = jnp.max(scores, axis=2, keepdims=True)
        powers = jnp.exp(scores - maximum)
        denominator = jnp.sum(powers, axis=2, keepdims=True)
        attention = (powers / denominator).astype(jnp.bfloat16)
        context = jnp.einsum("hqk,khd->qhd", attention, values, preferred_element_type=jnp.float32)
        return (context, maximum[:, :, 0] + jnp.log(denominator[:, :, 0]))

    contexts, log_sums = lax.map(one_block, jnp.arange(length // block_rows, dtype=jnp.int32))
    return (contexts.reshape(queries.shape), log_sums)


def attend_back(queries, key_rows, values, grad_context, log_sums, labels, block_rows, scaling):
    length = key_rows.shape[0]
    positions = jnp.arange(length, dtype=jnp.int32)

    def one_block(running, inputs):
        block_index, block_sums = inputs
        grad_keys, grad_values = running
        offset = block_index * block_rows
        query_part = lax.dynamic_slice_in_dim(queries, offset, block_rows, 0)
        grad_part = lax.dynamic_slice_in_dim(grad_context, offset, block_rows, 0)
        label_part = lax.dynamic_slice_in_dim(labels, offset, block_rows, 0)
        query_pos = offset + jnp.arange(block_rows, dtype=jnp.int32)
        scores = masked_scores(
            query_part, key_rows, label_part, labels, query_pos, positions, scaling
        )
        attention = jnp.exp(scores - block_sums[:, :, None])
        grad_values = grad_values + jnp.einsum(
            "hqk,qhd->khd",
            attention.astype(jnp.bfloat16),
            grad_part,
            preferred_element_type=jnp.float32,
        )
        grad_attention = jnp.einsum(
            "qhd,khd->hqk", grad_part, values, preferred_element_type=jnp.float32
        )
        row_terms = jnp.sum(attention * grad_attention, axis=2, keepdims=True)
        grad_scores = (attention * (grad_attention - row_terms)).astype(jnp.bfloat16)
        grad_queries = (
            jnp.einsum("hqk,khd->qhd", grad_scores, key_rows, preferred_element_type=jnp.float32)
            * scaling
        )
        grad_keys = (
            grad_keys
            + jnp.einsum(
                "hqk,qhd->khd", grad_scores, query_part, preferred_element_type=jnp.float32
            )
            * scaling
        )
        return ((grad_keys, grad_values), grad_queries)

    zero_block = jnp.zeros(key_rows.shape, jnp.float32)
    block_ids = jnp.arange(length // block_rows, dtype=jnp.int32)
    (grad_keys, grad_values), grad_queries = lax.scan(
        one_block, (zero_block, zero_block), (block_ids, log_sums)
    )
    return (grad_queries.reshape(queries.shape), grad_keys, grad_values)


def body(
    patches,
    cotangent,
    lengths,
    hashes,
    segments,
    attend_master,
    output_master,
    expand_master,
    reduce_master,
    gains,
    attend_left,
    attend_right,
    output_left,
    output_right,
    expand_left,
    expand_right,
    reduce_left,
    reduce_right,
    gains_left,
    gains_right,
):
    tensor_count = lax.axis_size("mp")
    head_width = HEADS * HD // tensor_count
    hidden_width = FF // tensor_count
    local_heads = head_width // HD
    scaling = HD ** (-0.5)
    block_rows = min(512, L)
    attend_w, output_w, expand_w, reduce_w = (
        lax.all_gather(attend_master.astype(jnp.bfloat16), "dp", axis=1, tiled=True),
        lax.all_gather(output_master.astype(jnp.bfloat16), "dp", axis=0, tiled=True),
        lax.all_gather(expand_master.astype(jnp.bfloat16), "dp", axis=1, tiled=True),
        lax.all_gather(reduce_master.astype(jnp.bfloat16), "dp", axis=0, tiled=True),
    )
    attend_w = to_matrix(attend_w, D)
    output_w = to_matrix(output_w, head_width)
    expand_w = to_matrix(expand_w, D)
    reduce_w = to_matrix(reduce_w, hidden_width)
    bucket_slots = (HASH_B + 127) // 128 * 128
    byte_counts = lengths.astype(jnp.float32)
    local_counts = jax.ops.segment_sum(
        jnp.ones_like(byte_counts), hashes, num_segments=bucket_slots
    )
    local_mass = jax.ops.segment_sum(byte_counts, hashes, num_segments=bucket_slots)
    counts, length_mass = lax.psum((local_counts, local_mass), ("dp", "mp"))
    patch_counts = counts[hashes]
    total_count = jnp.sum(counts)
    damped_mass = jnp.sum(length_mass * lax.rsqrt(jnp.maximum(counts, 1.0)))
    patch_weight = byte_counts * lax.rsqrt(patch_counts) * (total_count / damped_mass)
    grad_scale = lax.rsqrt(total_count)
    stream = patches.astype(jnp.float32)
    first_rms = lax.rsqrt(jnp.mean(stream * stream, axis=1, keepdims=True) + EPSILON)
    first_hat = stream * first_rms
    first_normed = lax.all_gather(
        (first_hat * gains[0]).astype(jnp.bfloat16), "mp", axis=0, tiled=True
    )
    group_rows = first_normed.shape[0]
    row_count = group_rows // L
    projected = jnp.einsum(
        "td,kdc->ktc", first_normed, attend_w, preferred_element_type=jnp.float32
    ).astype(jnp.bfloat16)
    heads_view = projected.reshape(3, row_count, L, local_heads, HD)
    attended, log_sums = lax.map(
        lambda parts: attend_row(parts[0], parts[1], parts[2], parts[3], block_rows, scaling),
        (heads_view[0], heads_view[1], heads_view[2], segments),
    )
    context = attended.reshape(group_rows, head_width).astype(jnp.bfloat16)
    middle = stream + lax.psum_scatter(
        jnp.dot(context, output_w, preferred_element_type=jnp.float32),
        "mp",
        scatter_dimension=0,
        tiled=True,
    )
    second_rms = lax.rsqrt(jnp.mean(middle * middle, axis=1, keepdims=True) + EPSILON)
    second_hat = middle * second_rms
    second_normed = lax.all_gather(
        (second_hat * gains[1]).astype(jnp.bfloat16), "mp", axis=0, tiled=True
    )
    gate_up = jnp.einsum("td,kdf->ktf", second_normed, expand_w, preferred_element_type=jnp.float32)
    gate_pre = gate_up[0]
    up_pre = gate_up[1]
    gate_sig = jax.nn.sigmoid(gate_pre)
    hidden = (gate_pre * gate_sig * up_pre).astype(jnp.bfloat16)
    result = middle + lax.psum_scatter(
        jnp.dot(hidden, reduce_w, preferred_element_type=jnp.float32).astype(jnp.bfloat16),
        "mp",
        scatter_dimension=0,
        tiled=True,
    ).astype(jnp.float32)
    activations = result.astype(jnp.bfloat16)
    grad_out = cotangent.astype(jnp.float32) * patch_weight[:, None]
    grad_rows = lax.all_gather(grad_out.astype(jnp.bfloat16), "mp", axis=0, tiled=True)
    reduce_local = jnp.einsum("tf,td->fd", hidden, grad_rows, preferred_element_type=jnp.float32)
    grad_hidden = jnp.einsum("td,fd->tf", grad_rows, reduce_w, preferred_element_type=jnp.float32)
    grad_up = grad_hidden * gate_pre * gate_sig
    grad_gate = grad_hidden * up_pre * gate_sig * (1.0 + gate_pre * (1.0 - gate_sig))
    grad_pair = jnp.stack([grad_gate, grad_up]).astype(jnp.bfloat16)
    expand_local = jnp.einsum(
        "td,ktf->kdf", second_normed, grad_pair, preferred_element_type=jnp.float32
    )
    second_back = lax.psum_scatter(
        jnp.einsum("ktf,kdf->td", grad_pair, expand_w, preferred_element_type=jnp.float32),
        "mp",
        scatter_dimension=0,
        tiled=True,
    )
    second_scaled = second_back * gains[1]
    gain_second = jnp.sum(second_back * second_hat, axis=0)
    middle_grad = grad_out + second_rms * (
        second_scaled - second_hat * jnp.mean(second_scaled * second_hat, axis=1, keepdims=True)
    )
    middle_rows = lax.all_gather(middle_grad.astype(jnp.bfloat16), "mp", axis=0, tiled=True)
    output_local = jnp.einsum("tc,td->cd", context, middle_rows, preferred_element_type=jnp.float32)
    grad_context = jnp.einsum(
        "td,cd->tc", middle_rows, output_w, preferred_element_type=jnp.float32
    ).astype(jnp.bfloat16)
    grad_heads = grad_context.reshape(row_count, L, local_heads, HD)
    grad_queries, grad_keys, grad_values = lax.map(
        lambda parts: attend_back(
            parts[0], parts[1], parts[2], parts[3], parts[4], parts[5], block_rows, scaling
        ),
        (heads_view[0], heads_view[1], heads_view[2], grad_heads, log_sums, segments),
    )
    grad_project = (
        jnp.stack([grad_queries, grad_keys, grad_values])
        .reshape(3, group_rows, head_width)
        .astype(jnp.bfloat16)
    )
    attend_local = jnp.einsum(
        "td,ktc->kdc", first_normed, grad_project, preferred_element_type=jnp.float32
    )
    first_back = lax.psum_scatter(
        jnp.einsum(
            "ktc,kdc->td", grad_project, attend_w, preferred_element_type=jnp.float32
        ).astype(jnp.bfloat16),
        "mp",
        scatter_dimension=0,
        tiled=True,
    ).astype(jnp.float32)
    first_scaled = first_back * gains[0]
    gain_first = jnp.sum(first_back * first_hat, axis=0)
    input_grad = middle_grad + first_rms * (
        first_scaled - first_hat * jnp.mean(first_scaled * first_hat, axis=1, keepdims=True)
    )
    gains_grad = lax.psum(jnp.stack([gain_first, gain_second]), ("dp", "mp")) * grad_scale
    summed = lax.psum(
        (
            to_blocks(attend_local, BLK, BLK),
            to_blocks(output_local, BLK, BLK),
            to_blocks(expand_local, BLK, FBLK),
            to_blocks(reduce_local, FBLK, BLK),
        ),
        "dp",
    )
    attend_owned = output_master.shape[0]
    expand_owned = reduce_master.shape[0]
    owner_index = lax.axis_index("dp")
    attend_sum = lax.dynamic_slice_in_dim(summed[0], owner_index * attend_owned, attend_owned, 1)
    output_sum = lax.dynamic_slice_in_dim(summed[1], owner_index * attend_owned, attend_owned, 0)
    expand_sum = lax.dynamic_slice_in_dim(summed[2], owner_index * expand_owned, expand_owned, 1)
    reduce_sum = lax.dynamic_slice_in_dim(summed[3], owner_index * expand_owned, expand_owned, 0)
    attend_grad = attend_sum * grad_scale
    output_grad = output_sum * grad_scale
    expand_grad = expand_sum * grad_scale
    reduce_grad = reduce_sum * grad_scale
    attend_weight, left_attend, right_attend = shampoo(
        attend_grad, attend_master, attend_left, attend_right, STEP_RATE * D ** (-0.5)
    )
    output_weight, left_output, right_output = shampoo(
        output_grad, output_master, output_left, output_right, STEP_RATE * OUT_FAN ** (-0.5)
    )
    expand_weight, left_expand, right_expand = shampoo(
        expand_grad, expand_master, expand_left, expand_right, STEP_RATE * D ** (-0.5)
    )
    reduce_weight, left_reduce, right_reduce = shampoo(
        reduce_grad, reduce_master, reduce_left, reduce_right, STEP_RATE * FF ** (-0.5)
    )
    gains_weight, left_gains, right_gains = gain_update(gains_grad, gains, gains_left, gains_right)
    return (
        activations,
        input_grad,
        attend_grad,
        attend_weight,
        left_attend,
        right_attend,
        output_grad,
        output_weight,
        left_output,
        right_output,
        expand_grad,
        expand_weight,
        left_expand,
        right_expand,
        reduce_grad,
        reduce_weight,
        left_reduce,
        right_reduce,
        gains_grad,
        gains_weight,
        left_gains,
        right_gains,
    )


def solution(mesh):
    return jax.shard_map(
        body,
        mesh=mesh,
        in_specs=(
            P(("dp", "mp"), None),
            P(("dp", "mp"), None),
            P(("dp", "mp")),
            P(("dp", "mp")),
            P("dp", None),
            P(None, ("dp", "mp"), None, None),
            P(("dp", "mp"), None, None),
            P(None, ("dp", "mp"), None, None),
            P(("dp", "mp"), None, None),
            P(),
            P(None, ("dp", "mp"), None, None),
            P(None, ("dp", "mp"), None, None),
            P(("dp", "mp"), None, None),
            P(("dp", "mp"), None, None),
            P(None, ("dp", "mp"), None, None),
            P(None, ("dp", "mp"), None, None),
            P(("dp", "mp"), None, None),
            P(("dp", "mp"), None, None),
            P(),
            P(),
        ),
        out_specs=(
            P(("dp", "mp"), None),
            P(("dp", "mp"), None),
            P(None, ("dp", "mp"), None, None),
            P(None, ("dp", "mp"), None, None),
            P(None, ("dp", "mp"), None, None),
            P(None, ("dp", "mp"), None, None),
            P(("dp", "mp"), None, None),
            P(("dp", "mp"), None, None),
            P(("dp", "mp"), None, None),
            P(("dp", "mp"), None, None),
            P(None, ("dp", "mp"), None, None),
            P(None, ("dp", "mp"), None, None),
            P(None, ("dp", "mp"), None, None),
            P(None, ("dp", "mp"), None, None),
            P(("dp", "mp"), None, None),
            P(("dp", "mp"), None, None),
            P(("dp", "mp"), None, None),
            P(("dp", "mp"), None, None),
            P(),
            P(),
            P(),
            P(),
        ),
        check_vma=False,
    )
```

profile of v0, /device:TPU:0, one launch (start us, length us, event | category | flops | bytes accessed | tf_op | source)
XLA Modules:
  0.0 1742.5 jit_solution(8216705094099200606)
XLA Ops:
  15.1 15.3 all_gather.26
  32.6 16.0 all-gather.10.cloned.1.call-done
  56.1 75.5 %all-gather.8.cloned.1.call-done = bf16[2048,1024]{1,0:T(8,128)(2,1)} async-done(((bf16[512,1024]{1,0:T(8,128)(2,1)}), bf16[2048,1024]{1,0:T(8,128)(2,1)}) %all-gather.8.cloned.1.call-update) | async-done | bytes 4194320 | tf_op jit(solution)/shard_map/all_gather | solution.py:214
  131.6 6.2 fusion.67
  139.3 63.7 %while.48 = (s32[]{:T(128)}, bf16[4,512,4,64]{1,3,2,0:T(8,128)(2,1)}, f32[4,4,512]{2,1,0:T(4,128)}, s32[4]{0:T(128)S(1)}, s32[2048]{0:T(1024)S(1)}, /*index=5*/b...) while((s32[]{:T(128)}, ...), condition=%wide.region_4.0_spmd.clone, body=%wide.region_1.4_spmd.clone.sunk | while | flops 1127217664 | bytes 65882372 | solution.py:109
  225.8 142.3 %reduce-scatter.5.cloned.1.call-done = f32[512,1024]{1,0:T(8,128)} async-done(((f32[2048,1024]{1,0:T(8,128)}), f32[512,1024]{1,0:T(8,128)}) %reduce-scatter.5.cloned.1.call-update) | async-done | bytes 2097168 | tf_op jit(solution)/shard_map/reduce_scatter | solution.py:228
  372.8 170.1 %all-reduce.5.cloned.1.call-done = (f32[500096]{0:T(1024)}, f32[500096]{0:T(1024)}) async-done(((f32[500096]{0:T(1024)}, f32[500096]{0:T(1024)}), (f32[500096]{0:T(1024)}, f32[500096]{0:T(1024)})) %all-reduce.5.cloned.1.call-update) | async-done | bytes 4000784 | tf_op jit(solution)/shard_map/psum | solution.py:205
  542.9 6.1 gather_fusion
  564.5 8.2 copy.111
  572.7 8.4 reshape.441
  581.1 11.6 convolution_bitcast_fusion
  592.7 42.7 %all-gather.18.cloned.1.call-done = bf16[2048,1024]{1,0:T(8,128)(2,1)} async-done(((bf16[512,1024]{1,0:T(8,128)(2,1)}), bf16[2048,1024]{1,0:T(8,128)(2,1)}) %all-gather.18.cloned.1.call-update) | async-done | bytes 4194320 | tf_op jit(solution)/shard_map/all_gather | solution.py:252
  635.5 11.8 fusion.77
  649.6 9.2 convolution_bitcast_fusion.1
  658.9 10.6 convolution_convert_fusion
  669.6 132.4 %reduce-scatter.9.cloned.1.call-done = f32[512,1024]{1,0:T(8,128)} async-done(((f32[2048,1024]{1,0:T(8,128)}), f32[512,1024]{1,0:T(8,128)}) %reduce-scatter.9.cloned.1.call-update) | async-done | bytes 2097168 | tf_op jit(solution)/shard_map/reduce_scatter | solution.py:261
  805.5 76.4 %reduce-scatter.7.cloned.1.call-done = bf16[512,1024]{1,0:T(8,128)(2,1)} async-done(((bf16[2048,1024]{1,0:T(8,128)(2,1)}), bf16[512,1024]{1,0:T(8,128)(2,1)}) %reduce-scatter.7.cloned.1.call-update) | async-done | bytes 1048592 | tf_op jit(solution)/shard_map/reduce_scatter | solution.py:244
  887.3 6.7 copy.94
  894.0 11.5 fusion.78
  905.5 6.4 copy.92
  911.9 11.2 reshape.447
  923.2 8.5 copy.93
  931.7 6.2 fusion.584
  937.8 30.8 %all-gather.20.cloned.1.call-done = bf16[2048,1024]{1,0:T(8,128)(2,1)} async-done(((bf16[512,1024]{1,0:T(8,128)(2,1)}), bf16[2048,1024]{1,0:T(8,128)(2,1)}) %all-gather.20.cloned.1.call-update) | async-done | bytes 4194320 | tf_op jit(solution)/shard_map/all_gather | solution.py:272
  974.1 194.7 %while.49 = (s32[]{:T(128)}, f32[2048,4,64]{0,2,1:T(8,128)}, f32[2048,4,64]{0,2,1:T(8,128)}, bf16[4,512,4,64]{1,3,2,0:T(8,128)(2,1)}, s32[4]{0:T(128)S(1)}, /*in...) while((s32[]{:T(128)}, f32[2048,4,64]{0,2,1:T(8,128)}, ...), condition=%wide.region_18.19_spmd.clone, body=%wide.region_16.18_spmd.clone.sunk | while | flops 2753165824 | bytes 193604048 | solution.py:155
  981.6 7.2 fusion.931
  988.8 11.4 multiply_reduce_fusion.16
  1000.2 10.8 multiply_convert_fusion.5
  1011.0 7.1 fusion.932
  1029.3 7.6 fusion.931
  1036.9 11.4 multiply_reduce_fusion.16
  1048.3 10.8 multiply_convert_fusion.5
  1059.1 7.1 fusion.932
  1078.1 7.6 fusion.931
  1085.7 11.4 multiply_reduce_fusion.16
  1097.1 10.8 multiply_convert_fusion.5
  1107.9 7.1 fusion.932
  1126.9 7.6 fusion.931
  1134.5 11.4 multiply_reduce_fusion.16
  1145.9 10.8 multiply_convert_fusion.5
  1156.7 7.1 fusion.932
  1181.9 6.2 fusion.99
  1191.8 6.7 copy.88
  1198.5 6.6 copy.90
  1205.1 5.9 fusion.548
  1212.7 6.8 bitcast_convert_fusion
  1219.6 254.6 %all-reduce.7.cloned.1.call-done = (f32[3,64,64,64]{3,2,1,0:T(8,128)}, f32[64,64,64]{2,1,0:T(8,128)}, f32[2,64,64,176]{3,2,1,0:T(8,128)}, f32[64,176,64]{1,2,0:T(8,128)}) async-done(((f32[3,64,64,64]{3,2,1,0:T(8,128)}, f32[64,64,64]{2,1,0:T(8,128)}, f32[2,64,64,176]{3,2,1,0:T(8,128)}, f32[64,176,64]{1,2,0:T(8,128)}), (f32[3,64,64,64]{3,2,1,0:T(8,128)}, f32[64,64,64]{2,1,0:T(8,128)}, ...) | async-done | bytes 12845072 | tf_op jit(solution)/shard_map/psum | solution.py:306
  1686.4 39.2 %psum.55 = f32[2,1024]{1,0:T(2,128)S(1)} all-reduce(f32[2,1024]{1,0:T(2,128)S(1)} %pad_maximum_fusion.8), channel_id=1, replica_groups=mesh['dp'=8,'mp'=4] {'dp','mp'}, use_global_device_ids=true, to_apply=%region_35.36 | all-reduce | flops 2048 | bytes 16384 | tf_op jit(solution)/shard_map/psum | solution.py:305
  (558 shorter events, 417.4 us)
Async XLA Ops:
  8.0 5.7 copy-start.9
  8.0 7.0 copy-start.37
  8.0 40.6 %all-gather.10.cloned.1.call-start = ((), (), s32[]{:S(2)}) async-start(), calls=%async_computation.5 | async-start | bytes 3538944 | tf_op jit(solution)/shard_map/all_gather | solution.py:190
  10.2 121.4 %all-gather.8.cloned.1.call-start = ((), (), s32[]{:S(2)}) async-start(), calls=%async_computation.4 | async-start | bytes 5242880 | tf_op jit(solution)/shard_map/all_gather | solution.py:214
  15.0 353.1 %reduce-scatter.5.cloned.1.call-start = ((), (), s32[]{:S(2)}) async-start(), calls=%async_computation.6 | async-start | bytes 10485760 | tf_op jit(solution)/shard_map/reduce_scatter | solution.py:228
  203.0 8.3 copy-start.12
  211.3 331.6 %all-reduce.5.cloned.1.call-start = ((), (), s32[]{:S(2)}) async-start(), calls=%async_computation.15 | async-start | bytes 8011776 | tf_op jit(solution)/shard_map/psum | solution.py:205
  221.7 146.5 %copy-start.10 = (bf16[512,1024]{1,0:T(8,128)(2,1)S(1)}, bf16[512,1024]{1,0:T(8,128)(2,1)}, u32[]{:S(2)}) copy-start(bf16[512,1024]{1,0:T(8,128)(2,1)} %param.24) | copy-start | bytes 3145732
  221.7 333.3 %all-gather.16.cloned.1.call-start = ((), (), s32[]{:S(2)}) async-start(), calls=%async_computation.9 | async-start | bytes 2359296 | tf_op jit(solution)/shard_map/all_gather | solution.py:193
  223.6 340.9 %all-gather.14.cloned.1.call-start = ((), (), s32[]{:S(2)}) async-start(), calls=%async_computation.8 | async-start | bytes 4718592 | tf_op jit(solution)/shard_map/all_gather | solution.py:192
  225.8 145.7 %copy-start.52 = (f32[1,1024]{1,0:T(1,128)S(1)}, f32[1,1024]{1,0:T(1,128)}, u32[]{:S(2)}) copy-start(f32[1,1024]{1,0:T(1,128)} %get-tuple-element.315) | copy-start | bytes 12292
  225.8 355.3 %all-gather.12.cloned.1.call-start = ((), (), s32[]{:S(2)}) async-start(), calls=%async_computation.7 | async-start | bytes 5242880 | tf_op jit(solution)/shard_map/all_gather | solution.py:236
  372.7 262.7 %all-gather.18.cloned.1.call-start = ((), (), s32[]{:S(2)}) async-start(), calls=%async_computation.11 | async-start | bytes 5242880 | tf_op jit(solution)/shard_map/all_gather | solution.py:252
  542.9 10.8 copy-start.18
  555.0 247.1 %reduce-scatter.9.cloned.1.call-start = ((), (), s32[]{:S(2)}) async-start(), calls=%async_computation.12 | async-start | bytes 10485760 | tf_op jit(solution)/shard_map/reduce_scatter | solution.py:261
  635.4 14.2 copy-start.23
  658.9 223.0 %reduce-scatter.7.cloned.1.call-start = ((), (), s32[]{:S(2)}) async-start(), calls=%async_computation.10 | async-start | bytes 5242880 | tf_op jit(solution)/shard_map/reduce_scatter | solution.py:244
  669.6 299.1 %all-gather.20.cloned.1.call-start = ((), (), s32[]{:S(2)}) async-start(), calls=%async_computation.13 | async-start | bytes 5242880 | tf_op jit(solution)/shard_map/all_gather | solution.py:272
  887.2 587.0 %all-reduce.7.cloned.1.call-start = ((), (), s32[]{:S(2)}) async-start(), calls=%async_computation.16 | async-start | bytes 41943040 | tf_op jit(solution)/shard_map/psum | solution.py:306
  923.1 8.5 copy-start.20
  923.1 8.5 copy-start.65
  931.6 37.0 %copy-start.28 = (bf16[256,1024]{1,0:T(8,128)(2,1)S(1)}, bf16[256,1024]{1,0:T(8,128)(2,1)}, u32[]{:S(2)}) copy-start(bf16[256,1024]{1,0:T(8,128)(2,1)} %reshape.439) | copy-start | bytes 1572868
  1011.0 7.1 copy-start
  1059.1 7.1 copy-start
  1107.9 7.1 copy-start
  1156.7 7.1 copy-start
  1168.8 8.5 copy-start.3
  1198.5 6.6 copy-start.17
  1210.9 473.4 %reduce-scatter.11.cloned.1.call-start = ((), (), s32[]{:S(2)}) async-start(), calls=%async_computation.14 | async-start | bytes 5242880 | tf_op jit(solution)/shard_map/reduce_scatter | solution.py:292
  1219.5 255.6 %copy-start.45 = (f32[8,64,64]{2,1,0:T(8,128)S(1)}, f32[8,64,64]{2,1,0:T(8,128)}, u32[]{:S(2)}) copy-start(f32[8,64,64]{2,1,0:T(8,128)} %param.37) | copy-start | bytes 393220
  1219.5 257.3 %copy-start.46 = (f32[8,64,64]{2,1,0:T(8,128)S(1)}, f32[8,64,64]{2,1,0:T(8,128)}, u32[]{:S(2)}) copy-start(f32[8,64,64]{2,1,0:T(8,128)} %param.36) | copy-start | bytes 393220
  1475.2 34.4 %copy-start.14 = (f32[8,64,64]{2,1,0:T(8,128)}, f32[8,64,64]{2,1,0:T(8,128)S(1)}, u32[]{:S(2)}) copy-start(f32[8,64,64]{2,1,0:T(8,128)S(1)} %dynamic-slice_multiply_fusion.3) | copy-start | bytes 393220
  1475.9 19.1 %copy-start.48 = (f32[8,64,64]{2,1,0:T(8,128)}, f32[8,64,64]{2,1,0:T(8,128)S(1)}, u32[]{:S(2)}) copy-start(f32[8,64,64]{2,1,0:T(8,128)S(1)} %get-tuple-element.340) | copy-start | bytes 393220
  1477.5 24.6 %copy-start.49 = (f32[8,64,64]{2,1,0:T(8,128)}, f32[8,64,64]{2,1,0:T(8,128)S(1)}, u32[]{:S(2)}) copy-start(f32[8,64,64]{2,1,0:T(8,128)S(1)} %get-tuple-element.338) | copy-start | bytes 393220
  1479.6 124.3 %copy-start.13 = (f32[8,176,64]{1,2,0:T(8,128)}, f32[8,176,64]{1,2,0:T(8,128)S(1)}, u32[]{:S(2)}) copy-start(f32[8,176,64]{1,2,0:T(8,128)S(1)} %dynamic-slice_multiply_fusion.2) | copy-start | bytes 1081348
  1480.4 29.9 %copy-start.50 = (f32[8,64,64]{2,1,0:T(8,128)}, f32[8,64,64]{2,1,0:T(8,128)S(1)}, u32[]{:S(2)}) copy-start(f32[8,64,64]{2,1,0:T(8,128)S(1)} %get-tuple-element.348) | copy-start | bytes 393220
  1482.9 122.7 %copy-start.6 = (f32[2,8,64,176]{3,2,1,0:T(8,128)}, f32[2,8,64,176]{3,2,1,0:T(8,128)S(1)}, u32[]{:S(2)}) copy-start(f32[2,8,64,176]{3,2,1,0:T(8,128)S(1)} %dynamic-slice_multiply_fusion) | copy-start | bytes 2162692
  1484.1 33.7 %copy-start.44 = (f32[2,8,64,64]{3,2,1,0:T(8,128)}, f32[2,8,64,64]{3,2,1,0:T(8,128)S(1)}, u32[]{:S(2)}) copy-start(f32[2,8,64,64]{3,2,1,0:T(8,128)S(1)} %get-tuple-element.342) | copy-start | bytes 786436
  1486.9 79.8 %copy-start.8 = (f32[3,8,64,64]{3,2,1,0:T(8,128)}, f32[3,8,64,64]{3,2,1,0:T(8,128)S(1)}, u32[]{:S(2)}) copy-start(f32[3,8,64,64]{3,2,1,0:T(8,128)S(1)} %dynamic-slice_multiply_fusion.1) | copy-start | bytes 1179652
  1488.5 43.9 %copy-start.41 = (f32[3,8,64,64]{3,2,1,0:T(8,128)}, f32[3,8,64,64]{3,2,1,0:T(8,128)S(1)}, u32[]{:S(2)}) copy-start(f32[3,8,64,64]{3,2,1,0:T(8,128)S(1)} %get-tuple-element.336) | copy-start | bytes 1179652
  1492.0 57.3 %copy-start.42 = (f32[3,8,64,64]{3,2,1,0:T(8,128)}, f32[3,8,64,64]{3,2,1,0:T(8,128)S(1)}, u32[]{:S(2)}) copy-start(f32[3,8,64,64]{3,2,1,0:T(8,128)S(1)} %get-tuple-element.334) | copy-start | bytes 1179652
  1608.7 53.7 %copy-start.26 = (f32[2,8,176,176]{3,2,1,0:T(8,128)}, f32[2,8,176,176]{3,2,1,0:T(8,128)S(1)}, u32[]{:S(2)}) copy-start(f32[2,8,176,176]{3,2,1,0:T(8,128)S(1)} %get-tuple-element.344) | copy-start | bytes 5947396
  1681.4 44.3 %copy-start.64 = (f32[2,2]{1,0:T(2,128)S(1)}, f32[2,2]{1,0:T(2,128)}, u32[]{:S(2)}) copy-start(f32[2,2]{1,0:T(2,128)} %param.42) | copy-start | bytes 52
  1681.4 48.6 %copy-start.61 = (f32[1024]{0:T(1024)S(1)}, f32[1024]{0:T(1024)}, u32[]{:S(2)}) copy-start(f32[1024]{0:T(1024)} %param.43) | copy-start | bytes 12292
  1681.4 49.3 %copy-start.58 = (f32[2,1024]{1,0:T(2,128)S(1)}, f32[2,1024]{1,0:T(2,128)}, u32[]{:S(2)}) copy-start(f32[2,1024]{1,0:T(2,128)} %param.33) | copy-start | bytes 24580
  1681.4 50.1 %copy-start.15 = (f32[512,1024]{1,0:T(8,128)S(1)}, f32[512,1024]{1,0:T(8,128)}, u32[]{:S(2)}) copy-start(f32[512,1024]{1,0:T(8,128)} %get-tuple-element.301) | copy-start | bytes 6291460
  1725.6 9.0 copy-start.60
  1726.5 8.2 copy-start.63
  (60 other events, 170.7 us)
Sparse Core Ops, SparseCore 0:
  11.4 37.2 all-gather.9
  50.8 80.7 all-gather.7
  211.4 156.6 reduce-scatter.4
  370.5 29.0 all-gather.15
  401.9 36.7 all-gather.13
  440.6 86.6 all-gather.11
  555.1 80.3 all-gather.17
  659.0 142.9 reduce-scatter.8
  804.3 77.4 reduce-scatter.6
  887.3 81.2 all-gather.19
  1211.1 263.0 all-reduce.6
  1476.4 76.7 reduce-scatter.10
Sparse Core Ops, SparseCore 1:
  221.8 321.1 all-reduce.4
where the time goes:
time: 1750 us; the launch traced here: 1740 us
  waiting for transfers between devices  941 us (54%)
  matrix products  472 us (27%)
  local copies, waits for them, and re-layouts  126 us (7%)
  other arithmetic  121 us (7%)
  blocking collectives  54.5 us (3%)
  between operations  21.1 us (1%)
    psum x1, waiting for transfers between devices, body(): lax.psum((to_blocks(attend_local, BLK, BLK), to_blocks(output_local, BLK,...  255 us
    dot_general x197, matrix products, product(): return jnp.einsum('...ij,...jk->...ik', first, second, precision=HIGHEST)  195 us
    psum x1, waiting for transfers between devices, body(): counts, length_mass = lax.psum((local_counts, local_mass), ('dp', 'mp'))  170 us
    reduce_scatter x1, waiting for transfers between devices, body(): lax.psum_scatter(jnp.dot(context, output_w, preferred_element_type=jnp.fl...  142 us
    reduce_scatter x1, waiting for transfers between devices, body(): lax.psum_scatter(jnp.einsum('ktf,kdf->td', grad_pair, expand_w, preferred...  132 us
    reduce_scatter x1, waiting for transfers between devices, body(): lax.psum_scatter(jnp.dot(hidden, reduce_w, preferred_element_type=jnp.flo...  76.4 us
    all_gather x1, waiting for transfers between devices, body(): lax.all_gather((first_hat * gains[0]).astype(jnp.bfloat16), 'mp', axis=0,...  75.5 us
    dot_general x4, matrix products, one_block(): jnp.einsum('qhd,khd->hqk', grad_part, values, preferred_element_type=jnp....  45.5 us
  transfers between devices with their start and end apart: 13, of which 9 were waited for; matrix products, arithmetic and copies ran while one was open for 21% of the time, Pallas kernels for 0%

commit v1 on v0

v1 whole, which is shorter than its diff:
```python
import functools

import jax
import jax.numpy as jnp
from jax import lax
from jax.experimental import pallas as pl
from jax.experimental.pallas import tpu as pltpu
from jax.sharding import PartitionSpec as P

D = 1024
HEADS = 16
HD = 64
FF = 2816
BLK = 64
FBLK = 176
ROOTS = 6
OUT_FAN = 8
SPAN = 1024

EPSILON = 1e-05
STEP_RATE = 16.0
GAIN_RATE = 2.0
MASKED = -1e30
F32 = jnp.float32
BF16 = jnp.bfloat16
PAIR = 2 * HD


def piece_shape(blocked_shape, group_rows, dp_size):
    per_owner, height, width = blocked_shape[-3:]
    column_blocks = dp_size * per_owner // (group_rows // height)
    if per_owner % column_blocks == 0:
        rows, columns = per_owner // column_blocks, column_blocks
    else:
        rows, columns = 1, per_owner
    grid_columns = column_blocks // columns
    return rows, columns, dp_size // grid_columns, grid_columns


def to_piece(blocked, rows, columns):
    leading = blocked.shape[:-3]
    height, width = blocked.shape[-2:]
    grid = blocked.reshape(leading + (rows, columns, height, width))
    return jnp.swapaxes(grid, -3, -2).reshape(leading + (rows * height, columns * width))


def from_piece(piece, rows, columns):
    leading = piece.shape[:-2]
    height, width = piece.shape[-2] // rows, piece.shape[-1] // columns
    grid = piece.reshape(leading + (rows, height, columns, width))
    return jnp.swapaxes(grid, -3, -2).reshape(leading + (rows * columns, height, width))


def gather_all(piece):
    return lax.all_gather(lax.all_gather(piece, "mp"), "dp")


def scatter_all(parts):
    reduced = lax.psum_scatter(parts, "dp", scatter_dimension=0, tiled=False)
    return lax.psum_scatter(reduced, "mp", scatter_dimension=0, tiled=False)


def weight_by_columns(master, dp_size):
    rows, columns, grid_rows, grid_columns = piece_shape(master.shape, D, dp_size)
    gathered = gather_all(to_piece(master.astype(BF16), rows, columns))
    dp, mp, members, height, width = gathered.shape
    grid = gathered.reshape(grid_rows, grid_columns, mp, members, height, width)
    grid = jnp.transpose(grid, (3, 0, 4, 2, 1, 5))
    return grid.reshape(members, grid_rows * height, mp * grid_columns * width)


def weight_by_rows(master, group_rows, dp_size):
    rows, columns, grid_rows, grid_columns = piece_shape(master.shape, group_rows, dp_size)
    gathered = gather_all(to_piece(master.astype(BF16), rows, columns))
    dp, mp, height, width = gathered.shape
    grid = gathered.reshape(grid_rows, grid_columns, mp, height, width)
    grid = jnp.transpose(grid, (2, 0, 3, 1, 4))
    return grid.reshape(mp * grid_rows * height, grid_columns * width)


def grad_by_columns(matrix, master, dp_size, mp_size):
    rows, columns, grid_rows, grid_columns = piece_shape(master.shape, D, dp_size)
    members = matrix.shape[0]
    height, width = rows * master.shape[-2], columns * master.shape[-1]
    grid = matrix.reshape(members, grid_rows, height, mp_size, grid_columns, width)
    grid = jnp.transpose(grid, (1, 4, 3, 0, 2, 5))
    parts = grid.reshape(dp_size, mp_size, members, height, width)
    return from_piece(scatter_all(parts).astype(F32), rows, columns)


def grad_by_rows(matrix, master, group_rows, dp_size, mp_size):
    rows, columns, grid_rows, grid_columns = piece_shape(master.shape, group_rows, dp_size)
    height, width = rows * master.shape[-2], columns * master.shape[-1]
    grid = matrix.reshape(mp_size, grid_rows, height, grid_columns, width)
    grid = jnp.transpose(grid, (1, 3, 0, 2, 4))
    parts = grid.reshape(dp_size, mp_size, height, width)
    return from_piece(scatter_all(parts).astype(F32), rows, columns)


def exchanges():
    for axis in ("dp", "mp"):
        size = lax.axis_size(axis)
        step = 1
        while step < size:
            yield axis, [(i, i ^ step) for i in range(size)]
            step *= 2


def gather_small(values):
    for axis, pairs in exchanges():
        values = jnp.concatenate([values, lax.ppermute(values, axis, pairs)], axis=0)
    return values


def sum_small(values):
    for axis, pairs in exchanges():
        values = values + lax.ppermute(values, axis, pairs)
    return values


def fill_bias(bias_ref, query_labels, key_labels, tile, tile_count, history):
    for t in range(tile_count):
        span = SPAN + tile
        key_pos = lax.broadcasted_iota(jnp.int32, (span, tile), 0) + (history - SPAN + t * tile)
        query_pos = lax.broadcasted_iota(jnp.int32, (span, tile), 1) + (history + t * tile)
        same = key_labels[pl.ds(history - SPAN + t * tile, span), :] == query_labels[:, pl.ds(t * tile, tile)]
        bias_ref[t] = jnp.where(same & (key_pos <= query_pos), 0.0, MASKED)


def head_rows(values, head):
    row = lax.broadcasted_iota(jnp.int32, values.shape, 0)
    return jnp.where((row >= head * HD) & (row < (head + 1) * HD), values, jnp.zeros_like(values))


def head_lanes(values, head):
    lane = lax.broadcasted_iota(jnp.int32, values.shape, 1)
    return jnp.where((lane >= head * HD) & (lane < (head + 1) * HD), values, jnp.zeros_like(values))


def attend_kernel(tile, history, query_labels, key_labels, q_ref, k_ref, v_ref, o_ref, lse_ref, bias_ref, vt_ref):
    tile_count = q_ref.shape[0] // tile
    span = SPAN + tile

    @pl.when(pl.program_id(0) == 0)
    def _():
        fill_bias(bias_ref, query_labels, key_labels, tile, tile_count, history)

    vt_ref[...] = v_ref[...].T
    for t in range(tile_count):
        base = history - SPAN + t * tile
        queries = (q_ref[pl.ds(t * tile, tile), :] * HD ** (-0.5)).astype(BF16).T
        keys = k_ref[pl.ds(base, span), :]
        outputs = []
        for head in range(2):
            scores = (
                jnp.dot(keys, head_rows(queries, head), preferred_element_type=F32) + bias_ref[t]
            )
            maximum = jnp.max(scores, axis=0, keepdims=True)
            powers = jnp.exp(scores - maximum)
            total = jnp.sum(powers, axis=0, keepdims=True)
            attention = (powers * (1.0 / total)).astype(BF16)
            outputs.append(
                jnp.dot(
                    vt_ref[pl.ds(head * HD, HD), pl.ds(base, span)],
                    attention,
                    preferred_element_type=F32,
                )
            )
            lse_ref[0, pl.ds(head, 1), pl.ds(t * tile, tile)] = maximum + jnp.log(total)
        o_ref[pl.ds(t * tile, tile), :] = jnp.concatenate(outputs, axis=0).T.astype(BF16)


def attend_back_kernel(
    tile, history, query_labels, key_labels, q_ref, k_ref, v_ref, o_ref, do_ref, lse_ref,
    dq_ref, dk_ref, dv_ref, bias_ref, kt_ref, dk_acc, dv_acc,
):
    tile_count = q_ref.shape[0] // tile
    span = SPAN + tile

    @pl.when(pl.program_id(0) == 0)
    def _():
        fill_bias(bias_ref, query_labels, key_labels, tile, tile_count, history)

    kt_ref[...] = k_ref[...].T
    dk_acc[...] = jnp.zeros_like(dk_acc)
    dv_acc[...] = jnp.zeros_like(dv_acc)
    for t in range(tile_count):
        base = history - SPAN + t * tile
        scaled = (q_ref[pl.ds(t * tile, tile), :] * HD ** (-0.5)).astype(BF16)
        grads = do_ref[pl.ds(t * tile, tile), :]
        scaled_t, grads_t = scaled.T, grads.T
        product_t = grads_t.astype(F32) * o_ref[pl.ds(t * tile, tile), :].T.astype(F32)
        keys = k_ref[pl.ds(base, span), :]
        values = v_ref[pl.ds(base, span), :]
        grad_queries = []
        for head in range(2):
            scores = (
                jnp.dot(keys, head_rows(scaled_t, head), preferred_element_type=F32) + bias_ref[t]
            )
            attention = jnp.exp(scores - lse_ref[0, pl.ds(head, 1), pl.ds(t * tile, tile)])
            row_terms = jnp.sum(product_t[head * HD : (head + 1) * HD], axis=0, keepdims=True)
            grad_attention = jnp.dot(values, head_rows(grads_t, head), preferred_element_type=F32)
            grad_scores = (attention * (grad_attention - row_terms)).astype(BF16)
            dv_acc[pl.ds(base, span), :] += jnp.dot(
                attention.astype(BF16), head_lanes(grads, head), preferred_element_type=F32
            )
            dk_acc[pl.ds(base, span), :] += jnp.dot(
                grad_scores, head_lanes(scaled, head), preferred_element_type=F32
            )
            grad_queries.append(
                jnp.dot(
                    kt_ref[pl.ds(head * HD, HD), pl.ds(base, span)],
                    grad_scores,
                    preferred_element_type=F32,
                )
            )
        dq_ref[pl.ds(t * tile, tile), :] = (
            jnp.concatenate(grad_queries, axis=0).T * HD ** (-0.5)
        ).astype(BF16)
    dk_ref[...] = dk_acc[...].astype(BF16)
    dv_ref[...] = dv_acc[...].astype(BF16)


def attention_specs(count, window):
    whole = lambda shape: pl.BlockSpec(shape, lambda h: (0,) * len(shape))
    own = pl.BlockSpec((count, PAIR), lambda h: (0, h))
    seen = pl.BlockSpec((window, PAIR), lambda h: (0, h))
    sums = pl.BlockSpec((1, 2, count), lambda h: (h, 0, 0))
    labels = [whole((1, count)), whole((window, 1))]
    return labels, own, seen, sums


def attend(queries, keys, values, query_labels, key_labels, tile):
    count, width = queries.shape
    window = keys.shape[0]
    pairs = width // PAIR
    labels, own, seen, sums = attention_specs(count, window)
    work = 2 * count * (SPAN + tile) * width
    return pl.pallas_call(
        functools.partial(attend_kernel, tile, window - count),
        grid=(pairs,),
        in_specs=labels + [own, seen, seen],
        out_specs=[own, sums],
        out_shape=[
            jax.ShapeDtypeStruct((count, width), BF16),
            jax.ShapeDtypeStruct((pairs, 2, count), F32),
        ],
        scratch_shapes=[
            pltpu.VMEM((count // tile, SPAN + tile, tile), F32),
            pltpu.VMEM((PAIR, window), BF16),
        ],
        cost_estimate=pl.CostEstimate(
            flops=2 * work, bytes_accessed=4 * (window + count) * width, transcendentals=0
        ),
        name="attend",
    )(query_labels, key_labels, queries, keys, values)


def attend_back(queries, keys, values, context, grads, sums_in, query_labels, key_labels, tile):
    count, width = queries.shape
    window = keys.shape[0]
    pairs = width // PAIR
    labels, own, seen, sums = attention_specs(count, window)
    work = 2 * count * (SPAN + tile) * width
    return pl.pallas_call(
        functools.partial(attend_back_kernel, tile, window - count),
        grid=(pairs,),
        in_specs=labels + [own, seen, seen, own, own, sums],
        out_specs=[own, seen, seen],
        out_shape=[
            jax.ShapeDtypeStruct((count, width), BF16),
            jax.ShapeDtypeStruct((window, width), BF16),
            jax.ShapeDtypeStruct((window, width), BF16),
        ],
        scratch_shapes=[
            pltpu.VMEM((count // tile, SPAN + tile, tile), F32),
            pltpu.VMEM((PAIR, window), BF16),
            pltpu.VMEM((window, PAIR), F32),
            pltpu.VMEM((window, PAIR), F32),
        ],
        cost_estimate=pl.CostEstimate(
            flops=5 * work, bytes_accessed=8 * (window + count) * width, transcendentals=0
        ),
        name="attend_back",
    )(query_labels, key_labels, queries, keys, values, context, grads, sums_in)


def product(first, second):
    return jnp.einsum("...ij,...jk->...ik", first, second, precision=lax.Precision.HIGH)


def quarter_root(statistic):
    matrix_size = statistic.shape[-1]
    identity = jnp.eye(matrix_size, dtype=F32)
    frobenius = jnp.sqrt(jnp.sum(statistic * statistic, axis=(-2, -1), keepdims=True) + 1e-06)
    matrix = statistic / frobenius
    estimate = None
    for iteration in range(ROOTS):
        update = (5.0 * identity - matrix) * 0.25
        estimate = update if estimate is None else product(estimate, update)
        if iteration < ROOTS - 1:
            squared = product(update, update)
            matrix = product(product(squared, squared), matrix)
    return estimate * lax.rsqrt(jnp.sqrt(frobenius))


def shampoo(gradient, master, left_old, right_old, step_size):
    highest = lax.Precision.HIGH
    left_new = 0.5 * left_old + 0.5 * jnp.einsum(
        "...ij,...kj->...ik", gradient, gradient, precision=highest
    )
    right_new = 0.5 * right_old + 0.5 * jnp.einsum(
        "...ji,...jk->...ik", gradient, gradient, precision=highest
    )
    direction = product(product(quarter_root(left_new), gradient), quarter_root(right_new))
    return (master - step_size * direction, left_new, right_new)


def two_by_two(first, second):
    (a, b), (c, d) = first
    (e, f), (g, h) = second
    return ((a * e + b * g, a * f + b * h), (c * e + d * g, c * f + d * h))


def quarter_root_pair(statistic):
    entries = tuple(tuple(statistic[i, j] for j in range(2)) for i in range(2))
    frobenius = jnp.sqrt(sum(v * v for row in entries for v in row) + 1e-06)
    matrix = tuple(tuple(v / frobenius for v in row) for row in entries)
    estimate = ((1.0, 0.0), (0.0, 1.0))
    for iteration in range(ROOTS):
        (a, b), (c, d) = matrix
        update = (((5.0 - a) * 0.25, -b * 0.25), (-c * 0.25, (5.0 - d) * 0.25))
        estimate = two_by_two(estimate, update)
        squared = two_by_two(update, update)
        matrix = two_by_two(two_by_two(squared, squared), matrix)
    scale = lax.rsqrt(jnp.sqrt(frobenius))
    return tuple(tuple(v * scale for v in row) for row in estimate)


def gain_update(gradient, gain_rows, left_old, right_old):
    outer = jnp.sum(gradient[:, None, :] * gradient[None, :, :], axis=2)
    left_new = 0.5 * left_old + 0.5 * outer
    right_new = 0.5 * right_old + 0.5 * jnp.sum(gradient * gradient, axis=0)
    (a, b), (c, d) = quarter_root_pair(left_new)
    first, second = gradient[0], gradient[1]
    mixed = jnp.stack([a * first + b * second, c * first + d * second])
    direction = mixed * lax.rsqrt(jnp.sqrt(right_new))
    return (gain_rows - GAIN_RATE * direction, left_new, right_new)


def dot(first, second):
    return jnp.dot(first, second, preferred_element_type=F32)


def dot_back(first, second):
    return lax.dot_general(first, second, (((1,), (1,)), ((), ())), preferred_element_type=F32)


def dot_weight(first, second):
    return lax.dot_general(first, second, (((0,), (0,)), ((), ())), preferred_element_type=F32)


def body(
    patches,
    cotangent,
    lengths,
    hashes,
    segments,
    attend_master,
    output_master,
    expand_master,
    reduce_master,
    gains,
    attend_left,
    attend_right,
    output_left,
    output_right,
    expand_left,
    expand_right,
    reduce_left,
    reduce_right,
    gains_left,
    gains_right,
):
    dp_size, mp_size = lax.axis_size("dp"), lax.axis_size("mp")
    mp_index = lax.axis_index("mp")
    count = patches.shape[0]
    head_width, hidden_width = D // mp_size, FF // mp_size
    total_patches = count * dp_size * mp_size
    earlier = -(-(SPAN - 1) // count)
    history = earlier * count
    tile = min(256, count)

    attend_w = weight_by_columns(attend_master, dp_size)
    output_w = weight_by_rows(output_master, head_width, dp_size)
    expand_w = weight_by_columns(expand_master, dp_size)
    reduce_w = weight_by_rows(reduce_master, hidden_width, dp_size)

    stream = patches.astype(F32)
    first_rms = lax.rsqrt(jnp.mean(stream * stream, axis=1, keepdims=True) + EPSILON)
    first_hat = stream * first_rms
    first_normed = (first_hat * gains[0]).astype(BF16)
    up_one = [(i, i + 1) for i in range(mp_size - 1)]
    down_one = [(i + 1, i) for i in range(mp_size - 1)]
    shards = [first_normed]
    for _ in range(earlier):
        shards.insert(0, lax.ppermute(shards[0], "mp", up_one))
    window = jnp.concatenate(shards, axis=0)

    row_labels = segments.reshape(-1)
    padded = jnp.concatenate([jnp.full((history,), -1, jnp.int32), row_labels])
    key_labels = lax.dynamic_slice_in_dim(padded, mp_index * count, history + count, 0)
    query_labels = key_labels[history:].reshape(1, count)
    key_labels = key_labels.reshape(-1, 1)

    all_hashes = gather_small(hashes)
    own_counts = jnp.sum((hashes[:, None] == all_hashes[None, :]).astype(F32), axis=1)
    raw_weight = lengths.astype(F32) * lax.rsqrt(own_counts)
    raw_total = sum_small(jnp.sum(raw_weight).reshape(1, 1))
    patch_weight = raw_weight * (total_patches / raw_total[0, 0])
    grad_out = cotangent.astype(F32) * patch_weight[:, None]
    grad_low = grad_out.astype(BF16)

    queries = dot(first_normed, attend_w[0]).astype(BF16)
    keys = dot(window, attend_w[1]).astype(BF16)
    values = dot(window, attend_w[2]).astype(BF16)
    context, log_sums = attend(queries, keys, values, query_labels, key_labels, tile)
    middle = stream + dot(context, output_w)

    second_rms = lax.rsqrt(jnp.mean(middle * middle, axis=1, keepdims=True) + EPSILON)
    second_hat = middle * second_rms
    second_normed = (second_hat * gains[1]).astype(BF16)
    gate_pre = dot(second_normed, expand_w[0])
    up_pre = dot(second_normed, expand_w[1])
    gate_sig = jax.nn.sigmoid(gate_pre)
    hidden = (gate_pre * gate_sig * up_pre).astype(BF16)
    activations = (middle + dot(hidden, reduce_w)).astype(BF16)

    grad_hidden = dot_back(grad_low, reduce_w)
    grad_up = (grad_hidden * gate_pre * gate_sig).astype(BF16)
    grad_gate = (grad_hidden * up_pre * gate_sig * (1.0 + gate_pre * (1.0 - gate_sig))).astype(BF16)
    reduce_local = dot_weight(hidden, grad_low).astype(BF16)
    expand_local = jnp.stack(
        [dot_weight(second_normed, grad_gate), dot_weight(second_normed, grad_up)]
    ).astype(BF16)
    reduce_sum = grad_by_rows(reduce_local, reduce_master, hidden_width, dp_size, mp_size)
    expand_sum = grad_by_columns(expand_local, expand_master, dp_size, mp_size)

    second_back = dot_back(grad_gate, expand_w[0]) + dot_back(grad_up, expand_w[1])
    second_scaled = second_back * gains[1]
    gain_second = jnp.sum(second_back * second_hat, axis=0)
    middle_grad = grad_out + second_rms * (
        second_scaled - second_hat * jnp.mean(second_scaled * second_hat, axis=1, keepdims=True)
    )
    middle_low = middle_grad.astype(BF16)
    output_local = dot_weight(context, middle_low).astype(BF16)
    grad_context = dot_back(middle_low, output_w).astype(BF16)
    output_sum = grad_by_rows(output_local, output_master, head_width, dp_size, mp_size)

    grad_queries, grad_keys, grad_values = attend_back(
        queries, keys, values, context, grad_context, log_sums, query_labels, key_labels, tile
    )
    attend_local = jnp.stack(
        [
            dot_weight(first_normed, grad_queries),
            dot_weight(window, grad_keys),
            dot_weight(window, grad_values),
        ]
    ).astype(BF16)
    attend_sum = grad_by_columns(attend_local, attend_master, dp_size, mp_size)
    window_back = dot_back(grad_keys, attend_w[1]) + dot_back(grad_values, attend_w[2])
    own_back = window_back[history:] + dot_back(grad_queries, attend_w[0])
    gain_first = (
        jnp.sum(own_back * first_normed.astype(F32), axis=0)
        + jnp.sum(window_back[:history] * window[:history].astype(F32), axis=0)
    ) / gains[0]
    carried = None
    for k in range(earlier):
        share = window_back[k * count : (k + 1) * count]
        share = share if carried is None else share + carried
        carried = lax.ppermute(share.astype(BF16), "mp", down_one).astype(F32)
    first_back = own_back + carried
    first_scaled = first_back * gains[0]
    input_grad = middle_grad + first_rms * (
        first_scaled - first_hat * jnp.mean(first_scaled * first_hat, axis=1, keepdims=True)
    )

    grad_scale = total_patches ** (-0.5)
    gains_grad = sum_small(jnp.stack([gain_first, gain_second])) * grad_scale
    attend_grad = attend_sum * grad_scale
    output_grad = output_sum * grad_scale
    expand_grad = expand_sum * grad_scale
    reduce_grad = reduce_sum * grad_scale
    reduce_weight, left_reduce, right_reduce = shampoo(
        reduce_grad, reduce_master, reduce_left, reduce_right, STEP_RATE * FF ** (-0.5)
    )
    expand_weight, left_expand, right_expand = shampoo(
        expand_grad, expand_master, expand_left, expand_right, STEP_RATE * D ** (-0.5)
    )
    output_weight, left_output, right_output = shampoo(
        output_grad, output_master, output_left, output_right, STEP_RATE * OUT_FAN ** (-0.5)
    )
    attend_weight, left_attend, right_attend = shampoo(
        attend_grad, attend_master, attend_left, attend_right, STEP_RATE * D ** (-0.5)
    )
    gains_weight, left_gains, right_gains = gain_update(gains_grad, gains, gains_left, gains_right)
    return (
        activations,
        input_grad,
        attend_grad,
        attend_weight,
        left_attend,
        right_attend,
        output_grad,
        output_weight,
        left_output,
        right_output,
        expand_grad,
        expand_weight,
        left_expand,
        right_expand,
        reduce_grad,
        reduce_weight,
        left_reduce,
        right_reduce,
        gains_grad,
        gains_weight,
        left_gains,
        right_gains,
    )


def solution(mesh):
    rows = P(("dp", "mp"), None)
    single = P(("dp", "mp"), None, None)
    stacked = P(None, ("dp", "mp"), None, None)
    return jax.shard_map(
        body,
        mesh=mesh,
        in_specs=(
            rows,
            rows,
            P(("dp", "mp")),
            P(("dp", "mp")),
            P("dp", None),
            stacked,
            single,
            stacked,
            single,
            P(),
            stacked,
            stacked,
            single,
            single,
            stacked,
            stacked,
            single,
            single,
            P(),
            P(),
        ),
        out_specs=(
            rows,
            rows,
            stacked,
            stacked,
            stacked,
            stacked,
            single,
            single,
            single,
            single,
            stacked,
            stacked,
            stacked,
            stacked,
            single,
            single,
            single,
            single,
            P(),
            P(),
            P(),
            P(),
        ),
        check_vma=False,
    )
```

time: 1750 us -> 753 us (0.43)
  waiting for transfers between devices: 941 us -> 109 us
  matrix products: 472 us -> 238 us
  other arithmetic: 121 us -> 33.4 us
  Pallas kernels: 0 us -> 67.6 us
  starting transfers between devices: 0.54 us -> 42.5 us
  local copies, waits for them, and re-layouts: 126 us -> 160 us
    psum x2 -> x0, waiting for transfers between devices: 425 us -> none  [the longest x1 255 us: body(): lax.psum((to_blocks(attend_local, BLK, BLK), to_blocks(output_local, BLK,...]
    reduce_scatter x4 -> x8, waiting for transfers between devices: 351 us -> 23.5 us  [the longest x4 23.4 us: scatter_all(): return lax.psum_scatter(reduced, 'mp', scatter_dimension=0, tiled=False)]
    dot_general x247 -> x197, matrix products: 472 us -> 238 us  [the longest x168 109 us: product(): jnp.einsum('...ij,...jk->...ik', first, second, precision=lax.Precision.H...]
    all_gather x7 -> x5, waiting for transfers between devices: 165 us -> 18.2 us  [gather_all(): return lax.all_gather(lax.all_gather(piece, 'mp'), 'dp')]
    pallas_call x0 -> x2, Pallas kernels: none -> 67.6 us  [the longest x1 36.5 us: attend(): pl.pallas_call(functools.partial(attend_kernel, tile, window - count), gr...]
    ppermute x0 -> x19, waiting for transfers between devices: none -> 66.6 us  [the longest x2 40.4 us: body(): carried = lax.ppermute(share.astype(BF16), 'mp', down_one).astype(F32)]
    another operation x6 -> x15, local copies, waits for them, and re-layouts: 13.3 us -> 69.5 us  [the longest x4 44.8 us: body(): jnp.stack([dot_weight(second_normed, grad_gate), dot_weight(second_normed...]
    convert_element_type x15 -> x6, other arithmetic: 59 us -> 4.52 us  [the longest x2 1.42 us: weight_by_columns(): gathered = gather_all(to_piece(master.astype(BF16), rows, columns))]
  transfers between devices with their start and end apart: 13 -> 32, of which waited for: 9 -> 13; matrix products, arithmetic and copies ran while one was open for 21% -> 42% of each run, Pallas kernels for 0% -> 9%
where the time goes in v1:
time: 753 us; the launch traced here: 744 us
  matrix products  238 us (32%)
  local copies, waits for them, and re-layouts  160 us (21%)
  waiting for transfers between devices  109 us (14%)
  Pallas kernels  67.6 us (9%)
  blocking collectives  64.5 us (9%)
  starting transfers between devices  42.5 us (6%)
  other arithmetic  33.4 us (4%)
  between operations  29.3 us (4%)
    dot_general x168, matrix products, product(): jnp.einsum('...ij,...jk->...ik', first, second, precision=lax.Precision.H...  109 us
    all_gather x3, blocking collectives, gather_all(): return lax.all_gather(lax.all_gather(piece, 'mp'), 'dp')  64.5 us
    another operation x4, local copies, waits for them, and re-layouts, body(): jnp.stack([dot_weight(second_normed, grad_gate), dot_weight(second_normed...  44.8 us
    dot_general x7, matrix products, dot_weight(): lax.dot_general(first, second, (((0,), (0,)), ((), ())), preferred_elemen...  41.2 us
    dot_general x7, matrix products, dot_back(): lax.dot_general(first, second, (((1,), (1,)), ((), ())), preferred_elemen...  40.4 us
    ppermute x2, waiting for transfers between devices, body(): carried = lax.ppermute(share.astype(BF16), 'mp', down_one).astype(F32)  40.4 us
    dot_general x7, matrix products, dot(): return jnp.dot(first, second, preferred_element_type=F32)  37.1 us
    pallas_call x1, Pallas kernels, attend(): pl.pallas_call(functools.partial(attend_kernel, tile, window - count), gr...  36.5 us
  transfers between devices with their start and end apart: 32, of which 13 were waited for; matrix products, arithmetic and copies ran while one was open for 42% of the time, Pallas kernels for 9%

profile of v1, /device:TPU:0, one launch (start us, length us, event | category | flops | bytes accessed | tf_op | source)
XLA Modules:
  0.0 743.8 jit_solution(7524766974620181061)
XLA Ops:
  10.7 16.9 %all_gather.39 = bf16[4,64,512]{2,1,0:T(8,128)(2,1)} all-gather(bf16[1,64,512]{2,1,0:T(8,128)(2,1)S(1)} %all_gather_reshape.13), channel_id=1, replica_groups=mesh['dp'=8,'mp'=4] {'mp'}, dimensions={0}, use_global_device_ids=true | all-gather | bytes 327680 | tf_op jit(solution)/shard_map/all_gather | solution.py:55
  27.8 28.3 %all_gather.45 = bf16[4,176,512]{2,1,0:T(8,128)(2,1)} all-gather(bf16[1,176,512]{2,1,0:T(8,128)(2,1)S(1)} %copy.160), channel_id=1, replica_groups=mesh['dp'=8,'mp'=4] {'mp'}, dimensions={0}, use_global_device_ids=true | all-gather | bytes 901120 | tf_op jit(solution)/shard_map/all_gather | solution.py:55
  56.9 19.4 %all_gather.36 = bf16[4,3,128,256]{3,2,1,0:T(8,128)(2,1)} all-gather(bf16[1,3,128,256]{3,2,1,0:T(8,128)(2,1)S(1)} %all_gather_reshape.12), channel_id=1, replica_groups=mesh['dp'=8,'mp'=4] {'mp'}, dimensions={0}, use_global_device_ids=true | all-gather | bytes 983040 | tf_op jit(solution)/shard_map/all_gather | solution.py:55
  88.6 15.1 %collective-permute-done.5 = s32[4096]{0:T(1024)S(1)} collective-permute-done((s32[4096]{0:T(1024)S(1)}, s32[4096]{0:T(1024)S(1)}, u32[]{:S(2)}, u32[]{:S(2)}) %collective-permute-start.5) | collective-permute-done | bytes 16416 | tf_op jit(solution)/shard_map/ppermute | solution.py:111
  108.6 4.4 convert_reduce_fusion
  112.9 5.6 collective-permute-start.1
  130.2 8.9 %collective-permute-start.10 = (f32[1,1]{1,0:T(1,128)}, f32[1,1]{1,0:T(1,128)}, u32[]{:S(2)}, u32[]{:S(2)}) collective-permute-start(f32[1,1]{1,0:T(1,128)} %add.531), channel_id=1, source_target_pairs={{0,1},{1,0},{2,3},{3,2},{4,5},{5,4},{6,7},{7,6},{8,9},{9,8},{10,11... | collective-permute-start | bytes 20 | tf_op jit(solution)/shard_map/ppermute | solution.py:117
  139.8 3.9 collective-permute-start.11
  145.0 3.9 copy.156
  150.9 10.2 %copy.161 = bf16[4,4,176,2,512]{4,3,2,1,0:T(2,128)(2,1)S(1)} copy(bf16[4,4,176,2,512]{4,2,0,3,1:T(8,128)(2,1)} %bitcast.403) | data formatting | bytes 11534336 | tf_op jit(solution)/shard_map/transpose | solution.py:77
  161.1 4.4 copy.195
  165.5 18.1 %all-gather.12.cloned.1.call-done = bf16[32,3,128,256]{3,2,1,0:T(8,128)(2,1)} async-done(((bf16[4,3,128,256]{3,2,1,0:T(8,128)(2,1)}), bf16[32,3,128,256]{3,2,1,0:T(8,128)(2,1)}) %all-gather.12.cloned.1.call-update) | async-done | bytes 6291472 | tf_op jit(solution)/shard_map/all_gather | solution.py:55
  183.6 9.0 %copy.153 = bf16[8,1,4,3,128,256]{4,0,5,2,1,3:T(8,128)(2,1)} copy(bf16[8,1,4,3,128,256]{5,4,3,2,0,1:T(8,128)(2,1)} %bitcast.402) | data formatting | bytes 12582912 | tf_op jit(solution)/shard_map/reshape | solution.py:67
  192.7 4.1 fusion.387
  199.5 6.4 convolution_convert_fusion.3.v_ref
  205.9 6.3 convolution_convert_fusion.4.k_ref
  212.2 36.5 %attend.1 = (bf16[512,1024]{1,0:T(8,128)(2,1)}, f32[8,2,512]{2,1,0:T(2,128)}) custom-call(s32[1,512]{1,0:T(1,128)} %bitcast.447, s32[1536,1]{1,0:T(8,128)} %reshape.451.key_labels, bf16[512,1024]{1,0:T(8,128)(2,1)} %fusion.58.q_ref, bf16[1536,1024]{1,0:T(8,128)(2,1)} %convolution_convert_fusion.4.k_ref, bf16[1536,1024]{1,0:T(8,128)(2,1)} %convolution_convert_fusion.3.v_ref), custom_call_target="tpu_custom_call" | custom-call | flops 2684354560 | bytes 8388608 | tf_op jit(solution)/shard_map/attend/pallas_call | solution.py:239
  253.4 17.0 %copy.249 = bf16[8,1,4,2,128,704]{4,0,5,2,1,3:T(8,128)(2,1)S(1)} copy(bf16[8,1,4,2,128,704]{4,5,3,2,0,1:T(8,128)(2,1)} %bitcast.399) | data formatting | bytes 23068672 | tf_op jit(solution)/shard_map/reshape | solution.py:67
  271.6 5.0 fusion.2
  276.7 5.0 fusion.6
  281.7 10.7 %multiply_convert_fusion.1 = (bf16[512,2816]{1,0:T(8,128)(2,1)}, bf16[512,2816]{1,0:T(8,128)(2,1)}, bf16[512,2816]{1,0:T(8,128)(2,1)}) fusion(f32[512,2816]{1,0:T(8,128)} %fusion.6, f32[512,2816]{1,0:T(8,128)} %fusion.2, bf16[2816,1024]{1,0:T(8,128)(2,1)S(1)} %bitcast.407, bf16[512,1024]{1,0:T(8,128)(2,1)S(1)} %copy-done.29, f32[512]{0:T(512)S(1)} %broadcast_multiply_fusion), kind=kOutput, calls=%fused_computation.13 | convolution fusion | flops 2977431552 | bytes 27002880 | tf_op jit(solution)/shard_map/dot_general | solution.py:356
  292.3 6.8 fusion
  307.7 4.5 reshape.436
  315.7 7.9 %convolution_convert_fusion = bf16[2816,1024]{1,0:T(8,128)(2,1)} fusion(bf16[512,2816]{1,0:T(8,128)(2,1)} %get-tuple-element.151, bf16[512,1024]{1,0:T(8,128)(2,1)} %param.21, f32[512]{0:T(512)S(1)} %broadcast_multiply_fusion), kind=kOutput, calls=%fused_computation.16 | convolution fusion | flops 2957246464 | bytes 9701376 | tf_op jit(solution)/shard_map/dot_general | solution.py:360
  323.6 10.6 %reshape.439 = bf16[4,4,176,2,512]{4,3,2,1,0:T(2,128)(2,1)} reshape(bf16[2816,1024]{1,0:T(8,128)(2,1)} %convolution_convert_fusion) | data formatting | bytes 11534336 | tf_op jit(solution)/shard_map/reshape | solution.py:94
  334.2 6.4 copy.179
  344.6 31.1 %attend_back.1 = (bf16[512,1024]{1,0:T(8,128)(2,1)}, bf16[1536,1024]{1,0:T(8,128)(2,1)}, bf16[1536,1024]{1,0:T(8,128)(2,1)}) custom-call(s32[1,512]{1,0:T(1,128)} %bitcast.448, s32[1536,1]{1,0:T(8,128)} %reshape.451.key_labels, bf16[512,1024]{1,0:T(8,128)(2,1)} %fusion.58.q_ref, bf16[1536,1024]{1,0:T(8,128)(2,1)} %convolution_convert_fusion.4.k_ref, ...), custom_call_target="tpu_custom_call" | custom-call | flops 6710886400 | bytes 16777216 | tf_op jit(solution)/shard_map/attend_back/pallas_call | solution.py:265
  375.7 7.7 %convolution_convert_fusion.7 = bf16[1024,1024]{1,0:T(8,128)(2,1)} fusion(bf16[1536,1024]{1,0:T(8,128)(2,1)} %get-tuple-element.29, bf16[512,1024]{1,0:T(8,128)(2,1)} %copy-done.30, bf16[512,1024]{1,0:T(8,128)(2,1)} %copy-done.36, bf16[512,1024]{1,0:T(8,128)(2,1)} %collective-permute-done.1), kind=kOutput, calls=%fused_computation.87 | convolution fusion | flops 3231711232 | bytes 8388608 | tf_op jit(solution)/shard_map/dot_general | solution.py:360
  383.4 4.6 stack.34
  391.5 7.1 convolution_convert_fusion.6
  398.7 4.6 stack.35
  409.5 4.6 stack.33
  420.3 6.2 fusion.38
  431.5 25.8 %collective-permute-done.12 = bf16[512,1024]{1,0:T(8,128)(2,1)S(1)} collective-permute-done((bf16[512,1024]{1,0:T(8,128)(2,1)S(1)}, bf16[512,1024]{1,0:T(8,128)(2,1)S(1)}, u32[]{:S(2)}, u32[]{:S(2)}) %collective-permute-start.12) | collective-permute-done | bytes 1048608 | tf_op jit(solution)/shard_map/ppermute | solution.py:481
  460.1 8.4 %add_convert_fusion = bf16[512,1024]{1,0:T(8,128)(2,1)} fusion(f32[512,1024]{1,0:T(8,128)} %copy-done.9, bf16[512,2816]{1,0:T(8,128)(2,1)} %get-tuple-element.151, bf16[2816,1024]{1,0:T(8,128)(2,1)} %bitcast.404), kind=kOutput, calls=%fused_computation.82 | convolution fusion | flops 2953838592 | bytes 11796480 | tf_op jit(solution)/shard_map/dot_general | solution.py:352
  470.8 14.6 %collective-permute-done.13 = bf16[512,1024]{1,0:T(8,128)(2,1)} collective-permute-done((bf16[512,1024]{1,0:T(8,128)(2,1)}, bf16[512,1024]{1,0:T(8,128)(2,1)}, u32[]{:S(2)}, u32[]{:S(2)}) %collective-permute-start.13) | collective-permute-done | bytes 1048608 | tf_op jit(solution)/shard_map/ppermute | solution.py:481
  485.4 5.9 multiply_reduce_fusion.2
  491.4 5.1 convolution_convert_fusion.2
  498.1 7.9 %convolution_convert_fusion.1 = bf16[1024,2816]{1,0:T(8,128)(2,1)} fusion(bf16[512,1024]{1,0:T(8,128)(2,1)} %multiply_convert_fusion.3, bf16[512,2816]{1,0:T(8,128)(2,1)} %get-tuple-element.152), kind=kOutput, calls=%fused_computation.17 | convolution fusion | flops 2955673600 | bytes 9699328 | tf_op jit(solution)/shard_map/dot_general | solution.py:360
  506.0 14.0 %reshape.449 = bf16[1,8,128,4,1,704]{5,3,2,1,4,0:T(4,128)(2,1)} reshape(bf16[1024,2816]{1,0:T(8,128)(2,1)} %convolution_convert_fusion.2) | data formatting | bytes 11534336 | tf_op jit(solution)/shard_map/stack | solution.py:443
  520.0 8.4 %copy.187 = bf16[1,8,128,4,1,704]{2,1,5,3,4,0:T(8,128)(2,1)} copy(bf16[1,8,128,4,1,704]{5,3,2,1,4,0:T(4,128)(2,1)} %reshape.449) | data formatting | bytes 11534336 | tf_op jit(solution)/shard_map/stack | solution.py:443
  528.5 14.0 %reshape.450 = bf16[1,8,128,4,1,704]{5,3,2,1,4,0:T(4,128)(2,1)} reshape(bf16[1024,2816]{1,0:T(8,128)(2,1)} %convolution_convert_fusion.1) | data formatting | bytes 11534336 | tf_op jit(solution)/shard_map/stack | solution.py:443
  542.5 8.4 %copy.188 = bf16[1,8,128,4,1,704]{2,1,5,3,4,0:T(8,128)(2,1)} copy(bf16[1,8,128,4,1,704]{5,3,2,1,4,0:T(4,128)(2,1)} %reshape.450) | data formatting | bytes 11534336 | tf_op jit(solution)/shard_map/stack | solution.py:443
  551.9 6.1 maximum_bitcast_fusion
  558.0 6.1 copy.176
  570.5 4.8 fusion.34
  661.9 23.4 %reduce-scatter.19.cloned.1.call-done = bf16[1,2,128,704]{2,3,1,0:T(8,128)(2,1)} async-done(((bf16[4,2,128,704]{2,3,1,0:T(8,128)(2,1)}), bf16[1,2,128,704]{2,3,1,0:T(8,128)(2,1)}) %reduce-scatter.19.cloned.1.call-update) | async-done | bytes 360464 | tf_op jit(solution)/shard_map/reduce_scatter | solution.py:60
  688.1 4.0 multiply_reduce_fusion
  (469 shorter events, 216.4 us)
Async XLA Ops:
  7.2 20.5 %copy-start.21 = (f32[8,176,64]{1,2,0:T(8,128)S(1)}, f32[8,176,64]{1,2,0:T(8,128)}, u32[]{:S(2)}) copy-start(f32[8,176,64]{1,2,0:T(8,128)} %param.28) | copy-start | bytes 1081348
  7.2 69.2 %all-gather.10.cloned.1.call-start = ((), (), s32[]{:S(2)}) async-start(), calls=%async_computation.8 | async-start | bytes 1802240 | tf_op jit(solution)/shard_map/all_gather | solution.py:55
  9.4 46.8 %copy-start.14 = (f32[3,8,64,64]{3,2,1,0:T(8,128)S(1)}, f32[3,8,64,64]{3,2,1,0:T(8,128)}, u32[]{:S(2)}) copy-start(f32[3,8,64,64]{3,2,1,0:T(8,128)} %param.25) | copy-start | bytes 1179652
  10.4 134.7 %all-gather.14.cloned.1.call-start = ((), (), s32[]{:S(2)}) async-start(), calls=%async_computation.18 | async-start | bytes 2359296 | tf_op jit(solution)/shard_map/all_gather | solution.py:55
  27.6 123.2 %all-gather.18.cloned.1.call-start = ((), (), s32[]{:S(2)}) async-start(), calls=%async_computation.20 | async-start | bytes 6488064 | tf_op jit(solution)/shard_map/all_gather | solution.py:55
  56.2 20.8 %copy-start.55 = (s32[512]{0:T(512)S(1)}, s32[512]{0:T(512)}, u32[]{:S(2)}) copy-start(s32[512]{0:T(512)} %param.23) | copy-start | bytes 6148
  56.2 20.9 %copy-start.5 = (bf16[512,1024]{1,0:T(8,128)(2,1)S(1)}, bf16[512,1024]{1,0:T(8,128)(2,1)}, u32[]{:S(2)}) copy-start(bf16[512,1024]{1,0:T(8,128)(2,1)} %param.20) | copy-start | bytes 3145732
  56.2 127.4 %all-gather.12.cloned.1.call-start = ((), (), s32[]{:S(2)}) async-start(), calls=%async_computation.17 | async-start | bytes 7077888 | tf_op jit(solution)/shard_map/all_gather | solution.py:55
  56.3 21.0 %copy-start.52 = (f32[2,1024]{1,0:T(2,128)S(1)}, f32[2,1024]{1,0:T(2,128)}, u32[]{:S(2)}) copy-start(f32[2,1024]{1,0:T(2,128)} %param.29) | copy-start | bytes 24580
  76.3 177.1 %all-gather.16.cloned.1.call-start = ((), (), s32[]{:S(2)}) async-start(), calls=%async_computation.19 | async-start | bytes 12976128 | tf_op jit(solution)/shard_map/all_gather | solution.py:55
  76.4 42.2 %copy-start.57 = (s32[512]{0:T(512)S(1)}, s32[512]{0:T(512)}, u32[]{:S(2)}) copy-start(s32[512]{0:T(512)} %param.22) | copy-start | bytes 6148
  76.9 383.1 %reduce-scatter.13.cloned.1.call-start = ((), (), s32[]{:S(2)}) async-start(), calls=%async_computation.11 | async-start | bytes 2359296 | tf_op jit(solution)/shard_map/reduce_scatter | solution.py:59
  77.0 3.6 collective-permute-start.2
  77.7 128.2 %copy-start.30 = (bf16[512,1024]{1,0:T(8,128)(2,1)}, bf16[512,1024]{1,0:T(8,128)(2,1)S(1)}, u32[]{:S(2)}) copy-start(bf16[512,1024]{1,0:T(8,128)(2,1)S(1)} %fusion.30) | copy-start | bytes 3145732
  77.7 35.3 %collective-permute-start = (bf16[512,1024]{1,0:T(8,128)(2,1)S(1)}, bf16[512,1024]{1,0:T(8,128)(2,1)S(1)}, u32[]{:S(2)}, u32[]{:S(2)}) collective-permute-start(bf16[512,1024]{1,0:T(8,128)(2,1)S(1)} %fusion.30), channel_id=1, source_target_pairs={{0,1},{1,2},{2,3},{4,5},{5,6},{6,7},{8,9},{9,10},{10,11},{12,13},{... | collective-permute-start | bytes 3145736 | tf_op jit(solution)/shard_map/ppermute | solution.py:407
  80.5 3.7 collective-permute-start.3
  84.2 3.8 collective-permute-start.4
  88.0 15.7 %collective-permute-start.5 = (s32[4096]{0:T(1024)S(1)}, s32[4096]{0:T(1024)S(1)}, u32[]{:S(2)}, u32[]{:S(2)}) collective-permute-start(s32[4096]{0:T(1024)S(1)} %pad_add_fusion), channel_id=1, source_target_pairs={{0,1},{1,0},{2,3},{3,2},{4,5},{5,4},{6,7},{7,6},{8,9},{9,8},{10,11... | collective-permute-start | bytes 49160 | tf_op jit(solution)/shard_map/ppermute | solution.py:111
  103.7 4.8 collective-permute-start.6
  112.9 92.9 %copy-start.36 = (bf16[512,1024]{1,0:T(8,128)(2,1)}, bf16[512,1024]{1,0:T(8,128)(2,1)S(1)}, u32[]{:S(2)}) copy-start(bf16[512,1024]{1,0:T(8,128)(2,1)S(1)} %collective-permute-done) | copy-start | bytes 3145732
  112.9 86.6 %collective-permute-start.1 = (bf16[512,1024]{1,0:T(8,128)(2,1)S(1)}, bf16[512,1024]{1,0:T(8,128)(2,1)}, u32[]{:S(2)}, u32[]{:S(2)}) collective-permute-start(bf16[512,1024]{1,0:T(8,128)(2,1)S(1)} %collective-permute-done), channel_id=1, source_target_pairs={{0,1},{1,2},{2,3},{4,5},{5,6},{6,7},{8,9},{9,10},{10,11},{12,13},{... | collective-permute-start | bytes 3145736 | tf_op jit(solution)/shard_map/ppermute | solution.py:407
  119.1 1.2 collective-permute-start.7
  121.7 3.6 collective-permute-start.8
  126.0 3.6 collective-permute-start.9
  130.2 8.9 %collective-permute-start.10 = (f32[1,1]{1,0:T(1,128)}, f32[1,1]{1,0:T(1,128)}, u32[]{:S(2)}, u32[]{:S(2)}) collective-permute-start(f32[1,1]{1,0:T(1,128)} %add.531), channel_id=1, source_target_pairs={{0,1},{1,0},{2,3},{3,2},{4,5},{5,4},{6,7},{7,6},{8,9},{9,8},{10,11... | collective-permute-start | bytes 20 | tf_op jit(solution)/shard_map/ppermute | solution.py:117
  139.8 4.5 collective-permute-start.11
  252.0 47.1 %copy-start.9 = (f32[512,1024]{1,0:T(8,128)}, f32[512,1024]{1,0:T(8,128)S(1)}, u32[]{:S(2)}) copy-start(f32[512,1024]{1,0:T(8,128)S(1)} %get-tuple-element.193) | copy-start | bytes 6291460
  315.7 154.6 %reduce-scatter.21.cloned.1.call-start = ((), (), s32[]{:S(2)}) async-start(), calls=%async_computation.15 | async-start | bytes 6488064 | tf_op jit(solution)/shard_map/reduce_scatter | solution.py:59
  340.7 155.8 %reduce-scatter.9.cloned.1.call-start = ((), (), s32[]{:S(2)}) async-start(), calls=%async_computation.9 | async-start | bytes 7077888 | tf_op jit(solution)/shard_map/reduce_scatter | solution.py:59
  420.2 165.3 %reduce-scatter.15.cloned.1.call-start = ((), (), s32[]{:S(2)}) async-start(), calls=%async_computation.12 | async-start | bytes 327680 | tf_op jit(solution)/shard_map/reduce_scatter | solution.py:60
  430.0 28.7 %copy-start.7 = (f32[1536,1024]{1,0:T(8,128)}, f32[1536,1024]{1,0:T(8,128)S(1)}, u32[]{:S(2)}) copy-start(f32[1536,1024]{1,0:T(8,128)S(1)} %convolution_add_fusion) | copy-start | bytes 18874372
  430.2 27.1 %collective-permute-start.12 = (bf16[512,1024]{1,0:T(8,128)(2,1)S(1)}, bf16[512,1024]{1,0:T(8,128)(2,1)S(1)}, u32[]{:S(2)}, u32[]{:S(2)}) collective-permute-start(bf16[512,1024]{1,0:T(8,128)(2,1)S(1)} %slice.112), channel_id=1, source_target_pairs={{1,0},{2,1},{3,2},{5,4},{6,5},{7,6},{9,8},{10,9},{11,10},{13,12},{... | collective-permute-start | bytes 3145736 | tf_op jit(solution)/shard_map/ppermute | solution.py:481
  458.7 26.7 %collective-permute-start.13 = (bf16[512,1024]{1,0:T(8,128)(2,1)}, bf16[512,1024]{1,0:T(8,128)(2,1)}, u32[]{:S(2)}, u32[]{:S(2)}) collective-permute-start(bf16[512,1024]{1,0:T(8,128)(2,1)} %fusion.45), channel_id=1, source_target_pairs={{1,0},{2,1},{3,2},{5,4},{6,5},{7,6},{9,8},{10,9},{11,10},{13,12},{... | collective-permute-start | bytes 3145736 | tf_op jit(solution)/shard_map/ppermute | solution.py:481
  460.0 140.9 %reduce-scatter.23.cloned.1.call-start = ((), (), s32[]{:S(2)}) async-start(), calls=%async_computation.16 | async-start | bytes 901120 | tf_op jit(solution)/shard_map/reduce_scatter | solution.py:60
  470.3 21.0 %copy-start.53 = (f32[2,1024]{1,0:T(2,128)S(1)}, f32[2,1024]{1,0:T(2,128)}, u32[]{:S(2)}) copy-start(f32[2,1024]{1,0:T(2,128)} %param.29) | copy-start | bytes 24580
  470.3 160.6 %reduce-scatter.11.cloned.1.call-start = ((), (), s32[]{:S(2)}) async-start(), calls=%async_computation.10 | async-start | bytes 983040 | tf_op jit(solution)/shard_map/reduce_scatter | solution.py:60
  470.8 20.6 %copy-start.33 = (bf16[512,1024]{1,0:T(8,128)(2,1)S(1)}, bf16[512,1024]{1,0:T(8,128)(2,1)}, u32[]{:S(2)}) copy-start(bf16[512,1024]{1,0:T(8,128)(2,1)} %multiply_convert_fusion.3) | copy-start | bytes 3145732
  470.8 20.6 %copy-start.63 = (bf16[512,2816]{1,0:T(8,128)(2,1)S(1)}, bf16[512,2816]{1,0:T(8,128)(2,1)}, u32[]{:S(2)}) copy-start(bf16[512,2816]{1,0:T(8,128)(2,1)} %get-tuple-element.150) | copy-start | bytes 8650756
  491.3 5.2 collective-permute-start.14
  496.5 156.8 %reduce-scatter.17.cloned.1.call-start = ((), (), s32[]{:S(2)}) async-start(), calls=%async_computation.13 | async-start | bytes 12976128 | tf_op jit(solution)/shard_map/reduce_scatter | solution.py:59
  496.6 54.3 %collective-permute-start.15 = (f32[2,1024]{1,0:T(2,128)S(1)}, f32[2,1024]{1,0:T(2,128)S(1)}, u32[]{:S(2)}, u32[]{:S(2)}) collective-permute-start(f32[2,1024]{1,0:T(2,128)S(1)} %fusion.377), channel_id=1, source_target_pairs={{0,8},{4,12},{8,0},{12,4},{16,24},{20,28},{24,16},{28,20},{1,9},{5... | collective-permute-start | bytes 24584 | tf_op jit(solution)/shard_map/ppermute | solution.py:117
  550.9 13.5 %collective-permute-start.16 = (f32[2,1024]{1,0:T(2,128)S(1)}, f32[2,1024]{1,0:T(2,128)S(1)}, u32[]{:S(2)}, u32[]{:S(2)}) collective-permute-start(f32[2,1024]{1,0:T(2,128)S(1)} %fusion.705), channel_id=1, source_target_pairs={{0,16},{4,20},{8,24},{12,28},{16,0},{20,4},{24,8},{28,12},{1,17},{... | collective-permute-start | bytes 24584 | tf_op jit(solution)/shard_map/ppermute | solution.py:117
  564.2 121.2 %reduce-scatter.19.cloned.1.call-start = ((), (), s32[]{:S(2)}) async-start(), calls=%async_computation.14 | async-start | bytes 1802240 | tf_op jit(solution)/shard_map/reduce_scatter | solution.py:60
  564.4 3.7 collective-permute-start.17
  568.2 7.2 collective-permute-start.18
  602.1 26.8 %copy-start.2 = (f32[1,176,512]{1,2,0:T(8,128)}, f32[1,176,512]{1,2,0:T(8,128)S(1)}, u32[]{:S(2)}) copy-start(f32[1,176,512]{1,2,0:T(8,128)S(1)} %copy.180) | copy-start | bytes 1081348
  632.5 23.8 %copy-start.1 = (f32[3,2,4,64,64]{4,3,2,1,0:T(8,128)}, f32[3,2,4,64,64]{4,3,2,1,0:T(8,128)S(1)}, u32[]{:S(2)}) copy-start(f32[3,2,4,64,64]{4,3,2,1,0:T(8,128)S(1)} %copy.166) | copy-start | bytes 1179652
  688.1 44.6 %copy-start = (f32[2,2,4,64,176]{4,3,2,1,0:T(8,128)}, f32[2,2,4,64,176]{4,3,2,1,0:T(8,128)S(1)}, u32[]{:S(2)}) copy-start(f32[2,2,4,64,176]{4,3,2,1,0:T(8,128)S(1)} %copy.178) | copy-start | bytes 2162692
  (51 other events, 245.3 us)
Sparse Core Ops, SparseCore 0:
  10.5 51.3 all-gather.9
  63.8 27.2 all-gather.13
  93.0 43.3 all-gather.17
  138.1 45.5 all-gather.11
  185.4 67.6 all-gather.15
  315.8 41.2 reduce-scatter.12
  360.9 59.0 reduce-scatter.20
  423.4 61.7 reduce-scatter.8
  487.5 19.6 reduce-scatter.14
  509.3 21.0 reduce-scatter.22
  532.8 22.2 reduce-scatter.10
  564.3 85.4 reduce-scatter.16
  653.4 31.8 reduce-scatter.18

commit v2 on v1

--- a/solution.py
+++ b/solution.py
@@ -26,6 +26,10 @@
 PAIR = 2 * HD
 
 
+CHIPS = 4
+LANES = 128
+
+
 def piece_shape(blocked_shape, group_rows, dp_size):
     per_owner, height, width = blocked_shape[-3:]
     column_blocks = dp_size * per_owner // (group_rows // height)
@@ -51,6 +55,91 @@
     return jnp.swapaxes(grid, -3, -2).reshape(leading + (rows * columns, height, width))
 
 
+def rows_of_columns(piece):
+    return jnp.swapaxes(piece, -1, -2).reshape(-1, LANES)
+
+
+def columns_of_rows(rows, members):
+    return jnp.swapaxes(rows.reshape(members, -1, LANES), -1, -2)
+
+
+def rows_of_rows(piece):
+    height, width = piece.shape
+    return jnp.swapaxes(piece.reshape(height, width // LANES, LANES), 0, 1).reshape(-1, LANES)
+
+
+def rows_to_rows(rows, blocks):
+    grid = jnp.swapaxes(rows.reshape(blocks, -1, LANES), 0, 1)
+    return grid.reshape(grid.shape[0], blocks * LANES)
+
+
+def together(*values):
+    return lax.optimization_barrier(values)
+
+
+def pairwise(values, axis, step):
+    return lax.ppermute(values, axis, [(i, i ^ step) for i in range(lax.axis_size(axis))])
+
+
+def gather_sides(slices):
+    return pairwise(slices, "dp", 2), pairwise(slices, "dp", 4), pairwise(slices, "dp", 1)
+
+
+def gather_corner(across_x, across_y, other):
+    half = across_x.shape[1] // 2
+    return (
+        pairwise(across_y[:, :half], "dp", 2),
+        pairwise(across_x[:, half:], "dp", 4),
+        pairwise(across_x, "dp", 1),
+        pairwise(across_y, "dp", 1),
+    )
+
+
+def gather_end(slices, across_x, across_y, other, corner_x, corner_y, other_x, other_y):
+    corner = jnp.concatenate([corner_x, corner_y], axis=1)
+    return (
+        slices, across_x, across_y, corner, other, other_x, other_y, pairwise(corner, "dp", 1)
+    )
+
+
+def part_sum(own_core, received, chip, low, high):
+    return own_core[chip, :, low:high].astype(F32) + received[chip, :, low:high].astype(F32)
+
+
+def reduce_chips_corner(own_core, received):
+    half = own_core.shape[2] // 2
+    corner_x = pairwise(part_sum(own_core, received, 3, 0, half).astype(BF16), "dp", 2)
+    corner_y = pairwise(part_sum(own_core, received, 3, half, None).astype(BF16), "dp", 4)
+    return corner_x, corner_y
+
+
+def reduce_chips_sides(own_core, received, corner_x, corner_y):
+    half = own_core.shape[2] // 2
+    to_y = jnp.concatenate(
+        [
+            part_sum(own_core, received, 2, 0, half) + corner_x.astype(F32),
+            part_sum(own_core, received, 2, half, None),
+        ],
+        axis=1,
+    ).astype(BF16)
+    to_x = jnp.concatenate(
+        [
+            part_sum(own_core, received, 1, 0, half),
+            part_sum(own_core, received, 1, half, None) + corner_y.astype(F32),
+        ],
+        axis=1,
+    ).astype(BF16)
+    return pairwise(to_x, "dp", 2), pairwise(to_y, "dp", 4)
+
+
+def reduce_chips_own(own_core, received, from_x, from_y):
+    return part_sum(own_core, received, 0, 0, None) + from_x.astype(F32) + from_y.astype(F32)
+
+
+def coordinate(fast):
+    return lax.axis_index("dp").astype(jnp.int32).reshape(1) if fast else jnp.zeros((1,), jnp.int32)
+
+
 def gather_all(piece):
     return lax.all_gather(lax.all_gather(piece, "mp"), "dp")
 
@@ -63,7 +152,7 @@
 def weight_by_columns(master, dp_size):
     rows, columns, grid_rows, grid_columns = piece_shape(master.shape, D, dp_size)
     gathered = gather_all(to_piece(master.astype(BF16), rows, columns))
-    dp, mp, members, height, width = gathered.shape
+    mp, members, height, width = gathered.shape[1:]
     grid = gathered.reshape(grid_rows, grid_columns, mp, members, height, width)
     grid = jnp.transpose(grid, (3, 0, 4, 2, 1, 5))
     return grid.reshape(members, grid_rows * height, mp * grid_columns * width)
@@ -72,7 +161,7 @@
 def weight_by_rows(master, group_rows, dp_size):
     rows, columns, grid_rows, grid_columns = piece_shape(master.shape, group_rows, dp_size)
     gathered = gather_all(to_piece(master.astype(BF16), rows, columns))
-    dp, mp, height, width = gathered.shape
+    mp, height, width = gathered.shape[1:]
     grid = gathered.reshape(grid_rows, grid_columns, mp, height, width)
     grid = jnp.transpose(grid, (2, 0, 3, 1, 4))
     return grid.reshape(mp * grid_rows * height, grid_columns * width)
@@ -97,6 +186,238 @@
     return from_piece(scatter_all(parts).astype(F32), rows, columns)
 
 
+def cut_columns(matrices, mp_size):
+    members, _, width = matrices.shape
+    grid = matrices.reshape(members, CHIPS, 2, LANES, mp_size, width // mp_size)
+    return jnp.transpose(grid, (1, 2, 4, 0, 5, 3)).reshape(CHIPS, 2, mp_size, -1, LANES)
+
+
+def join_columns(pieces, members):
+    grid = pieces.reshape(pieces.shape[:3] + (members, -1, LANES))
+    return jnp.transpose(grid, (3, 0, 1, 5, 2, 4)).reshape(members, D, -1)
+
+
+def cut_rows(matrix, mp_size):
+    grid = matrix.reshape(mp_size, CHIPS, matrix.shape[0] // (mp_size * CHIPS), 2, D // (2 * LANES), LANES)
+    return jnp.transpose(grid, (1, 3, 0, 4, 2, 5)).reshape(CHIPS, 2, mp_size, -1, LANES)
+
+
+def join_rows(pieces):
+    grid = pieces.reshape(pieces.shape[:3] + (D // (2 * LANES), -1, LANES))
+    return jnp.transpose(grid, (2, 0, 4, 1, 3, 5)).reshape(-1, D)
+
+
+def lanes_of(device, relative):
+    return pl.ds(pl.multiple_of((device ^ relative) * LANES, LANES), LANES)
+
+
+def half_lanes(device, core, block):
+    start = ((device & 1) ^ core) * (D // 2) + block * LANES
+    return pl.ds(pl.multiple_of(start, LANES), LANES)
+
+
+def rows_at(device, chip, height):
+    return pl.ds(pl.multiple_of(((device >> 1) ^ chip) * height, 16), height)
+
+
+def join_attend_kernel(device_ref, *refs):
+    device = device_ref[0]
+    attend_ref, output_ref = refs[2 * CHIPS :]
+    height = attend_ref.shape[1]
+    for core in range(2):
+        for chip in range(CHIPS):
+            piece = refs[core * CHIPS + chip]
+            lanes = lanes_of(device, 2 * chip + core)
+            for member in range(3):
+                attend_ref[member, :, lanes] = piece[0, pl.ds(member * height, height), :]
+            rows = rows_at(device, chip, height // CHIPS)
+            for block in range(D // (2 * LANES)):
+                output_ref[rows, half_lanes(device, core, block)] = piece[
+                    0, pl.ds(3 * height + block * (height // CHIPS), height // CHIPS), :
+                ]
+
+
+def cut_attend_kernel(device_ref, query, key, value, output, first, second):
+    device = device_ref[0]
+    height = query.shape[0]
+    for core, pieces in enumerate((first, second)):
+        for chip in range(CHIPS):
+            lanes = lanes_of(device, 2 * chip + core)
+            for member, matrix in enumerate((query, key, value)):
+                pieces[chip, 0, pl.ds(member * height, height), :] = matrix[:, lanes]
+            rows = rows_at(device, chip, height // CHIPS)
+            for block in range(D // (2 * LANES)):
+                pieces[chip, 0, pl.ds(3 * height + block * (height // CHIPS), height // CHIPS), :] = (
+                    output[rows, half_lanes(device, core, block)]
+                )
+
+
+def grid_call(
+    kernel, grid, in_specs, out_specs, out_shape, name, scratch=(), cost=None, aliases=None
+):
+    return pl.pallas_call(
+        kernel,
+        grid_spec=pltpu.PrefetchScalarGridSpec(
+            num_scalar_prefetch=1,
+            grid=grid,
+            in_specs=in_specs,
+            out_specs=out_specs,
+            scratch_shapes=scratch,
+        ),
+        out_shape=out_shape,
+        input_output_aliases=aliases or {},
+        cost_estimate=cost,
+        name=name,
+    )
+
+
+def moved(count):
+    return pl.CostEstimate(flops=0, bytes_accessed=2 * count, transcendentals=0)
+
+
+def join_attend(device, pieces):
+    slices = pieces[0].shape[0]
+    height = D // slices
+    piece = pl.BlockSpec((1, 4 * height, LANES), lambda k, d: (k, 0, 0))
+    return grid_call(
+        join_attend_kernel,
+        (slices,),
+        [piece] * (2 * CHIPS),
+        [
+            pl.BlockSpec((3, height, D), lambda k, d: (0, k, 0)),
+            pl.BlockSpec((height, D), lambda k, d: (k, 0)),
+        ],
+        [jax.ShapeDtypeStruct((3, D, D), BF16), jax.ShapeDtypeStruct((D, D), BF16)],
+        "join_attend",
+        cost=moved(8 * D * D),
+    )(device, *pieces)
+
+
+def cut_attend(device, matrices, slices):
+    height = matrices[0].shape[0] // slices
+    matrix = pl.BlockSpec((height, D), lambda k, d: (k, 0))
+    piece = pl.BlockSpec((CHIPS, 1, 4 * height, LANES), lambda k, d: (0, k, 0, 0))
+    shape = jax.ShapeDtypeStruct((CHIPS, slices, 4 * height, LANES), BF16)
+    return grid_call(
+        cut_attend_kernel,
+        (slices,),
+        [matrix] * 4,
+        [piece, piece],
+        [shape, shape],
+        "cut_attend",
+        cost=moved(8 * slices * height * D),
+    )(device, *matrices)
+
+
+def hidden_kernel(
+    kept, device_ref, normed_ref, grads_ref, *refs
+):
+    parts = refs[: 6 * CHIPS]
+    result_ref, back_ref, first, second = refs[6 * CHIPS + kept : 6 * CHIPS + kept + 4]
+    (
+        normed_t, grads_t, w_gate, w_up, w_down, hidden_t, dgate_t, dup_t, moved_ref
+    ) = refs[6 * CHIPS + kept + 4 :]
+    device = device_ref[0]
+    width = w_gate.shape[0]
+    height = width // CHIPS
+    blocks = D // (2 * LANES)
+
+    @pl.when(pl.program_id(0) == 0)
+    def _():
+        normed_t[...] = normed_ref[...].T
+        grads_t[...] = grads_ref[...].T
+        result_ref[...] = jnp.zeros_like(result_ref)
+        back_ref[...] = jnp.zeros_like(back_ref)
+
+    for core in range(2):
+        for chip in range(CHIPS):
+            gate, up, down = parts[3 * (core * CHIPS + chip) : 3 * (core * CHIPS + chip + 1)]
+            lanes = lanes_of(device, 2 * chip + core)
+            w_gate[:, lanes] = gate[0]
+            w_up[:, lanes] = up[0]
+            for block in range(blocks):
+                w_down[rows_at(device, chip, height), half_lanes(device, core, block)] = down[
+                    0, pl.ds(block * height, height), :
+                ]
+
+    @pl.loop(0, CHIPS)
+    def _(j):
+        start = pl.multiple_of(j * height, 16)
+        rows = pl.ds(start, height)
+        gate_pre = jnp.dot(w_gate[rows, :], normed_t[...], preferred_element_type=F32)
+        up_pre = jnp.dot(w_up[rows, :], normed_t[...], preferred_element_type=F32)
+        grad_hidden = jnp.dot(w_down[rows, :], grads_t[...], preferred_element_type=F32)
+        sig = jax.nn.sigmoid(gate_pre)
+        silu = gate_pre * sig
+        hidden = (silu * up_pre).astype(BF16)
+        dup = (grad_hidden * silu).astype(BF16)
+        dgate = (grad_hidden * up_pre * sig * (1.0 + gate_pre * (1.0 - sig))).astype(BF16)
+        hidden_t[rows, :] = hidden
+        dup_t[rows, :] = dup
+        dgate_t[rows, :] = dgate
+
+        moved_ref[...] = jnp.dot(hidden, grads_ref[...], preferred_element_type=F32).astype(BF16)
+        chip = (device >> 1) ^ j
+        for core, pieces in enumerate((first, second)):
+            for block in range(blocks):
+                pieces[chip, 0, pl.ds(2 * width + block * height, height), :] = moved_ref[
+                    :, half_lanes(device, core, block)
+                ]
+        for member, values in enumerate((dgate, dup)):
+            moved_ref[...] = jnp.dot(values, normed_ref[...], preferred_element_type=F32).astype(BF16)
+            target = pl.ds(pl.multiple_of(member * width + start, 16), height)
+            for core, pieces in enumerate((first, second)):
+                for chip in range(CHIPS):
+                    pieces[chip, 0, target, :] = moved_ref[:, lanes_of(device, 2 * chip + core)]
+
+    tile = min(256, normed_ref.shape[0])
+    for t in range(normed_ref.shape[0] // tile):
+        rows = pl.ds(t * tile, tile)
+        result_ref[rows, :] += jnp.dot(
+            hidden_t[:, rows].T, w_down[...], preferred_element_type=F32
+        )
+        back_ref[rows, :] += jnp.dot(
+            dgate_t[:, rows].T, w_gate[...], preferred_element_type=F32
+        ) + jnp.dot(dup_t[:, rows].T, w_up[...], preferred_element_type=F32)
+
+
+def hidden_layer(device, normed, grads, pieces, width, start, slices, earlier=()):
+    count = normed.shape[0]
+    whole = pl.BlockSpec((count, D), lambda k, d: (0, 0))
+    piece = lambda part: pl.BlockSpec((1, width, LANES), lambda k, d: (start + k, part, 0))
+    out_piece = pl.BlockSpec((CHIPS, 1, 3 * width, LANES), lambda k, d: (0, start + k, 0, 0))
+    shape = jax.ShapeDtypeStruct((CHIPS, pieces[0].shape[0], 3 * width, LANES), BF16)
+    total = jax.ShapeDtypeStruct((count, D), F32)
+    first_kept = 3 + 6 * CHIPS
+    return grid_call(
+        functools.partial(hidden_kernel, len(earlier)),
+        (slices,),
+        [whole, whole]
+        + [piece(part) for part in range(3)] * (2 * CHIPS)
+        + [pl.BlockSpec(memory_space=pl.ANY)] * len(earlier),
+        [whole, whole, out_piece, out_piece],
+        [total, total, shape, shape],
+        "hidden_layer",
+        scratch=[
+            pltpu.VMEM((D, count), BF16),
+            pltpu.VMEM((D, count), BF16),
+            pltpu.VMEM((width, D), BF16),
+            pltpu.VMEM((width, D), BF16),
+            pltpu.VMEM((width, D), BF16),
+            pltpu.VMEM((width, count), BF16),
+            pltpu.VMEM((width, count), BF16),
+            pltpu.VMEM((width, count), BF16),
+            pltpu.VMEM((width // CHIPS, D), BF16),
+        ],
+        cost=pl.CostEstimate(
+            flops=18 * slices * width * D * count,
+            bytes_accessed=12 * slices * width * D,
+            transcendentals=0,
+        ),
+        aliases={first_kept + i: 2 + i for i in range(len(earlier))},
+    )(device, normed, grads, *[piece for piece in pieces for _ in range(3)], *earlier)
+
+
 def exchanges():
     for axis in ("dp", "mp"):
         size = lax.axis_size(axis)
@@ -106,6 +427,18 @@
             step *= 2
 
 
+def hash_rows(hashes):
+    digits = jnp.stack([hashes >> 14, (hashes >> 7) & 127, hashes & 127])
+    rows = digits.astype(BF16).reshape(-1, LANES)
+    return jnp.pad(rows, ((0, -rows.shape[0] % 32), (0, 0)))
+
+
+def rows_hash(rows, count):
+    used = 3 * count // LANES
+    digits = rows[..., :used, :].reshape(-1, 3, count).astype(F32)
+    return ((digits[:, 0] * 128.0 + digits[:, 1]) * 128.0 + digits[:, 2]).reshape(-1)
+
+
 def gather_small(values):
     for axis, pairs in exchanges():
         values = jnp.concatenate([values, lax.ppermute(values, axis, pairs)], axis=0)
@@ -137,7 +470,9 @@
     return jnp.where((lane >= head * HD) & (lane < (head + 1) * HD), values, jnp.zeros_like(values))
 
 
-def attend_kernel(tile, history, query_labels, key_labels, q_ref, k_ref, v_ref, o_ref, lse_ref, bias_ref, vt_ref):
+def attend_kernel(
+    tile, history, query_labels, key_labels, q_ref, k_ref, v_ref, o_ref, lse_ref, bias_ref, vt_ref
+):
     tile_count = q_ref.shape[0] // tile
     span = SPAN + tile
 
@@ -221,28 +556,30 @@
     dv_ref[...] = dv_acc[...].astype(BF16)
 
 
-def attention_specs(count, window):
+def attention_specs(count, window, start):
     whole = lambda shape: pl.BlockSpec(shape, lambda h: (0,) * len(shape))
-    own = pl.BlockSpec((count, PAIR), lambda h: (0, h))
-    seen = pl.BlockSpec((window, PAIR), lambda h: (0, h))
+    specs = []
+    for first in (start, 0):
+        own = pl.BlockSpec((count, PAIR), lambda h, first=first: (0, first + h))
+        seen = pl.BlockSpec((window, PAIR), lambda h, first=first: (0, first + h))
+        specs.append((own, seen))
     sums = pl.BlockSpec((1, 2, count), lambda h: (h, 0, 0))
     labels = [whole((1, count)), whole((window, 1))]
-    return labels, own, seen, sums
-
-
-def attend(queries, keys, values, query_labels, key_labels, tile):
-    count, width = queries.shape
-    window = keys.shape[0]
-    pairs = width // PAIR
-    labels, own, seen, sums = attention_specs(count, window)
-    work = 2 * count * (SPAN + tile) * width
+    return labels, specs[0], specs[1], sums
+
+
+def attend(inputs, tile, start, pairs):
+    _, _, queries, keys, _ = inputs
+    count, window = queries.shape[0], keys.shape[0]
+    labels, (own, seen), (own_out, _), sums = attention_specs(count, window, start)
+    work = 2 * count * (SPAN + tile) * PAIR * pairs
     return pl.pallas_call(
         functools.partial(attend_kernel, tile, window - count),
         grid=(pairs,),
         in_specs=labels + [own, seen, seen],
-        out_specs=[own, sums],
+        out_specs=[own_out, sums],
         out_shape=[
-            jax.ShapeDtypeStruct((count, width), BF16),
+            jax.ShapeDtypeStruct((count, pairs * PAIR), BF16),
             jax.ShapeDtypeStruct((pairs, 2, count), F32),
         ],
         scratch_shapes=[
@@ -250,27 +587,26 @@
             pltpu.VMEM((PAIR, window), BF16),
         ],
         cost_estimate=pl.CostEstimate(
-            flops=2 * work, bytes_accessed=4 * (window + count) * width, transcendentals=0
+            flops=4 * work, bytes_accessed=4 * (window + count) * PAIR * pairs, transcendentals=0
         ),
         name="attend",
-    )(query_labels, key_labels, queries, keys, values)
-
-
-def attend_back(queries, keys, values, context, grads, sums_in, query_labels, key_labels, tile):
-    count, width = queries.shape
-    window = keys.shape[0]
-    pairs = width // PAIR
-    labels, own, seen, sums = attention_specs(count, window)
-    work = 2 * count * (SPAN + tile) * width
+    )(*inputs)
+
+
+def attend_back(inputs, context, grads, log_sums, tile, start, pairs):
+    _, _, queries, keys, _ = inputs
+    count, window = queries.shape[0], keys.shape[0]
+    labels, (own, seen), (own_out, seen_out), sums = attention_specs(count, window, start)
+    work = 2 * count * (SPAN + tile) * PAIR * pairs
     return pl.pallas_call(
         functools.partial(attend_back_kernel, tile, window - count),
         grid=(pairs,),
-        in_specs=labels + [own, seen, seen, own, own, sums],
-        out_specs=[own, seen, seen],
+        in_specs=labels + [own, seen, seen, own_out, own, sums],
+        out_specs=[own_out, seen_out, seen_out],
         out_shape=[
-            jax.ShapeDtypeStruct((count, width), BF16),
-            jax.ShapeDtypeStruct((window, width), BF16),
-            jax.ShapeDtypeStruct((window, width), BF16),
+            jax.ShapeDtypeStruct((count, pairs * PAIR), BF16),
+            jax.ShapeDtypeStruct((window, pairs * PAIR), BF16),
+            jax.ShapeDtypeStruct((window, pairs * PAIR), BF16),
         ],
         scratch_shapes=[
             pltpu.VMEM((count // tile, SPAN + tile, tile), F32),
@@ -279,41 +615,207 @@
             pltpu.VMEM((window, PAIR), F32),
         ],
         cost_estimate=pl.CostEstimate(
-            flops=5 * work, bytes_accessed=8 * (window + count) * width, transcendentals=0
+            flops=10 * work, bytes_accessed=8 * (window + count) * PAIR * pairs, transcendentals=0
         ),
         name="attend_back",
-    )(query_labels, key_labels, queries, keys, values, context, grads, sums_in)
-
-
-def product(first, second):
-    return jnp.einsum("...ij,...jk->...ik", first, second, precision=lax.Precision.HIGH)
-
-
-def quarter_root(statistic):
-    matrix_size = statistic.shape[-1]
-    identity = jnp.eye(matrix_size, dtype=F32)
-    frobenius = jnp.sqrt(jnp.sum(statistic * statistic, axis=(-2, -1), keepdims=True) + 1e-06)
-    matrix = statistic / frobenius
-    estimate = None
-    for iteration in range(ROOTS):
-        update = (5.0 * identity - matrix) * 0.25
-        estimate = update if estimate is None else product(estimate, update)
-        if iteration < ROOTS - 1:
-            squared = product(update, update)
-            matrix = product(product(squared, squared), matrix)
-    return estimate * lax.rsqrt(jnp.sqrt(frobenius))
-
-
-def shampoo(gradient, master, left_old, right_old, step_size):
-    highest = lax.Precision.HIGH
-    left_new = 0.5 * left_old + 0.5 * jnp.einsum(
-        "...ij,...kj->...ik", gradient, gradient, precision=highest
+    )(*inputs, context, grads, log_sums)
+
+
+def project_back_kernel(first_own, *refs):
+    queries, keys, values = refs[0:2], refs[2:4], refs[4:6]
+    weights, normed, back_ref, gain_ref = refs[6:]
+    half = queries[0].shape[1]
+    tile = pl.program_id(0)
+    back = None
+    for member, parts in ((1, keys), (2, values)):
+        for i, part in enumerate(parts):
+            term = mxu(part[...], weights[member, pl.ds(i * half, half), :])
+            back = term if back is None else back + term
+    back_ref[...] = back
+
+    @pl.when(tile >= first_own)
+    def _():
+        back_ref[...] += mxu(queries[0][...], weights[0, pl.ds(0, half), :]) + mxu(
+            queries[1][...], weights[0, pl.ds(half, half), :]
+        )
+
+    @pl.when(tile == 0)
+    def _():
+        gain_ref[...] = jnp.zeros_like(gain_ref)
+
+    gain_ref[...] += jnp.sum(back_ref[...] * normed[...].astype(F32), axis=0, keepdims=True)
+
+
+def project_back(first, second, weights, window):
+    count, half = first[0].shape
+    rows = window.shape[0]
+    tile = min(256, count)
+    first_own = (rows - count) // tile
+    own = pl.BlockSpec((tile, half), lambda i: (jnp.maximum(i - first_own, 0), 0))
+    seen = pl.BlockSpec((tile, half), lambda i: (i, 0))
+    wide = pl.BlockSpec((tile, D), lambda i: (i, 0))
+    return pl.pallas_call(
+        functools.partial(project_back_kernel, first_own),
+        grid=(rows // tile,),
+        in_specs=[own, own, seen, seen, seen, seen, pl.BlockSpec((3, D, D), lambda i: (0, 0, 0)), wide],
+        out_specs=[wide, pl.BlockSpec((1, D), lambda i: (0, 0))],
+        out_shape=[jax.ShapeDtypeStruct((rows, D), F32), jax.ShapeDtypeStruct((1, D), F32)],
+        cost_estimate=pl.CostEstimate(
+            flops=2 * D * D * (2 * rows + count), bytes_accessed=12 * rows * D, transcendentals=0
+        ),
+        name="project_back",
+    )(first[0], second[0], first[1], second[1], first[2], second[2], weights, window)
+
+
+def split(values):
+    high = values.astype(BF16)
+    return high, (values - high.astype(F32)).astype(BF16)
+
+
+def dot_split(first, second, contract):
+    dims = ((contract, contract), ((), ()))
+    (a, b), (c, d) = split(first), split(second)
+    multiply = lambda x, y: lax.dot_general(x, y, dims, preferred_element_type=F32)
+    return multiply(a, c) + multiply(b, c) + multiply(a, d)
+
+
+def total_of(values):
+    return jnp.sum(jnp.sum(values, axis=0, keepdims=True), axis=1, keepdims=True)
+
+
+def mxu(first, second):
+    return jnp.dot(first, second, preferred_element_type=F32)
+
+
+class Chain:
+    def __init__(self, matrix, rows, spread):
+        self.matrix, self.rows, self.spread = matrix, rows, spread
+
+    def square(self):
+        self.low = self.matrix.astype(BF16)
+        height = self.rows.shape[0]
+        stacked = jnp.concatenate([self.rows.astype(BF16), self.low], axis=0)
+        both = mxu(stacked, self.spread(self.low))
+        self.rows = 1.25 * self.rows - 0.25 * both[:height]
+        self.rest = (0.0625 * both[height:] - 0.625 * self.low.astype(F32)).astype(BF16)
+
+    def half(self):
+        self.right = self.spread(self.rest)
+        self.matrix = 1.5625 * self.matrix + mxu(self.low, self.right)
+
+    def whole(self):
+        self.matrix = 1.5625 * self.matrix + mxu(self.matrix.astype(BF16), self.right)
+
+    def last(self):
+        self.rows = 1.25 * self.rows - 0.25 * mxu(
+            self.rows.astype(BF16), self.spread(self.matrix.astype(BF16))
+        )
+
+
+def run_chains(chains):
+    for _ in range(ROOTS - 1):
+        for chain in chains:
+            chain.square()
+        for chain in chains:
+            chain.half()
+        for chain in chains:
+            chain.whole()
+    for chain in chains:
+        chain.last()
+
+
+def quarter(norm):
+    return lax.rsqrt(jnp.sqrt(norm))
+
+
+def shampoo_kernel(
+    step_size, pack, grad_ref, master_ref, short_ref, long_ref, weight_ref, short_out, long_out
+):
+    blocks, short, width = grad_ref.shape
+    side = pack * short
+    row = lax.broadcasted_iota(jnp.int32, (side, side), 0)
+    lane = lax.broadcasted_iota(jnp.int32, (side, side), 1)
+    mask = jnp.where(lax.div(row, short) == lax.div(lane, short), 1.0, 0.0).astype(BF16)
+    eye = jnp.where(
+        lax.broadcasted_iota(jnp.int32, (short, side), 0)
+        == lax.rem(lax.broadcasted_iota(jnp.int32, (short, side), 1), short),
+        1.0,
+        0.0,
     )
-    right_new = 0.5 * right_old + 0.5 * jnp.einsum(
-        "...ji,...jk->...ik", gradient, gradient, precision=highest
-    )
-    direction = product(product(quarter_root(left_new), gradient), quarter_root(right_new))
-    return (master - step_size * direction, left_new, right_new)
+    spread = lambda values: jnp.concatenate([values] * pack, axis=0) * mask
+    beside = lambda values: jnp.concatenate(values, axis=1)
+    alone = lambda values: values
+    packed_long = width == short
+
+    shorts, longs, rows, scales = [], [], [], []
+    for b in range(blocks):
+        grad = grad_ref[b]
+        short_new = 0.5 * short_ref[b] + 0.5 * dot_split(grad, grad, (1,))
+        grad_t = grad.T
+        long_new = 0.5 * long_ref[b] + 0.5 * dot_split(grad_t, grad_t, (1,))
+        short_out[b] = short_new
+        long_out[b] = long_new
+        short_norm = jnp.sqrt(total_of(short_new * short_new) + 1e-06)
+        long_norm = jnp.sqrt(total_of(long_new * long_new) + 1e-06)
+        shorts.append(short_new / short_norm)
+        longs.append(long_new / long_norm)
+        rows.append(grad)
+        scales.append(step_size * quarter(short_norm) * quarter(long_norm))
+    groups = [range(i, i + pack) for i in range(0, blocks, pack)]
+    left = [Chain(beside([shorts[b] for b in g]), eye, spread) for g in groups]
+    if packed_long:
+        right = [
+            Chain(beside([longs[b] for b in g]), beside([rows[b] for b in g]), spread) for g in groups
+        ]
+    else:
+        right = [Chain(longs[b], rows[b], alone) for b in range(blocks)]
+    run_chains(left + right)
+    for i, g in enumerate(groups):
+        high, low = split(left[i].rows)
+        if packed_long:
+            second, second_low = split(right[i].rows)
+            second, second_low = spread(second), spread(second_low)
+            steps = mxu(high, second) + mxu(low, second) + mxu(high, second_low)
+            steps = [steps[:, j * short : (j + 1) * short] for j in range(pack)]
+        else:
+            second, second_low = split(jnp.concatenate([right[b].rows for b in g], axis=0))
+            high, low = spread(high), spread(low)
+            steps = mxu(high, second) + mxu(low, second) + mxu(high, second_low)
+            steps = [steps[j * short : (j + 1) * short] for j in range(pack)]
+        for b, step in zip(g, steps):
+            weight_ref[b] = master_ref[b] - scales[b] * step
+
+
+def shampoo(gradient, master, short_old, long_old, step_size, blocks):
+    count, short, width = gradient.shape
+    blocks = min(blocks, count)
+    pack = min(4, blocks)
+    spec = lambda *shape: pl.BlockSpec((blocks,) + shape, lambda i: (i, 0, 0))
+    specs = [spec(short, width), spec(short, short), spec(width, width)]
+    shape = lambda *dims: jax.ShapeDtypeStruct((count,) + dims, F32)
+    return pl.pallas_call(
+        functools.partial(shampoo_kernel, step_size, pack),
+        grid=(count // blocks,),
+        in_specs=specs[:1] + specs,
+        out_specs=specs,
+        out_shape=[shape(short, width), shape(short, short), shape(width, width)],
+        cost_estimate=pl.CostEstimate(
+            flops=40 * count * width * width * width,
+            bytes_accessed=8 * count * (width * width + short * short + 2 * short * width),
+            transcendentals=0,
+        ),
+        name="shampoo",
+    )(gradient, master, short_old, long_old)
+def step_rows(gradient, master, left, right, step_size, blocks):
+    flat = lambda values: values.reshape((-1,) + values.shape[-2:])
+    outs = shampoo(flat(gradient), flat(master), flat(left), flat(right), step_size, blocks)
+    return tuple(v.reshape(gradient.shape[:-2] + v.shape[-2:]) for v in outs)
+
+
+def step_columns(gradient, master, left, right, step_size, blocks):
+    turn = lambda values: jnp.swapaxes(values, -1, -2)
+    weight, right, left = shampoo(turn(gradient), turn(master), right, left, step_size, blocks)
+    return turn(weight), left, right
 
 
 def two_by_two(first, second):
@@ -386,122 +888,327 @@
     mp_index = lax.axis_index("mp")
     count = patches.shape[0]
     head_width, hidden_width = D // mp_size, FF // mp_size
+    head_rows_width = head_width // CHIPS
     total_patches = count * dp_size * mp_size
     earlier = -(-(SPAN - 1) // count)
     history = earlier * count
     tile = min(256, count)
-
-    attend_w = weight_by_columns(attend_master, dp_size)
-    output_w = weight_by_rows(output_master, head_width, dp_size)
-    expand_w = weight_by_columns(expand_master, dp_size)
-    reduce_w = weight_by_rows(reduce_master, hidden_width, dp_size)
+    fast = dp_size == 2 * CHIPS and mp_size == 4
+    device = coordinate(fast)
+    grids = {
+        name: piece_shape(master.shape, rows, dp_size)
+        for name, master, rows in (
+            ("attend", attend_master, D),
+            ("output", output_master, head_width),
+            ("expand", expand_master, D),
+            ("reduce", reduce_master, hidden_width),
+        )
+    }
 
     stream = patches.astype(F32)
     first_rms = lax.rsqrt(jnp.mean(stream * stream, axis=1, keepdims=True) + EPSILON)
     first_hat = stream * first_rms
     first_normed = (first_hat * gains[0]).astype(BF16)
-    up_one = [(i, i + 1) for i in range(mp_size - 1)]
-    down_one = [(i + 1, i) for i in range(mp_size - 1)]
-    shards = [first_normed]
-    for _ in range(earlier):
-        shards.insert(0, lax.ppermute(shards[0], "mp", up_one))
-    window = jnp.concatenate(shards, axis=0)
 
     row_labels = segments.reshape(-1)
     padded = jnp.concatenate([jnp.full((history,), -1, jnp.int32), row_labels])
     key_labels = lax.dynamic_slice_in_dim(padded, mp_index * count, history + count, 0)
     query_labels = key_labels[history:].reshape(1, count)
     key_labels = key_labels.reshape(-1, 1)
-
-    all_hashes = gather_small(hashes)
-    own_counts = jnp.sum((hashes[:, None] == all_hashes[None, :]).astype(F32), axis=1)
-    raw_weight = lengths.astype(F32) * lax.rsqrt(own_counts)
-    raw_total = sum_small(jnp.sum(raw_weight).reshape(1, 1))
-    patch_weight = raw_weight * (total_patches / raw_total[0, 0])
-    grad_out = cotangent.astype(F32) * patch_weight[:, None]
+    up_one = [(i, i + 1) for i in range(mp_size - 1)]
+    down_one = [(i + 1, i) for i in range(mp_size - 1)]
+    half_pairs = HEADS * HD // PAIR // 2
+
+    def count_own(all_hashes):
+        own = hashes.astype(F32)
+        return jnp.sum((own[:, None] == all_hashes[None, :]).astype(F32), axis=1)
+
+    def halo(values):
+        return lax.ppermute(values, "mp", up_one)
+
+    if fast:
+        attend_rows = jnp.concatenate(
+            [
+                rows_of_columns(to_piece(attend_master.astype(BF16), *grids["attend"][:2])),
+                rows_of_rows(to_piece(output_master.astype(BF16), *grids["output"][:2])),
+                hash_rows(hashes),
+            ]
+        )
+        slice_two = pairwise(attend_rows, "mp", 2)
+        slice_one = pairwise(attend_rows, "mp", 1)
+        halo_source, slice_two = together(first_normed, slice_two)
+        slice_three = pairwise(slice_two, "mp", 1)
+        near_halo = halo(halo_source)
+        attend_slices = jnp.stack([attend_rows, slice_one, slice_two, slice_three])
+        sides = gather_sides(attend_slices)
+        near_halo, sides = together(near_halo, sides)
+        corners = gather_corner(*sides)
+        shards = [near_halo, first_normed]
+        for _ in range(earlier - 1):
+            shards.insert(0, halo(shards[0]))
+        shards[0], corners = together(shards[0], corners)
+        attend_pieces = gather_end(attend_slices, *sides, *corners)
+        window = jnp.concatenate(shards, axis=0)
+        all_hashes = jnp.concatenate(
+            [rows_hash(piece[:, 4 * head_width :], count) for piece in attend_pieces]
+        )
+    else:
+        attend_cut = jnp.concatenate(
+            [
+                cut_columns(weight_by_columns(attend_master, dp_size), mp_size),
+                cut_rows(weight_by_rows(output_master, head_width, dp_size), mp_size),
+            ],
+            axis=3,
+        )
+        attend_pieces = [attend_cut[chip, core] for core in range(2) for chip in range(CHIPS)]
+        hidden_cut = jnp.concatenate(
+            [
+                cut_columns(weight_by_columns(expand_master, dp_size), mp_size),
+                cut_rows(weight_by_rows(reduce_master, hidden_width, dp_size), mp_size),
+            ],
+            axis=3,
+        )
+        near_pieces, far_pieces = (
+            [hidden_cut[chip, core, k : k + 2] for core in range(2) for chip in range(CHIPS)]
+            for k in (0, 2)
+        )
+        shards = [first_normed]
+        for _ in range(earlier):
+            shards.insert(0, halo(shards[0]))
+        window = jnp.concatenate(shards, axis=0)
+        all_hashes = gather_small(hashes).astype(F32)
+
+    raw_weight = lengths.astype(F32) * lax.rsqrt(count_own(all_hashes))
+    raw_total = jnp.sum(raw_weight).reshape(1, 1)
+    steps = list(exchanges())
+    grad_out = cotangent.astype(F32) * raw_weight[:, None]
     grad_low = grad_out.astype(BF16)
 
-    queries = dot(first_normed, attend_w[0]).astype(BF16)
-    keys = dot(window, attend_w[1]).astype(BF16)
-    values = dot(window, attend_w[2]).astype(BF16)
-    context, log_sums = attend(queries, keys, values, query_labels, key_labels, tile)
-    middle = stream + dot(context, output_w)
+    if fast:
+        hidden_rows = jnp.concatenate(
+            [
+                rows_of_columns(to_piece(expand_master.astype(BF16), *grids["expand"][:2])),
+                rows_of_rows(to_piece(reduce_master.astype(BF16), *grids["reduce"][:2])),
+            ]
+        )
+        window, hidden_rows = together(window, hidden_rows)
+        slice_one = pairwise(hidden_rows, "mp", 1)
+        slice_two = pairwise(hidden_rows, "mp", 2)
+    attend_w, output_w = join_attend(device, attend_pieces)
+    queries = dot_back(first_normed, attend_w[0]).astype(BF16)
+    keys = dot_back(window, attend_w[1]).astype(BF16)
+    values = dot_back(window, attend_w[2]).astype(BF16)
+    labels = (query_labels, key_labels)
+    if fast:
+        queries, slice_one = together(queries, slice_one)
+        near = jnp.stack([hidden_rows, slice_one])
+        sides = gather_sides(near)
+    inputs = labels + (queries, keys, values)
+    context_a, sums_a = attend(inputs, tile, 0, half_pairs)
+    if fast:
+        queries, context_a, sides, slice_two = together(queries, context_a, sides, slice_two)
+        inputs = labels + (queries, keys, values)
+        corners = gather_corner(*sides)
+        slice_three = pairwise(slice_two, "mp", 1)
+        moved = lax.ppermute(raw_total, *steps[0])
+    context_b, sums_b = attend(inputs, tile, half_pairs, half_pairs)
+    if fast:
+        context_b, corners, slice_three, moved = together(context_b, corners, slice_three, moved)
+        raw_total = raw_total + moved
+        moved = lax.ppermute(raw_total, *steps[1])
+        near_pieces = gather_end(near, *sides, *corners)
+        far = jnp.stack([slice_two, slice_three])
+        sides = gather_sides(far)
+    half = context_a.shape[1]
+    middle = stream + dot(context_a, output_w[:half]) + dot(context_b, output_w[half:])
 
     second_rms = lax.rsqrt(jnp.mean(middle * middle, axis=1, keepdims=True) + EPSILON)
     second_hat = middle * second_rms
     second_normed = (second_hat * gains[1]).astype(BF16)
-    gate_pre = dot(second_normed, expand_w[0])
-    up_pre = dot(second_normed, expand_w[1])
-    gate_sig = jax.nn.sigmoid(gate_pre)
-    hidden = (gate_pre * gate_sig * up_pre).astype(BF16)
-    activations = (middle + dot(hidden, reduce_w)).astype(BF16)
-
-    grad_hidden = dot_back(grad_low, reduce_w)
-    grad_up = (grad_hidden * gate_pre * gate_sig).astype(BF16)
-    grad_gate = (grad_hidden * up_pre * gate_sig * (1.0 + gate_pre * (1.0 - gate_sig))).astype(BF16)
-    reduce_local = dot_weight(hidden, grad_low).astype(BF16)
-    expand_local = jnp.stack(
-        [dot_weight(second_normed, grad_gate), dot_weight(second_normed, grad_up)]
-    ).astype(BF16)
-    reduce_sum = grad_by_rows(reduce_local, reduce_master, hidden_width, dp_size, mp_size)
-    expand_sum = grad_by_columns(expand_local, expand_master, dp_size, mp_size)
-
-    second_back = dot_back(grad_gate, expand_w[0]) + dot_back(grad_up, expand_w[1])
+    if fast:
+        second_normed, near_pieces, moved = together(second_normed, near_pieces, moved)
+        raw_total = raw_total + moved
+        moved = lax.ppermute(raw_total, *steps[2])
+        share_a = hidden_layer(device, second_normed, grad_low, near_pieces, hidden_width, 0, 1)
+        share_a, sides, moved = together(share_a, sides, moved)
+        raw_total = raw_total + moved
+        moved = lax.ppermute(raw_total, *steps[3])
+        corners = gather_corner(*sides)
+        share_b = hidden_layer(
+            device, second_normed, grad_low, near_pieces, hidden_width, 1, 1, share_a[2:]
+        )
+        share_b, corners, moved = together(share_b, corners, moved)
+        raw_total = raw_total + moved
+        moved = lax.ppermute(raw_total, *steps[4])
+        far_pieces = gather_end(far, *sides, *corners)
+        near_grads = share_b[2:]
+        near_received = pairwise(near_grads[1], "dp", 1)
+        share_c = hidden_layer(device, second_normed, grad_low, far_pieces, hidden_width, 0, 2)
+        share_c, near_received, moved = together(share_c, near_received, moved)
+        raw_total = raw_total + moved
+        far_grads = share_c[2:]
+        far_received = pairwise(far_grads[1], "dp", 1)
+        near_corners = reduce_chips_corner(near_grads[0], near_received)
+        second_back = share_a[1] + share_b[1] + share_c[1]
+        activations = (middle + share_a[0] + share_b[0] + share_c[0]).astype(BF16)
+    else:
+        share_a = hidden_layer(device, second_normed, grad_low, near_pieces, hidden_width, 0, 2)
+        share_c = hidden_layer(device, second_normed, grad_low, far_pieces, hidden_width, 0, 2)
+        near_grads, far_grads = share_a[2:], share_c[2:]
+        raw_total = sum_small(raw_total)
+        second_back = share_a[1] + share_c[1]
+        activations = (middle + share_a[0] + share_c[0]).astype(BF16)
+
+    weight_scale = total_patches / raw_total[0, 0]
+
     second_scaled = second_back * gains[1]
     gain_second = jnp.sum(second_back * second_hat, axis=0)
     middle_grad = grad_out + second_rms * (
         second_scaled - second_hat * jnp.mean(second_scaled * second_hat, axis=1, keepdims=True)
     )
     middle_low = middle_grad.astype(BF16)
-    output_local = dot_weight(context, middle_low).astype(BF16)
     grad_context = dot_back(middle_low, output_w).astype(BF16)
-    output_sum = grad_by_rows(output_local, output_master, head_width, dp_size, mp_size)
-
-    grad_queries, grad_keys, grad_values = attend_back(
-        queries, keys, values, context, grad_context, log_sums, query_labels, key_labels, tile
+
+    def weight_grads(context_part, parts):
+        grad_queries, grad_keys, grad_values = parts
+        return [
+            dot_weight(grad_queries, first_normed).astype(BF16),
+            dot_weight(grad_keys, window).astype(BF16),
+            dot_weight(grad_values, window).astype(BF16),
+            dot_weight(context_part, middle_low).astype(BF16),
+        ]
+
+    slices_half = mp_size // 2
+    if fast:
+        grad_context, near_corners, far_received = together(grad_context, near_corners, far_received)
+        near_sides = reduce_chips_sides(near_grads[0], near_received, *near_corners)
+        far_corners = reduce_chips_corner(far_grads[0], far_received)
+    backs_a = attend_back(inputs, context_a, grad_context, sums_a, tile, 0, half_pairs)
+    cut_a = cut_attend(device, weight_grads(context_a, backs_a), slices_half)
+    if fast:
+        received_a = pairwise(cut_a[1], "dp", 1)
+        grad_context, cut_a, near_sides, far_corners = together(
+            grad_context, cut_a, near_sides, far_corners
+        )
+        near_own = reduce_chips_own(near_grads[0], near_received, *near_sides)
+        near_one = pairwise(near_own[1].astype(BF16), "mp", 1)
+        far_sides = reduce_chips_sides(far_grads[0], far_received, *far_corners)
+    backs_b = attend_back(inputs, context_b, grad_context, sums_b, tile, half_pairs, half_pairs)
+    if fast:
+        backs_b, far_sides, received_a = together(backs_b, far_sides, received_a)
+        far_own = reduce_chips_own(far_grads[0], far_received, *far_sides)
+        far_three = pairwise(far_own[1].astype(BF16), "mp", 1)
+        corners_a = reduce_chips_corner(cut_a[0], received_a)
+    cut_b = cut_attend(device, weight_grads(context_b, backs_b), slices_half)
+    if fast:
+        received_b = pairwise(cut_b[1], "dp", 1)
+        backs_b, cut_b, corners_a, far_three, near_one = together(
+            backs_b, cut_b, corners_a, far_three, near_one
+        )
+        far_two = pairwise((far_own[0] + far_three.astype(F32)).astype(BF16), "mp", 2)
+        sides_a = reduce_chips_sides(cut_a[0], received_a, *corners_a)
+    window_back, gain_first = project_back(backs_a, backs_b, attend_w, window)
+    gain_sums = jnp.stack([gain_first[0] / gains[0], gain_second])
+
+    def halo_back(share):
+        return lax.ppermute(share.astype(BF16), "mp", down_one)
+
+    shares = [window_back[k * count : (k + 1) * count] for k in range(earlier)]
+    if fast:
+        window_back, received_b, sides_a = together(window_back, received_b, sides_a)
+        shares = [window_back[k * count : (k + 1) * count] for k in range(earlier)]
+        carried = halo_back(shares[0])
+        corners_b = reduce_chips_corner(cut_b[0], received_b)
+        own_a = reduce_chips_own(cut_a[0], received_a, *sides_a)
+        one_a = pairwise(own_a[1].astype(BF16), "mp", 1)
+        moved = lax.ppermute(gain_sums, *steps[0])
+    else:
+        carried = halo_back(shares[0])
+        for share in shares[1:]:
+            carried = halo_back(share + carried.astype(F32))
+        gain_sums = sum_small(gain_sums)
+    grad_scale = weight_scale * total_patches ** (-0.5)
+    reduce_step, expand_step = STEP_RATE * FF ** (-0.5), STEP_RATE * D ** (-0.5)
+    if fast:
+        hidden_sum = near_own[0] + near_one.astype(F32) + far_two.astype(F32)
+        hidden_sum = hidden_sum * grad_scale
+        expand_grad = from_piece(
+            columns_of_rows(hidden_sum[: 2 * hidden_width], 2), *grids["expand"][:2]
+        )
+        reduce_grad = from_piece(
+            rows_to_rows(hidden_sum[2 * hidden_width : 3 * hidden_width], D // (2 * LANES)),
+            *grids["reduce"][:2]
+        )
+        reduce_grad, expand_grad, corners_b, moved = together(
+            reduce_grad, expand_grad, corners_b, moved
+        )
+        gain_sums = gain_sums + moved
+        moved = lax.ppermute(gain_sums, *steps[1])
+        sides_b = reduce_chips_sides(cut_b[0], received_b, *corners_b)
+        reduce_out = step_columns(reduce_grad, reduce_master, reduce_left, reduce_right, reduce_step, 4)
+        reduce_out, expand_grad, sides_b, carried, one_a, moved = together(
+            reduce_out, expand_grad, sides_b, carried, one_a, moved
+        )
+        gain_sums = gain_sums + moved
+        moved = lax.ppermute(gain_sums, *steps[2])
+        own_b = reduce_chips_own(cut_b[0], received_b, *sides_b)
+        three_b = pairwise(own_b[1].astype(BF16), "mp", 1)
+        for share in shares[1:]:
+            carried = halo_back(share + carried.astype(F32))
+        expand_out = step_rows(expand_grad, expand_master, expand_left, expand_right, expand_step, 8)
+        expand_out, three_b, moved = together(expand_out, three_b, moved)
+        gain_sums = gain_sums + moved
+        moved = lax.ppermute(gain_sums, *steps[3])
+        two_b = pairwise((own_b[0] + three_b.astype(F32)).astype(BF16), "mp", 2)
+        attend_sum = (own_a[0] + one_a.astype(F32) + two_b.astype(F32)) * grad_scale
+        attend_sum, carried, moved = together(attend_sum, carried, moved)
+        gain_sums = gain_sums + moved
+        gain_sums = gain_sums + lax.ppermute(gain_sums, *steps[4])
+        output_grad = from_piece(
+            rows_to_rows(attend_sum[3 * head_width :], D // (2 * LANES)), *grids["output"][:2]
+        )
+        attend_grad = from_piece(columns_of_rows(attend_sum[: 3 * head_width], 3), *grids["attend"][:2])
+    else:
+        hidden_cut = jnp.stack(
+            [jnp.concatenate([near_grads[core], far_grads[core]], axis=1) for core in range(2)], axis=1
+        )
+        attend_cut = jnp.stack(
+            [jnp.concatenate([cut_a[core], cut_b[core]], axis=1) for core in range(2)], axis=1
+        )
+        expand_grad = grad_scale * grad_by_columns(
+            join_columns(hidden_cut[:, :, :, : 2 * hidden_width], 2), expand_master, dp_size, mp_size
+        )
+        reduce_grad = grad_scale * grad_by_rows(
+            join_rows(hidden_cut[:, :, :, 2 * hidden_width :]),
+            reduce_master,
+            hidden_width,
+            dp_size,
+            mp_size,
+        )
+        output_grad = grad_scale * grad_by_rows(
+            join_rows(attend_cut[:, :, :, 3 * head_width :]), output_master, head_width, dp_size, mp_size
+        )
+        attend_grad = grad_scale * grad_by_columns(
+            join_columns(attend_cut[:, :, :, : 3 * head_width], 3), attend_master, dp_size, mp_size
+        )
+        reduce_out = step_columns(reduce_grad, reduce_master, reduce_left, reduce_right, reduce_step, 4)
+        expand_out = step_rows(expand_grad, expand_master, expand_left, expand_right, expand_step, 8)
+    first_back = window_back[history:] + carried.astype(F32)
+    first_scaled = first_back * gains[0]
+    input_grad = weight_scale * (
+        middle_grad
+        + first_rms
+        * (first_scaled - first_hat * jnp.mean(first_scaled * first_hat, axis=1, keepdims=True))
     )
-    attend_local = jnp.stack(
-        [
-            dot_weight(first_normed, grad_queries),
-            dot_weight(window, grad_keys),
-            dot_weight(window, grad_values),
-        ]
-    ).astype(BF16)
-    attend_sum = grad_by_columns(attend_local, attend_master, dp_size, mp_size)
-    window_back = dot_back(grad_keys, attend_w[1]) + dot_back(grad_values, attend_w[2])
-    own_back = window_back[history:] + dot_back(grad_queries, attend_w[0])
-    gain_first = (
-        jnp.sum(own_back * first_normed.astype(F32), axis=0)
-        + jnp.sum(window_back[:history] * window[:history].astype(F32), axis=0)
-    ) / gains[0]
-    carried = None
-    for k in range(earlier):
-        share = window_back[k * count : (k + 1) * count]
-        share = share if carried is None else share + carried
-        carried = lax.ppermute(share.astype(BF16), "mp", down_one).astype(F32)
-    first_back = own_back + carried
-    first_scaled = first_back * gains[0]
-    input_grad = middle_grad + first_rms * (
-        first_scaled - first_hat * jnp.mean(first_scaled * first_hat, axis=1, keepdims=True)
+
+    reduce_weight, left_reduce, right_reduce = reduce_out
+    expand_weight, left_expand, right_expand = expand_out
+    gains_grad = gain_sums * grad_scale
+    output_weight, left_output, right_output = step_rows(
+        output_grad, output_master, output_left, output_right, STEP_RATE * OUT_FAN ** (-0.5), 8
     )
-
-    grad_scale = total_patches ** (-0.5)
-    gains_grad = sum_small(jnp.stack([gain_first, gain_second])) * grad_scale
-    attend_grad = attend_sum * grad_scale
-    output_grad = output_sum * grad_scale
-    expand_grad = expand_sum * grad_scale
-    reduce_grad = reduce_sum * grad_scale
-    reduce_weight, left_reduce, right_reduce = shampoo(
-        reduce_grad, reduce_master, reduce_left, reduce_right, STEP_RATE * FF ** (-0.5)
-    )
-    expand_weight, left_expand, right_expand = shampoo(
-        expand_grad, expand_master, expand_left, expand_right, STEP_RATE * D ** (-0.5)
-    )
-    output_weight, left_output, right_output = shampoo(
-        output_grad, output_master, output_left, output_right, STEP_RATE * OUT_FAN ** (-0.5)
-    )
-    attend_weight, left_attend, right_attend = shampoo(
-        attend_grad, attend_master, attend_left, attend_right, STEP_RATE * D ** (-0.5)
+    attend_weight, left_attend, right_attend = step_rows(
+        attend_grad, attend_master, attend_left, attend_right, STEP_RATE * D ** (-0.5), 8
     )
     gains_weight, left_gains, right_gains = gain_update(gains_grad, gains, gains_left, gains_right)
     return (

time: 753 us -> 594 us (0.79)
  matrix products: 238 us -> 45.4 us
  Pallas kernels: 67.6 us -> 211 us
  local copies, waits for them, and re-layouts: 160 us -> 48.1 us
  blocking collectives: 64.5 us -> 0 us
  starting transfers between devices: 42.5 us -> 97.9 us
  other arithmetic: 33.4 us -> 86.6 us
  waiting for transfers between devices: 109 us -> 85.7 us
  between operations: 29.3 us -> 13.8 us
    pallas_call x0 -> x11, Pallas kernels: none -> 137 us  [the longest x3 61.9 us: hidden_layer(): grid_call(functools.partial(hidden_kernel, len(earlier)), (slices,), [who...]
    dot_general x176 -> x0, matrix products: 119 us -> none  [the longest x168 109 us: product(): jnp.einsum('...ij,...jk->...ik', first, second, precision=lax.Precision.H...]
    another operation x15 -> x7, local copies, waits for them, and re-layouts: 69.5 us -> 1.82 us  [the longest x2 0.92 us: rows_of_rows(): piece.reshape(height, width // LANES, LANES)]
    all_gather x3 -> x0, blocking collectives: 64.5 us -> none  [gather_all(): return lax.all_gather(lax.all_gather(piece, 'mp'), 'dp')]
    ppermute x19 -> x70, starting transfers between devices: 41.4 us -> 97.9 us  [the longest x56 53 us: pairwise(): lax.ppermute(values, axis, [(i, i ^ step) for i in range(lax.axis_size(ax...]
    reshape x8, local copies, waits for them, and re-layouts: 61 us -> 11.8 us  [the longest x2 5.15 us: from_piece(): grid = piece.reshape(leading + (rows, height, columns, width))]
    dot_general x7 -> x2, matrix products: 37.1 us -> 3.01 us  [dot(): return jnp.dot(first, second, preferred_element_type=F32)]
    reduce_scatter x8 -> x0, waiting for transfers between devices: 23.5 us -> none  [the longest x4 23.4 us: scatter_all(): return lax.psum_scatter(reduced, 'mp', scatter_dimension=0, tiled=False)]
  transfers between devices with their start and end apart: 32 -> 70, of which waited for: 13 -> 18; matrix products, arithmetic and copies ran while one was open for 42% -> 27% of each run, Pallas kernels for 9% -> 36%
where the time goes in v2:
time: 594 us; the launch traced here: 588 us
  Pallas kernels  211 us (36%)
  starting transfers between devices  97.9 us (16%)
  other arithmetic  86.6 us (15%)
  waiting for transfers between devices  85.7 us (14%)
  local copies, waits for them, and re-layouts  48.1 us (8%)
  matrix products  45.4 us (8%)
  between operations  13.8 us (2%)
    ppermute x56, waiting for transfers between devices, pairwise(): lax.ppermute(values, axis, [(i, i ^ step) for i in range(lax.axis_size(ax...  65.9 us
    pallas_call x3, Pallas kernels, hidden_layer(): grid_call(functools.partial(hidden_kernel, len(earlier)), (slices,), [who...  61.9 us
    ppermute x56, starting transfers between devices, pairwise(): lax.ppermute(values, axis, [(i, i ^ step) for i in range(lax.axis_size(ax...  53 us
    pallas_call x4, Pallas kernels, shampoo(): pl.pallas_call(functools.partial(shampoo_kernel, step_size, pack), grid=(...  44.6 us
    pallas_call x2, Pallas kernels, attend(): pl.pallas_call(functools.partial(attend_kernel, tile, window - count), gr...  39.3 us
    pallas_call x2, Pallas kernels, attend_back(): pl.pallas_call(functools.partial(attend_back_kernel, tile, window - count...  34 us
    dot_general x4, matrix products, dot_back(): lax.dot_general(first, second, (((1,), (1,)), ((), ())), preferred_elemen...  21.9 us
    ppermute x1, starting transfers between devices, body(): moved = lax.ppermute(raw_total, *steps[1])  21.8 us
  transfers between devices with their start and end apart: 70, of which 18 were waited for; matrix products, arithmetic and copies ran while one was open for 27% of the time, Pallas kernels for 36%

profile of v2, /device:TPU:0, one launch (start us, length us, event | category | flops | bytes accessed | tf_op | source)
XLA Modules:
  0.0 588.0 jit_solution(13048817652081420464)
XLA Ops:
  3.7 4.1 collective-permute-start.1
  10.1 10.1 %collective-permute-done.1 = bf16[1056,128]{1,0:T(8,128)(2,1)S(1)} collective-permute-done((bf16[1056,128]{1,0:T(8,128)(2,1)S(1)}, bf16[1056,128]{1,0:T(8,128)(2,1)S(1)}, u32[]{:S(2)}, u32[]{:S(2)}) %collective-permute-start.1) | collective-permute-done | bytes 270368 | tf_op jit(solution)/shard_map/ppermute | solution.py:81
  20.8 4.3 collective-permute-start.3
  43.3 5.9 %collective-permute-done.3 = bf16[512,1024]{1,0:T(8,128)(2,1)} collective-permute-done((bf16[512,1024]{1,0:T(8,128)(2,1)S(1)}, bf16[512,1024]{1,0:T(8,128)(2,1)}, u32[]{:S(2)}, u32[]{:S(2)}) %collective-permute-start.3) | collective-permute-done | bytes 1048608 | tf_op jit(solution)/shard_map/ppermute | solution.py:927
  49.2 2.9 collective-permute-done.4.refs_1_
  58.5 5.5 collective-permute-start.7
  65.0 6.0 %collective-permute-done.8 = bf16[4,528,128]{2,1,0:T(8,128)(2,1)} collective-permute-done((bf16[4,528,128]{2,1,0:T(8,128)(2,1)}, bf16[4,528,128]{2,1,0:T(8,128)(2,1)}, u32[]{:S(2)}, u32[]{:S(2)}) %collective-permute-start.8) | collective-permute-done | bytes 540704 | tf_op jit(solution)/shard_map/ppermute | solution.py:81
  71.4 13.8 %collective-permute-done.7 = bf16[512,1024]{1,0:T(8,128)(2,1)} collective-permute-done((bf16[512,1024]{1,0:T(8,128)(2,1)}, bf16[512,1024]{1,0:T(8,128)(2,1)}, u32[]{:S(2)}, u32[]{:S(2)}) %collective-permute-start.7) | collective-permute-done | bytes 1048608 | tf_op jit(solution)/shard_map/ppermute | solution.py:927
  85.2 3.4 pad_maximum_fusion.refs_7_
  91.2 3.2 collective-permute-start.17
  102.0 7.7 %join_attend.1 = (bf16[3,1024,1024]{2,1,0:T(8,128)(2,1)}, bf16[1024,1024]{1,0:T(8,128)(2,1)}) custom-call(s32[1]{0:T(128)} %bitcast.1.device_ref, bf16[4,1056,128]{2,1,0:T(8,128)(2,1)} %copy-done.13, bf16[4,1056,128]{2,1,0:T(8,128)(2,1)} %copy-done.24, bf16[4,1056,128]{2,1,0:T(8,128)(2,1)} %collective-permute-done.5.refs_2_, ...), custom_call_target="tpu_custom_call" | custom-call | bytes 16777216 | tf_op jit(solution)/shard_map/join_attend/pallas_call | solution.py:282
  109.7 3.8 fusion.21.q_ref
  118.2 7.8 %convolution_convert_fusion.v_ref = bf16[1536,1024]{1,0:T(8,128)(2,1)} fusion(bf16[1536,1024]{1,0:T(8,128)(2,1)} %pad_maximum_fusion.refs_7_, bf16[3,1024,1024]{2,1,0:T(8,128)(2,1)} %get-tuple-element.185.refs_6_), kind=kOutput, calls=%fused_computation.1 | convolution fusion | flops 3222798336 | bytes 8388608 | tf_op jit(solution)/shard_map/dot_general | solution.py:858
  126.0 6.4 %convolution_convert_fusion.1.k_ref = bf16[1536,1024]{1,0:T(8,128)(2,1)} fusion(bf16[1536,1024]{1,0:T(8,128)(2,1)S(1)} %copy-done.21, bf16[3,1024,1024]{2,1,0:T(8,128)(2,1)} %get-tuple-element.185.refs_6_), kind=kOutput, calls=%fused_computation.2 | convolution fusion | flops 3222798336 | bytes 8388608 | tf_op jit(solution)/shard_map/dot_general | solution.py:858
  132.5 19.6 %attend.2 = (bf16[512,512]{1,0:T(8,128)(2,1)}, f32[4,2,512]{2,1,0:T(2,128)}) custom-call(s32[1,512]{1,0:T(1,128)} %bitcast.302, s32[1536,1]{1,0:T(8,128)} %reshape.447.key_labels, bf16[512,1024]{1,0:T(8,128)(2,1)} %fusion.21.q_ref, bf16[1536,1024]{1,0:T(8,128)(2,1)} %convolution_convert_fusion.1.k_ref, bf16[1536,1024]{1,0:T(8,128)(2,1)} %convolution_convert_fusion.v_ref), custom_call_target="tpu_custom_call" | custom-call | flops 2684354560 | bytes 4194304 | tf_op jit(solution)/shard_map/attend/pallas_call | solution.py:576
  152.7 4.2 convert_reduce_fusion
  164.3 19.7 %attend.3 = (bf16[512,512]{1,0:T(8,128)(2,1)}, f32[4,2,512]{2,1,0:T(2,128)}) custom-call(s32[1,512]{1,0:T(1,128)} %bitcast.303, s32[1536,1]{1,0:T(8,128)} %reshape.447.key_labels, bf16[512,1024]{1,0:T(8,128)(2,1)} %fusion.21.q_ref, bf16[1536,1024]{1,0:T(8,128)(2,1)} %convolution_convert_fusion.1.k_ref, bf16[1536,1024]{1,0:T(8,128)(2,1)} %convolution_convert_fusion.v_ref), custom_call_target="tpu_custom_call" | custom-call | flops 2684354560 | bytes 4194304 | tf_op jit(solution)/shard_map/attend/pallas_call | solution.py:576
  194.5 21.8 %collective-permute-start.25 = (f32[1,1]{1,0:T(1,128)}, f32[1,1]{1,0:T(1,128)}, u32[]{:S(2)}, u32[]{:S(2)}) collective-permute-start(f32[1,1]{1,0:T(1,128)} %add.719), channel_id=1, source_target_pairs={{0,8},{4,12},{8,0},{12,4},{16,24},{20,28},{24,16},{28,20},{1,9},{5... | collective-permute-start | bytes 20 | tf_op jit(solution)/shard_map/ppermute | solution.py:1018
  221.4 16.9 %hidden_layer.3 = (f32[512,1024]{1,0:T(8,128)}, f32[512,1024]{1,0:T(8,128)}, bf16[4,2,2112,128]{3,2,1,0:T(8,128)(2,1)}, bf16[4,2,2112,128]{3,2,1,0:T(8,128)(2,1)}) custom-call(s32[1]{0:T(128)} %bitcast.1.device_ref, bf16[512,1024]{1,0:T(8,128)(2,1)} %multiply_convert_fusion.normed_ref, bf16[512,1024]{1,0:T(8,128)(2,1)} %fusion.17.grads_ref, ...), custom_call_target="tpu_custom_call" | custom-call | flops 6643777536 | bytes 8650752 | tf_op jit(solution)/shard_map/hidden_layer/pallas_call | solution.py:392
  241.7 3.3 collective-permute-start.34
  247.1 17.1 %hidden_layer.4 = (f32[512,1024]{1,0:T(8,128)}, f32[512,1024]{1,0:T(8,128)}, bf16[4,2,2112,128]{3,2,1,0:T(8,128)(2,1)}, bf16[4,2,2112,128]{3,2,1,0:T(8,128)(2,1)}) custom-call(s32[1]{0:T(128)} %bitcast.1.device_ref, bf16[512,1024]{1,0:T(8,128)(2,1)} %multiply_convert_fusion.normed_ref, ...), custom_call_target="tpu_custom_call", output_to_operand_aliasing={{2}: (27, {}), {3}: (28, {})} | custom-call | flops 6643777536 | bytes 8650752 | tf_op jit(solution)/shard_map/hidden_layer/pallas_call | solution.py:392
  267.8 5.1 collective-permute-done.35.refs_21_.refs_22_.refs_23_
  273.8 27.8 %hidden_layer.5 = (f32[512,1024]{1,0:T(8,128)}, f32[512,1024]{1,0:T(8,128)}, bf16[4,2,2112,128]{3,2,1,0:T(8,128)(2,1)}, bf16[4,2,2112,128]{3,2,1,0:T(8,128)(2,1)}) custom-call(s32[1]{0:T(128)} %bitcast.1.device_ref, bf16[512,1024]{1,0:T(8,128)(2,1)} %multiply_convert_fusion.normed_ref, bf16[512,1024]{1,0:T(8,128)(2,1)} %fusion.17.grads_ref, ...), custom_call_target="tpu_custom_call" | custom-call | flops 13287555072 | bytes 17301504 | tf_op jit(solution)/shard_map/hidden_layer/pallas_call | solution.py:392
  302.5 4.3 fusion.44
  308.9 2.8 multiply_reduce_fusion
  317.9 3.8 convolution_convert_fusion.6.do_ref
  322.3 3.9 fusion.48
  334.7 17.1 %attend_back.2 = (bf16[512,512]{1,0:T(8,128)(2,1)}, bf16[1536,512]{1,0:T(8,128)(2,1)}, bf16[1536,512]{1,0:T(8,128)(2,1)}) custom-call(s32[1,512]{1,0:T(1,128)} %bitcast.304, s32[1536,1]{1,0:T(8,128)} %reshape.447.key_labels, bf16[512,1024]{1,0:T(8,128)(2,1)} %fusion.21.q_ref, bf16[1536,1024]{1,0:T(8,128)(2,1)} %convolution_convert_fusion.1.k_ref, ...), custom_call_target="tpu_custom_call" | custom-call | flops 6710886400 | bytes 8388608 | tf_op jit(solution)/shard_map/attend_back/pallas_call | solution.py:601
  351.8 5.3 convolution_convert_fusion.4.value
  358.9 2.8 convolution_convert_fusion.5.key
  361.7 4.1 cut_attend.2
  376.8 16.9 %attend_back.3 = (bf16[512,512]{1,0:T(8,128)(2,1)}, bf16[1536,512]{1,0:T(8,128)(2,1)}, bf16[1536,512]{1,0:T(8,128)(2,1)}) custom-call(s32[1,512]{1,0:T(1,128)} %bitcast.305, s32[1536,1]{1,0:T(8,128)} %reshape.447.key_labels, bf16[512,1024]{1,0:T(8,128)(2,1)} %fusion.21.q_ref, bf16[1536,1024]{1,0:T(8,128)(2,1)} %convolution_convert_fusion.1.k_ref, ...), custom_call_target="tpu_custom_call" | custom-call | flops 6710886400 | bytes 8388608 | tf_op jit(solution)/shard_map/attend_back/pallas_call | solution.py:601
  397.6 2.9 fusion.4
  401.4 3.1 fusion.65
  406.2 2.8 convolution_convert_fusion.2.value
  413.5 4.1 cut_attend.3
  421.7 14.9 %project_back.1 = (f32[1536,1024]{1,0:T(8,128)}, f32[1,1024]{1,0:T(1,128)}) custom-call(bf16[512,512]{1,0:T(8,128)(2,1)} %get-tuple-element.253.refs_0_, bf16[512,512]{1,0:T(8,128)(2,1)} %get-tuple-element.280.refs_1_, bf16[1536,512]{1,0:T(8,128)(2,1)} %get-tuple-element.254.refs_2_, bf16[1536,512]{1,0:T(8,128)(2,1)} %get-tuple-element.281.refs_3_, ...), custom_call_target="tpu_custom_call" | custom-call | flops 7516192768 | bytes 18874368 | tf_op jit(solution)/shard_map/project_back/pallas_call | solution.py:657
  443.4 4.0 collective-permute-done.55
  452.3 3.0 reshape.419
  478.1 9.7 %shampoo.4 = (f32[8,64,176]{2,1,0:T(8,128)}, f32[8,64,64]{2,1,0:T(8,128)}, f32[8,176,176]{2,1,0:T(8,128)}) custom-call(f32[8,64,176]{2,1,0:T(8,128)} %bitcast.274, f32[8,64,176]{2,1,0:T(8,128)} %bitcast.277, f32[8,64,64]{2,1,0:T(8,128)} %short_ref.2, f32[8,176,176]{2,1,0:T(8,128)} %long_ref.2), custom_call_target="tpu_custom_call" | custom-call | flops 1744568320 | bytes 3686400 | tf_op jit(solution)/shard_map/shampoo/pallas_call | solution.py:796
  487.8 9.9 %collective-permute-done.62 = bf16[1024,128]{1,0:T(8,128)(2,1)} collective-permute-done((bf16[1024,128]{1,0:T(8,128)(2,1)S(1)}, bf16[1024,128]{1,0:T(8,128)(2,1)}, u32[]{:S(2)}, u32[]{:S(2)}) %collective-permute-start.62) | collective-permute-done | bytes 262176 | tf_op jit(solution)/shard_map/ppermute | solution.py:81
  501.7 3.2 add_convert_fusion
  506.2 15.9 %shampoo.5 = (f32[16,64,176]{2,1,0:T(8,128)}, f32[16,64,64]{2,1,0:T(8,128)}, f32[16,176,176]{2,1,0:T(8,128)}) custom-call(f32[16,64,176]{2,1,0:T(8,128)} %bitcast.266, f32[16,64,176]{2,1,0:T(8,128)} %bitcast.265, f32[16,64,64]{2,1,0:T(8,128)} %bitcast.310, f32[16,176,176]{2,1,0:T(8,128)} %bitcast.306), custom_call_target="tpu_custom_call" | custom-call | flops 3489136640 | bytes 7372800 | tf_op jit(solution)/shard_map/shampoo/pallas_call | solution.py:796
  523.4 4.2 collective-permute-start.66
  527.5 15.0 %collective-permute-done.66 = bf16[1024,128]{1,0:T(8,128)(2,1)S(1)} collective-permute-done((bf16[1024,128]{1,0:T(8,128)(2,1)S(1)}, bf16[1024,128]{1,0:T(8,128)(2,1)S(1)}, u32[]{:S(2)}, u32[]{:S(2)}) %collective-permute-start.66) | collective-permute-done | bytes 262176 | tf_op jit(solution)/shard_map/ppermute | solution.py:81
  553.0 4.0 fusion.10
  557.0 13.4 %shampoo.6 = (f32[24,64,64]{2,1,0:T(8,128)}, f32[24,64,64]{2,1,0:T(8,128)}, f32[24,64,64]{2,1,0:T(8,128)}) custom-call(f32[24,64,64]{2,1,0:T(8,128)} %bitcast.253, f32[24,64,64]{2,1,0:T(8,128)} %bitcast.252, f32[24,64,64]{2,1,0:T(8,128)} %bitcast.270, f32[24,64,64]{2,1,0:T(8,128)} %bitcast.271), custom_call_target="tpu_custom_call" | custom-call | flops 251658240 | bytes 3145728 | tf_op jit(solution)/shard_map/shampoo/pallas_call | solution.py:796
  571.4 5.6 shampoo.7
  (393 shorter events, 177.1 us)
Async XLA Ops:
  20.8 28.4 %collective-permute-start.3 = (bf16[512,1024]{1,0:T(8,128)(2,1)S(1)}, bf16[512,1024]{1,0:T(8,128)(2,1)}, u32[]{:S(2)}, u32[]{:S(2)}) collective-permute-start(bf16[512,1024]{1,0:T(8,128)(2,1)S(1)} %fusion.5), channel_id=1, source_target_pairs={{0,1},{1,2},{2,3},{4,5},{5,6},{6,7},{8,9},{9,10},{10,11},{12,13},{... | collective-permute-start | bytes 3145736 | tf_op jit(solution)/shard_map/ppermute | solution.py:927
  28.0 24.1 %collective-permute-start.4 = (bf16[4,1056,128]{2,1,0:T(8,128)(2,1)S(1)}, bf16[4,1056,128]{2,1,0:T(8,128)(2,1)S(1)}, u32[]{:S(2)}, u32[]{:S(2)}) collective-permute-start(bf16[4,1056,128]{2,1,0:T(8,128)(2,1)S(1)} %pad_maximum_fusion.1.refs_0_), channel_id=1, source_target_pairs={{0,8},{4,12},{8,0},{12,4},{16,24},{20,28},{24,16},{28,20},{1,9},{5... | collective-permute-start | bytes 3244040 | tf_op jit(solution)/shard_map/ppermute | solution.py:81
  29.4 23.8 %collective-permute-start.5 = (bf16[4,1056,128]{2,1,0:T(8,128)(2,1)S(1)}, bf16[4,1056,128]{2,1,0:T(8,128)(2,1)}, u32[]{:S(2)}, u32[]{:S(2)}) collective-permute-start(bf16[4,1056,128]{2,1,0:T(8,128)(2,1)S(1)} %pad_maximum_fusion.1.refs_0_), channel_id=1, source_target_pairs={{0,16},{4,20},{8,24},{12,28},{16,0},{20,4},{24,8},{28,12},{1,17},{... | collective-permute-start | bytes 3244040 | tf_op jit(solution)/shard_map/ppermute | solution.py:81
  30.9 22.3 %collective-permute-start.6 = (bf16[4,1056,128]{2,1,0:T(8,128)(2,1)S(1)}, bf16[4,1056,128]{2,1,0:T(8,128)(2,1)}, u32[]{:S(2)}, u32[]{:S(2)}) collective-permute-start(bf16[4,1056,128]{2,1,0:T(8,128)(2,1)S(1)} %pad_maximum_fusion.1.refs_0_), channel_id=1, source_target_pairs={{0,4},{4,0},{8,12},{12,8},{16,20},{20,16},{24,28},{28,24},{1,5},{5... | collective-permute-start | bytes 3244040 | tf_op jit(solution)/shard_map/ppermute | solution.py:81
  53.2 32.0 %collective-permute-start.11 = (bf16[4,1056,128]{2,1,0:T(8,128)(2,1)}, bf16[4,1056,128]{2,1,0:T(8,128)(2,1)S(1)}, u32[]{:S(2)}, u32[]{:S(2)}) collective-permute-start(bf16[4,1056,128]{2,1,0:T(8,128)(2,1)} %collective-permute-done.5.refs_2_), channel_id=1, source_target_pairs={{0,4},{4,0},{8,12},{12,8},{16,20},{20,16},{24,28},{28,24},{1,5},{5... | collective-permute-start | bytes 3244040 | tf_op jit(solution)/shard_map/ppermute | solution.py:81
  55.1 30.1 %collective-permute-start.10 = (bf16[4,1056,128]{2,1,0:T(8,128)(2,1)S(1)}, bf16[4,1056,128]{2,1,0:T(8,128)(2,1)}, u32[]{:S(2)}, u32[]{:S(2)}) collective-permute-start(bf16[4,1056,128]{2,1,0:T(8,128)(2,1)S(1)} %collective-permute-done.4.refs_1_), channel_id=1, source_target_pairs={{0,4},{4,0},{8,12},{12,8},{16,20},{20,16},{24,28},{28,24},{1,5},{5... | collective-permute-start | bytes 3244040 | tf_op jit(solution)/shard_map/ppermute | solution.py:81
  58.5 26.7 %collective-permute-start.7 = (bf16[512,1024]{1,0:T(8,128)(2,1)}, bf16[512,1024]{1,0:T(8,128)(2,1)}, u32[]{:S(2)}, u32[]{:S(2)}) collective-permute-start(bf16[512,1024]{1,0:T(8,128)(2,1)} %collective-permute-done.3), channel_id=1, source_target_pairs={{0,1},{1,2},{2,3},{4,5},{5,6},{6,7},{8,9},{9,10},{10,11},{12,13},{... | collective-permute-start | bytes 3145736 | tf_op jit(solution)/shard_map/ppermute | solution.py:927
  88.6 25.5 %collective-permute-start.13 = (bf16[2112,128]{1,0:T(8,128)(2,1)}, bf16[2112,128]{1,0:T(8,128)(2,1)}, u32[]{:S(2)}, u32[]{:S(2)}) collective-permute-start(bf16[2112,128]{1,0:T(8,128)(2,1)} %pad_maximum_fusion.8), channel_id=1, source_target_pairs={{0,1},{1,0},{2,3},{3,2},{4,5},{5,4},{6,7},{7,6},{8,9},{9,8},{10,11... | collective-permute-start | bytes 1622024 | tf_op jit(solution)/shard_map/ppermute | solution.py:81
  91.2 60.8 %collective-permute-start.17 = (bf16[2112,128]{1,0:T(8,128)(2,1)}, bf16[2112,128]{1,0:T(8,128)(2,1)}, u32[]{:S(2)}, u32[]{:S(2)}) collective-permute-start(bf16[2112,128]{1,0:T(8,128)(2,1)} %pad_maximum_fusion.8), channel_id=1, source_target_pairs={{0,2},{1,3},{2,0},{3,1},{4,6},{5,7},{6,4},{7,5},{8,10},{9,11},{10,... | collective-permute-start | bytes 1622024 | tf_op jit(solution)/shard_map/ppermute | solution.py:81
  115.4 36.6 %collective-permute-start.14 = (bf16[2,2112,128]{2,1,0:T(8,128)(2,1)S(1)}, bf16[2,2112,128]{2,1,0:T(8,128)(2,1)S(1)}, u32[]{:S(2)}, u32[]{:S(2)}) collective-permute-start(bf16[2,2112,128]{2,1,0:T(8,128)(2,1)S(1)} %pad_maximum_fusion.2.refs_0_.refs_1_.refs_2_), channel_id=1, source_target_pairs={{0,8},{4,12},{8,0},{12,4},{16,24},{20,28},{24,16},{28,20},{1,9},{5... | collective-permute-start | bytes 3244040 | tf_op jit(solution)/shard_map/ppermute | solution.py:81
  117.0 35.1 %collective-permute-start.15 = (bf16[2,2112,128]{2,1,0:T(8,128)(2,1)S(1)}, bf16[2,2112,128]{2,1,0:T(8,128)(2,1)S(1)}, u32[]{:S(2)}, u32[]{:S(2)}) collective-permute-start(bf16[2,2112,128]{2,1,0:T(8,128)(2,1)S(1)} %pad_maximum_fusion.2.refs_0_.refs_1_.refs_2_), channel_id=1, source_target_pairs={{0,16},{4,20},{8,24},{12,28},{16,0},{20,4},{24,8},{28,12},{1,17},{... | collective-permute-start | bytes 3244040 | tf_op jit(solution)/shard_map/ppermute | solution.py:81
  117.5 34.6 %collective-permute-start.16 = (bf16[2,2112,128]{2,1,0:T(8,128)(2,1)S(1)}, bf16[2,2112,128]{2,1,0:T(8,128)(2,1)}, u32[]{:S(2)}, u32[]{:S(2)}) collective-permute-start(bf16[2,2112,128]{2,1,0:T(8,128)(2,1)S(1)} %pad_maximum_fusion.2.refs_0_.refs_1_.refs_2_), channel_id=1, source_target_pairs={{0,4},{4,0},{8,12},{12,8},{16,20},{20,16},{24,28},{28,24},{1,5},{5... | collective-permute-start | bytes 3244040 | tf_op jit(solution)/shard_map/ppermute | solution.py:81
  152.1 34.1 %collective-permute-start.20 = (bf16[2,2112,128]{2,1,0:T(8,128)(2,1)S(1)}, bf16[2,2112,128]{2,1,0:T(8,128)(2,1)S(1)}, u32[]{:S(2)}, u32[]{:S(2)}) collective-permute-start(bf16[2,2112,128]{2,1,0:T(8,128)(2,1)S(1)} %collective-permute-done.14.refs_3_.refs_4_.refs_5_), channel_id=1, source_target_pairs={{0,4},{4,0},{8,12},{12,8},{16,20},{20,16},{24,28},{28,24},{1,5},{5... | collective-permute-start | bytes 3244040 | tf_op jit(solution)/shard_map/ppermute | solution.py:81
  152.7 33.5 %collective-permute-start.21 = (bf16[2,2112,128]{2,1,0:T(8,128)(2,1)S(1)}, bf16[2,2112,128]{2,1,0:T(8,128)(2,1)}, u32[]{:S(2)}, u32[]{:S(2)}) collective-permute-start(bf16[2,2112,128]{2,1,0:T(8,128)(2,1)S(1)} %collective-permute-done.15.refs_6_.refs_7_.refs_8_), channel_id=1, source_target_pairs={{0,4},{4,0},{8,12},{12,8},{16,20},{20,16},{24,28},{28,24},{1,5},{5... | collective-permute-start | bytes 3244040 | tf_op jit(solution)/shard_map/ppermute | solution.py:81
  162.1 24.1 %collective-permute-start.18 = (bf16[2,1056,128]{2,1,0:T(8,128)(2,1)}, bf16[2,1056,128]{2,1,0:T(8,128)(2,1)}, u32[]{:S(2)}, u32[]{:S(2)}) collective-permute-start(bf16[2,1056,128]{2,1,0:T(8,128)(2,1)} %slice.401), channel_id=1, source_target_pairs={{0,8},{4,12},{8,0},{12,4},{16,24},{20,28},{24,16},{28,20},{1,9},{5... | collective-permute-start | bytes 1622024 | tf_op jit(solution)/shard_map/ppermute | solution.py:81
  162.6 23.5 %collective-permute-start.19 = (bf16[2,1056,128]{2,1,0:T(8,128)(2,1)}, bf16[2,1056,128]{2,1,0:T(8,128)(2,1)}, u32[]{:S(2)}, u32[]{:S(2)}) collective-permute-start(bf16[2,1056,128]{2,1,0:T(8,128)(2,1)} %slice.402), channel_id=1, source_target_pairs={{0,16},{4,20},{8,24},{12,28},{16,0},{20,4},{24,8},{28,12},{1,17},{... | collective-permute-start | bytes 1622024 | tf_op jit(solution)/shard_map/ppermute | solution.py:81
  164.2 22.0 %collective-permute-start.22 = (bf16[2112,128]{1,0:T(8,128)(2,1)}, bf16[2112,128]{1,0:T(8,128)(2,1)}, u32[]{:S(2)}, u32[]{:S(2)}) collective-permute-start(bf16[2112,128]{1,0:T(8,128)(2,1)} %collective-permute-done.17), channel_id=1, source_target_pairs={{0,1},{1,0},{2,3},{3,2},{4,5},{5,4},{6,7},{7,6},{8,9},{9,8},{10,11... | collective-permute-start | bytes 1622024 | tf_op jit(solution)/shard_map/ppermute | solution.py:81
  189.6 29.2 %collective-permute-start.24 = (bf16[2,2112,128]{2,1,0:T(8,128)(2,1)S(1)}, bf16[2,2112,128]{2,1,0:T(8,128)(2,1)S(1)}, u32[]{:S(2)}, u32[]{:S(2)}) collective-permute-start(bf16[2,2112,128]{2,1,0:T(8,128)(2,1)S(1)} %constant_dynamic-update-slice_fusion.3.refs_9_.refs_10_.refs_11_), channel_id=1, source_target_pairs={{0,4},{4,0},{8,12},{12,8},{16,20},{20,16},{24,28},{28,24},{1,5},{5... | collective-permute-start | bytes 3244040 | tf_op jit(solution)/shard_map/ppermute | solution.py:81
  191.3 47.1 %collective-permute-start.26 = (bf16[2,2112,128]{2,1,0:T(8,128)(2,1)S(1)}, bf16[2,2112,128]{2,1,0:T(8,128)(2,1)}, u32[]{:S(2)}, u32[]{:S(2)}) collective-permute-start(bf16[2,2112,128]{2,1,0:T(8,128)(2,1)S(1)} %pad_maximum_fusion.3.refs_0_.refs_1_.refs_2_), channel_id=1, source_target_pairs={{0,8},{4,12},{8,0},{12,4},{16,24},{20,28},{24,16},{28,20},{1,9},{5... | collective-permute-start | bytes 3244040 | tf_op jit(solution)/shard_map/ppermute | solution.py:81
  192.8 45.5 %collective-permute-start.27 = (bf16[2,2112,128]{2,1,0:T(8,128)(2,1)S(1)}, bf16[2,2112,128]{2,1,0:T(8,128)(2,1)}, u32[]{:S(2)}, u32[]{:S(2)}) collective-permute-start(bf16[2,2112,128]{2,1,0:T(8,128)(2,1)S(1)} %pad_maximum_fusion.3.refs_0_.refs_1_.refs_2_), channel_id=1, source_target_pairs={{0,16},{4,20},{8,24},{12,28},{16,0},{20,4},{24,8},{28,12},{1,17},{... | collective-permute-start | bytes 3244040 | tf_op jit(solution)/shard_map/ppermute | solution.py:81
  193.3 45.0 %collective-permute-start.28 = (bf16[2,2112,128]{2,1,0:T(8,128)(2,1)S(1)}, bf16[2,2112,128]{2,1,0:T(8,128)(2,1)}, u32[]{:S(2)}, u32[]{:S(2)}) collective-permute-start(bf16[2,2112,128]{2,1,0:T(8,128)(2,1)S(1)} %pad_maximum_fusion.3.refs_0_.refs_1_.refs_2_), channel_id=1, source_target_pairs={{0,4},{4,0},{8,12},{12,8},{16,20},{20,16},{24,28},{28,24},{1,5},{5... | collective-permute-start | bytes 3244040 | tf_op jit(solution)/shard_map/ppermute | solution.py:81
  194.5 24.2 %collective-permute-start.25 = (f32[1,1]{1,0:T(1,128)}, f32[1,1]{1,0:T(1,128)}, u32[]{:S(2)}, u32[]{:S(2)}) collective-permute-start(f32[1,1]{1,0:T(1,128)} %add.719), channel_id=1, source_target_pairs={{0,8},{4,12},{8,0},{12,4},{16,24},{20,28},{24,16},{28,20},{1,9},{5... | collective-permute-start | bytes 20 | tf_op jit(solution)/shard_map/ppermute | solution.py:1018
  238.4 25.9 %collective-permute-start.32 = (bf16[2,2112,128]{2,1,0:T(8,128)(2,1)}, bf16[2,2112,128]{2,1,0:T(8,128)(2,1)}, u32[]{:S(2)}, u32[]{:S(2)}) collective-permute-start(bf16[2,2112,128]{2,1,0:T(8,128)(2,1)} %collective-permute-done.26.refs_3_.refs_4_.refs_5_), channel_id=1, source_target_pairs={{0,4},{4,0},{8,12},{12,8},{16,20},{20,16},{24,28},{28,24},{1,5},{5... | collective-permute-start | bytes 3244040 | tf_op jit(solution)/shard_map/ppermute | solution.py:81
  238.4 25.8 %collective-permute-start.33 = (bf16[2,2112,128]{2,1,0:T(8,128)(2,1)}, bf16[2,2112,128]{2,1,0:T(8,128)(2,1)}, u32[]{:S(2)}, u32[]{:S(2)}) collective-permute-start(bf16[2,2112,128]{2,1,0:T(8,128)(2,1)} %collective-permute-done.27.refs_6_.refs_7_.refs_8_), channel_id=1, source_target_pairs={{0,4},{4,0},{8,12},{12,8},{16,20},{20,16},{24,28},{28,24},{1,5},{5... | collective-permute-start | bytes 3244040 | tf_op jit(solution)/shard_map/ppermute | solution.py:81
  241.7 22.5 %collective-permute-start.34 = (f32[1,1]{1,0:T(1,128)}, f32[1,1]{1,0:T(1,128)}, u32[]{:S(2)}, u32[]{:S(2)}) collective-permute-start(f32[1,1]{1,0:T(1,128)} %add.722), channel_id=1, source_target_pairs={{0,1},{1,0},{2,3},{3,2},{4,5},{5,4},{6,7},{7,6},{8,9},{9,8},{10,11... | collective-permute-start | bytes 20 | tf_op jit(solution)/shard_map/ppermute | solution.py:1035
  264.2 37.4 %collective-permute-start.36 = (bf16[4,2,2112,128]{3,2,1,0:T(8,128)(2,1)}, bf16[4,2,2112,128]{3,2,1,0:T(8,128)(2,1)}, u32[]{:S(2)}, u32[]{:S(2)}) collective-permute-start(bf16[4,2,2112,128]{3,2,1,0:T(8,128)(2,1)} %get-tuple-element.241), channel_id=1, source_target_pairs={{0,4},{4,0},{8,12},{12,8},{16,20},{20,16},{24,28},{28,24},{1,5},{5... | collective-permute-start | bytes 12976136 | tf_op jit(solution)/shard_map/ppermute | solution.py:81
  265.6 36.1 %collective-permute-start.37 = (f32[1,1]{1,0:T(1,128)}, f32[1,1]{1,0:T(1,128)}, u32[]{:S(2)}, u32[]{:S(2)}) collective-permute-start(f32[1,1]{1,0:T(1,128)} %add.724), channel_id=1, source_target_pairs={{0,2},{1,3},{2,0},{3,1},{4,6},{5,7},{6,4},{7,5},{8,10},{9,11},{10,... | collective-permute-start | bytes 20 | tf_op jit(solution)/shard_map/ppermute | solution.py:1042
  301.7 20.6 %collective-permute-start.40 = (bf16[4,2,2112,128]{3,2,1,0:T(8,128)(2,1)}, bf16[4,2,2112,128]{3,2,1,0:T(8,128)(2,1)}, u32[]{:S(2)}, u32[]{:S(2)}) collective-permute-start(bf16[4,2,2112,128]{3,2,1,0:T(8,128)(2,1)} %get-tuple-element.250), channel_id=1, source_target_pairs={{0,4},{4,0},{8,12},{12,8},{16,20},{20,16},{24,28},{28,24},{1,5},{5... | collective-permute-start | bytes 12976136 | tf_op jit(solution)/shard_map/ppermute | solution.py:81
  326.2 39.6 %collective-permute-start.43 = (bf16[2,1056,128]{2,1,0:T(8,128)(2,1)}, bf16[2,1056,128]{2,1,0:T(8,128)(2,1)}, u32[]{:S(2)}, u32[]{:S(2)}) collective-permute-start(bf16[2,1056,128]{2,1,0:T(8,128)(2,1)} %get-tuple-element.342), channel_id=1, source_target_pairs={{0,8},{4,12},{8,0},{12,4},{16,24},{20,28},{24,16},{28,20},{1,9},{5... | collective-permute-start | bytes 1622024 | tf_op jit(solution)/shard_map/ppermute | solution.py:81
  326.8 39.0 %collective-permute-start.44 = (bf16[2,1056,128]{2,1,0:T(8,128)(2,1)}, bf16[2,1056,128]{2,1,0:T(8,128)(2,1)}, u32[]{:S(2)}, u32[]{:S(2)}) collective-permute-start(bf16[2,1056,128]{2,1,0:T(8,128)(2,1)} %get-tuple-element.341), channel_id=1, source_target_pairs={{0,16},{4,20},{8,24},{12,28},{16,0},{20,4},{24,8},{28,12},{1,17},{... | collective-permute-start | bytes 1622024 | tf_op jit(solution)/shard_map/ppermute | solution.py:81
  331.0 34.9 %collective-permute-start.42 = (bf16[2,2112,128]{2,1,0:T(8,128)(2,1)}, bf16[2,2112,128]{2,1,0:T(8,128)(2,1)}, u32[]{:S(2)}, u32[]{:S(2)}) collective-permute-start(bf16[2,2112,128]{2,1,0:T(8,128)(2,1)} %pad_maximum_fusion.5), channel_id=1, source_target_pairs={{0,16},{4,20},{8,24},{12,28},{16,0},{20,4},{24,8},{28,12},{1,17},{... | collective-permute-start | bytes 3244040 | tf_op jit(solution)/shard_map/ppermute | solution.py:81
  333.2 32.6 %collective-permute-start.41 = (bf16[2,2112,128]{2,1,0:T(8,128)(2,1)}, bf16[2,2112,128]{2,1,0:T(8,128)(2,1)}, u32[]{:S(2)}, u32[]{:S(2)}) collective-permute-start(bf16[2,2112,128]{2,1,0:T(8,128)(2,1)} %pad_maximum_fusion.4), channel_id=1, source_target_pairs={{0,8},{4,12},{8,0},{12,4},{16,24},{20,28},{24,16},{28,20},{1,9},{5... | collective-permute-start | bytes 3244040 | tf_op jit(solution)/shard_map/ppermute | solution.py:81
  365.8 27.8 %collective-permute-start.47 = (bf16[4,2,1024,128]{3,2,1,0:T(8,128)(2,1)}, bf16[4,2,1024,128]{3,2,1,0:T(8,128)(2,1)}, u32[]{:S(2)}, u32[]{:S(2)}) collective-permute-start(bf16[4,2,1024,128]{3,2,1,0:T(8,128)(2,1)} %get-tuple-element.257), channel_id=1, source_target_pairs={{0,4},{4,0},{8,12},{12,8},{16,20},{20,16},{24,28},{28,24},{1,5},{5... | collective-permute-start | bytes 6291464 | tf_op jit(solution)/shard_map/ppermute | solution.py:81
  369.3 26.6 %collective-permute-start.46 = (bf16[2,2112,128]{2,1,0:T(8,128)(2,1)}, bf16[2,2112,128]{2,1,0:T(8,128)(2,1)}, u32[]{:S(2)}, u32[]{:S(2)}) collective-permute-start(bf16[2,2112,128]{2,1,0:T(8,128)(2,1)} %pad_maximum_fusion.7), channel_id=1, source_target_pairs={{0,16},{4,20},{8,24},{12,28},{16,0},{20,4},{24,8},{28,12},{1,17},{... | collective-permute-start | bytes 3244040 | tf_op jit(solution)/shard_map/ppermute | solution.py:81
  371.3 26.3 %collective-permute-start.45 = (bf16[2,2112,128]{2,1,0:T(8,128)(2,1)}, bf16[2,2112,128]{2,1,0:T(8,128)(2,1)}, u32[]{:S(2)}, u32[]{:S(2)}) collective-permute-start(bf16[2,2112,128]{2,1,0:T(8,128)(2,1)} %pad_maximum_fusion.6), channel_id=1, source_target_pairs={{0,8},{4,12},{8,0},{12,4},{16,24},{20,28},{24,16},{28,20},{1,9},{5... | collective-permute-start | bytes 3244040 | tf_op jit(solution)/shard_map/ppermute | solution.py:81
  376.6 40.9 %collective-permute-start.51 = (bf16[2112,128]{1,0:T(8,128)(2,1)}, bf16[2112,128]{1,0:T(8,128)(2,1)}, u32[]{:S(2)}, u32[]{:S(2)}) collective-permute-start(bf16[2112,128]{1,0:T(8,128)(2,1)} %fusion.50), channel_id=1, source_target_pairs={{0,1},{1,0},{2,3},{3,2},{4,5},{5,4},{6,7},{7,6},{8,9},{9,8},{10,11... | collective-permute-start | bytes 1622024 | tf_op jit(solution)/shard_map/ppermute | solution.py:81
  417.6 41.1 %collective-permute-start.52 = (bf16[4,2,1024,128]{3,2,1,0:T(8,128)(2,1)}, bf16[4,2,1024,128]{3,2,1,0:T(8,128)(2,1)}, u32[]{:S(2)}, u32[]{:S(2)}) collective-permute-start(bf16[4,2,1024,128]{3,2,1,0:T(8,128)(2,1)} %get-tuple-element.273), channel_id=1, source_target_pairs={{0,4},{4,0},{8,12},{12,8},{16,20},{20,16},{24,28},{28,24},{1,5},{5... | collective-permute-start | bytes 6291464 | tf_op jit(solution)/shard_map/ppermute | solution.py:81
  419.9 27.5 %collective-permute-start.55 = (bf16[2112,128]{1,0:T(8,128)(2,1)}, bf16[2112,128]{1,0:T(8,128)(2,1)}, u32[]{:S(2)}, u32[]{:S(2)}) collective-permute-start(bf16[2112,128]{1,0:T(8,128)(2,1)} %fusion.25), channel_id=1, source_target_pairs={{0,2},{1,3},{2,0},{3,1},{4,6},{5,7},{6,4},{7,5},{8,10},{9,11},{10,... | collective-permute-start | bytes 1622024 | tf_op jit(solution)/shard_map/ppermute | solution.py:81
  437.4 31.3 %collective-permute-start.58 = (f32[2,1024]{1,0:T(2,128)S(1)}, f32[2,1024]{1,0:T(2,128)S(1)}, u32[]{:S(2)}, u32[]{:S(2)}) collective-permute-start(f32[2,1024]{1,0:T(2,128)S(1)} %pad_maximum_fusion.13), channel_id=1, source_target_pairs={{0,4},{4,0},{8,12},{12,8},{16,20},{20,16},{24,28},{28,24},{1,5},{5... | collective-permute-start | bytes 24584 | tf_op jit(solution)/shard_map/ppermute | solution.py:1124
  465.6 32.1 %collective-permute-start.61 = (bf16[512,1024]{1,0:T(8,128)(2,1)}, bf16[512,1024]{1,0:T(8,128)(2,1)}, u32[]{:S(2)}, u32[]{:S(2)}) collective-permute-start(bf16[512,1024]{1,0:T(8,128)(2,1)} %slice.759), channel_id=1, source_target_pairs={{1,0},{2,1},{3,2},{5,4},{6,5},{7,6},{9,8},{10,9},{11,10},{13,12},{... | collective-permute-start | bytes 3145736 | tf_op jit(solution)/shard_map/ppermute | solution.py:1114
  471.9 25.8 %collective-permute-start.60 = (bf16[2,1024,128]{2,1,0:T(8,128)(2,1)}, bf16[2,1024,128]{2,1,0:T(8,128)(2,1)}, u32[]{:S(2)}, u32[]{:S(2)}) collective-permute-start(bf16[2,1024,128]{2,1,0:T(8,128)(2,1)} %pad_maximum_fusion.12), channel_id=1, source_target_pairs={{0,16},{4,20},{8,24},{12,28},{16,0},{20,4},{24,8},{28,12},{1,17},{... | collective-permute-start | bytes 1572872 | tf_op jit(solution)/shard_map/ppermute | solution.py:81
  473.6 24.1 %collective-permute-start.59 = (bf16[2,1024,128]{2,1,0:T(8,128)(2,1)}, bf16[2,1024,128]{2,1,0:T(8,128)(2,1)}, u32[]{:S(2)}, u32[]{:S(2)}) collective-permute-start(bf16[2,1024,128]{2,1,0:T(8,128)(2,1)} %pad_maximum_fusion.11), channel_id=1, source_target_pairs={{0,8},{4,12},{8,0},{12,4},{16,24},{20,28},{24,16},{28,20},{1,9},{5... | collective-permute-start | bytes 1572872 | tf_op jit(solution)/shard_map/ppermute | solution.py:81
  474.1 23.6 %collective-permute-start.62 = (bf16[1024,128]{1,0:T(8,128)(2,1)S(1)}, bf16[1024,128]{1,0:T(8,128)(2,1)}, u32[]{:S(2)}, u32[]{:S(2)}) collective-permute-start(bf16[1024,128]{1,0:T(8,128)(2,1)S(1)} %fusion.70), channel_id=1, source_target_pairs={{0,1},{1,0},{2,3},{3,2},{4,5},{5,4},{6,7},{7,6},{8,9},{9,8},{10,11... | collective-permute-start | bytes 786440 | tf_op jit(solution)/shard_map/ppermute | solution.py:81
  476.5 21.1 %collective-permute-start.63 = (f32[2,1024]{1,0:T(2,128)S(1)}, f32[2,1024]{1,0:T(2,128)S(1)}, u32[]{:S(2)}, u32[]{:S(2)}) collective-permute-start(f32[2,1024]{1,0:T(2,128)S(1)} %fusion.85), channel_id=1, source_target_pairs={{0,8},{4,12},{8,0},{12,4},{16,24},{20,28},{24,16},{28,20},{1,9},{5... | collective-permute-start | bytes 24584 | tf_op jit(solution)/shard_map/ppermute | solution.py:1146
  497.7 24.5 %collective-permute-start.65 = (f32[2,1024]{1,0:T(2,128)S(1)}, f32[2,1024]{1,0:T(2,128)S(1)}, u32[]{:S(2)}, u32[]{:S(2)}) collective-permute-start(f32[2,1024]{1,0:T(2,128)S(1)} %fusion.111), channel_id=1, source_target_pairs={{0,16},{4,20},{8,24},{12,28},{16,0},{20,4},{24,8},{28,12},{1,17},{... | collective-permute-start | bytes 24584 | tf_op jit(solution)/shard_map/ppermute | solution.py:1153
  501.6 20.6 %collective-permute-start.64 = (bf16[1024,128]{1,0:T(8,128)(2,1)S(1)}, bf16[1024,128]{1,0:T(8,128)(2,1)}, u32[]{:S(2)}, u32[]{:S(2)}) collective-permute-start(bf16[1024,128]{1,0:T(8,128)(2,1)S(1)} %fusion.71), channel_id=1, source_target_pairs={{0,1},{1,0},{2,3},{3,2},{4,5},{5,4},{6,7},{7,6},{8,9},{9,8},{10,11... | collective-permute-start | bytes 786440 | tf_op jit(solution)/shard_map/ppermute | solution.py:81
  505.0 38.8 %collective-permute-start.67 = (bf16[512,1024]{1,0:T(8,128)(2,1)}, bf16[512,1024]{1,0:T(8,128)(2,1)}, u32[]{:S(2)}, u32[]{:S(2)}) collective-permute-start(bf16[512,1024]{1,0:T(8,128)(2,1)} %add_convert_fusion), channel_id=1, source_target_pairs={{1,0},{2,1},{3,2},{5,4},{6,5},{7,6},{9,8},{10,9},{11,10},{13,12},{... | collective-permute-start | bytes 3145736 | tf_op jit(solution)/shard_map/ppermute | solution.py:1114
  545.2 31.8 %collective-permute-start.69 = (f32[2,1024]{1,0:T(2,128)}, f32[2,1024]{1,0:T(2,128)}, u32[]{:S(2)}, u32[]{:S(2)}) collective-permute-start(f32[2,1024]{1,0:T(2,128)} %add.806), channel_id=1, source_target_pairs={{0,2},{1,3},{2,0},{3,1},{4,6},{5,7},{6,4},{7,5},{8,10},{9,11},{10,... | collective-permute-start | bytes 24584 | tf_op jit(solution)/shard_map/ppermute | solution.py:1166
  (88 other events, 962.9 us)

commit v3 on v2

--- a/solution.py
+++ b/solution.py
@@ -1,4 +1,5 @@
 import functools
+import math
 
 import jax
 import jax.numpy as jnp
@@ -86,54 +87,149 @@
 
 
 def gather_corner(across_x, across_y, other):
-    half = across_x.shape[1] // 2
+    half = across_x.shape[0] // 2
     return (
-        pairwise(across_y[:, :half], "dp", 2),
-        pairwise(across_x[:, half:], "dp", 4),
-        pairwise(across_x, "dp", 1),
-        pairwise(across_y, "dp", 1),
+        pairwise(across_y[:half], "dp", 2),
+        pairwise(across_x[half:], "dp", 4),
+        pairwise(jnp.concatenate([across_x, across_y]), "dp", 1),
     )
 
 
-def gather_end(slices, across_x, across_y, other, corner_x, corner_y, other_x, other_y):
-    corner = jnp.concatenate([corner_x, corner_y], axis=1)
+def gather_end(slices, across_x, across_y, other, corner_x, corner_y, other_sides):
+    corner = jnp.concatenate([corner_x, corner_y])
     return (
-        slices, across_x, across_y, corner, other, other_x, other_y, pairwise(corner, "dp", 1)
+        slices, across_x, across_y, corner, other, other_sides, other_sides, pairwise(corner, "dp", 1)
     )
 
 
-def part_sum(own_core, received, chip, low, high):
-    return own_core[chip, :, low:high].astype(F32) + received[chip, :, low:high].astype(F32)
-
-
-def reduce_chips_corner(own_core, received):
-    half = own_core.shape[2] // 2
-    corner_x = pairwise(part_sum(own_core, received, 3, 0, half).astype(BF16), "dp", 2)
-    corner_y = pairwise(part_sum(own_core, received, 3, half, None).astype(BF16), "dp", 4)
-    return corner_x, corner_y
-
-
-def reduce_chips_sides(own_core, received, corner_x, corner_y):
-    half = own_core.shape[2] // 2
-    to_y = jnp.concatenate(
-        [
-            part_sum(own_core, received, 2, 0, half) + corner_x.astype(F32),
-            part_sum(own_core, received, 2, half, None),
-        ],
-        axis=1,
-    ).astype(BF16)
-    to_x = jnp.concatenate(
-        [
-            part_sum(own_core, received, 1, 0, half),
-            part_sum(own_core, received, 1, half, None) + corner_y.astype(F32),
-        ],
-        axis=1,
-    ).astype(BF16)
+def first_slices(pieces):
+    return [0] * 6 + [pieces[6].shape[0] - pieces[0].shape[0], 0]
+
+
+def add_up(*refs):
+    total = refs[0][...].astype(F32)
+    for ref in refs[1:]:
+        total = total + ref[...].astype(F32)
+    return total
+
+
+def add_call(kernel, slices, in_specs, out_specs, out_shape, name, *operands):
+    return pl.pallas_call(
+        kernel,
+        grid=(slices,),
+        in_specs=in_specs,
+        out_specs=out_specs,
+        out_shape=out_shape,
+        cost_estimate=moved(sum(v.size // CHIPS for v in operands)),
+        name=name,
+    )(*operands)
+
+
+def chip_slice(chip, rows):
+    return pl.BlockSpec((1, 1, rows, LANES), lambda k: (chip, k, 0, 0))
+
+
+def one_slice(rows, first=0, last=None):
+    if last is None:
+        return pl.BlockSpec((1, rows, LANES), lambda k: (k, 0, 0))
+    return pl.BlockSpec((1, rows, LANES), lambda k: (jnp.clip(k, first, last) - first, 0, 0))
+
+
+def corner_kernel(half, own, received, to_x, to_y):
+    total = add_up(own, received)[0].astype(BF16)
+
+    @pl.when(pl.program_id(0) < half)
+    def _():
+        to_x[...] = total
+
+    @pl.when(pl.program_id(0) >= half)
+    def _():
+        to_y[...] = total
+
+
+def corner_sums(own_core, received):
+    slices, rows = own_core.shape[1:3]
+    half = slices // 2
+    shape = jax.ShapeDtypeStruct((half, rows, LANES), BF16)
+    to_x, to_y = add_call(
+        functools.partial(corner_kernel, half),
+        slices,
+        [chip_slice(3, rows)] * 2,
+        [one_slice(rows, 0, half - 1), one_slice(rows, half, slices - 1)],
+        [shape, shape],
+        "add_corner",
+        own_core,
+        received,
+    )
+    return to_x, to_y
+
+
+def send_planar(to_x, to_y):
     return pairwise(to_x, "dp", 2), pairwise(to_y, "dp", 4)
 
 
-def reduce_chips_own(own_core, received, from_x, from_y):
-    return part_sum(own_core, received, 0, 0, None) + from_x.astype(F32) + from_y.astype(F32)
+def sides_kernel(half, own_x, received_x, own_y, received_y, corner_x, corner_y, to_x, to_y):
+    @pl.when(pl.program_id(0) < half)
+    def _():
+        to_x[...] = add_up(own_x, received_x)[0].astype(BF16)
+        to_y[...] = (add_up(own_y, received_y)[0] + corner_x[...].astype(F32)).astype(BF16)
+
+    @pl.when(pl.program_id(0) >= half)
+    def _():
+        to_x[...] = (add_up(own_x, received_x)[0] + corner_y[...].astype(F32)).astype(BF16)
+        to_y[...] = add_up(own_y, received_y)[0].astype(BF16)
+
+
+def side_sums(own_core, received, corner_x, corner_y):
+    slices, rows = own_core.shape[1:3]
+    half = slices // 2
+    shape = jax.ShapeDtypeStruct((slices, rows, LANES), BF16)
+    to_x, to_y = add_call(
+        functools.partial(sides_kernel, half),
+        slices,
+        [chip_slice(1, rows)] * 2
+        + [chip_slice(2, rows)] * 2
+        + [one_slice(rows, 0, half - 1), one_slice(rows, half, slices - 1)],
+        [one_slice(rows)] * 2,
+        [shape, shape],
+        "add_sides",
+        own_core,
+        received,
+        own_core,
+        received,
+        corner_x,
+        corner_y,
+    )
+    return to_x, to_y
+
+
+def own_kernel(own, received, from_x, from_y, kept, sent):
+    total = add_up(own, received)[0] + add_up(from_x, from_y)
+
+    @pl.when(pl.program_id(0) == 0)
+    def _():
+        kept[...] = total
+
+    @pl.when(pl.program_id(0) == 1)
+    def _():
+        sent[...] = total.astype(BF16)
+
+
+def own_sums(own_core, received, from_x, from_y):
+    rows = own_core.shape[2]
+    kept, sent = add_call(
+        own_kernel,
+        2,
+        [chip_slice(0, rows)] * 2 + [one_slice(rows)] * 2,
+        [one_slice(rows, 0, 0)] * 2,
+        [jax.ShapeDtypeStruct((1, rows, LANES), F32), jax.ShapeDtypeStruct((1, rows, LANES), BF16)],
+        "add_own",
+        own_core,
+        received,
+        from_x,
+        from_y,
+    )
+    return kept[0], sent[0]
 
 
 def coordinate(fast):
@@ -220,10 +316,12 @@
     return pl.ds(pl.multiple_of(((device >> 1) ^ chip) * height, 16), height)
 
 
-def join_attend_kernel(device_ref, *refs):
+def project_kernel(shard_count, device_ref, *refs):
+    shards, refs = refs[:shard_count], refs[shard_count:]
+    attend_ref, output_ref, query_ref, key_ref, value_ref, window_ref = refs[2 * CHIPS :]
     device = device_ref[0]
-    attend_ref, output_ref = refs[2 * CHIPS :]
     height = attend_ref.shape[1]
+    count = query_ref.shape[0]
     for core in range(2):
         for chip in range(CHIPS):
             piece = refs[core * CHIPS + chip]
@@ -235,6 +333,13 @@
                 output_ref[rows, half_lanes(device, core, block)] = piece[
                     0, pl.ds(3 * height + block * (height // CHIPS), height // CHIPS), :
                 ]
+    columns = pl.ds(pl.multiple_of(pl.program_id(0) * height, LANES), height)
+    query_ref[...] = dot_back(shards[-1][...], attend_ref[0]).astype(BF16)
+    for i, shard in enumerate(shards):
+        rows = pl.ds(i * count, count)
+        key_ref[rows, :] = dot_back(shard[...], attend_ref[1]).astype(BF16)
+        value_ref[rows, :] = dot_back(shard[...], attend_ref[2]).astype(BF16)
+        window_ref[rows, :] = shard[:, columns]
 
 
 def cut_attend_kernel(device_ref, query, key, value, output, first, second):
@@ -275,22 +380,33 @@
     return pl.CostEstimate(flops=0, bytes_accessed=2 * count, transcendentals=0)
 
 
-def join_attend(device, pieces):
+def project(device, shards, pieces):
     slices = pieces[0].shape[0]
     height = D // slices
-    piece = pl.BlockSpec((1, 4 * height, LANES), lambda k, d: (k, 0, 0))
+    count = shards[0].shape[0]
+    rows = count * len(shards)
+    piece = lambda first: pl.BlockSpec((1, 4 * height, LANES), lambda k, d: (first + k, 0, 0))
+    columns = lambda rows: pl.BlockSpec((rows, height), lambda k, d: (0, k))
+    wide = lambda rows: jax.ShapeDtypeStruct((rows, D), BF16)
     return grid_call(
-        join_attend_kernel,
+        functools.partial(project_kernel, len(shards)),
         (slices,),
-        [piece] * (2 * CHIPS),
+        [pl.BlockSpec((count, D), lambda k, d: (0, 0))] * len(shards)
+        + [piece(first) for first in first_slices(pieces)],
         [
             pl.BlockSpec((3, height, D), lambda k, d: (0, k, 0)),
             pl.BlockSpec((height, D), lambda k, d: (k, 0)),
+            columns(count),
+            columns(rows),
+            columns(rows),
+            columns(rows),
         ],
-        [jax.ShapeDtypeStruct((3, D, D), BF16), jax.ShapeDtypeStruct((D, D), BF16)],
-        "join_attend",
-        cost=moved(8 * D * D),
-    )(device, *pieces)
+        [jax.ShapeDtypeStruct((3, D, D), BF16), wide(D), wide(count), wide(rows), wide(rows), wide(rows)],
+        "project",
+        cost=pl.CostEstimate(
+            flops=2 * D * D * (2 * rows + count), bytes_accessed=16 * D * D, transcendentals=0
+        ),
+    )(device, *shards, *pieces)
 
 
 def cut_attend(device, matrices, slices):
@@ -340,10 +456,11 @@
                     0, pl.ds(block * height, height), :
                 ]
 
-    @pl.loop(0, CHIPS)
-    def _(j):
-        start = pl.multiple_of(j * height, 16)
-        rows = pl.ds(start, height)
+    joint = 2 * height
+
+    for j in range(width // joint):
+        start = j * joint
+        rows = pl.ds(start, joint)
         gate_pre = jnp.dot(w_gate[rows, :], normed_t[...], preferred_element_type=F32)
         up_pre = jnp.dot(w_up[rows, :], normed_t[...], preferred_element_type=F32)
         grad_hidden = jnp.dot(w_down[rows, :], grads_t[...], preferred_element_type=F32)
@@ -357,34 +474,31 @@
         dgate_t[rows, :] = dgate
 
         moved_ref[...] = jnp.dot(hidden, grads_ref[...], preferred_element_type=F32).astype(BF16)
-        chip = (device >> 1) ^ j
-        for core, pieces in enumerate((first, second)):
-            for block in range(blocks):
-                pieces[chip, 0, pl.ds(2 * width + block * height, height), :] = moved_ref[
-                    :, half_lanes(device, core, block)
-                ]
+        for part in range(2):
+            chip = (device >> 1) ^ (2 * j + part)
+            for core, pieces in enumerate((first, second)):
+                for block in range(blocks):
+                    pieces[chip, 0, pl.ds(2 * width + block * height, height), :] = moved_ref[
+                        pl.ds(part * height, height), half_lanes(device, core, block)
+                    ]
         for member, values in enumerate((dgate, dup)):
             moved_ref[...] = jnp.dot(values, normed_ref[...], preferred_element_type=F32).astype(BF16)
-            target = pl.ds(pl.multiple_of(member * width + start, 16), height)
+            target = pl.ds(member * width + start, joint)
             for core, pieces in enumerate((first, second)):
                 for chip in range(CHIPS):
                     pieces[chip, 0, target, :] = moved_ref[:, lanes_of(device, 2 * chip + core)]
 
-    tile = min(256, normed_ref.shape[0])
-    for t in range(normed_ref.shape[0] // tile):
-        rows = pl.ds(t * tile, tile)
-        result_ref[rows, :] += jnp.dot(
-            hidden_t[:, rows].T, w_down[...], preferred_element_type=F32
-        )
-        back_ref[rows, :] += jnp.dot(
-            dgate_t[:, rows].T, w_gate[...], preferred_element_type=F32
-        ) + jnp.dot(dup_t[:, rows].T, w_up[...], preferred_element_type=F32)
+    result_ref[...] += jnp.dot(hidden_t[...].T, w_down[...], preferred_element_type=F32)
+    back_ref[...] += jnp.dot(dgate_t[...].T, w_gate[...], preferred_element_type=F32)
+    back_ref[...] += jnp.dot(dup_t[...].T, w_up[...], preferred_element_type=F32)
 
 
 def hidden_layer(device, normed, grads, pieces, width, start, slices, earlier=()):
     count = normed.shape[0]
     whole = pl.BlockSpec((count, D), lambda k, d: (0, 0))
-    piece = lambda part: pl.BlockSpec((1, width, LANES), lambda k, d: (start + k, part, 0))
+    piece = lambda first, part: pl.BlockSpec(
+        (1, width, LANES), lambda k, d: (first + start + k, part, 0)
+    )
     out_piece = pl.BlockSpec((CHIPS, 1, 3 * width, LANES), lambda k, d: (0, start + k, 0, 0))
     shape = jax.ShapeDtypeStruct((CHIPS, pieces[0].shape[0], 3 * width, LANES), BF16)
     total = jax.ShapeDtypeStruct((count, D), F32)
@@ -393,7 +507,7 @@
         functools.partial(hidden_kernel, len(earlier)),
         (slices,),
         [whole, whole]
-        + [piece(part) for part in range(3)] * (2 * CHIPS)
+        + [piece(first, part) for first in first_slices(pieces) for part in range(3)]
         + [pl.BlockSpec(memory_space=pl.ANY)] * len(earlier),
         [whole, whole, out_piece, out_piece],
         [total, total, shape, shape],
@@ -407,7 +521,7 @@
             pltpu.VMEM((width, count), BF16),
             pltpu.VMEM((width, count), BF16),
             pltpu.VMEM((width, count), BF16),
-            pltpu.VMEM((width // CHIPS, D), BF16),
+            pltpu.VMEM((2 * width // CHIPS, D), BF16),
         ],
         cost=pl.CostEstimate(
             flops=18 * slices * width * D * count,
@@ -419,12 +533,20 @@
 
 
 def exchanges():
-    for axis in ("dp", "mp"):
-        size = lax.axis_size(axis)
-        step = 1
-        while step < size:
-            yield axis, [(i, i ^ step) for i in range(size)]
-            step *= 2
+    axes = ("dp", "mp")
+    size = lax.axis_size(axes)
+    masks = [1 << bit for bit in range(size.bit_length() - 1)]
+    if size == 32:
+        masks = [3, 5, 9, 17, 7]
+    return [(axes, [(i, i ^ mask) for i in range(size)]) for mask in masks]
+
+
+def neighbours(values, axis, steps):
+    return [pairwise(values, axis, step) for step in steps]
+
+
+def sum_of_four(values, others):
+    return (values + others[0]) + (others[1] + others[2])
 
 
 def hash_rows(hashes):
@@ -481,26 +603,32 @@
         fill_bias(bias_ref, query_labels, key_labels, tile, tile_count, history)
 
     vt_ref[...] = v_ref[...].T
+    chunk = math.gcd(span, 256)
     for t in range(tile_count):
         base = history - SPAN + t * tile
         queries = (q_ref[pl.ds(t * tile, tile), :] * HD ** (-0.5)).astype(BF16).T
-        keys = k_ref[pl.ds(base, span), :]
         outputs = []
         for head in range(2):
-            scores = (
-                jnp.dot(keys, head_rows(queries, head), preferred_element_type=F32) + bias_ref[t]
-            )
-            maximum = jnp.max(scores, axis=0, keepdims=True)
-            powers = jnp.exp(scores - maximum)
-            total = jnp.sum(powers, axis=0, keepdims=True)
-            attention = (powers * (1.0 / total)).astype(BF16)
-            outputs.append(
-                jnp.dot(
-                    vt_ref[pl.ds(head * HD, HD), pl.ds(base, span)],
-                    attention,
+            rows = head_rows(queries, head)
+            scores, maximum = [], None
+            for start in range(0, span, chunk):
+                part = (
+                    jnp.dot(k_ref[pl.ds(base + start, chunk), :], rows, preferred_element_type=F32)
+                    + bias_ref[t, pl.ds(start, chunk), :]
+                )
+                top = jnp.max(part, axis=0, keepdims=True)
+                maximum = top if maximum is None else jnp.maximum(maximum, top)
+                scores.append(part)
+            total, weighted = 0.0, 0.0
+            for i, part in enumerate(scores):
+                powers = jnp.exp(part - maximum)
+                total = total + jnp.sum(powers, axis=0, keepdims=True)
+                weighted = weighted + jnp.dot(
+                    vt_ref[pl.ds(head * HD, HD), pl.ds(base + i * chunk, chunk)],
+                    powers.astype(BF16),
                     preferred_element_type=F32,
                 )
-            )
+            outputs.append(weighted * (1.0 / total))
             lse_ref[0, pl.ds(head, 1), pl.ds(t * tile, tile)] = maximum + jnp.log(total)
         o_ref[pl.ds(t * tile, tile), :] = jnp.concatenate(outputs, axis=0).T.astype(BF16)
 
@@ -621,50 +749,68 @@
     )(*inputs, context, grads, log_sums)
 
 
-def project_back_kernel(first_own, *refs):
+def project_back_kernel(per_shard, *refs):
     queries, keys, values = refs[0:2], refs[2:4], refs[4:6]
-    weights, normed, back_ref, gain_ref = refs[6:]
+    weights, normed = refs[6:8]
+    back_refs, gain_ref, total = refs[8:-2], refs[-2], refs[-1]
     half = queries[0].shape[1]
-    tile = pl.program_id(0)
+    shard = lax.div(pl.program_id(0), per_shard)
     back = None
     for member, parts in ((1, keys), (2, values)):
         for i, part in enumerate(parts):
             term = mxu(part[...], weights[member, pl.ds(i * half, half), :])
             back = term if back is None else back + term
-    back_ref[...] = back
-
-    @pl.when(tile >= first_own)
+    total[...] = back
+
+    @pl.when(shard == len(back_refs) - 1)
     def _():
-        back_ref[...] += mxu(queries[0][...], weights[0, pl.ds(0, half), :]) + mxu(
+        total[...] += mxu(queries[0][...], weights[0, pl.ds(0, half), :]) + mxu(
             queries[1][...], weights[0, pl.ds(half, half), :]
         )
 
-    @pl.when(tile == 0)
+    for i, ref in enumerate(back_refs):
+
+        @pl.when(shard == i)
+        def _(ref=ref):
+            ref[...] = total[...].astype(ref.dtype)
+
+    @pl.when(pl.program_id(0) == 0)
     def _():
         gain_ref[...] = jnp.zeros_like(gain_ref)
 
-    gain_ref[...] += jnp.sum(back_ref[...] * normed[...].astype(F32), axis=0, keepdims=True)
+    gain_ref[...] += jnp.sum(total[...] * normed[...].astype(F32), axis=0, keepdims=True)
 
 
 def project_back(first, second, weights, window):
     count, half = first[0].shape
     rows = window.shape[0]
+    shards = rows // count
     tile = min(256, count)
-    first_own = (rows - count) // tile
-    own = pl.BlockSpec((tile, half), lambda i: (jnp.maximum(i - first_own, 0), 0))
+    per_shard = count // tile
+    shard_spec = lambda width, shard: pl.BlockSpec(
+        (tile, width), lambda i: (jnp.clip(i - shard * per_shard, 0, per_shard - 1), 0)
+    )
+    own = shard_spec(half, shards - 1)
     seen = pl.BlockSpec((tile, half), lambda i: (i, 0))
     wide = pl.BlockSpec((tile, D), lambda i: (i, 0))
-    return pl.pallas_call(
-        functools.partial(project_back_kernel, first_own),
+    shapes = [
+        jax.ShapeDtypeStruct((count, D), BF16 if shard == 0 and shards > 1 else F32)
+        for shard in range(shards)
+    ]
+    outs = pl.pallas_call(
+        functools.partial(project_back_kernel, per_shard),
         grid=(rows // tile,),
         in_specs=[own, own, seen, seen, seen, seen, pl.BlockSpec((3, D, D), lambda i: (0, 0, 0)), wide],
-        out_specs=[wide, pl.BlockSpec((1, D), lambda i: (0, 0))],
-        out_shape=[jax.ShapeDtypeStruct((rows, D), F32), jax.ShapeDtypeStruct((1, D), F32)],
+        out_specs=[shard_spec(D, shard) for shard in range(shards)]
+        + [pl.BlockSpec((1, D), lambda i: (0, 0))],
+        out_shape=shapes + [jax.ShapeDtypeStruct((1, D), F32)],
+        scratch_shapes=[pltpu.VMEM((tile, D), F32)],
         cost_estimate=pl.CostEstimate(
             flops=2 * D * D * (2 * rows + count), bytes_accessed=12 * rows * D, transcendentals=0
         ),
         name="project_back",
     )(first[0], second[0], first[1], second[1], first[2], second[2], weights, window)
+    return outs[:-1], outs[-1]
 
 
 def split(values):
@@ -728,10 +874,9 @@
     return lax.rsqrt(jnp.sqrt(norm))
 
 
-def shampoo_kernel(
-    step_size, pack, grad_ref, master_ref, short_ref, long_ref, weight_ref, short_out, long_out
-):
-    blocks, short, width = grad_ref.shape
+def shampoo_blocks(step_size, pack, grads, shorts_old, longs_old, short_out, long_out):
+    blocks = len(grads)
+    short, width = grads[0].shape
     side = pack * short
     row = lax.broadcasted_iota(jnp.int32, (side, side), 0)
     lane = lax.broadcasted_iota(jnp.int32, (side, side), 1)
@@ -747,43 +892,132 @@
     alone = lambda values: values
     packed_long = width == short
 
-    shorts, longs, rows, scales = [], [], [], []
-    for b in range(blocks):
-        grad = grad_ref[b]
-        short_new = 0.5 * short_ref[b] + 0.5 * dot_split(grad, grad, (1,))
+    shorts, longs, scales = [], [], []
+    for b, grad in enumerate(grads):
+        short_new = 0.5 * shorts_old(b) + 0.5 * dot_split(grad, grad, (1,))
         grad_t = grad.T
-        long_new = 0.5 * long_ref[b] + 0.5 * dot_split(grad_t, grad_t, (1,))
-        short_out[b] = short_new
-        long_out[b] = long_new
+        long_new = 0.5 * longs_old(b) + 0.5 * dot_split(grad_t, grad_t, (1,))
+        short_out(b, short_new)
+        long_out(b, long_new)
         short_norm = jnp.sqrt(total_of(short_new * short_new) + 1e-06)
         long_norm = jnp.sqrt(total_of(long_new * long_new) + 1e-06)
         shorts.append(short_new / short_norm)
         longs.append(long_new / long_norm)
-        rows.append(grad)
         scales.append(step_size * quarter(short_norm) * quarter(long_norm))
     groups = [range(i, i + pack) for i in range(0, blocks, pack)]
     left = [Chain(beside([shorts[b] for b in g]), eye, spread) for g in groups]
     if packed_long:
         right = [
-            Chain(beside([longs[b] for b in g]), beside([rows[b] for b in g]), spread) for g in groups
+            Chain(beside([longs[b] for b in g]), beside([grads[b] for b in g]), spread) for g in groups
         ]
     else:
-        right = [Chain(longs[b], rows[b], alone) for b in range(blocks)]
+        right = [Chain(longs[b], grads[b], alone) for b in range(blocks)]
     run_chains(left + right)
+    steps = []
     for i, g in enumerate(groups):
         high, low = split(left[i].rows)
         if packed_long:
             second, second_low = split(right[i].rows)
             second, second_low = spread(second), spread(second_low)
-            steps = mxu(high, second) + mxu(low, second) + mxu(high, second_low)
-            steps = [steps[:, j * short : (j + 1) * short] for j in range(pack)]
+            total = mxu(high, second) + mxu(low, second) + mxu(high, second_low)
+            parts = [total[:, j * short : (j + 1) * short] for j in range(pack)]
         else:
             second, second_low = split(jnp.concatenate([right[b].rows for b in g], axis=0))
             high, low = spread(high), spread(low)
-            steps = mxu(high, second) + mxu(low, second) + mxu(high, second_low)
-            steps = [steps[j * short : (j + 1) * short] for j in range(pack)]
-        for b, step in zip(g, steps):
-            weight_ref[b] = master_ref[b] - scales[b] * step
+            total = mxu(high, second) + mxu(low, second) + mxu(high, second_low)
+            parts = [total[j * short : (j + 1) * short] for j in range(pack)]
+        steps += [scales[b] * part for b, part in zip(g, parts)]
+    return steps
+
+
+def put(ref, lead=()):
+    def store(b, values):
+        ref[lead + (b,)] = values
+
+    return store
+
+
+def shampoo_kernel(
+    step_size, pack, grad_ref, master_ref, short_ref, long_ref, weight_ref, short_out, long_out
+):
+    blocks = grad_ref.shape[0]
+    steps = shampoo_blocks(
+        step_size,
+        pack,
+        [grad_ref[b] for b in range(blocks)],
+        lambda b: short_ref[b],
+        lambda b: long_ref[b],
+        put(short_out),
+        put(long_out),
+    )
+    for b, step in enumerate(steps):
+        weight_ref[b] = master_ref[b] - step
+
+
+def shampoo_rows_kernel(
+    step_size, turned, across, kept, scale_ref, own, one, two, master_ref, short_ref, long_ref, *refs
+):
+    grad_ref, weight_ref, short_out, long_out = refs[kept:]
+    rows = own[0] + one[...].astype(F32) + two[...].astype(F32)
+    rows = rows * scale_ref[0]
+    groups = 4
+    height = rows.shape[0] // groups
+    grads = [None] * (2 * groups)
+    for group in range(groups):
+        slab = rows[group * height : (group + 1) * height]
+        tall = slab.T if turned else None
+        for half in range(2):
+            b = half * groups + group if across else 2 * group + half
+            lanes = slice(half * BLK, (half + 1) * BLK)
+            grads[b] = tall[lanes] if turned else slab[:, lanes]
+            grad_ref[0, b] = grads[b]
+    steps = shampoo_blocks(
+        step_size,
+        4,
+        grads,
+        lambda b: short_ref[0, b],
+        lambda b: long_ref[0, b],
+        put(short_out, (0,)),
+        put(long_out, (0,)),
+    )
+    for b, step in enumerate(steps):
+        weight_ref[0, b] = master_ref[0, b] - step
+
+
+def shampoo_rows(
+    terms, scale, master, short_old, long_old, step_size, first, turned, across, start=0, stop=None, earlier=()
+):
+    members, blocks, height, width = master.shape
+    stop = members if stop is None else stop
+    short, long = short_old.shape[-1], long_old.shape[-1]
+    rows = blocks // 2 * long
+    spec = lambda *shape: pl.BlockSpec((1, blocks) + shape, lambda i: (start + i, 0, 0, 0))
+    shape = lambda *dims: jax.ShapeDtypeStruct((members, blocks) + dims, F32)
+    term = pl.BlockSpec((rows, LANES), lambda i: (first + start + i, 0))
+    own = pl.BlockSpec((1, rows, LANES), lambda i: (0, first + start + i, 0))
+    return pl.pallas_call(
+        functools.partial(shampoo_rows_kernel, step_size, turned, across, len(earlier)),
+        grid=(stop - start,),
+        in_specs=[
+            pl.BlockSpec(memory_space=pltpu.SMEM),
+            own,
+            term,
+            term,
+            spec(height, width),
+            spec(short, short),
+            spec(long, long),
+        ]
+        + [pl.BlockSpec(memory_space=pl.ANY)] * len(earlier),
+        out_specs=[spec(height, width), spec(height, width), spec(short, short), spec(long, long)],
+        out_shape=[shape(height, width), shape(height, width), shape(short, short), shape(long, long)],
+        input_output_aliases={7 + i: i for i in range(len(earlier))},
+        cost_estimate=pl.CostEstimate(
+            flops=160 * (stop - start) * blocks * long * long * long,
+            bytes_accessed=8 * (stop - start) * blocks * (long * long + short * short + 2 * short * long),
+            transcendentals=0,
+        ),
+        name="shampoo_rows",
+    )(scale.reshape(1), terms[0][None], terms[1], terms[2], master, short_old, long_old, *earlier)
 
 
 def shampoo(gradient, master, short_old, long_old, step_size, blocks):
@@ -812,8 +1046,11 @@
     return tuple(v.reshape(gradient.shape[:-2] + v.shape[-2:]) for v in outs)
 
 
+def turn(values):
+    return jnp.swapaxes(values, -1, -2)
+
+
 def step_columns(gradient, master, left, right, step_size, blocks):
-    turn = lambda values: jnp.swapaxes(values, -1, -2)
     weight, right, left = shampoo(turn(gradient), turn(master), right, left, step_size, blocks)
     return turn(weight), left, right
 
@@ -825,9 +1062,8 @@
 
 
 def quarter_root_pair(statistic):
-    entries = tuple(tuple(statistic[i, j] for j in range(2)) for i in range(2))
-    frobenius = jnp.sqrt(sum(v * v for row in entries for v in row) + 1e-06)
-    matrix = tuple(tuple(v / frobenius for v in row) for row in entries)
+    frobenius = jnp.sqrt(sum(v * v for row in statistic for v in row) + 1e-06)
+    matrix = tuple(tuple(v / frobenius for v in row) for row in statistic)
     estimate = ((1.0, 0.0), (0.0, 1.0))
     for iteration in range(ROOTS):
         (a, b), (c, d) = matrix
@@ -839,15 +1075,34 @@
     return tuple(tuple(v * scale for v in row) for row in estimate)
 
 
+def gain_kernel(grad_ref, gain_ref, left_ref, right_ref, weight_ref, left_out, right_out):
+    grads = [grad_ref[pl.ds(i, 1), :] for i in range(2)]
+    inner = lambda i, j: jnp.sum(grads[i] * grads[j], axis=1, keepdims=True)
+    products = ((inner(0, 0), inner(0, 1)), (inner(1, 0), inner(1, 1)))
+    left = tuple(
+        tuple(
+            0.5 * left_ref[pl.ds(i, 1), pl.ds(j, 1)] + 0.5 * products[i][j] for j in range(2)
+        )
+        for i in range(2)
+    )
+    left_out[...] = jnp.concatenate([jnp.concatenate(row, axis=1) for row in left], axis=0)
+    right = 0.5 * right_ref[...] + 0.5 * (grads[0] * grads[0] + grads[1] * grads[1])
+    right_out[...] = right
+    root = quarter_root_pair(left)
+    scale = GAIN_RATE * lax.rsqrt(jnp.sqrt(right))
+    for i in range(2):
+        mixed = root[i][0] * grads[0] + root[i][1] * grads[1]
+        weight_ref[pl.ds(i, 1), :] = gain_ref[pl.ds(i, 1), :] - scale * mixed
+
+
 def gain_update(gradient, gain_rows, left_old, right_old):
-    outer = jnp.sum(gradient[:, None, :] * gradient[None, :, :], axis=2)
-    left_new = 0.5 * left_old + 0.5 * outer
-    right_new = 0.5 * right_old + 0.5 * jnp.sum(gradient * gradient, axis=0)
-    (a, b), (c, d) = quarter_root_pair(left_new)
-    first, second = gradient[0], gradient[1]
-    mixed = jnp.stack([a * first + b * second, c * first + d * second])
-    direction = mixed * lax.rsqrt(jnp.sqrt(right_new))
-    return (gain_rows - GAIN_RATE * direction, left_new, right_new)
+    shapes = [gain_rows.shape, left_old.shape, (1, right_old.size)]
+    weight, left_new, right_new = pl.pallas_call(
+        gain_kernel,
+        out_shape=[jax.ShapeDtypeStruct(shape, F32) for shape in shapes],
+        name="gain_update",
+    )(gradient, gain_rows, left_old, right_old.reshape(1, -1))
+    return weight, left_new, right_new.reshape(-1)
 
 
 def dot(first, second):
@@ -948,9 +1203,8 @@
             shards.insert(0, halo(shards[0]))
         shards[0], corners = together(shards[0], corners)
         attend_pieces = gather_end(attend_slices, *sides, *corners)
-        window = jnp.concatenate(shards, axis=0)
         all_hashes = jnp.concatenate(
-            [rows_hash(piece[:, 4 * head_width :], count) for piece in attend_pieces]
+            [rows_hash(piece[:, 4 * head_width :], count) for i, piece in enumerate(attend_pieces) if i != 6]
         )
     else:
         attend_cut = jnp.concatenate(
@@ -975,12 +1229,11 @@
         shards = [first_normed]
         for _ in range(earlier):
             shards.insert(0, halo(shards[0]))
-        window = jnp.concatenate(shards, axis=0)
         all_hashes = gather_small(hashes).astype(F32)
 
     raw_weight = lengths.astype(F32) * lax.rsqrt(count_own(all_hashes))
     raw_total = jnp.sum(raw_weight).reshape(1, 1)
-    steps = list(exchanges())
+    steps = exchanges()
     grad_out = cotangent.astype(F32) * raw_weight[:, None]
     grad_low = grad_out.astype(BF16)
 
@@ -991,13 +1244,10 @@
                 rows_of_rows(to_piece(reduce_master.astype(BF16), *grids["reduce"][:2])),
             ]
         )
-        window, hidden_rows = together(window, hidden_rows)
+        shards[0], hidden_rows = together(shards[0], hidden_rows)
         slice_one = pairwise(hidden_rows, "mp", 1)
         slice_two = pairwise(hidden_rows, "mp", 2)
-    attend_w, output_w = join_attend(device, attend_pieces)
-    queries = dot_back(first_normed, attend_w[0]).astype(BF16)
-    keys = dot_back(window, attend_w[1]).astype(BF16)
-    values = dot_back(window, attend_w[2]).astype(BF16)
+    attend_w, output_w, queries, keys, values, window = project(device, shards, attend_pieces)
     labels = (query_labels, key_labels)
     if fast:
         queries, slice_one = together(queries, slice_one)
@@ -1048,7 +1298,7 @@
         raw_total = raw_total + moved
         far_grads = share_c[2:]
         far_received = pairwise(far_grads[1], "dp", 1)
-        near_corners = reduce_chips_corner(near_grads[0], near_received)
+        near_corners = send_planar(*corner_sums(near_grads[0], near_received))
         second_back = share_a[1] + share_b[1] + share_c[1]
         activations = (middle + share_a[0] + share_b[0] + share_c[0]).astype(BF16)
     else:
@@ -1069,105 +1319,139 @@
     middle_low = middle_grad.astype(BF16)
     grad_context = dot_back(middle_low, output_w).astype(BF16)
 
-    def weight_grads(context_part, parts):
-        grad_queries, grad_keys, grad_values = parts
+    def key_grads(parts):
+        return dot_weight(parts[1], window).astype(BF16)
+
+    def weight_grads(context_part, parts, keys_part):
         return [
-            dot_weight(grad_queries, first_normed).astype(BF16),
-            dot_weight(grad_keys, window).astype(BF16),
-            dot_weight(grad_values, window).astype(BF16),
+            dot_weight(parts[0], first_normed).astype(BF16),
+            keys_part,
+            dot_weight(parts[2], window).astype(BF16),
             dot_weight(context_part, middle_low).astype(BF16),
         ]
 
     slices_half = mp_size // 2
     if fast:
-        grad_context, near_corners, far_received = together(grad_context, near_corners, far_received)
-        near_sides = reduce_chips_sides(near_grads[0], near_received, *near_corners)
-        far_corners = reduce_chips_corner(far_grads[0], far_received)
+        grad_context, near_corners = together(grad_context, near_corners)
+        near_sides = side_sums(near_grads[0], near_received, *near_corners)
+        grad_context, near_sides = together(grad_context, near_sides)
+        near_sides = send_planar(*near_sides)
     backs_a = attend_back(inputs, context_a, grad_context, sums_a, tile, 0, half_pairs)
-    cut_a = cut_attend(device, weight_grads(context_a, backs_a), slices_half)
+    keys_a = key_grads(backs_a)
     if fast:
+        backs_a, keys_a, near_sides, far_received = together(backs_a, keys_a, near_sides, far_received)
+        far_corners = corner_sums(far_grads[0], far_received)
+        near_own, near_one = own_sums(near_grads[0], near_received, *near_sides)
+        backs_a, far_corners, near_one = together(backs_a, far_corners, near_one)
+        far_corners = send_planar(*far_corners)
+        near_one = pairwise(near_one, "mp", 1)
+    cut_a = cut_attend(device, weight_grads(context_a, backs_a, keys_a), slices_half)
+    if fast:
+        cut_a, grad_context, far_corners = together(cut_a, grad_context, far_corners)
+        far_sides = side_sums(far_grads[0], far_received, *far_corners)
+        cut_a, grad_context, far_sides = together(cut_a, grad_context, far_sides)
+        far_sides = send_planar(*far_sides)
         received_a = pairwise(cut_a[1], "dp", 1)
-        grad_context, cut_a, near_sides, far_corners = together(
-            grad_context, cut_a, near_sides, far_corners
-        )
-        near_own = reduce_chips_own(near_grads[0], near_received, *near_sides)
-        near_one = pairwise(near_own[1].astype(BF16), "mp", 1)
-        far_sides = reduce_chips_sides(far_grads[0], far_received, *far_corners)
     backs_b = attend_back(inputs, context_b, grad_context, sums_b, tile, half_pairs, half_pairs)
+    keys_b = key_grads(backs_b)
     if fast:
-        backs_b, far_sides, received_a = together(backs_b, far_sides, received_a)
-        far_own = reduce_chips_own(far_grads[0], far_received, *far_sides)
-        far_three = pairwise(far_own[1].astype(BF16), "mp", 1)
-        corners_a = reduce_chips_corner(cut_a[0], received_a)
-    cut_b = cut_attend(device, weight_grads(context_b, backs_b), slices_half)
+        backs_b, keys_b, far_sides, received_a, near_one = together(
+            backs_b, keys_b, far_sides, received_a, near_one
+        )
+        far_own, far_three = own_sums(far_grads[0], far_received, *far_sides)
+        corners_a = corner_sums(cut_a[0], received_a)
+        backs_b, far_three, corners_a = together(backs_b, far_three, corners_a)
+        far_three = pairwise(far_three, "mp", 1)
+        corners_a = send_planar(*corners_a)
+    cut_b = cut_attend(device, weight_grads(context_b, backs_b, keys_b), slices_half)
     if fast:
+        backs_b, cut_b, corners_a, far_three = together(backs_b, cut_b, corners_a, far_three)
+        sides_a = side_sums(cut_a[0], received_a, *corners_a)
+        far_two = (far_own + far_three.astype(F32)).astype(BF16)
+        backs_b, cut_b, sides_a, far_two = together(backs_b, cut_b, sides_a, far_two)
+        sides_a = send_planar(*sides_a)
+        far_two = pairwise(far_two, "mp", 2)
         received_b = pairwise(cut_b[1], "dp", 1)
-        backs_b, cut_b, corners_a, far_three, near_one = together(
-            backs_b, cut_b, corners_a, far_three, near_one
-        )
-        far_two = pairwise((far_own[0] + far_three.astype(F32)).astype(BF16), "mp", 2)
-        sides_a = reduce_chips_sides(cut_a[0], received_a, *corners_a)
-    window_back, gain_first = project_back(backs_a, backs_b, attend_w, window)
+    shares, gain_first = project_back(backs_a, backs_b, attend_w, window)
     gain_sums = jnp.stack([gain_first[0] / gains[0], gain_second])
 
     def halo_back(share):
         return lax.ppermute(share.astype(BF16), "mp", down_one)
 
-    shares = [window_back[k * count : (k + 1) * count] for k in range(earlier)]
+    def first_grad(carried):
+        first_back = shares[-1] + carried.astype(F32)
+        first_scaled = first_back * gains[0]
+        return weight_scale * (
+            middle_grad
+            + first_rms
+            * (first_scaled - first_hat * jnp.mean(first_scaled * first_hat, axis=1, keepdims=True))
+        )
+
     if fast:
-        window_back, received_b, sides_a = together(window_back, received_b, sides_a)
-        shares = [window_back[k * count : (k + 1) * count] for k in range(earlier)]
+        shares, received_b, sides_a, far_two = together(shares, received_b, sides_a, far_two)
+        corners_b = corner_sums(cut_b[0], received_b)
+        own_a, one_a = own_sums(cut_a[0], received_a, *sides_a)
+        shares, corners_b, one_a, far_two = together(shares, corners_b, one_a, far_two)
+        corners_b = send_planar(*corners_b)
         carried = halo_back(shares[0])
-        corners_b = reduce_chips_corner(cut_b[0], received_b)
-        own_a = reduce_chips_own(cut_a[0], received_a, *sides_a)
-        one_a = pairwise(own_a[1].astype(BF16), "mp", 1)
-        moved = lax.ppermute(gain_sums, *steps[0])
+        one_a = pairwise(one_a, "mp", 1)
     else:
         carried = halo_back(shares[0])
-        for share in shares[1:]:
+        for share in shares[1:-1]:
             carried = halo_back(share + carried.astype(F32))
         gain_sums = sum_small(gain_sums)
+        input_grad = first_grad(carried)
     grad_scale = weight_scale * total_patches ** (-0.5)
-    reduce_step, expand_step = STEP_RATE * FF ** (-0.5), STEP_RATE * D ** (-0.5)
+    reduce_step, output_step = STEP_RATE * FF ** (-0.5), STEP_RATE * OUT_FAN ** (-0.5)
+    expand_step = attend_step = STEP_RATE * D ** (-0.5)
     if fast:
-        hidden_sum = near_own[0] + near_one.astype(F32) + far_two.astype(F32)
-        hidden_sum = hidden_sum * grad_scale
-        expand_grad = from_piece(
-            columns_of_rows(hidden_sum[: 2 * hidden_width], 2), *grids["expand"][:2]
-        )
-        reduce_grad = from_piece(
-            rows_to_rows(hidden_sum[2 * hidden_width : 3 * hidden_width], D // (2 * LANES)),
-            *grids["reduce"][:2]
-        )
-        reduce_grad, expand_grad, corners_b, moved = together(
-            reduce_grad, expand_grad, corners_b, moved
-        )
+        far_two, corners_b = together(far_two, corners_b)
+        sides_b = side_sums(cut_b[0], received_b, *corners_b)
+        far_two, sides_b = together(far_two, sides_b)
+        sides_b = send_planar(*sides_b)
+        terms = (near_own, near_one, far_two)
+        reduce_out = shampoo_rows(
+            terms, grad_scale, turn(reduce_master)[None], reduce_right[None], reduce_left[None],
+            reduce_step, 2, True, False,
+        )
+        reduce_out, terms, sides_b, carried, one_a, gain_sums = together(
+            reduce_out, terms, sides_b, carried, one_a, gain_sums
+        )
+        own_b, three_b = own_sums(cut_b[0], received_b, *sides_b)
+        carried = [(share + carried.astype(F32)).astype(BF16) for share in shares[1:-1]]
+        terms, three_b, carried, gain_sums = together(terms, three_b, carried, gain_sums)
+        three_b = pairwise(three_b, "mp", 1)
+        carried = halo_back(carried[0])
+        planar = neighbours(gain_sums, "dp", (2, 4, 6))
+        expand_inputs = (grad_scale, expand_master, expand_left, expand_right, expand_step, 0, True, True)
+        expand_out = shampoo_rows(terms, *expand_inputs, 0, 1)
+        expand_out, terms, three_b, planar = together(expand_out, terms, three_b, planar)
+        gain_sums = sum_of_four(gain_sums, planar)
+        two_b = (own_b + three_b.astype(F32)).astype(BF16)
+        terms, two_b, gain_sums = together(terms, two_b, gain_sums)
+        two_b = pairwise(two_b, "mp", 2)
+        moved = pairwise(gain_sums, "dp", 1)
+        expand_out = shampoo_rows(terms, *expand_inputs, 1, 2, expand_out)
+        input_grad = first_grad(carried)
+        expand_out, two_b, input_grad, moved = together(expand_out, two_b, input_grad, moved)
         gain_sums = gain_sums + moved
-        moved = lax.ppermute(gain_sums, *steps[1])
-        sides_b = reduce_chips_sides(cut_b[0], received_b, *corners_b)
-        reduce_out = step_columns(reduce_grad, reduce_master, reduce_left, reduce_right, reduce_step, 4)
-        reduce_out, expand_grad, sides_b, carried, one_a, moved = together(
-            reduce_out, expand_grad, sides_b, carried, one_a, moved
-        )
-        gain_sums = gain_sums + moved
-        moved = lax.ppermute(gain_sums, *steps[2])
-        own_b = reduce_chips_own(cut_b[0], received_b, *sides_b)
-        three_b = pairwise(own_b[1].astype(BF16), "mp", 1)
-        for share in shares[1:]:
-            carried = halo_back(share + carried.astype(F32))
-        expand_out = step_rows(expand_grad, expand_master, expand_left, expand_right, expand_step, 8)
-        expand_out, three_b, moved = together(expand_out, three_b, moved)
-        gain_sums = gain_sums + moved
-        moved = lax.ppermute(gain_sums, *steps[3])
-        two_b = pairwise((own_b[0] + three_b.astype(F32)).astype(BF16), "mp", 2)
-        attend_sum = (own_a[0] + one_a.astype(F32) + two_b.astype(F32)) * grad_scale
-        attend_sum, carried, moved = together(attend_sum, carried, moved)
-        gain_sums = gain_sums + moved
-        gain_sums = gain_sums + lax.ppermute(gain_sums, *steps[4])
-        output_grad = from_piece(
-            rows_to_rows(attend_sum[3 * head_width :], D // (2 * LANES)), *grids["output"][:2]
-        )
-        attend_grad = from_piece(columns_of_rows(attend_sum[: 3 * head_width], 3), *grids["attend"][:2])
+        along = neighbours(gain_sums, "mp", (1, 2, 3))
+        terms = (own_a, one_a, two_b)
+        attend_out = shampoo_rows(
+            terms, grad_scale, attend_master, attend_left, attend_right, attend_step, 0, True, True
+        )
+        attend_out, terms, along = together(attend_out, terms, along)
+        gain_sums = sum_of_four(gain_sums, along)
+        output_out = shampoo_rows(
+            terms, grad_scale, output_master[None], output_left[None], output_right[None], output_step,
+            3, False, False,
+        )
+        alone = lambda outs: [v[0] for v in outs]
+        reduce_grad, reduce_weight, right_reduce, left_reduce = alone(reduce_out)
+        reduce_grad, reduce_weight = turn(reduce_grad), turn(reduce_weight)
+        expand_grad, expand_weight, left_expand, right_expand = expand_out
+        attend_grad, attend_weight, left_attend, right_attend = attend_out
+        output_grad, output_weight, left_output, right_output = alone(output_out)
     else:
         hidden_cut = jnp.stack(
             [jnp.concatenate([near_grads[core], far_grads[core]], axis=1) for core in range(2)], axis=1
@@ -1191,25 +1475,20 @@
         attend_grad = grad_scale * grad_by_columns(
             join_columns(attend_cut[:, :, :, : 3 * head_width], 3), attend_master, dp_size, mp_size
         )
-        reduce_out = step_columns(reduce_grad, reduce_master, reduce_left, reduce_right, reduce_step, 4)
-        expand_out = step_rows(expand_grad, expand_master, expand_left, expand_right, expand_step, 8)
-    first_back = window_back[history:] + carried.astype(F32)
-    first_scaled = first_back * gains[0]
-    input_grad = weight_scale * (
-        middle_grad
-        + first_rms
-        * (first_scaled - first_hat * jnp.mean(first_scaled * first_hat, axis=1, keepdims=True))
-    )
-
-    reduce_weight, left_reduce, right_reduce = reduce_out
-    expand_weight, left_expand, right_expand = expand_out
+        reduce_weight, left_reduce, right_reduce = step_columns(
+            reduce_grad, reduce_master, reduce_left, reduce_right, reduce_step, 4
+        )
+        expand_weight, left_expand, right_expand = step_rows(
+            expand_grad, expand_master, expand_left, expand_right, expand_step, 8
+        )
+        output_weight, left_output, right_output = step_rows(
+            output_grad, output_master, output_left, output_right, output_step, 8
+        )
+        attend_weight, left_attend, right_attend = step_rows(
+            attend_grad, attend_master, attend_left, attend_right, attend_step, 8
+        )
+
     gains_grad = gain_sums * grad_scale
-    output_weight, left_output, right_output = step_rows(
-        output_grad, output_master, output_left, output_right, STEP_RATE * OUT_FAN ** (-0.5), 8
-    )
-    attend_weight, left_attend, right_attend = step_rows(
-        attend_grad, attend_master, attend_left, attend_right, STEP_RATE * D ** (-0.5), 8
-    )
     gains_weight, left_gains, right_gains = gain_update(gains_grad, gains, gains_left, gains_right)
     return (
         activations,

time: 594 us -> 556 us (0.936)
  other arithmetic: 86.6 us -> 47.1 us
  Pallas kernels: 211 us -> 247 us
  waiting for transfers between devices: 85.7 us -> 113 us
  local copies, waits for them, and re-layouts: 48.1 us -> 22.6 us
  starting transfers between devices: 97.9 us -> 82.5 us
  matrix products: 45.4 us -> 33.2 us
  between operations: 13.8 us -> 5.79 us
    pallas_call x6 -> x20, Pallas kernels: 67.2 us -> 118 us  [the longest x5 47.6 us: shampoo_rows(): pl.pallas_call(functools.partial(shampoo_rows_kernel, step_size, turned,...]
    add x10 -> x1, other arithmetic: 22.2 us -> 0.01 us  [sum_of_four(): return values + others[0] + (others[1] + others[2])]
    dot_general x4 -> x1, matrix products: 21.9 us -> 2.28 us  [dot_back(): lax.dot_general(first, second, (((1,), (1,)), ((), ())), preferred_elemen...]
    ppermute x1, starting transfers between devices: 21.8 us -> 3.47 us  [body(): moved = lax.ppermute(raw_total, *steps[1])]
    ppermute x56 -> x60, waiting for transfers between devices: 65.9 us -> 80.8 us  [pairwise(): lax.ppermute(values, axis, [(i, i ^ step) for i in range(lax.axis_size(ax...]
    pallas_call x2, Pallas kernels: 39.3 us -> 29.4 us  [attend(): pl.pallas_call(functools.partial(attend_kernel, tile, window - count), gr...]
    reshape x6 -> x0, local copies, waits for them, and re-layouts: 9.41 us -> none  [the longest x2 5.15 us: from_piece(): grid = piece.reshape(leading + (rows, height, columns, width))]
    another operation x4 -> x0, other arithmetic: 7.72 us -> none
  transfers between devices with their start and end apart: 70 -> 69, of which waited for: 18 -> 23; matrix products, arithmetic and copies ran while one was open for 27% -> 14% of each run, Pallas kernels for 36% -> 39%
where the time goes in v3:
time: 556 us; the launch traced here: 551 us
  Pallas kernels  247 us (44%)
  waiting for transfers between devices  113 us (20%)
  starting transfers between devices  82.5 us (15%)
  other arithmetic  47.1 us (8%)
  matrix products  33.2 us (6%)
  local copies, waits for them, and re-layouts  22.6 us (4%)
  between operations  5.79 us (1%)
    ppermute x60, waiting for transfers between devices, pairwise(): lax.ppermute(values, axis, [(i, i ^ step) for i in range(lax.axis_size(ax...  80.8 us
    pallas_call x3, Pallas kernels, hidden_layer(): grid_call(functools.partial(hidden_kernel, len(earlier)), (slices,), [who...  57.5 us
    ppermute x60, starting transfers between devices, pairwise(): lax.ppermute(values, axis, [(i, i ^ step) for i in range(lax.axis_size(ax...  55.8 us
    pallas_call x5, Pallas kernels, shampoo_rows(): pl.pallas_call(functools.partial(shampoo_rows_kernel, step_size, turned,...  47.6 us
    pallas_call x12, Pallas kernels, add_call(): pl.pallas_call(kernel, grid=(slices,), in_specs=in_specs, out_specs=out_s...  36.4 us
    pallas_call x2, Pallas kernels, attend_back(): pl.pallas_call(functools.partial(attend_back_kernel, tile, window - count...  33.5 us
    pallas_call x2, Pallas kernels, attend(): pl.pallas_call(functools.partial(attend_kernel, tile, window - count), gr...  29.4 us
    dot_general x8, matrix products, dot_weight(): lax.dot_general(first, second, (((0,), (0,)), ((), ())), preferred_elemen...  28.1 us
  transfers between devices with their start and end apart: 69, of which 23 were waited for; matrix products, arithmetic and copies ran while one was open for 14% of the time, Pallas kernels for 39%

profile of v3, /device:TPU:0, one launch (start us, length us, event | category | flops | bytes accessed | tf_op | source)
XLA Modules:
  0.0 551.2 jit_solution(9606717950814984438)
XLA Ops:
  4.6 4.1 collective-permute-start
  11.0 10.1 %collective-permute-done = bf16[1056,128]{1,0:T(8,128)(2,1)S(1)} collective-permute-done((bf16[1056,128]{1,0:T(8,128)(2,1)S(1)}, bf16[1056,128]{1,0:T(8,128)(2,1)S(1)}, u32[]{:S(2)}, u32[]{:S(2)}) %collective-permute-start) | collective-permute-done | bytes 270368 | tf_op jit(solution)/shard_map/ppermute | solution.py:82
  21.7 7.0 %collective-permute-done.3 = bf16[1056,128]{1,0:T(8,128)(2,1)S(1)} collective-permute-done((bf16[1056,128]{1,0:T(8,128)(2,1)S(1)}, bf16[1056,128]{1,0:T(8,128)(2,1)S(1)}, u32[]{:S(2)}, u32[]{:S(2)}) %collective-permute-start.3) | collective-permute-done | bytes 270368 | tf_op jit(solution)/shard_map/ppermute | solution.py:82
  31.7 3.6 collective-permute-start.1
  35.4 23.0 %collective-permute-done.1.refs_1_ = bf16[512,1024]{1,0:T(8,128)(2,1)S(1)} collective-permute-done((bf16[512,1024]{1,0:T(8,128)(2,1)S(1)}, bf16[512,1024]{1,0:T(8,128)(2,1)S(1)}, u32[]{:S(2)}, u32[]{:S(2)}) %collective-permute-start.1) | collective-permute-done | bytes 1048608 | tf_op jit(solution)/shard_map/ppermute | solution.py:1182
  64.9 5.6 %collective-permute-start.7 = (bf16[512,1024]{1,0:T(8,128)(2,1)}, bf16[512,1024]{1,0:T(8,128)(2,1)}, u32[]{:S(2)}, u32[]{:S(2)}) collective-permute-start(bf16[512,1024]{1,0:T(8,128)(2,1)} %copy-done.57), channel_id=1, source_target_pairs={{0,1},{1,2},{2,3},{4,5},{5,6},{6,7},{8,9},{9,10},{10,11},{12,13},{... | collective-permute-start | bytes 3145736 | tf_op jit(solution)/shard_map/ppermute | solution.py:1182
  76.6 12.8 %collective-permute-done.8 = bf16[2,1056,128]{2,1,0:T(8,128)(2,1)S(1)} collective-permute-done((bf16[2,1056,128]{2,1,0:T(8,128)(2,1)}, bf16[2,1056,128]{2,1,0:T(8,128)(2,1)S(1)}, u32[]{:S(2)}, u32[]{:S(2)}) %collective-permute-start.8) | collective-permute-done | bytes 540704 | tf_op jit(solution)/shard_map/ppermute | solution.py:82
  95.6 3.4 collective-permute-start.16
  100.0 16.5 %project.1 = (bf16[3,1024,1024]{2,1,0:T(8,128)(2,1)}, bf16[1024,1024]{1,0:T(8,128)(2,1)}, bf16[512,1024]{1,0:T(8,128)(2,1)}, bf16[1536,1024]{1,0:T(8,128)(2,1)},...) custom-call(s32[1]{0:T(128)} %bitcast.device_ref, bf16[512,1024]{1,0:T(8,128)(2,1)} %collective-permute-done.7.refs_0_, ...), custom_call_target="tpu_custom_call" | custom-call | flops 7516192768 | bytes 16777216 | tf_op jit(solution)/shard_map/project/pallas_call | solution.py:391
  116.5 3.5 collective-permute-done.12
  124.4 14.5 %attend.2 = (bf16[512,512]{1,0:T(8,128)(2,1)}, f32[4,2,512]{2,1,0:T(2,128)}) custom-call(s32[1,512]{1,0:T(1,128)} %bitcast.146, s32[1536,1]{1,0:T(8,128)} %reshape.250.key_labels, bf16[512,1024]{1,0:T(8,128)(2,1)} %get-tuple-element.313.q_ref, bf16[1536,1024]{1,0:T(8,128)(2,1)} %get-tuple-element.307.k_ref, bf16[1536,1024]{1,0:T(8,128)(2,1)} %get-tuple-element.308.v_ref), custom_call_target="tpu_custom_call" | custom-call | flops 2684354560 | bytes 4194304 | tf_op jit(solution)/shard_map/attend/pallas_call | solution.py:704
  138.9 8.1 %collective-permute-done.13.refs_3_.refs_4_.refs_5_ = bf16[2,2112,128]{2,1,0:T(8,128)(2,1)S(1)} collective-permute-done((bf16[2,2112,128]{2,1,0:T(8,128)(2,1)S(1)}, bf16[2,2112,128]{2,1,0:T(8,128)(2,1)S(1)}, u32[]{:S(2)}, u32[]{:S(2)}) %collective-permute-start.13) | collective-permute-done | bytes 1081376 | tf_op jit(solution)/shard_map/ppermute | solution.py:82
  150.8 4.2 convert_reduce_fusion
  164.2 14.9 %attend.3 = (bf16[512,512]{1,0:T(8,128)(2,1)}, f32[4,2,512]{2,1,0:T(2,128)}) custom-call(s32[1,512]{1,0:T(1,128)} %bitcast.147, s32[1536,1]{1,0:T(8,128)} %reshape.250.key_labels, bf16[512,1024]{1,0:T(8,128)(2,1)} %get-tuple-element.313.q_ref, bf16[1536,1024]{1,0:T(8,128)(2,1)} %get-tuple-element.307.k_ref, bf16[1536,1024]{1,0:T(8,128)(2,1)} %get-tuple-element.308.v_ref), custom_call_target="tpu_custom_call" | custom-call | flops 2684354560 | bytes 4194304 | tf_op jit(solution)/shard_map/attend/pallas_call | solution.py:704
  189.4 3.5 collective-permute-start.23
  199.1 15.5 %hidden_layer.3 = (f32[512,1024]{1,0:T(8,128)}, f32[512,1024]{1,0:T(8,128)}, bf16[4,2,2112,128]{3,2,1,0:T(8,128)(2,1)}, bf16[4,2,2112,128]{3,2,1,0:T(8,128)(2,1)}) custom-call(s32[1]{0:T(128)} %bitcast.device_ref, bf16[512,1024]{1,0:T(8,128)(2,1)} %multiply_convert_fusion.normed_ref, bf16[512,1024]{1,0:T(8,128)(2,1)} %fusion.11.grads_ref, ...), custom_call_target="tpu_custom_call" | custom-call | flops 6643777536 | bytes 8650752 | tf_op jit(solution)/shard_map/hidden_layer/pallas_call | solution.py:506
  222.3 4.3 collective-permute-start.31
  226.6 15.6 %hidden_layer.4 = (f32[512,1024]{1,0:T(8,128)}, f32[512,1024]{1,0:T(8,128)}, bf16[4,2,2112,128]{3,2,1,0:T(8,128)(2,1)}, bf16[4,2,2112,128]{3,2,1,0:T(8,128)(2,1)}) custom-call(s32[1]{0:T(128)} %bitcast.device_ref, bf16[512,1024]{1,0:T(8,128)(2,1)} %multiply_convert_fusion.normed_ref, ...), custom_call_target="tpu_custom_call", output_to_operand_aliasing={{2}: (27, {}), {3}: (28, {})} | custom-call | flops 6643777536 | bytes 8650752 | tf_op jit(solution)/shard_map/hidden_layer/pallas_call | solution.py:506
  246.8 4.5 collective-permute-done.32.refs_21_.refs_22_.refs_23_
  252.3 26.4 %hidden_layer.5 = (f32[512,1024]{1,0:T(8,128)}, f32[512,1024]{1,0:T(8,128)}, bf16[4,2,2112,128]{3,2,1,0:T(8,128)(2,1)}, bf16[4,2,2112,128]{3,2,1,0:T(8,128)(2,1)}) custom-call(s32[1]{0:T(128)} %bitcast.device_ref, bf16[512,1024]{1,0:T(8,128)(2,1)} %multiply_convert_fusion.normed_ref, bf16[512,1024]{1,0:T(8,128)(2,1)} %fusion.11.grads_ref, ...), custom_call_target="tpu_custom_call" | custom-call | flops 13287555072 | bytes 17301504 | tf_op jit(solution)/shard_map/hidden_layer/pallas_call | solution.py:506
  278.9 3.2 add_corner.4
  284.0 3.8 multiply_reduce_fusion
  288.5 3.4 multiply_add_fusion
  298.1 3.8 add_sides.4
  303.2 16.7 %attend_back.2 = (bf16[512,512]{1,0:T(8,128)(2,1)}, bf16[1536,512]{1,0:T(8,128)(2,1)}, bf16[1536,512]{1,0:T(8,128)(2,1)}) custom-call(s32[1,512]{1,0:T(1,128)} %bitcast.148, s32[1536,1]{1,0:T(8,128)} %reshape.250.key_labels, bf16[512,1024]{1,0:T(8,128)(2,1)} %get-tuple-element.313.q_ref, bf16[1536,1024]{1,0:T(8,128)(2,1)} %get-tuple-element.307.k_ref, ...), custom_call_target="tpu_custom_call" | custom-call | flops 6710886400 | bytes 8388608 | tf_op jit(solution)/shard_map/attend_back/pallas_call | solution.py:729
  319.9 5.1 convolution_convert_fusion.3.key
  328.2 3.9 add_own.4
  339.6 4.8 convolution_convert_fusion.2.value
  344.3 4.1 cut_attend.2
  349.4 3.9 add_sides.5
  356.5 16.8 %attend_back.3 = (bf16[512,512]{1,0:T(8,128)(2,1)}, bf16[1536,512]{1,0:T(8,128)(2,1)}, bf16[1536,512]{1,0:T(8,128)(2,1)}) custom-call(s32[1,512]{1,0:T(1,128)} %bitcast.149, s32[1536,1]{1,0:T(8,128)} %reshape.250.key_labels, bf16[512,1024]{1,0:T(8,128)(2,1)} %get-tuple-element.313.q_ref, bf16[1536,1024]{1,0:T(8,128)(2,1)} %get-tuple-element.307.k_ref, ...), custom_call_target="tpu_custom_call" | custom-call | flops 6710886400 | bytes 8388608 | tf_op jit(solution)/shard_map/attend_back/pallas_call | solution.py:729
  373.2 5.2 convolution_convert_fusion.1.key
  382.5 3.9 add_own.5
  390.3 5.1 convolution_convert_fusion.value
  398.6 4.4 cut_attend.3
  411.4 15.8 %project_back.1 = (bf16[512,1024]{1,0:T(8,128)(2,1)}, f32[512,1024]{1,0:T(8,128)}, f32[512,1024]{1,0:T(8,128)}, f32[1,1024]{1,0:T(1,128)}) custom-call(bf16[512,512]{1,0:T(8,128)(2,1)} %get-tuple-element.394.refs_0_, bf16[512,512]{1,0:T(8,128)(2,1)} %get-tuple-element.448.refs_1_, bf16[1536,512]{1,0:T(8,128)(2,1)} %get-tuple-element.449.refs_2_, ...), custom_call_target="tpu_custom_call" | custom-call | flops 7516192768 | bytes 18874368 | tf_op jit(solution)/shard_map/project_back/pallas_call | solution.py:800
  427.2 10.9 %collective-permute-done.52.two = bf16[2112,128]{1,0:T(8,128)(2,1)} collective-permute-done((bf16[2112,128]{1,0:T(8,128)(2,1)}, bf16[2112,128]{1,0:T(8,128)(2,1)}, u32[]{:S(2)}, u32[]{:S(2)}) %collective-permute-start.52) | collective-permute-done | bytes 540704 | tf_op jit(solution)/shard_map/ppermute | solution.py:82
  449.1 4.1 collective-permute-done.53.corner_x
  458.6 9.3 %shampoo_rows.5 = (f32[1,8,64,176]{3,2,1,0:T(8,128)}, f32[1,8,64,176]{3,2,1,0:T(8,128)}, f32[1,8,64,64]{3,2,1,0:T(8,128)}, f32[1,8,176,176]{3,2,1,0:T(8,128)}) custom-call(f32[1]{0:T(128)} %bitcast.39.scale_ref, f32[1,2112,128]{2,1,0:T(8,128)} %get-tuple-element.385.own, bf16[2112,128]{1,0:T(8,128)(2,1)} %collective-permute-done.45.one, ...), custom_call_target="tpu_custom_call" | custom-call | flops 6978273280 | bytes 3686400 | tf_op jit(solution)/shard_map/shampoo_rows/pallas_call | solution.py:998
  467.8 7.8 %collective-permute-done.58.one = bf16[1024,128]{1,0:T(8,128)(2,1)} collective-permute-done((bf16[1024,128]{1,0:T(8,128)(2,1)}, bf16[1024,128]{1,0:T(8,128)(2,1)}, u32[]{:S(2)}, u32[]{:S(2)}) %collective-permute-start.58) | collective-permute-done | bytes 262176 | tf_op jit(solution)/shard_map/ppermute | solution.py:82
  486.3 9.3 %shampoo_rows.6 = (f32[2,8,64,176]{3,2,1,0:T(8,128)}, f32[2,8,64,176]{3,2,1,0:T(8,128)}, f32[2,8,64,64]{3,2,1,0:T(8,128)}, f32[2,8,176,176]{3,2,1,0:T(8,128)}) custom-call(f32[1]{0:T(128)} %bitcast.39.scale_ref, f32[1,2112,128]{2,1,0:T(8,128)} %get-tuple-element.385.own, bf16[2112,128]{1,0:T(8,128)(2,1)} %collective-permute-done.45.one, ...), custom_call_target="tpu_custom_call" | custom-call | flops 6978273280 | bytes 3686400 | tf_op jit(solution)/shard_map/shampoo_rows/pallas_call | solution.py:998
  496.4 4.1 collective-permute-start.63
  500.5 9.6 %shampoo_rows.7 = (f32[2,8,64,176]{3,2,1,0:T(8,128)}, f32[2,8,64,176]{3,2,1,0:T(8,128)}, f32[2,8,64,64]{3,2,1,0:T(8,128)}, f32[2,8,176,176]{3,2,1,0:T(8,128)}) custom-call(f32[1]{0:T(128)} %bitcast.39.scale_ref, f32[1,2112,128]{2,1,0:T(8,128)} %get-tuple-element.385.own, ...), custom_call_target="tpu_custom_call", output_to_operand_aliasing={{0}: (7, {}), {1}: (8, {}), {2}: (9, {}), {3}: (10, {})} | custom-call | flops 6978273280 | bytes 3686400 | tf_op jit(solution)/shard_map/shampoo_rows/pallas_call | solution.py:998
  510.1 6.0 %collective-permute-done.64 = bf16[512,1024]{1,0:T(8,128)(2,1)} collective-permute-done((bf16[512,1024]{1,0:T(8,128)(2,1)}, bf16[512,1024]{1,0:T(8,128)(2,1)}, u32[]{:S(2)}, u32[]{:S(2)}) %collective-permute-start.64) | collective-permute-done | bytes 1048608 | tf_op jit(solution)/shard_map/ppermute | solution.py:1379
  518.6 3.3 fusion.8
  522.8 3.6 collective-permute-start.66
  528.8 13.6 %shampoo_rows.8 = (f32[3,8,64,64]{3,2,1,0:T(8,128)}, f32[3,8,64,64]{3,2,1,0:T(8,128)}, f32[3,8,64,64]{3,2,1,0:T(8,128)}, f32[3,8,64,64]{3,2,1,0:T(8,128)}) custom-call(f32[1]{0:T(128)} %bitcast.39.scale_ref, f32[1,1024,128]{2,1,0:T(8,128)} %get-tuple-element.531.own, bf16[1024,128]{1,0:T(8,128)(2,1)} %collective-permute-done.58.one, ...), custom_call_target="tpu_custom_call" | custom-call | flops 1006632960 | bytes 3145728 | tf_op jit(solution)/shard_map/shampoo_rows/pallas_call | solution.py:998
  545.1 5.8 %shampoo_rows.9 = (f32[1,8,64,64]{3,2,1,0:T(8,128)}, f32[1,8,64,64]{3,2,1,0:T(8,128)}, f32[1,8,64,64]{3,2,1,0:T(8,128)}, f32[1,8,64,64]{3,2,1,0:T(8,128)}) custom-call(f32[1]{0:T(128)} %bitcast.39.scale_ref, f32[1,1024,128]{2,1,0:T(8,128)} %get-tuple-element.531.own, bf16[1024,128]{1,0:T(8,128)(2,1)} %collective-permute-done.58.one, ...), custom_call_target="tpu_custom_call" | custom-call | flops 335544320 | bytes 1048576 | tf_op jit(solution)/shard_map/shampoo_rows/pallas_call | solution.py:998
  (346 shorter events, 153.1 us)
Async XLA Ops:
  4.6 16.5 %collective-permute-start = (bf16[1056,128]{1,0:T(8,128)(2,1)S(1)}, bf16[1056,128]{1,0:T(8,128)(2,1)S(1)}, u32[]{:S(2)}, u32[]{:S(2)}) collective-permute-start(bf16[1056,128]{1,0:T(8,128)(2,1)S(1)} %get-tuple-element.572), channel_id=1, source_target_pairs={{0,2},{1,3},{2,0},{3,1},{4,6},{5,7},{6,4},{7,5},{8,10},{9,11},{10,... | collective-permute-start | bytes 811016 | tf_op jit(solution)/shard_map/ppermute | solution.py:82
  28.9 29.5 %collective-permute-start.4 = (bf16[4,1056,128]{2,1,0:T(8,128)(2,1)S(1)}, bf16[4,1056,128]{2,1,0:T(8,128)(2,1)S(1)}, u32[]{:S(2)}, u32[]{:S(2)}) collective-permute-start(bf16[4,1056,128]{2,1,0:T(8,128)(2,1)S(1)} %pad_maximum_fusion.3.refs_3_), channel_id=1, source_target_pairs={{0,8},{4,12},{8,0},{12,4},{16,24},{20,28},{24,16},{28,20},{1,9},{5... | collective-permute-start | bytes 3244040 | tf_op jit(solution)/shard_map/ppermute | solution.py:82
  30.2 28.2 %collective-permute-start.5 = (bf16[4,1056,128]{2,1,0:T(8,128)(2,1)S(1)}, bf16[4,1056,128]{2,1,0:T(8,128)(2,1)S(1)}, u32[]{:S(2)}, u32[]{:S(2)}) collective-permute-start(bf16[4,1056,128]{2,1,0:T(8,128)(2,1)S(1)} %pad_maximum_fusion.3.refs_3_), channel_id=1, source_target_pairs={{0,16},{4,20},{8,24},{12,28},{16,0},{20,4},{24,8},{28,12},{1,17},{... | collective-permute-start | bytes 3244040 | tf_op jit(solution)/shard_map/ppermute | solution.py:82
  31.7 27.6 %collective-permute-start.6 = (bf16[4,1056,128]{2,1,0:T(8,128)(2,1)S(1)}, bf16[4,1056,128]{2,1,0:T(8,128)(2,1)}, u32[]{:S(2)}, u32[]{:S(2)}) collective-permute-start(bf16[4,1056,128]{2,1,0:T(8,128)(2,1)S(1)} %pad_maximum_fusion.3.refs_3_), channel_id=1, source_target_pairs={{0,4},{4,0},{8,12},{12,8},{16,20},{20,16},{24,28},{28,24},{1,5},{5... | collective-permute-start | bytes 3244040 | tf_op jit(solution)/shard_map/ppermute | solution.py:82
  31.7 26.6 %collective-permute-start.1 = (bf16[512,1024]{1,0:T(8,128)(2,1)S(1)}, bf16[512,1024]{1,0:T(8,128)(2,1)S(1)}, u32[]{:S(2)}, u32[]{:S(2)}) collective-permute-start(bf16[512,1024]{1,0:T(8,128)(2,1)S(1)} %fusion.3.refs_2_), channel_id=1, source_target_pairs={{0,1},{1,2},{2,3},{4,5},{5,6},{6,7},{8,9},{9,10},{10,11},{12,13},{... | collective-permute-start | bytes 3145736 | tf_op jit(solution)/shard_map/ppermute | solution.py:1182
  61.0 31.7 %collective-permute-start.10 = (bf16[8,1056,128]{2,1,0:T(8,128)(2,1)}, bf16[8,1056,128]{2,1,0:T(8,128)(2,1)}, u32[]{:S(2)}, u32[]{:S(2)}) collective-permute-start(bf16[8,1056,128]{2,1,0:T(8,128)(2,1)} %pad_maximum_fusion), channel_id=1, source_target_pairs={{0,4},{4,0},{8,12},{12,8},{16,20},{20,16},{24,28},{28,24},{1,5},{5... | collective-permute-start | bytes 6488072 | tf_op jit(solution)/shard_map/ppermute | solution.py:82
  64.9 27.8 %collective-permute-start.7 = (bf16[512,1024]{1,0:T(8,128)(2,1)}, bf16[512,1024]{1,0:T(8,128)(2,1)}, u32[]{:S(2)}, u32[]{:S(2)}) collective-permute-start(bf16[512,1024]{1,0:T(8,128)(2,1)} %copy-done.57), channel_id=1, source_target_pairs={{0,1},{1,2},{2,3},{4,5},{5,6},{6,7},{8,9},{9,10},{10,11},{12,13},{... | collective-permute-start | bytes 3145736 | tf_op jit(solution)/shard_map/ppermute | solution.py:1182
  93.0 27.0 %collective-permute-start.12 = (bf16[2112,128]{1,0:T(8,128)(2,1)}, bf16[2112,128]{1,0:T(8,128)(2,1)S(1)}, u32[]{:S(2)}, u32[]{:S(2)}) collective-permute-start(bf16[2112,128]{1,0:T(8,128)(2,1)} %pad_maximum_fusion.6), channel_id=1, source_target_pairs={{0,1},{1,0},{2,3},{3,2},{4,5},{5,4},{6,7},{7,6},{8,9},{9,8},{10,11... | collective-permute-start | bytes 1622024 | tf_op jit(solution)/shard_map/ppermute | solution.py:82
  95.6 43.3 %collective-permute-start.16 = (bf16[2112,128]{1,0:T(8,128)(2,1)}, bf16[2112,128]{1,0:T(8,128)(2,1)}, u32[]{:S(2)}, u32[]{:S(2)}) collective-permute-start(bf16[2112,128]{1,0:T(8,128)(2,1)} %pad_maximum_fusion.6), channel_id=1, source_target_pairs={{0,2},{1,3},{2,0},{3,1},{4,6},{5,7},{6,4},{7,5},{8,10},{9,11},{10,... | collective-permute-start | bytes 1622024 | tf_op jit(solution)/shard_map/ppermute | solution.py:82
  121.2 25.8 %collective-permute-start.13 = (bf16[2,2112,128]{2,1,0:T(8,128)(2,1)S(1)}, bf16[2,2112,128]{2,1,0:T(8,128)(2,1)S(1)}, u32[]{:S(2)}, u32[]{:S(2)}) collective-permute-start(bf16[2,2112,128]{2,1,0:T(8,128)(2,1)S(1)} %pad_maximum_fusion.4.refs_0_.refs_1_.refs_2_), channel_id=1, source_target_pairs={{0,8},{4,12},{8,0},{12,4},{16,24},{20,28},{24,16},{28,20},{1,9},{5... | collective-permute-start | bytes 3244040 | tf_op jit(solution)/shard_map/ppermute | solution.py:82
  121.8 25.5 %collective-permute-start.14 = (bf16[2,2112,128]{2,1,0:T(8,128)(2,1)S(1)}, bf16[2,2112,128]{2,1,0:T(8,128)(2,1)S(1)}, u32[]{:S(2)}, u32[]{:S(2)}) collective-permute-start(bf16[2,2112,128]{2,1,0:T(8,128)(2,1)S(1)} %pad_maximum_fusion.4.refs_0_.refs_1_.refs_2_), channel_id=1, source_target_pairs={{0,16},{4,20},{8,24},{12,28},{16,0},{20,4},{24,8},{28,12},{1,17},{... | collective-permute-start | bytes 3244040 | tf_op jit(solution)/shard_map/ppermute | solution.py:82
  122.3 25.0 %collective-permute-start.15 = (bf16[2,2112,128]{2,1,0:T(8,128)(2,1)S(1)}, bf16[2,2112,128]{2,1,0:T(8,128)(2,1)}, u32[]{:S(2)}, u32[]{:S(2)}) collective-permute-start(bf16[2,2112,128]{2,1,0:T(8,128)(2,1)S(1)} %pad_maximum_fusion.4.refs_0_.refs_1_.refs_2_), channel_id=1, source_target_pairs={{0,4},{4,0},{8,12},{12,8},{16,20},{20,16},{24,28},{28,24},{1,5},{5... | collective-permute-start | bytes 3244040 | tf_op jit(solution)/shard_map/ppermute | solution.py:82
  150.0 31.1 %collective-permute-start.19 = (bf16[4,2112,128]{2,1,0:T(8,128)(2,1)}, bf16[4,2112,128]{2,1,0:T(8,128)(2,1)S(1)}, u32[]{:S(2)}, u32[]{:S(2)}) collective-permute-start(bf16[4,2112,128]{2,1,0:T(8,128)(2,1)} %pad_maximum_fusion.1), channel_id=1, source_target_pairs={{0,4},{4,0},{8,12},{12,8},{16,20},{20,16},{24,28},{28,24},{1,5},{5... | collective-permute-start | bytes 6488072 | tf_op jit(solution)/shard_map/ppermute | solution.py:82
  155.6 25.5 %collective-permute-start.21 = (f32[1,1]{1,0:T(1,128)}, f32[1,1]{1,0:T(1,128)}, u32[]{:S(2)}, u32[]{:S(2)}) collective-permute-start(f32[1,1]{1,0:T(1,128)} %bitcast.34), channel_id=1, source_target_pairs={{0,3},{1,2},{2,1},{3,0},{4,7},{5,6},{6,5},{7,4},{8,11},{9,10},{10,... | collective-permute-start | bytes 20 | tf_op jit(solution)/shard_map/ppermute | solution.py:1263
  162.4 18.7 %collective-permute-start.17 = (bf16[1,2112,128]{2,1,0:T(8,128)(2,1)}, bf16[1,2112,128]{2,1,0:T(8,128)(2,1)S(1)}, u32[]{:S(2)}, u32[]{:S(2)}) collective-permute-start(bf16[1,2112,128]{2,1,0:T(8,128)(2,1)} %slice.139), channel_id=1, source_target_pairs={{0,8},{4,12},{8,0},{12,4},{16,24},{20,28},{24,16},{28,20},{1,9},{5... | collective-permute-start | bytes 1622024 | tf_op jit(solution)/shard_map/ppermute | solution.py:82
  163.7 17.4 %collective-permute-start.18 = (bf16[1,2112,128]{2,1,0:T(8,128)(2,1)}, bf16[1,2112,128]{2,1,0:T(8,128)(2,1)}, u32[]{:S(2)}, u32[]{:S(2)}) collective-permute-start(bf16[1,2112,128]{2,1,0:T(8,128)(2,1)} %slice.140), channel_id=1, source_target_pairs={{0,16},{4,20},{8,24},{12,28},{16,0},{20,4},{24,8},{28,12},{1,17},{... | collective-permute-start | bytes 1622024 | tf_op jit(solution)/shard_map/ppermute | solution.py:82
  164.2 16.9 %collective-permute-start.20 = (bf16[2112,128]{1,0:T(8,128)(2,1)}, bf16[2112,128]{1,0:T(8,128)(2,1)}, u32[]{:S(2)}, u32[]{:S(2)}) collective-permute-start(bf16[2112,128]{1,0:T(8,128)(2,1)} %collective-permute-done.16), channel_id=1, source_target_pairs={{0,1},{1,0},{2,3},{3,2},{4,5},{5,4},{6,7},{7,6},{8,9},{9,8},{10,11... | collective-permute-start | bytes 1622024 | tf_op jit(solution)/shard_map/ppermute | solution.py:82
  185.9 28.7 %collective-permute-start.24 = (bf16[2,2112,128]{2,1,0:T(8,128)(2,1)}, bf16[2,2112,128]{2,1,0:T(8,128)(2,1)}, u32[]{:S(2)}, u32[]{:S(2)}) collective-permute-start(bf16[2,2112,128]{2,1,0:T(8,128)(2,1)} %pad_maximum_fusion.5.refs_0_.refs_1_.refs_2_), channel_id=1, source_target_pairs={{0,8},{4,12},{8,0},{12,4},{16,24},{20,28},{24,16},{28,20},{1,9},{5... | collective-permute-start | bytes 3244040 | tf_op jit(solution)/shard_map/ppermute | solution.py:82
  186.6 28.0 %collective-permute-start.25 = (bf16[2,2112,128]{2,1,0:T(8,128)(2,1)}, bf16[2,2112,128]{2,1,0:T(8,128)(2,1)S(1)}, u32[]{:S(2)}, u32[]{:S(2)}) collective-permute-start(bf16[2,2112,128]{2,1,0:T(8,128)(2,1)} %pad_maximum_fusion.5.refs_0_.refs_1_.refs_2_), channel_id=1, source_target_pairs={{0,16},{4,20},{8,24},{12,28},{16,0},{20,4},{24,8},{28,12},{1,17},{... | collective-permute-start | bytes 3244040 | tf_op jit(solution)/shard_map/ppermute | solution.py:82
  188.1 26.5 %collective-permute-start.26 = (bf16[2,2112,128]{2,1,0:T(8,128)(2,1)}, bf16[2,2112,128]{2,1,0:T(8,128)(2,1)}, u32[]{:S(2)}, u32[]{:S(2)}) collective-permute-start(bf16[2,2112,128]{2,1,0:T(8,128)(2,1)} %pad_maximum_fusion.5.refs_0_.refs_1_.refs_2_), channel_id=1, source_target_pairs={{0,4},{4,0},{8,12},{12,8},{16,20},{20,16},{24,28},{28,24},{1,5},{5... | collective-permute-start | bytes 3244040 | tf_op jit(solution)/shard_map/ppermute | solution.py:82
  196.9 17.7 %collective-permute-start.27 = (f32[1,1]{1,0:T(1,128)}, f32[1,1]{1,0:T(1,128)}, u32[]{:S(2)}, u32[]{:S(2)}) collective-permute-start(f32[1,1]{1,0:T(1,128)} %add.209), channel_id=1, source_target_pairs={{0,9},{1,8},{2,11},{3,10},{4,13},{5,12},{6,15},{7,14},{8,1},{9,0},... | collective-permute-start | bytes 20 | tf_op jit(solution)/shard_map/ppermute | solution.py:1281
  217.7 24.6 %collective-permute-start.30 = (bf16[4,2112,128]{2,1,0:T(8,128)(2,1)}, bf16[4,2112,128]{2,1,0:T(8,128)(2,1)}, u32[]{:S(2)}, u32[]{:S(2)}) collective-permute-start(bf16[4,2112,128]{2,1,0:T(8,128)(2,1)} %pad_maximum_fusion.2), channel_id=1, source_target_pairs={{0,4},{4,0},{8,12},{12,8},{16,20},{20,16},{24,28},{28,24},{1,5},{5... | collective-permute-start | bytes 6488072 | tf_op jit(solution)/shard_map/ppermute | solution.py:82
  220.4 21.8 %collective-permute-start.28 = (bf16[1,2112,128]{2,1,0:T(8,128)(2,1)}, bf16[1,2112,128]{2,1,0:T(8,128)(2,1)S(1)}, u32[]{:S(2)}, u32[]{:S(2)}) collective-permute-start(bf16[1,2112,128]{2,1,0:T(8,128)(2,1)} %slice.171), channel_id=1, source_target_pairs={{0,8},{4,12},{8,0},{12,4},{16,24},{20,28},{24,16},{28,20},{1,9},{5... | collective-permute-start | bytes 1622024 | tf_op jit(solution)/shard_map/ppermute | solution.py:82
  221.2 21.1 %collective-permute-start.29 = (bf16[1,2112,128]{2,1,0:T(8,128)(2,1)}, bf16[1,2112,128]{2,1,0:T(8,128)(2,1)S(1)}, u32[]{:S(2)}, u32[]{:S(2)}) collective-permute-start(bf16[1,2112,128]{2,1,0:T(8,128)(2,1)} %slice.172), channel_id=1, source_target_pairs={{0,16},{4,20},{8,24},{12,28},{16,0},{20,4},{24,8},{28,12},{1,17},{... | collective-permute-start | bytes 1622024 | tf_op jit(solution)/shard_map/ppermute | solution.py:82
  222.3 20.0 %collective-permute-start.31 = (f32[1,1]{1,0:T(1,128)}, f32[1,1]{1,0:T(1,128)}, u32[]{:S(2)}, u32[]{:S(2)}) collective-permute-start(f32[1,1]{1,0:T(1,128)} %add.211), channel_id=1, source_target_pairs={{0,17},{1,16},{2,19},{3,18},{4,21},{5,20},{6,23},{7,22},{8,25},{9,... | collective-permute-start | bytes 20 | tf_op jit(solution)/shard_map/ppermute | solution.py:1285
  242.3 36.3 %collective-permute-start.33 = (bf16[4,2,2112,128]{3,2,1,0:T(8,128)(2,1)}, bf16[4,2,2112,128]{3,2,1,0:T(8,128)(2,1)}, u32[]{:S(2)}, u32[]{:S(2)}) collective-permute-start(bf16[4,2,2112,128]{3,2,1,0:T(8,128)(2,1)} %get-tuple-element.358), channel_id=1, source_target_pairs={{0,4},{4,0},{8,12},{12,8},{16,20},{20,16},{24,28},{28,24},{1,5},{5... | collective-permute-start | bytes 12976136 | tf_op jit(solution)/shard_map/ppermute | solution.py:82
  244.6 34.0 %collective-permute-start.34 = (f32[1,1]{1,0:T(1,128)}, f32[1,1]{1,0:T(1,128)}, u32[]{:S(2)}, u32[]{:S(2)}) collective-permute-start(f32[1,1]{1,0:T(1,128)} %add.213), channel_id=1, source_target_pairs={{0,7},{1,6},{2,5},{3,4},{4,3},{5,2},{6,1},{7,0},{8,15},{9,14},{10,... | collective-permute-start | bytes 20 | tf_op jit(solution)/shard_map/ppermute | solution.py:1292
  278.6 49.6 %collective-permute-start.39 = (bf16[4,2,2112,128]{3,2,1,0:T(8,128)(2,1)}, bf16[4,2,2112,128]{3,2,1,0:T(8,128)(2,1)}, u32[]{:S(2)}, u32[]{:S(2)}) collective-permute-start(bf16[4,2,2112,128]{3,2,1,0:T(8,128)(2,1)} %get-tuple-element.382), channel_id=1, source_target_pairs={{0,4},{4,0},{8,12},{12,8},{16,20},{20,16},{24,28},{28,24},{1,5},{5... | collective-permute-start | bytes 12976136 | tf_op jit(solution)/shard_map/ppermute | solution.py:82
  301.9 25.2 %collective-permute-start.37 = (bf16[2,2112,128]{2,1,0:T(8,128)(2,1)}, bf16[2,2112,128]{2,1,0:T(8,128)(2,1)S(1)}, u32[]{:S(2)}, u32[]{:S(2)}) collective-permute-start(bf16[2,2112,128]{2,1,0:T(8,128)(2,1)} %get-tuple-element.380), channel_id=1, source_target_pairs={{0,8},{4,12},{8,0},{12,4},{16,24},{20,28},{24,16},{28,20},{1,9},{5... | collective-permute-start | bytes 3244040 | tf_op jit(solution)/shard_map/ppermute | solution.py:82
  302.8 25.4 %collective-permute-start.38 = (bf16[2,2112,128]{2,1,0:T(8,128)(2,1)}, bf16[2,2112,128]{2,1,0:T(8,128)(2,1)}, u32[]{:S(2)}, u32[]{:S(2)}) collective-permute-start(bf16[2,2112,128]{2,1,0:T(8,128)(2,1)} %get-tuple-element.381), channel_id=1, source_target_pairs={{0,16},{4,20},{8,24},{12,28},{16,0},{20,4},{24,8},{28,12},{1,17},{... | collective-permute-start | bytes 3244040 | tf_op jit(solution)/shard_map/ppermute | solution.py:82
  353.3 28.5 %collective-permute-start.44 = (bf16[4,2,1024,128]{3,2,1,0:T(8,128)(2,1)}, bf16[4,2,1024,128]{3,2,1,0:T(8,128)(2,1)}, u32[]{:S(2)}, u32[]{:S(2)}) collective-permute-start(bf16[4,2,1024,128]{3,2,1,0:T(8,128)(2,1)} %get-tuple-element.415), channel_id=1, source_target_pairs={{0,4},{4,0},{8,12},{12,8},{16,20},{20,16},{24,28},{28,24},{1,5},{5... | collective-permute-start | bytes 6291464 | tf_op jit(solution)/shard_map/ppermute | solution.py:82
  355.0 23.4 %collective-permute-start.45 = (bf16[2112,128]{1,0:T(8,128)(2,1)}, bf16[2112,128]{1,0:T(8,128)(2,1)}, u32[]{:S(2)}, u32[]{:S(2)}) collective-permute-start(bf16[2112,128]{1,0:T(8,128)(2,1)} %bitcast.40), channel_id=1, source_target_pairs={{0,1},{1,0},{2,3},{3,2},{4,5},{5,4},{6,7},{7,6},{8,9},{9,8},{10,11... | collective-permute-start | bytes 1622024 | tf_op jit(solution)/shard_map/ppermute | solution.py:82
  355.0 26.5 %collective-permute-start.42 = (bf16[2,2112,128]{2,1,0:T(8,128)(2,1)}, bf16[2,2112,128]{2,1,0:T(8,128)(2,1)S(1)}, u32[]{:S(2)}, u32[]{:S(2)}) collective-permute-start(bf16[2,2112,128]{2,1,0:T(8,128)(2,1)} %get-tuple-element.413), channel_id=1, source_target_pairs={{0,8},{4,12},{8,0},{12,4},{16,24},{20,28},{24,16},{28,20},{1,9},{5... | collective-permute-start | bytes 3244040 | tf_op jit(solution)/shard_map/ppermute | solution.py:82
  355.5 26.3 %collective-permute-start.43 = (bf16[2,2112,128]{2,1,0:T(8,128)(2,1)}, bf16[2,2112,128]{2,1,0:T(8,128)(2,1)}, u32[]{:S(2)}, u32[]{:S(2)}) collective-permute-start(bf16[2,2112,128]{2,1,0:T(8,128)(2,1)} %get-tuple-element.414), channel_id=1, source_target_pairs={{0,16},{4,20},{8,24},{12,28},{16,0},{20,4},{24,8},{28,12},{1,17},{... | collective-permute-start | bytes 3244040 | tf_op jit(solution)/shard_map/ppermute | solution.py:82
  408.7 29.4 %collective-permute-start.49 = (bf16[4,2,1024,128]{3,2,1,0:T(8,128)(2,1)}, bf16[4,2,1024,128]{3,2,1,0:T(8,128)(2,1)}, u32[]{:S(2)}, u32[]{:S(2)}) collective-permute-start(bf16[4,2,1024,128]{3,2,1,0:T(8,128)(2,1)} %get-tuple-element.456), channel_id=1, source_target_pairs={{0,4},{4,0},{8,12},{12,8},{16,20},{20,16},{24,28},{28,24},{1,5},{5... | collective-permute-start | bytes 6291464 | tf_op jit(solution)/shard_map/ppermute | solution.py:82
  408.7 18.5 %collective-permute-start.50 = (bf16[2,1024,128]{2,1,0:T(8,128)(2,1)}, bf16[2,1024,128]{2,1,0:T(8,128)(2,1)S(1)}, u32[]{:S(2)}, u32[]{:S(2)}) collective-permute-start(bf16[2,1024,128]{2,1,0:T(8,128)(2,1)} %get-tuple-element.457), channel_id=1, source_target_pairs={{0,8},{4,12},{8,0},{12,4},{16,24},{20,28},{24,16},{28,20},{1,9},{5... | collective-permute-start | bytes 1572872 | tf_op jit(solution)/shard_map/ppermute | solution.py:82
  410.1 17.0 %collective-permute-start.51 = (bf16[2,1024,128]{2,1,0:T(8,128)(2,1)}, bf16[2,1024,128]{2,1,0:T(8,128)(2,1)S(1)}, u32[]{:S(2)}, u32[]{:S(2)}) collective-permute-start(bf16[2,1024,128]{2,1,0:T(8,128)(2,1)} %get-tuple-element.458), channel_id=1, source_target_pairs={{0,16},{4,20},{8,24},{12,28},{16,0},{20,4},{24,8},{28,12},{1,17},{... | collective-permute-start | bytes 1572872 | tf_op jit(solution)/shard_map/ppermute | solution.py:82
  411.2 26.8 %collective-permute-start.52 = (bf16[2112,128]{1,0:T(8,128)(2,1)}, bf16[2112,128]{1,0:T(8,128)(2,1)}, u32[]{:S(2)}, u32[]{:S(2)}) collective-permute-start(bf16[2112,128]{1,0:T(8,128)(2,1)} %fusion.12), channel_id=1, source_target_pairs={{0,2},{1,3},{2,0},{3,1},{4,6},{5,7},{6,4},{7,5},{8,10},{9,11},{10,... | collective-permute-start | bytes 1622024 | tf_op jit(solution)/shard_map/ppermute | solution.py:82
  442.8 32.9 %collective-permute-start.57 = (bf16[512,1024]{1,0:T(8,128)(2,1)}, bf16[512,1024]{1,0:T(8,128)(2,1)S(1)}, u32[]{:S(2)}, u32[]{:S(2)}) collective-permute-start(bf16[512,1024]{1,0:T(8,128)(2,1)} %get-tuple-element.486), channel_id=1, source_target_pairs={{1,0},{2,1},{3,2},{5,4},{6,5},{7,6},{9,8},{10,9},{11,10},{13,12},{... | collective-permute-start | bytes 3145736 | tf_op jit(solution)/shard_map/ppermute | solution.py:1379
  446.4 29.3 %collective-permute-start.58 = (bf16[1024,128]{1,0:T(8,128)(2,1)}, bf16[1024,128]{1,0:T(8,128)(2,1)}, u32[]{:S(2)}, u32[]{:S(2)}) collective-permute-start(bf16[1024,128]{1,0:T(8,128)(2,1)} %bitcast.152), channel_id=1, source_target_pairs={{0,1},{1,0},{2,3},{3,2},{4,5},{5,4},{6,7},{7,6},{8,9},{9,8},{10,11... | collective-permute-start | bytes 786440 | tf_op jit(solution)/shard_map/ppermute | solution.py:82
  456.5 19.2 %collective-permute-start.55 = (bf16[2,1024,128]{2,1,0:T(8,128)(2,1)}, bf16[2,1024,128]{2,1,0:T(8,128)(2,1)}, u32[]{:S(2)}, u32[]{:S(2)}) collective-permute-start(bf16[2,1024,128]{2,1,0:T(8,128)(2,1)} %get-tuple-element.484), channel_id=1, source_target_pairs={{0,8},{4,12},{8,0},{12,4},{16,24},{20,28},{24,16},{28,20},{1,9},{5... | collective-permute-start | bytes 1572872 | tf_op jit(solution)/shard_map/ppermute | solution.py:82
  457.7 18.0 %collective-permute-start.56 = (bf16[2,1024,128]{2,1,0:T(8,128)(2,1)}, bf16[2,1024,128]{2,1,0:T(8,128)(2,1)}, u32[]{:S(2)}, u32[]{:S(2)}) collective-permute-start(bf16[2,1024,128]{2,1,0:T(8,128)(2,1)} %get-tuple-element.485), channel_id=1, source_target_pairs={{0,16},{4,20},{8,24},{12,28},{16,0},{20,4},{24,8},{28,12},{1,17},{... | collective-permute-start | bytes 1572872 | tf_op jit(solution)/shard_map/ppermute | solution.py:82
  484.8 31.3 %collective-permute-start.64 = (bf16[512,1024]{1,0:T(8,128)(2,1)}, bf16[512,1024]{1,0:T(8,128)(2,1)}, u32[]{:S(2)}, u32[]{:S(2)}) collective-permute-start(bf16[512,1024]{1,0:T(8,128)(2,1)} %add_convert_fusion), channel_id=1, source_target_pairs={{1,0},{2,1},{3,2},{5,4},{6,5},{7,6},{9,8},{10,9},{11,10},{13,12},{... | collective-permute-start | bytes 3145736 | tf_op jit(solution)/shard_map/ppermute | solution.py:1379
  496.4 26.3 %collective-permute-start.63 = (bf16[1024,128]{1,0:T(8,128)(2,1)}, bf16[1024,128]{1,0:T(8,128)(2,1)S(1)}, u32[]{:S(2)}, u32[]{:S(2)}) collective-permute-start(bf16[1024,128]{1,0:T(8,128)(2,1)} %fusion.20), channel_id=1, source_target_pairs={{0,2},{1,3},{2,0},{3,1},{4,6},{5,7},{6,4},{7,5},{8,10},{9,11},{10,... | collective-permute-start | bytes 786440 | tf_op jit(solution)/shard_map/ppermute | solution.py:82
  500.5 21.3 %collective-permute-start.65 = (f32[2,1024]{1,0:T(2,128)S(1)}, f32[2,1024]{1,0:T(2,128)S(1)}, u32[]{:S(2)}, u32[]{:S(2)}) collective-permute-start(f32[2,1024]{1,0:T(2,128)S(1)} %add_add_fusion.1), channel_id=1, source_target_pairs={{0,4},{4,0},{8,12},{12,8},{16,20},{20,16},{24,28},{28,24},{1,5},{5... | collective-permute-start | bytes 24584 | tf_op jit(solution)/shard_map/ppermute | solution.py:82
  522.8 19.6 %collective-permute-start.66 = (f32[2,1024]{1,0:T(2,128)S(1)}, f32[2,1024]{1,0:T(2,128)S(1)}, u32[]{:S(2)}, u32[]{:S(2)}) collective-permute-start(f32[2,1024]{1,0:T(2,128)S(1)} %add.227), channel_id=1, source_target_pairs={{0,1},{1,0},{2,3},{3,2},{4,5},{5,4},{6,7},{7,6},{8,9},{9,8},{10,11... | collective-permute-start | bytes 24584 | tf_op jit(solution)/shard_map/ppermute | solution.py:82
  526.4 16.0 %collective-permute-start.67 = (f32[2,1024]{1,0:T(2,128)S(1)}, f32[2,1024]{1,0:T(2,128)S(1)}, u32[]{:S(2)}, u32[]{:S(2)}) collective-permute-start(f32[2,1024]{1,0:T(2,128)S(1)} %add.227), channel_id=1, source_target_pairs={{0,2},{1,3},{2,0},{3,1},{4,6},{5,7},{6,4},{7,5},{8,10},{9,11},{10,... | collective-permute-start | bytes 24584 | tf_op jit(solution)/shard_map/ppermute | solution.py:82
  526.4 16.0 %collective-permute-start.68 = (f32[2,1024]{1,0:T(2,128)S(1)}, f32[2,1024]{1,0:T(2,128)S(1)}, u32[]{:S(2)}, u32[]{:S(2)}) collective-permute-start(f32[2,1024]{1,0:T(2,128)S(1)} %add.227), channel_id=1, source_target_pairs={{0,3},{1,2},{2,1},{3,0},{4,7},{5,6},{6,5},{7,4},{8,11},{9,10},{10,... | collective-permute-start | bytes 24584 | tf_op jit(solution)/shard_map/ppermute | solution.py:82
  (83 other events, 862.5 us)

commit v4 on v3

--- a/solution.py
+++ b/solution.py
@@ -539,6 +539,16 @@
     if size == 32:
         masks = [3, 5, 9, 17, 7]
     return [(axes, [(i, i ^ mask) for i in range(size)]) for mask in masks]
+
+
+def scalar_rows(value):
+    row = lax.broadcasted_iota(jnp.int32, (32, LANES), 0)
+    rows = jnp.zeros((32, LANES), F32)
+    for i in range(3):
+        part = lax.reduce_precision(value, 8, 7)
+        rows = jnp.where(row == i, part, rows)
+        value = value - part
+    return rows.astype(BF16)
 
 
 def neighbours(values, axis, steps):
@@ -1232,8 +1242,7 @@
         all_hashes = gather_small(hashes).astype(F32)
 
     raw_weight = lengths.astype(F32) * lax.rsqrt(count_own(all_hashes))
-    raw_total = jnp.sum(raw_weight).reshape(1, 1)
-    steps = exchanges()
+    raw_total = jnp.sum(raw_weight.reshape(-1, LANES), axis=0, keepdims=True)
     grad_out = cotangent.astype(F32) * raw_weight[:, None]
     grad_low = grad_out.astype(BF16)
 
@@ -1246,28 +1255,30 @@
         )
         shards[0], hidden_rows = together(shards[0], hidden_rows)
         slice_one = pairwise(hidden_rows, "mp", 1)
-        slice_two = pairwise(hidden_rows, "mp", 2)
     attend_w, output_w, queries, keys, values, window = project(device, shards, attend_pieces)
     labels = (query_labels, key_labels)
     if fast:
-        queries, slice_one = together(queries, slice_one)
+        queries, slice_one, late_rows = together(queries, slice_one, hidden_rows)
+        slice_two = pairwise(late_rows, "mp", 2)
         near = jnp.stack([hidden_rows, slice_one])
         sides = gather_sides(near)
     inputs = labels + (queries, keys, values)
     context_a, sums_a = attend(inputs, tile, 0, half_pairs)
     if fast:
-        queries, context_a, sides, slice_two = together(queries, context_a, sides, slice_two)
+        queries, context_a, sides, slice_two, grad_low, raw_total = together(
+            queries, context_a, sides, slice_two, grad_low, raw_total
+        )
         inputs = labels + (queries, keys, values)
         corners = gather_corner(*sides)
         slice_three = pairwise(slice_two, "mp", 1)
-        moved = lax.ppermute(raw_total, *steps[0])
     context_b, sums_b = attend(inputs, tile, half_pairs, half_pairs)
     if fast:
-        context_b, corners, slice_three, moved = together(context_b, corners, slice_three, moved)
-        raw_total = raw_total + moved
-        moved = lax.ppermute(raw_total, *steps[1])
+        context_b, corners, slice_three = together(context_b, corners, slice_three)
         near_pieces = gather_end(near, *sides, *corners)
-        far = jnp.stack([slice_two, slice_three])
+        total_rows = scalar_rows(raw_total)
+        far = jnp.concatenate(
+            [jnp.stack([slice_two, slice_three]), jnp.stack([total_rows, total_rows])], axis=1
+        )
         sides = gather_sides(far)
     half = context_a.shape[1]
     middle = stream + dot(context_a, output_w[:half]) + dot(context_b, output_w[half:])
@@ -1276,31 +1287,29 @@
     second_hat = middle * second_rms
     second_normed = (second_hat * gains[1]).astype(BF16)
     if fast:
-        second_normed, near_pieces, moved = together(second_normed, near_pieces, moved)
-        raw_total = raw_total + moved
-        moved = lax.ppermute(raw_total, *steps[2])
-        share_a = hidden_layer(device, second_normed, grad_low, near_pieces, hidden_width, 0, 1)
-        share_a, sides, moved = together(share_a, sides, moved)
-        raw_total = raw_total + moved
-        moved = lax.ppermute(raw_total, *steps[3])
+        second_normed, near_pieces = together(second_normed, near_pieces)
+        share_a = hidden_layer(device, second_normed, grad_low, near_pieces, hidden_width, 0, 2)
+        share_a, sides = together(share_a, sides)
         corners = gather_corner(*sides)
-        share_b = hidden_layer(
-            device, second_normed, grad_low, near_pieces, hidden_width, 1, 1, share_a[2:]
-        )
-        share_b, corners, moved = together(share_b, corners, moved)
-        raw_total = raw_total + moved
-        moved = lax.ppermute(raw_total, *steps[4])
         far_pieces = gather_end(far, *sides, *corners)
+        share_b = share_a
         near_grads = share_b[2:]
         near_received = pairwise(near_grads[1], "dp", 1)
         share_c = hidden_layer(device, second_normed, grad_low, far_pieces, hidden_width, 0, 2)
-        share_c, near_received, moved = together(share_c, near_received, moved)
-        raw_total = raw_total + moved
+        totals = [
+            piece[first, 3 * hidden_width : 3 * hidden_width + 8].astype(F32)
+            for piece, first in zip(far_pieces, first_slices(far_pieces))
+        ]
+        totals = [totals[chip] + totals[CHIPS + chip] for chip in range(CHIPS)]
+        totals = (totals[0] + totals[1]) + (totals[2] + totals[3])
+        raw_total = (totals[2:3] + totals[1:2]) + totals[0:1]
+        share_c, near_received, raw_total = together(share_c, near_received, raw_total)
+        along = neighbours(raw_total, "mp", (1, 2, 3))
         far_grads = share_c[2:]
         far_received = pairwise(far_grads[1], "dp", 1)
         near_corners = send_planar(*corner_sums(near_grads[0], near_received))
-        second_back = share_a[1] + share_b[1] + share_c[1]
-        activations = (middle + share_a[0] + share_b[0] + share_c[0]).astype(BF16)
+        second_back = share_a[1] + share_c[1]
+        results = (middle, share_a[0], share_c[0])
     else:
         share_a = hidden_layer(device, second_normed, grad_low, near_pieces, hidden_width, 0, 2)
         share_c = hidden_layer(device, second_normed, grad_low, far_pieces, hidden_width, 0, 2)
@@ -1309,7 +1318,6 @@
         second_back = share_a[1] + share_c[1]
         activations = (middle + share_a[0] + share_c[0]).astype(BF16)
 
-    weight_scale = total_patches / raw_total[0, 0]
 
     second_scaled = second_back * gains[1]
     gain_second = jnp.sum(second_back * second_hat, axis=0)
@@ -1332,10 +1340,13 @@
 
     slices_half = mp_size // 2
     if fast:
-        grad_context, near_corners = together(grad_context, near_corners)
+        grad_context, near_corners, along = together(grad_context, near_corners, along)
+        raw_total = sum_of_four(raw_total, along)
         near_sides = side_sums(near_grads[0], near_received, *near_corners)
         grad_context, near_sides = together(grad_context, near_sides)
         near_sides = send_planar(*near_sides)
+    weight_scale = total_patches / jnp.sum(raw_total)
+    grad_scale = weight_scale * total_patches ** (-0.5)
     backs_a = attend_back(inputs, context_a, grad_context, sums_a, tile, 0, half_pairs)
     keys_a = key_grads(backs_a)
     if fast:
@@ -1368,7 +1379,8 @@
         backs_b, cut_b, corners_a, far_three = together(backs_b, cut_b, corners_a, far_three)
         sides_a = side_sums(cut_a[0], received_a, *corners_a)
         far_two = (far_own + far_three.astype(F32)).astype(BF16)
-        backs_b, cut_b, sides_a, far_two = together(backs_b, cut_b, sides_a, far_two)
+        backs_b, cut_b, sides_a, far_two, results = together(backs_b, cut_b, sides_a, far_two, results)
+        activations = (results[0] + results[1] + results[2]).astype(BF16)
         sides_a = send_planar(*sides_a)
         far_two = pairwise(far_two, "mp", 2)
         received_b = pairwise(cut_b[1], "dp", 1)
@@ -1388,7 +1400,9 @@
         )
 
     if fast:
-        shares, received_b, sides_a, far_two = together(shares, received_b, sides_a, far_two)
+        shares, received_b, sides_a, far_two, activations = together(
+            shares, received_b, sides_a, far_two, activations
+        )
         corners_b = corner_sums(cut_b[0], received_b)
         own_a, one_a = own_sums(cut_a[0], received_a, *sides_a)
         shares, corners_b, one_a, far_two = together(shares, corners_b, one_a, far_two)
@@ -1401,7 +1415,6 @@
             carried = halo_back(share + carried.astype(F32))
         gain_sums = sum_small(gain_sums)
         input_grad = first_grad(carried)
-    grad_scale = weight_scale * total_patches ** (-0.5)
     reduce_step, output_step = STEP_RATE * FF ** (-0.5), STEP_RATE * OUT_FAN ** (-0.5)
     expand_step = attend_step = STEP_RATE * D ** (-0.5)
     if fast:
@@ -1414,8 +1427,8 @@
             terms, grad_scale, turn(reduce_master)[None], reduce_right[None], reduce_left[None],
             reduce_step, 2, True, False,
         )
-        reduce_out, terms, sides_b, carried, one_a, gain_sums = together(
-            reduce_out, terms, sides_b, carried, one_a, gain_sums
+        reduce_out, terms, sides_b, carried, gain_sums = together(
+            reduce_out, terms, sides_b, carried, gain_sums
         )
         own_b, three_b = own_sums(cut_b[0], received_b, *sides_b)
         carried = [(share + carried.astype(F32)).astype(BF16) for share in shares[1:-1]]
@@ -1433,7 +1446,9 @@
         moved = pairwise(gain_sums, "dp", 1)
         expand_out = shampoo_rows(terms, *expand_inputs, 1, 2, expand_out)
         input_grad = first_grad(carried)
-        expand_out, two_b, input_grad, moved = together(expand_out, two_b, input_grad, moved)
+        expand_out, two_b, one_a, input_grad, moved = together(
+            expand_out, two_b, one_a, input_grad, moved
+        )
         gain_sums = gain_sums + moved
         along = neighbours(gain_sums, "mp", (1, 2, 3))
         terms = (own_a, one_a, two_b)

time: 556 us -> 540 us (0.971)
  waiting for transfers between devices: 113 us -> 106 us
  starting transfers between devices: 82.5 us -> 75.9 us
    ppermute x5 -> x0, starting transfers between devices: 14.7 us -> none  [the longest x1 4.31 us: body(): moved = lax.ppermute(raw_total, *steps[3])]
    ppermute x2, waiting for transfers between devices: 26.1 us -> 18 us  [halo(): return lax.ppermute(values, 'mp', up_one)]
    ppermute x60 -> x63, starting transfers between devices: 55.8 us -> 63.4 us  [pairwise(): lax.ppermute(values, axis, [(i, i ^ step) for i in range(lax.axis_size(ax...]
    ppermute x2, waiting for transfers between devices: 6.03 us -> 11.6 us  [halo_back(): return lax.ppermute(share.astype(BF16), 'mp', down_one)]
    pallas_call x3 -> x2, Pallas kernels: 57.5 us -> 52.3 us  [hidden_layer(): grid_call(functools.partial(hidden_kernel, len(earlier)), (slices,), [who...]
    ppermute x60 -> x63, waiting for transfers between devices: 80.8 us -> 76 us  [pairwise(): lax.ppermute(values, axis, [(i, i ^ step) for i in range(lax.axis_size(ax...]
  transfers between devices with their start and end apart: 69 -> 67, of which waited for: 23 -> 23; matrix products, arithmetic and copies ran while one was open for 14% -> 16% of each run, Pallas kernels for 39% -> 39%
where the time goes in v4:
time: 540 us; the launch traced here: 535 us
  Pallas kernels  243 us (45%)
  waiting for transfers between devices  106 us (20%)
  starting transfers between devices  75.9 us (14%)
  other arithmetic  50.4 us (9%)
  matrix products  36.3 us (7%)
  local copies, waits for them, and re-layouts  21.2 us (4%)
    ppermute x63, waiting for transfers between devices, pairwise(): lax.ppermute(values, axis, [(i, i ^ step) for i in range(lax.axis_size(ax...  76 us
    ppermute x63, starting transfers between devices, pairwise(): lax.ppermute(values, axis, [(i, i ^ step) for i in range(lax.axis_size(ax...  63.4 us
    pallas_call x2, Pallas kernels, hidden_layer(): grid_call(functools.partial(hidden_kernel, len(earlier)), (slices,), [who...  52.3 us
    pallas_call x5, Pallas kernels, shampoo_rows(): pl.pallas_call(functools.partial(shampoo_rows_kernel, step_size, turned,...  47.8 us
    pallas_call x12, Pallas kernels, add_call(): pl.pallas_call(kernel, grid=(slices,), in_specs=in_specs, out_specs=out_s...  36.5 us
    pallas_call x2, Pallas kernels, attend_back(): pl.pallas_call(functools.partial(attend_back_kernel, tile, window - count...  33.5 us
    dot_general x8, matrix products, dot_weight(): lax.dot_general(first, second, (((0,), (0,)), ((), ())), preferred_elemen...  31.4 us
    pallas_call x2, Pallas kernels, attend(): pl.pallas_call(functools.partial(attend_kernel, tile, window - count), gr...  29.7 us
  transfers between devices with their start and end apart: 67, of which 23 were waited for; matrix products, arithmetic and copies ran while one was open for 16% of the time, Pallas kernels for 39%

profile of v4, /device:TPU:0, one launch (start us, length us, event | category | flops | bytes accessed | tf_op | source)
XLA Modules:
  0.0 534.7 jit_solution(4917668872030577778)
XLA Ops:
  4.6 3.1 collective-permute-start.2
  11.9 10.5 %collective-permute-done = bf16[1056,128]{1,0:T(8,128)(2,1)S(1)} collective-permute-done((bf16[1056,128]{1,0:T(8,128)(2,1)S(1)}, bf16[1056,128]{1,0:T(8,128)(2,1)S(1)}, u32[]{:S(2)}, u32[]{:S(2)}) %collective-permute-start) | collective-permute-done | bytes 270368 | tf_op jit(solution)/shard_map/ppermute | solution.py:82
  22.9 6.0 %collective-permute-done.3 = bf16[1056,128]{1,0:T(8,128)(2,1)S(1)} collective-permute-done((bf16[1056,128]{1,0:T(8,128)(2,1)S(1)}, bf16[1056,128]{1,0:T(8,128)(2,1)S(1)}, u32[]{:S(2)}, u32[]{:S(2)}) %collective-permute-start.3) | collective-permute-done | bytes 270368 | tf_op jit(solution)/shard_map/ppermute | solution.py:82
  33.0 4.2 collective-permute-start.1
  47.5 11.5 %collective-permute-done.1.refs_1_ = bf16[512,1024]{1,0:T(8,128)(2,1)} collective-permute-done((bf16[512,1024]{1,0:T(8,128)(2,1)}, bf16[512,1024]{1,0:T(8,128)(2,1)}, u32[]{:S(2)}, u32[]{:S(2)}) %collective-permute-start.1) | collective-permute-done | bytes 1048608 | tf_op jit(solution)/shard_map/ppermute | solution.py:1192
  64.0 5.6 %collective-permute-start.7 = (bf16[512,1024]{1,0:T(8,128)(2,1)}, bf16[512,1024]{1,0:T(8,128)(2,1)}, u32[]{:S(2)}, u32[]{:S(2)}) collective-permute-start(bf16[512,1024]{1,0:T(8,128)(2,1)} %collective-permute-done.1.refs_1_), channel_id=1, source_target_pairs={{0,1},{1,2},{2,3},{4,5},{5,6},{6,7},{8,9},{9,10},{10,11},{12,13},{... | collective-permute-start | bytes 3145736 | tf_op jit(solution)/shard_map/ppermute | solution.py:1192
  71.6 13.5 %collective-permute-done.9 = bf16[2,1056,128]{2,1,0:T(8,128)(2,1)S(1)} collective-permute-done((bf16[2,1056,128]{2,1,0:T(8,128)(2,1)}, bf16[2,1056,128]{2,1,0:T(8,128)(2,1)S(1)}, u32[]{:S(2)}, u32[]{:S(2)}) %collective-permute-start.9) | collective-permute-done | bytes 540704 | tf_op jit(solution)/shard_map/ppermute | solution.py:82
  85.3 6.5 %collective-permute-done.7.refs_0_ = bf16[512,1024]{1,0:T(8,128)(2,1)} collective-permute-done((bf16[512,1024]{1,0:T(8,128)(2,1)}, bf16[512,1024]{1,0:T(8,128)(2,1)}, u32[]{:S(2)}, u32[]{:S(2)}) %collective-permute-start.7) | collective-permute-done | bytes 1048608 | tf_op jit(solution)/shard_map/ppermute | solution.py:1192
  95.6 16.5 %project.1 = (bf16[3,1024,1024]{2,1,0:T(8,128)(2,1)}, bf16[1024,1024]{1,0:T(8,128)(2,1)}, bf16[512,1024]{1,0:T(8,128)(2,1)}, bf16[1536,1024]{1,0:T(8,128)(2,1)},...) custom-call(s32[1]{0:T(128)} %bitcast.2.device_ref, bf16[512,1024]{1,0:T(8,128)(2,1)} %collective-permute-done.7.refs_0_, ...), custom_call_target="tpu_custom_call" | custom-call | flops 7516192768 | bytes 16777216 | tf_op jit(solution)/shard_map/project/pallas_call | solution.py:391
  118.2 4.2 convert_reduce_fusion
  122.4 14.6 %attend.2 = (bf16[512,512]{1,0:T(8,128)(2,1)}, f32[4,2,512]{2,1,0:T(2,128)}) custom-call(s32[1,512]{1,0:T(1,128)} %bitcast.155, s32[1536,1]{1,0:T(8,128)} %reshape.400.key_labels, bf16[512,1024]{1,0:T(8,128)(2,1)} %get-tuple-element.307.q_ref, bf16[1536,1024]{1,0:T(8,128)(2,1)} %get-tuple-element.302.k_ref, bf16[1536,1024]{1,0:T(8,128)(2,1)} %get-tuple-element.303.v_ref), custom_call_target="tpu_custom_call" | custom-call | flops 2684354560 | bytes 4194304 | tf_op jit(solution)/shard_map/attend/pallas_call | solution.py:714
  138.3 4.9 collective-permute-done.16
  143.1 3.2 pad_maximum_fusion.2
  152.1 15.1 %attend.3 = (bf16[512,512]{1,0:T(8,128)(2,1)}, f32[4,2,512]{2,1,0:T(2,128)}) custom-call(s32[1,512]{1,0:T(1,128)} %bitcast.156, s32[1536,1]{1,0:T(8,128)} %reshape.400.key_labels, bf16[512,1024]{1,0:T(8,128)(2,1)} %get-tuple-element.307.q_ref, bf16[1536,1024]{1,0:T(8,128)(2,1)} %get-tuple-element.302.k_ref, bf16[1536,1024]{1,0:T(8,128)(2,1)} %get-tuple-element.303.v_ref), custom_call_target="tpu_custom_call" | custom-call | flops 2684354560 | bytes 4194304 | tf_op jit(solution)/shard_map/attend/pallas_call | solution.py:714
  177.5 26.0 %hidden_layer.2 = (f32[512,1024]{1,0:T(8,128)}, f32[512,1024]{1,0:T(8,128)}, bf16[4,2,2112,128]{3,2,1,0:T(8,128)(2,1)}, bf16[4,2,2112,128]{3,2,1,0:T(8,128)(2,1)}) custom-call(s32[1]{0:T(128)} %bitcast.2.device_ref, bf16[512,1024]{1,0:T(8,128)(2,1)} %multiply_convert_fusion.normed_ref, bf16[512,1024]{1,0:T(8,128)(2,1)} %fusion.11.grads_ref, ...), custom_call_target="tpu_custom_call" | custom-call | flops 13287555072 | bytes 17301504 | tf_op jit(solution)/shard_map/hidden_layer/pallas_call | solution.py:506
  211.0 8.7 %collective-permute-done.25 = bf16[1,2144,128]{2,1,0:T(8,128)(2,1)S(1)} collective-permute-done((bf16[1,2144,128]{2,1,0:T(8,128)(2,1)S(1)}, bf16[1,2144,128]{2,1,0:T(8,128)(2,1)S(1)}, u32[]{:S(2)}, u32[]{:S(2)}) %collective-permute-start.25) | collective-permute-done | bytes 548896 | tf_op jit(solution)/shard_map/ppermute | solution.py:82
  219.7 4.4 collective-permute-done.26
  228.8 26.3 %hidden_layer.3 = (f32[512,1024]{1,0:T(8,128)}, f32[512,1024]{1,0:T(8,128)}, bf16[4,2,2112,128]{3,2,1,0:T(8,128)(2,1)}, bf16[4,2,2112,128]{3,2,1,0:T(8,128)(2,1)}) custom-call(s32[1]{0:T(128)} %bitcast.2.device_ref, bf16[512,1024]{1,0:T(8,128)(2,1)} %multiply_convert_fusion.normed_ref, bf16[512,1024]{1,0:T(8,128)(2,1)} %fusion.11.grads_ref, ...), custom_call_target="tpu_custom_call" | custom-call | flops 13287555072 | bytes 17301504 | tf_op jit(solution)/shard_map/hidden_layer/pallas_call | solution.py:506
  258.8 3.0 add_corner.4
  263.8 3.0 multiply_reduce_fusion
  276.5 3.8 add_sides.4
  283.3 16.7 %attend_back.2 = (bf16[512,512]{1,0:T(8,128)(2,1)}, bf16[1536,512]{1,0:T(8,128)(2,1)}, bf16[1536,512]{1,0:T(8,128)(2,1)}) custom-call(s32[1,512]{1,0:T(1,128)} %bitcast.157, s32[1536,1]{1,0:T(8,128)} %reshape.400.key_labels, bf16[512,1024]{1,0:T(8,128)(2,1)} %get-tuple-element.307.q_ref, bf16[1536,1024]{1,0:T(8,128)(2,1)} %get-tuple-element.302.k_ref, ...), custom_call_target="tpu_custom_call" | custom-call | flops 6710886400 | bytes 8388608 | tf_op jit(solution)/shard_map/attend_back/pallas_call | solution.py:739
  300.0 5.1 convolution_convert_fusion.3.key
  306.3 3.9 add_own.4
  310.2 3.2 add_corner.5
  315.5 3.1 convolution_convert_fusion.8.query
  318.6 4.7 convolution_convert_fusion.2.value
  323.3 4.1 cut_attend.2
  327.4 3.9 add_sides.5
  331.3 3.5 convolution_convert_fusion.5.output
  337.4 16.7 %attend_back.3 = (bf16[512,512]{1,0:T(8,128)(2,1)}, bf16[1536,512]{1,0:T(8,128)(2,1)}, bf16[1536,512]{1,0:T(8,128)(2,1)}) custom-call(s32[1,512]{1,0:T(1,128)} %bitcast.158, s32[1536,1]{1,0:T(8,128)} %reshape.400.key_labels, bf16[512,1024]{1,0:T(8,128)(2,1)} %get-tuple-element.307.q_ref, bf16[1536,1024]{1,0:T(8,128)(2,1)} %get-tuple-element.302.k_ref, ...), custom_call_target="tpu_custom_call" | custom-call | flops 6710886400 | bytes 8388608 | tf_op jit(solution)/shard_map/attend_back/pallas_call | solution.py:739
  354.2 5.1 convolution_convert_fusion.1.key
  362.9 3.9 add_own.5
  371.5 5.1 convolution_convert_fusion.value
  379.5 4.3 cut_attend.3
  393.8 15.8 %project_back.1 = (bf16[512,1024]{1,0:T(8,128)(2,1)}, f32[512,1024]{1,0:T(8,128)}, f32[512,1024]{1,0:T(8,128)}, f32[1,1024]{1,0:T(1,128)}) custom-call(bf16[512,512]{1,0:T(8,128)(2,1)} %get-tuple-element.374.refs_0_, bf16[512,512]{1,0:T(8,128)(2,1)} %get-tuple-element.429.refs_1_, bf16[1536,512]{1,0:T(8,128)(2,1)} %get-tuple-element.430.refs_2_, ...), custom_call_target="tpu_custom_call" | custom-call | flops 7516192768 | bytes 18874368 | tf_op jit(solution)/shard_map/project_back/pallas_call | solution.py:810
  409.6 3.7 add_convert_fusion.1
  413.3 5.4 %collective-permute-done.50.two = bf16[2112,128]{1,0:T(8,128)(2,1)} collective-permute-done((bf16[2112,128]{1,0:T(8,128)(2,1)}, bf16[2112,128]{1,0:T(8,128)(2,1)}, u32[]{:S(2)}, u32[]{:S(2)}) %collective-permute-start.50) | collective-permute-done | bytes 540704 | tf_op jit(solution)/shard_map/ppermute | solution.py:82
  430.0 4.4 collective-permute-done.51.corner_x
  440.1 9.4 %shampoo_rows.5 = (f32[1,8,64,176]{3,2,1,0:T(8,128)}, f32[1,8,64,176]{3,2,1,0:T(8,128)}, f32[1,8,64,64]{3,2,1,0:T(8,128)}, f32[1,8,176,176]{3,2,1,0:T(8,128)}) custom-call(f32[1]{0:T(128)} %bitcast.46.scale_ref, f32[1,2112,128]{2,1,0:T(8,128)} %get-tuple-element.448.own, bf16[2112,128]{1,0:T(8,128)(2,1)} %collective-permute-done.43.one, ...), custom_call_target="tpu_custom_call" | custom-call | flops 6978273280 | bytes 3686400 | tf_op jit(solution)/shard_map/shampoo_rows/pallas_call | solution.py:1008
  463.1 9.3 %shampoo_rows.6 = (f32[2,8,64,176]{3,2,1,0:T(8,128)}, f32[2,8,64,176]{3,2,1,0:T(8,128)}, f32[2,8,64,64]{3,2,1,0:T(8,128)}, f32[2,8,176,176]{3,2,1,0:T(8,128)}) custom-call(f32[1]{0:T(128)} %bitcast.46.scale_ref, f32[1,2112,128]{2,1,0:T(8,128)} %get-tuple-element.448.own, bf16[2112,128]{1,0:T(8,128)(2,1)} %collective-permute-done.43.one, ...), custom_call_target="tpu_custom_call" | custom-call | flops 6978273280 | bytes 3686400 | tf_op jit(solution)/shard_map/shampoo_rows/pallas_call | solution.py:1008
  476.9 9.4 %shampoo_rows.7 = (f32[2,8,64,176]{3,2,1,0:T(8,128)}, f32[2,8,64,176]{3,2,1,0:T(8,128)}, f32[2,8,64,64]{3,2,1,0:T(8,128)}, f32[2,8,176,176]{3,2,1,0:T(8,128)}) custom-call(f32[1]{0:T(128)} %bitcast.46.scale_ref, f32[1,2112,128]{2,1,0:T(8,128)} %get-tuple-element.448.own, ...), custom_call_target="tpu_custom_call", output_to_operand_aliasing={{0}: (7, {}), {1}: (8, {}), {2}: (9, {}), {3}: (10, {})} | custom-call | flops 6978273280 | bytes 3686400 | tf_op jit(solution)/shard_map/shampoo_rows/pallas_call | solution.py:1008
  486.3 11.6 %collective-permute-done.62 = bf16[512,1024]{1,0:T(8,128)(2,1)} collective-permute-done((bf16[512,1024]{1,0:T(8,128)(2,1)}, bf16[512,1024]{1,0:T(8,128)(2,1)}, u32[]{:S(2)}, u32[]{:S(2)}) %collective-permute-start.62) | collective-permute-done | bytes 1048608 | tf_op jit(solution)/shard_map/ppermute | solution.py:1391
  499.8 3.3 fusion.8
  503.0 4.4 collective-permute-done.60.two
  507.4 4.1 collective-permute-start.65
  511.8 13.9 %shampoo_rows.8 = (f32[3,8,64,64]{3,2,1,0:T(8,128)}, f32[3,8,64,64]{3,2,1,0:T(8,128)}, f32[3,8,64,64]{3,2,1,0:T(8,128)}, f32[3,8,64,64]{3,2,1,0:T(8,128)}) custom-call(f32[1]{0:T(128)} %bitcast.46.scale_ref, f32[1,1024,128]{2,1,0:T(8,128)} %get-tuple-element.521.own, bf16[1024,128]{1,0:T(8,128)(2,1)} %copy-done.26, ...), custom_call_target="tpu_custom_call" | custom-call | flops 1006632960 | bytes 3145728 | tf_op jit(solution)/shard_map/shampoo_rows/pallas_call | solution.py:1008
  528.3 5.8 %shampoo_rows.9 = (f32[1,8,64,64]{3,2,1,0:T(8,128)}, f32[1,8,64,64]{3,2,1,0:T(8,128)}, f32[1,8,64,64]{3,2,1,0:T(8,128)}, f32[1,8,64,64]{3,2,1,0:T(8,128)}) custom-call(f32[1]{0:T(128)} %bitcast.46.scale_ref, f32[1,1024,128]{2,1,0:T(8,128)} %get-tuple-element.521.own, bf16[1024,128]{1,0:T(8,128)(2,1)} %copy-done.26, ...), custom_call_target="tpu_custom_call" | custom-call | flops 335544320 | bytes 1048576 | tf_op jit(solution)/shard_map/shampoo_rows/pallas_call | solution.py:1008
  (303 shorter events, 153.7 us)
Async XLA Ops:
  4.6 18.2 %collective-permute-start.2 = (bf16[1056,128]{1,0:T(8,128)(2,1)S(1)}, bf16[1056,128]{1,0:T(8,128)(2,1)S(1)}, u32[]{:S(2)}, u32[]{:S(2)}) collective-permute-start(bf16[1056,128]{1,0:T(8,128)(2,1)S(1)} %get-tuple-element.559), channel_id=1, source_target_pairs={{0,1},{1,0},{2,3},{3,2},{4,5},{5,4},{6,7},{7,6},{8,9},{9,8},{10,11... | collective-permute-start | bytes 811016 | tf_op jit(solution)/shard_map/ppermute | solution.py:82
  7.7 14.7 %collective-permute-start = (bf16[1056,128]{1,0:T(8,128)(2,1)S(1)}, bf16[1056,128]{1,0:T(8,128)(2,1)S(1)}, u32[]{:S(2)}, u32[]{:S(2)}) collective-permute-start(bf16[1056,128]{1,0:T(8,128)(2,1)S(1)} %get-tuple-element.559), channel_id=1, source_target_pairs={{0,2},{1,3},{2,0},{3,1},{4,6},{5,7},{6,4},{7,5},{8,10},{9,11},{10,... | collective-permute-start | bytes 811016 | tf_op jit(solution)/shard_map/ppermute | solution.py:82
  30.0 29.0 %collective-permute-start.6 = (bf16[4,1056,128]{2,1,0:T(8,128)(2,1)}, bf16[4,1056,128]{2,1,0:T(8,128)(2,1)}, u32[]{:S(2)}, u32[]{:S(2)}) collective-permute-start(bf16[4,1056,128]{2,1,0:T(8,128)(2,1)} %pad_maximum_fusion.3.refs_3_), channel_id=1, source_target_pairs={{0,4},{4,0},{8,12},{12,8},{16,20},{20,16},{24,28},{28,24},{1,5},{5... | collective-permute-start | bytes 3244040 | tf_op jit(solution)/shard_map/ppermute | solution.py:82
  30.0 29.0 %collective-permute-start.5 = (bf16[4,1056,128]{2,1,0:T(8,128)(2,1)}, bf16[4,1056,128]{2,1,0:T(8,128)(2,1)S(1)}, u32[]{:S(2)}, u32[]{:S(2)}) collective-permute-start(bf16[4,1056,128]{2,1,0:T(8,128)(2,1)} %pad_maximum_fusion.3.refs_3_), channel_id=1, source_target_pairs={{0,16},{4,20},{8,24},{12,28},{16,0},{20,4},{24,8},{28,12},{1,17},{... | collective-permute-start | bytes 3244040 | tf_op jit(solution)/shard_map/ppermute | solution.py:82
  31.5 27.5 %collective-permute-start.4 = (bf16[4,1056,128]{2,1,0:T(8,128)(2,1)}, bf16[4,1056,128]{2,1,0:T(8,128)(2,1)S(1)}, u32[]{:S(2)}, u32[]{:S(2)}) collective-permute-start(bf16[4,1056,128]{2,1,0:T(8,128)(2,1)} %pad_maximum_fusion.3.refs_3_), channel_id=1, source_target_pairs={{0,8},{4,12},{8,0},{12,4},{16,24},{20,28},{24,16},{28,20},{1,9},{5... | collective-permute-start | bytes 3244040 | tf_op jit(solution)/shard_map/ppermute | solution.py:82
  33.0 26.0 %collective-permute-start.1 = (bf16[512,1024]{1,0:T(8,128)(2,1)}, bf16[512,1024]{1,0:T(8,128)(2,1)}, u32[]{:S(2)}, u32[]{:S(2)}) collective-permute-start(bf16[512,1024]{1,0:T(8,128)(2,1)} %fusion.3.refs_2_), channel_id=1, source_target_pairs={{0,1},{1,2},{2,3},{4,5},{5,6},{6,7},{8,9},{9,10},{10,11},{12,13},{... | collective-permute-start | bytes 3145736 | tf_op jit(solution)/shard_map/ppermute | solution.py:1192
  60.7 31.1 %collective-permute-start.10 = (bf16[8,1056,128]{2,1,0:T(8,128)(2,1)}, bf16[8,1056,128]{2,1,0:T(8,128)(2,1)}, u32[]{:S(2)}, u32[]{:S(2)}) collective-permute-start(bf16[8,1056,128]{2,1,0:T(8,128)(2,1)} %pad_maximum_fusion.1), channel_id=1, source_target_pairs={{0,4},{4,0},{8,12},{12,8},{16,20},{20,16},{24,28},{28,24},{1,5},{5... | collective-permute-start | bytes 6488072 | tf_op jit(solution)/shard_map/ppermute | solution.py:82
  64.0 27.8 %collective-permute-start.7 = (bf16[512,1024]{1,0:T(8,128)(2,1)}, bf16[512,1024]{1,0:T(8,128)(2,1)}, u32[]{:S(2)}, u32[]{:S(2)}) collective-permute-start(bf16[512,1024]{1,0:T(8,128)(2,1)} %collective-permute-done.1.refs_1_), channel_id=1, source_target_pairs={{0,1},{1,2},{2,3},{4,5},{5,6},{6,7},{8,9},{9,10},{10,11},{12,13},{... | collective-permute-start | bytes 3145736 | tf_op jit(solution)/shard_map/ppermute | solution.py:1192
  70.4 14.7 %collective-permute-start.9 = (bf16[2,1056,128]{2,1,0:T(8,128)(2,1)}, bf16[2,1056,128]{2,1,0:T(8,128)(2,1)S(1)}, u32[]{:S(2)}, u32[]{:S(2)}) collective-permute-start(bf16[2,1056,128]{2,1,0:T(8,128)(2,1)} %slice.179), channel_id=1, source_target_pairs={{0,16},{4,20},{8,24},{12,28},{16,0},{20,4},{24,8},{28,12},{1,17},{... | collective-permute-start | bytes 1622024 | tf_op jit(solution)/shard_map/ppermute | solution.py:82
  92.9 19.2 %collective-permute-start.12 = (bf16[2112,128]{1,0:T(8,128)(2,1)}, bf16[2112,128]{1,0:T(8,128)(2,1)S(1)}, u32[]{:S(2)}, u32[]{:S(2)}) collective-permute-start(bf16[2112,128]{1,0:T(8,128)(2,1)} %pad_maximum_fusion.5), channel_id=1, source_target_pairs={{0,1},{1,0},{2,3},{3,2},{4,5},{5,4},{6,7},{7,6},{8,9},{9,8},{10,11... | collective-permute-start | bytes 1622024 | tf_op jit(solution)/shard_map/ppermute | solution.py:82
  114.3 28.8 %collective-permute-start.15 = (bf16[2,2112,128]{2,1,0:T(8,128)(2,1)}, bf16[2,2112,128]{2,1,0:T(8,128)(2,1)}, u32[]{:S(2)}, u32[]{:S(2)}) collective-permute-start(bf16[2,2112,128]{2,1,0:T(8,128)(2,1)} %pad_maximum_fusion.4.refs_0_.refs_1_.refs_2_), channel_id=1, source_target_pairs={{0,4},{4,0},{8,12},{12,8},{16,20},{20,16},{24,28},{28,24},{1,5},{5... | collective-permute-start | bytes 3244040 | tf_op jit(solution)/shard_map/ppermute | solution.py:82
  114.5 28.6 %collective-permute-start.14 = (bf16[2,2112,128]{2,1,0:T(8,128)(2,1)}, bf16[2,2112,128]{2,1,0:T(8,128)(2,1)S(1)}, u32[]{:S(2)}, u32[]{:S(2)}) collective-permute-start(bf16[2,2112,128]{2,1,0:T(8,128)(2,1)} %pad_maximum_fusion.4.refs_0_.refs_1_.refs_2_), channel_id=1, source_target_pairs={{0,16},{4,20},{8,24},{12,28},{16,0},{20,4},{24,8},{28,12},{1,17},{... | collective-permute-start | bytes 3244040 | tf_op jit(solution)/shard_map/ppermute | solution.py:82
  115.0 28.1 %collective-permute-start.13 = (bf16[2,2112,128]{2,1,0:T(8,128)(2,1)}, bf16[2,2112,128]{2,1,0:T(8,128)(2,1)}, u32[]{:S(2)}, u32[]{:S(2)}) collective-permute-start(bf16[2,2112,128]{2,1,0:T(8,128)(2,1)} %pad_maximum_fusion.4.refs_0_.refs_1_.refs_2_), channel_id=1, source_target_pairs={{0,8},{4,12},{8,0},{12,4},{16,24},{20,28},{24,16},{28,20},{1,9},{5... | collective-permute-start | bytes 3244040 | tf_op jit(solution)/shard_map/ppermute | solution.py:82
  116.3 26.8 %collective-permute-start.16 = (bf16[2112,128]{1,0:T(8,128)(2,1)}, bf16[2112,128]{1,0:T(8,128)(2,1)}, u32[]{:S(2)}, u32[]{:S(2)}) collective-permute-start(bf16[2112,128]{1,0:T(8,128)(2,1)} %pad_maximum_fusion.5), channel_id=1, source_target_pairs={{0,2},{1,3},{2,0},{3,1},{4,6},{5,7},{6,4},{7,5},{8,10},{9,11},{10,... | collective-permute-start | bytes 1622024 | tf_op jit(solution)/shard_map/ppermute | solution.py:82
  146.3 22.8 %collective-permute-start.19 = (bf16[4,2112,128]{2,1,0:T(8,128)(2,1)}, bf16[4,2112,128]{2,1,0:T(8,128)(2,1)}, u32[]{:S(2)}, u32[]{:S(2)}) collective-permute-start(bf16[4,2112,128]{2,1,0:T(8,128)(2,1)} %pad_maximum_fusion.2), channel_id=1, source_target_pairs={{0,4},{4,0},{8,12},{12,8},{16,20},{20,16},{24,28},{28,24},{1,5},{5... | collective-permute-start | bytes 6488072 | tf_op jit(solution)/shard_map/ppermute | solution.py:82
  149.0 20.0 %collective-permute-start.18 = (bf16[1,2112,128]{2,1,0:T(8,128)(2,1)}, bf16[1,2112,128]{2,1,0:T(8,128)(2,1)}, u32[]{:S(2)}, u32[]{:S(2)}) collective-permute-start(bf16[1,2112,128]{2,1,0:T(8,128)(2,1)} %slice.210), channel_id=1, source_target_pairs={{0,16},{4,20},{8,24},{12,28},{16,0},{20,4},{24,8},{28,12},{1,17},{... | collective-permute-start | bytes 1622024 | tf_op jit(solution)/shard_map/ppermute | solution.py:82
  150.6 18.5 %collective-permute-start.17 = (bf16[1,2112,128]{2,1,0:T(8,128)(2,1)}, bf16[1,2112,128]{2,1,0:T(8,128)(2,1)}, u32[]{:S(2)}, u32[]{:S(2)}) collective-permute-start(bf16[1,2112,128]{2,1,0:T(8,128)(2,1)} %slice.209), channel_id=1, source_target_pairs={{0,8},{4,12},{8,0},{12,4},{16,24},{20,28},{24,16},{28,20},{1,9},{5... | collective-permute-start | bytes 1622024 | tf_op jit(solution)/shard_map/ppermute | solution.py:82
  152.1 17.0 %collective-permute-start.20 = (bf16[2112,128]{1,0:T(8,128)(2,1)}, bf16[2112,128]{1,0:T(8,128)(2,1)}, u32[]{:S(2)}, u32[]{:S(2)}) collective-permute-start(bf16[2112,128]{1,0:T(8,128)(2,1)} %collective-permute-done.16), channel_id=1, source_target_pairs={{0,1},{1,0},{2,3},{3,2},{4,5},{5,4},{6,7},{7,6},{8,9},{9,8},{10,11... | collective-permute-start | bytes 1622024 | tf_op jit(solution)/shard_map/ppermute | solution.py:82
  174.1 29.4 %collective-permute-start.24 = (bf16[2,2144,128]{2,1,0:T(8,128)(2,1)}, bf16[2,2144,128]{2,1,0:T(8,128)(2,1)}, u32[]{:S(2)}, u32[]{:S(2)}) collective-permute-start(bf16[2,2144,128]{2,1,0:T(8,128)(2,1)} %maximum_maximum_fusion.refs_0_.refs_1_.refs_2_), channel_id=1, source_target_pairs={{0,4},{4,0},{8,12},{12,8},{16,20},{20,16},{24,28},{28,24},{1,5},{5... | collective-permute-start | bytes 3293192 | tf_op jit(solution)/shard_map/ppermute | solution.py:82
  174.3 29.3 %collective-permute-start.23 = (bf16[2,2144,128]{2,1,0:T(8,128)(2,1)}, bf16[2,2144,128]{2,1,0:T(8,128)(2,1)}, u32[]{:S(2)}, u32[]{:S(2)}) collective-permute-start(bf16[2,2144,128]{2,1,0:T(8,128)(2,1)} %maximum_maximum_fusion.refs_0_.refs_1_.refs_2_), channel_id=1, source_target_pairs={{0,16},{4,20},{8,24},{12,28},{16,0},{20,4},{24,8},{28,12},{1,17},{... | collective-permute-start | bytes 3293192 | tf_op jit(solution)/shard_map/ppermute | solution.py:82
  174.8 28.8 %collective-permute-start.22 = (bf16[2,2144,128]{2,1,0:T(8,128)(2,1)}, bf16[2,2144,128]{2,1,0:T(8,128)(2,1)}, u32[]{:S(2)}, u32[]{:S(2)}) collective-permute-start(bf16[2,2144,128]{2,1,0:T(8,128)(2,1)} %maximum_maximum_fusion.refs_0_.refs_1_.refs_2_), channel_id=1, source_target_pairs={{0,8},{4,12},{8,0},{12,4},{16,24},{20,28},{24,16},{28,20},{1,9},{5... | collective-permute-start | bytes 3293192 | tf_op jit(solution)/shard_map/ppermute | solution.py:82
  203.6 51.4 %collective-permute-start.29 = (bf16[4,2,2112,128]{3,2,1,0:T(8,128)(2,1)}, bf16[4,2,2112,128]{3,2,1,0:T(8,128)(2,1)}, u32[]{:S(2)}, u32[]{:S(2)}) collective-permute-start(bf16[4,2,2112,128]{3,2,1,0:T(8,128)(2,1)} %get-tuple-element.343), channel_id=1, source_target_pairs={{0,4},{4,0},{8,12},{12,8},{16,20},{20,16},{24,28},{28,24},{1,5},{5... | collective-permute-start | bytes 12976136 | tf_op jit(solution)/shard_map/ppermute | solution.py:82
  204.8 14.9 %collective-permute-start.25 = (bf16[1,2144,128]{2,1,0:T(8,128)(2,1)S(1)}, bf16[1,2144,128]{2,1,0:T(8,128)(2,1)S(1)}, u32[]{:S(2)}, u32[]{:S(2)}) collective-permute-start(bf16[1,2144,128]{2,1,0:T(8,128)(2,1)S(1)} %slice.213), channel_id=1, source_target_pairs={{0,8},{4,12},{8,0},{12,4},{16,24},{20,28},{24,16},{28,20},{1,9},{5... | collective-permute-start | bytes 1646600 | tf_op jit(solution)/shard_map/ppermute | solution.py:82
  208.1 19.0 %collective-permute-start.27 = (bf16[4,2144,128]{2,1,0:T(8,128)(2,1)S(1)}, bf16[4,2144,128]{2,1,0:T(8,128)(2,1)S(1)}, u32[]{:S(2)}, u32[]{:S(2)}) collective-permute-start(bf16[4,2144,128]{2,1,0:T(8,128)(2,1)S(1)} %pad_maximum_fusion), channel_id=1, source_target_pairs={{0,4},{4,0},{8,12},{12,8},{16,20},{20,16},{24,28},{28,24},{1,5},{5... | collective-permute-start | bytes 6586376 | tf_op jit(solution)/shard_map/ppermute | solution.py:82
  209.4 14.7 %collective-permute-start.26 = (bf16[1,2144,128]{2,1,0:T(8,128)(2,1)S(1)}, bf16[1,2144,128]{2,1,0:T(8,128)(2,1)S(1)}, u32[]{:S(2)}, u32[]{:S(2)}) collective-permute-start(bf16[1,2144,128]{2,1,0:T(8,128)(2,1)S(1)} %slice.214), channel_id=1, source_target_pairs={{0,16},{4,20},{8,24},{12,28},{16,0},{20,4},{24,8},{28,12},{1,17},{... | collective-permute-start | bytes 1646600 | tf_op jit(solution)/shard_map/ppermute | solution.py:82
  255.1 51.3 %collective-permute-start.37 = (bf16[4,2,2112,128]{3,2,1,0:T(8,128)(2,1)}, bf16[4,2,2112,128]{3,2,1,0:T(8,128)(2,1)}, u32[]{:S(2)}, u32[]{:S(2)}) collective-permute-start(bf16[4,2,2112,128]{3,2,1,0:T(8,128)(2,1)} %get-tuple-element.363), channel_id=1, source_target_pairs={{0,4},{4,0},{8,12},{12,8},{16,20},{20,16},{24,28},{28,24},{1,5},{5... | collective-permute-start | bytes 12976136 | tf_op jit(solution)/shard_map/ppermute | solution.py:82
  255.3 15.4 %collective-permute-start.34 = (f32[1,128]{1,0:T(1,128)S(1)}, f32[1,128]{1,0:T(1,128)S(1)}, u32[]{:S(2)}, u32[]{:S(2)}) collective-permute-start(f32[1,128]{1,0:T(1,128)S(1)} %add_bitcast_fusion), channel_id=1, source_target_pairs={{0,3},{1,2},{2,1},{3,0},{4,7},{5,6},{6,5},{7,4},{8,11},{9,10},{10,... | collective-permute-start | bytes 1544 | tf_op jit(solution)/shard_map/ppermute | solution.py:82
  258.1 15.2 %collective-permute-start.33 = (f32[1,128]{1,0:T(1,128)S(1)}, f32[1,128]{1,0:T(1,128)S(1)}, u32[]{:S(2)}, u32[]{:S(2)}) collective-permute-start(f32[1,128]{1,0:T(1,128)S(1)} %add_bitcast_fusion), channel_id=1, source_target_pairs={{0,2},{1,3},{2,0},{3,1},{4,6},{5,7},{6,4},{7,5},{8,10},{9,11},{10,... | collective-permute-start | bytes 1544 | tf_op jit(solution)/shard_map/ppermute | solution.py:82
  280.3 24.9 %collective-permute-start.35 = (bf16[2,2112,128]{2,1,0:T(8,128)(2,1)}, bf16[2,2112,128]{2,1,0:T(8,128)(2,1)}, u32[]{:S(2)}, u32[]{:S(2)}) collective-permute-start(bf16[2,2112,128]{2,1,0:T(8,128)(2,1)} %get-tuple-element.361), channel_id=1, source_target_pairs={{0,8},{4,12},{8,0},{12,4},{16,24},{20,28},{24,16},{28,20},{1,9},{5... | collective-permute-start | bytes 3244040 | tf_op jit(solution)/shard_map/ppermute | solution.py:82
  281.8 24.5 %collective-permute-start.36 = (bf16[2,2112,128]{2,1,0:T(8,128)(2,1)}, bf16[2,2112,128]{2,1,0:T(8,128)(2,1)}, u32[]{:S(2)}, u32[]{:S(2)}) collective-permute-start(bf16[2,2112,128]{2,1,0:T(8,128)(2,1)} %get-tuple-element.362), channel_id=1, source_target_pairs={{0,16},{4,20},{8,24},{12,28},{16,0},{20,4},{24,8},{28,12},{1,17},{... | collective-permute-start | bytes 3244040 | tf_op jit(solution)/shard_map/ppermute | solution.py:82
  331.3 31.6 %collective-permute-start.42 = (bf16[4,2,1024,128]{3,2,1,0:T(8,128)(2,1)}, bf16[4,2,1024,128]{3,2,1,0:T(8,128)(2,1)}, u32[]{:S(2)}, u32[]{:S(2)}) collective-permute-start(bf16[4,2,1024,128]{3,2,1,0:T(8,128)(2,1)} %get-tuple-element.395), channel_id=1, source_target_pairs={{0,4},{4,0},{8,12},{12,8},{16,20},{20,16},{24,28},{28,24},{1,5},{5... | collective-permute-start | bytes 6291464 | tf_op jit(solution)/shard_map/ppermute | solution.py:82
  334.8 24.5 %collective-permute-start.43 = (bf16[2112,128]{1,0:T(8,128)(2,1)}, bf16[2112,128]{1,0:T(8,128)(2,1)}, u32[]{:S(2)}, u32[]{:S(2)}) collective-permute-start(bf16[2112,128]{1,0:T(8,128)(2,1)} %bitcast.43), channel_id=1, source_target_pairs={{0,1},{1,0},{2,3},{3,2},{4,5},{5,4},{6,7},{7,6},{8,9},{9,8},{10,11... | collective-permute-start | bytes 1622024 | tf_op jit(solution)/shard_map/ppermute | solution.py:82
  335.5 26.3 %collective-permute-start.40 = (bf16[2,2112,128]{2,1,0:T(8,128)(2,1)}, bf16[2,2112,128]{2,1,0:T(8,128)(2,1)}, u32[]{:S(2)}, u32[]{:S(2)}) collective-permute-start(bf16[2,2112,128]{2,1,0:T(8,128)(2,1)} %get-tuple-element.393), channel_id=1, source_target_pairs={{0,8},{4,12},{8,0},{12,4},{16,24},{20,28},{24,16},{28,20},{1,9},{5... | collective-permute-start | bytes 3244040 | tf_op jit(solution)/shard_map/ppermute | solution.py:82
  336.9 26.0 %collective-permute-start.41 = (bf16[2,2112,128]{2,1,0:T(8,128)(2,1)}, bf16[2,2112,128]{2,1,0:T(8,128)(2,1)}, u32[]{:S(2)}, u32[]{:S(2)}) collective-permute-start(bf16[2,2112,128]{2,1,0:T(8,128)(2,1)} %get-tuple-element.394), channel_id=1, source_target_pairs={{0,16},{4,20},{8,24},{12,28},{16,0},{20,4},{24,8},{28,12},{1,17},{... | collective-permute-start | bytes 3244040 | tf_op jit(solution)/shard_map/ppermute | solution.py:82
  368.9 14.9 %collective-permute-start.44 = (bf16[1,1024,128]{2,1,0:T(8,128)(2,1)}, bf16[1,1024,128]{2,1,0:T(8,128)(2,1)S(1)}, u32[]{:S(2)}, u32[]{:S(2)}) collective-permute-start(bf16[1,1024,128]{2,1,0:T(8,128)(2,1)} %get-tuple-element.413), channel_id=1, source_target_pairs={{0,8},{4,12},{8,0},{12,4},{16,24},{20,28},{24,16},{28,20},{1,9},{5... | collective-permute-start | bytes 786440 | tf_op jit(solution)/shard_map/ppermute | solution.py:82
  388.9 29.8 %collective-permute-start.47 = (bf16[4,2,1024,128]{3,2,1,0:T(8,128)(2,1)}, bf16[4,2,1024,128]{3,2,1,0:T(8,128)(2,1)}, u32[]{:S(2)}, u32[]{:S(2)}) collective-permute-start(bf16[4,2,1024,128]{3,2,1,0:T(8,128)(2,1)} %get-tuple-element.437), channel_id=1, source_target_pairs={{0,4},{4,0},{8,12},{12,8},{16,20},{20,16},{24,28},{28,24},{1,5},{5... | collective-permute-start | bytes 6291464 | tf_op jit(solution)/shard_map/ppermute | solution.py:82
  388.9 24.4 %collective-permute-start.48 = (bf16[2,1024,128]{2,1,0:T(8,128)(2,1)}, bf16[2,1024,128]{2,1,0:T(8,128)(2,1)}, u32[]{:S(2)}, u32[]{:S(2)}) collective-permute-start(bf16[2,1024,128]{2,1,0:T(8,128)(2,1)} %get-tuple-element.438), channel_id=1, source_target_pairs={{0,8},{4,12},{8,0},{12,4},{16,24},{20,28},{24,16},{28,20},{1,9},{5... | collective-permute-start | bytes 1572872 | tf_op jit(solution)/shard_map/ppermute | solution.py:82
  390.4 22.9 %collective-permute-start.49 = (bf16[2,1024,128]{2,1,0:T(8,128)(2,1)}, bf16[2,1024,128]{2,1,0:T(8,128)(2,1)}, u32[]{:S(2)}, u32[]{:S(2)}) collective-permute-start(bf16[2,1024,128]{2,1,0:T(8,128)(2,1)} %get-tuple-element.439), channel_id=1, source_target_pairs={{0,16},{4,20},{8,24},{12,28},{16,0},{20,4},{24,8},{28,12},{1,17},{... | collective-permute-start | bytes 1572872 | tf_op jit(solution)/shard_map/ppermute | solution.py:82
  391.8 26.9 %collective-permute-start.50 = (bf16[2112,128]{1,0:T(8,128)(2,1)}, bf16[2112,128]{1,0:T(8,128)(2,1)}, u32[]{:S(2)}, u32[]{:S(2)}) collective-permute-start(bf16[2112,128]{1,0:T(8,128)(2,1)} %fusion.12), channel_id=1, source_target_pairs={{0,2},{1,3},{2,0},{3,1},{4,6},{5,7},{6,4},{7,5},{8,10},{9,11},{10,... | collective-permute-start | bytes 1622024 | tf_op jit(solution)/shard_map/ppermute | solution.py:82
  423.4 28.8 %collective-permute-start.55 = (bf16[512,1024]{1,0:T(8,128)(2,1)}, bf16[512,1024]{1,0:T(8,128)(2,1)}, u32[]{:S(2)}, u32[]{:S(2)}) collective-permute-start(bf16[512,1024]{1,0:T(8,128)(2,1)} %get-tuple-element.476), channel_id=1, source_target_pairs={{1,0},{2,1},{3,2},{5,4},{6,5},{7,6},{9,8},{10,9},{11,10},{13,12},{... | collective-permute-start | bytes 3145736 | tf_op jit(solution)/shard_map/ppermute | solution.py:1391
  427.3 75.7 %collective-permute-start.61 = (bf16[1024,128]{1,0:T(8,128)(2,1)}, bf16[1024,128]{1,0:T(8,128)(2,1)S(1)}, u32[]{:S(2)}, u32[]{:S(2)}) collective-permute-start(bf16[1024,128]{1,0:T(8,128)(2,1)} %bitcast.47), channel_id=1, source_target_pairs={{0,1},{1,0},{2,3},{3,2},{4,5},{5,4},{6,7},{7,6},{8,9},{9,8},{10,11... | collective-permute-start | bytes 786440 | tf_op jit(solution)/shard_map/ppermute | solution.py:82
  457.5 14.9 %collective-permute-start.59 = (f32[2,1024]{1,0:T(2,128)S(1)}, f32[2,1024]{1,0:T(2,128)S(1)}, u32[]{:S(2)}, u32[]{:S(2)}) collective-permute-start(f32[2,1024]{1,0:T(2,128)S(1)} %pad_maximum_fusion.6), channel_id=1, source_target_pairs={{0,24},{4,28},{8,16},{12,20},{16,8},{20,12},{24,0},{28,4},{1,25},{... | collective-permute-start | bytes 24584 | tf_op jit(solution)/shard_map/ppermute | solution.py:82
  459.0 15.0 %collective-permute-start.58 = (f32[2,1024]{1,0:T(2,128)S(1)}, f32[2,1024]{1,0:T(2,128)S(1)}, u32[]{:S(2)}, u32[]{:S(2)}) collective-permute-start(f32[2,1024]{1,0:T(2,128)S(1)} %pad_maximum_fusion.6), channel_id=1, source_target_pairs={{0,16},{4,20},{8,24},{12,28},{16,0},{20,4},{24,8},{28,12},{1,17},{... | collective-permute-start | bytes 24584 | tf_op jit(solution)/shard_map/ppermute | solution.py:82
  472.5 25.4 %collective-permute-start.62 = (bf16[512,1024]{1,0:T(8,128)(2,1)}, bf16[512,1024]{1,0:T(8,128)(2,1)}, u32[]{:S(2)}, u32[]{:S(2)}) collective-permute-start(bf16[512,1024]{1,0:T(8,128)(2,1)} %add_convert_fusion), channel_id=1, source_target_pairs={{1,0},{2,1},{3,2},{5,4},{6,5},{7,6},{9,8},{10,9},{11,10},{13,12},{... | collective-permute-start | bytes 3145736 | tf_op jit(solution)/shard_map/ppermute | solution.py:1391
  474.8 28.2 %collective-permute-start.63 = (f32[2,1024]{1,0:T(2,128)S(1)}, f32[2,1024]{1,0:T(2,128)S(1)}, u32[]{:S(2)}, u32[]{:S(2)}) collective-permute-start(f32[2,1024]{1,0:T(2,128)S(1)} %add_add_fusion), channel_id=1, source_target_pairs={{0,4},{4,0},{8,12},{12,8},{16,20},{20,16},{24,28},{28,24},{1,5},{5... | collective-permute-start | bytes 24584 | tf_op jit(solution)/shard_map/ppermute | solution.py:82
  474.8 32.6 %collective-permute-start.60 = (bf16[1024,128]{1,0:T(8,128)(2,1)}, bf16[1024,128]{1,0:T(8,128)(2,1)}, u32[]{:S(2)}, u32[]{:S(2)}) collective-permute-start(bf16[1024,128]{1,0:T(8,128)(2,1)} %fusion.20), channel_id=1, source_target_pairs={{0,2},{1,3},{2,0},{3,1},{4,6},{5,7},{6,4},{7,5},{8,10},{9,11},{10,... | collective-permute-start | bytes 786440 | tf_op jit(solution)/shard_map/ppermute | solution.py:82
  507.4 18.3 %collective-permute-start.66 = (f32[2,1024]{1,0:T(2,128)S(1)}, f32[2,1024]{1,0:T(2,128)S(1)}, u32[]{:S(2)}, u32[]{:S(2)}) collective-permute-start(f32[2,1024]{1,0:T(2,128)S(1)} %add.254), channel_id=1, source_target_pairs={{0,3},{1,2},{2,1},{3,0},{4,7},{5,6},{6,5},{7,4},{8,11},{9,10},{10,... | collective-permute-start | bytes 24584 | tf_op jit(solution)/shard_map/ppermute | solution.py:82
  507.4 18.3 %collective-permute-start.65 = (f32[2,1024]{1,0:T(2,128)S(1)}, f32[2,1024]{1,0:T(2,128)S(1)}, u32[]{:S(2)}, u32[]{:S(2)}) collective-permute-start(f32[2,1024]{1,0:T(2,128)S(1)} %add.254), channel_id=1, source_target_pairs={{0,2},{1,3},{2,0},{3,1},{4,6},{5,7},{6,4},{7,5},{8,10},{9,11},{10,... | collective-permute-start | bytes 24584 | tf_op jit(solution)/shard_map/ppermute | solution.py:82
  (58 other events, 494.5 us)

commit v5 on v4

--- a/solution.py
+++ b/solution.py
@@ -86,12 +86,12 @@
     return pairwise(slices, "dp", 2), pairwise(slices, "dp", 4), pairwise(slices, "dp", 1)
 
 
-def gather_corner(across_x, across_y, other):
+def gather_corner(across_x, across_y, other, both=None):
     half = across_x.shape[0] // 2
     return (
         pairwise(across_y[:half], "dp", 2),
         pairwise(across_x[half:], "dp", 4),
-        pairwise(jnp.concatenate([across_x, across_y]), "dp", 1),
+        pairwise(jnp.concatenate([across_x, across_y]) if both is None else both, "dp", 1),
     )
 
 
@@ -1265,11 +1265,13 @@
     inputs = labels + (queries, keys, values)
     context_a, sums_a = attend(inputs, tile, 0, half_pairs)
     if fast:
-        queries, context_a, sides, slice_two, grad_low, raw_total = together(
-            queries, context_a, sides, slice_two, grad_low, raw_total
-        )
+        queries, context_a, sides, grad_low, raw_total = together(
+            queries, context_a, sides, grad_low, raw_total
+        )
+        near_sides = jnp.concatenate(sides[:2])
+        queries, slice_two, near_sides = together(queries, slice_two, near_sides)
         inputs = labels + (queries, keys, values)
-        corners = gather_corner(*sides)
+        corners = gather_corner(*sides, near_sides)
         slice_three = pairwise(slice_two, "mp", 1)
     context_b, sums_b = attend(inputs, tile, half_pairs, half_pairs)
     if fast:

time: 540 us -> 536 us (level)
  transfers between devices with their start and end apart: 67 -> 67, of which waited for: 23 -> 26; matrix products, arithmetic and copies ran while one was open for 16% -> 17% of each run, Pallas kernels for 39% -> 40%
where the time goes in v5:
time: 536 us; the launch traced here: 531 us
  Pallas kernels  243 us (45%)
  waiting for transfers between devices  102 us (19%)
  starting transfers between devices  77.2 us (14%)
  other arithmetic  49.2 us (9%)
  matrix products  36.4 us (7%)
  local copies, waits for them, and re-layouts  20.8 us (4%)
    ppermute x63, waiting for transfers between devices, pairwise(): lax.ppermute(values, axis, [(i, i ^ step) for i in range(lax.axis_size(ax...  73.5 us
    ppermute x63, starting transfers between devices, pairwise(): lax.ppermute(values, axis, [(i, i ^ step) for i in range(lax.axis_size(ax...  64.7 us
    pallas_call x2, Pallas kernels, hidden_layer(): grid_call(functools.partial(hidden_kernel, len(earlier)), (slices,), [who...  52.4 us
    pallas_call x5, Pallas kernels, shampoo_rows(): pl.pallas_call(functools.partial(shampoo_rows_kernel, step_size, turned,...  47.8 us
    pallas_call x12, Pallas kernels, add_call(): pl.pallas_call(kernel, grid=(slices,), in_specs=in_specs, out_specs=out_s...  36.5 us
    pallas_call x2, Pallas kernels, attend_back(): pl.pallas_call(functools.partial(attend_back_kernel, tile, window - count...  33.5 us
    dot_general x8, matrix products, dot_weight(): lax.dot_general(first, second, (((0,), (0,)), ((), ())), preferred_elemen...  31.4 us
    pallas_call x2, Pallas kernels, attend(): pl.pallas_call(functools.partial(attend_kernel, tile, window - count), gr...  29.6 us
  transfers between devices with their start and end apart: 67, of which 26 were waited for; matrix products, arithmetic and copies ran while one was open for 17% of the time, Pallas kernels for 40%

profile of v5, /device:TPU:0, one launch (start us, length us, event | category | flops | bytes accessed | tf_op | source)
XLA Modules:
  0.0 530.9 jit_solution(17654332380650206340)
XLA Ops:
  4.6 3.1 collective-permute-start.2
  11.9 10.5 %collective-permute-done = bf16[1056,128]{1,0:T(8,128)(2,1)S(1)} collective-permute-done((bf16[1056,128]{1,0:T(8,128)(2,1)S(1)}, bf16[1056,128]{1,0:T(8,128)(2,1)S(1)}, u32[]{:S(2)}, u32[]{:S(2)}) %collective-permute-start) | collective-permute-done | bytes 270368 | tf_op jit(solution)/shard_map/ppermute | solution.py:82
  22.9 6.0 %collective-permute-done.3 = bf16[1056,128]{1,0:T(8,128)(2,1)S(1)} collective-permute-done((bf16[1056,128]{1,0:T(8,128)(2,1)S(1)}, bf16[1056,128]{1,0:T(8,128)(2,1)S(1)}, u32[]{:S(2)}, u32[]{:S(2)}) %collective-permute-start.3) | collective-permute-done | bytes 270368 | tf_op jit(solution)/shard_map/ppermute | solution.py:82
  33.0 4.2 collective-permute-start.1
  47.6 11.4 %collective-permute-done.1.refs_1_ = bf16[512,1024]{1,0:T(8,128)(2,1)} collective-permute-done((bf16[512,1024]{1,0:T(8,128)(2,1)}, bf16[512,1024]{1,0:T(8,128)(2,1)}, u32[]{:S(2)}, u32[]{:S(2)}) %collective-permute-start.1) | collective-permute-done | bytes 1048608 | tf_op jit(solution)/shard_map/ppermute | solution.py:1192
  64.0 5.6 %collective-permute-start.7 = (bf16[512,1024]{1,0:T(8,128)(2,1)}, bf16[512,1024]{1,0:T(8,128)(2,1)}, u32[]{:S(2)}, u32[]{:S(2)}) collective-permute-start(bf16[512,1024]{1,0:T(8,128)(2,1)} %collective-permute-done.1.refs_1_), channel_id=1, source_target_pairs={{0,1},{1,2},{2,3},{4,5},{5,6},{6,7},{8,9},{9,10},{10,11},{12,13},{... | collective-permute-start | bytes 3145736 | tf_op jit(solution)/shard_map/ppermute | solution.py:1192
  71.6 13.5 %collective-permute-done.9 = bf16[2,1056,128]{2,1,0:T(8,128)(2,1)S(1)} collective-permute-done((bf16[2,1056,128]{2,1,0:T(8,128)(2,1)}, bf16[2,1056,128]{2,1,0:T(8,128)(2,1)S(1)}, u32[]{:S(2)}, u32[]{:S(2)}) %collective-permute-start.9) | collective-permute-done | bytes 540704 | tf_op jit(solution)/shard_map/ppermute | solution.py:82
  85.3 6.5 %collective-permute-done.7.refs_0_ = bf16[512,1024]{1,0:T(8,128)(2,1)} collective-permute-done((bf16[512,1024]{1,0:T(8,128)(2,1)}, bf16[512,1024]{1,0:T(8,128)(2,1)}, u32[]{:S(2)}, u32[]{:S(2)}) %collective-permute-start.7) | collective-permute-done | bytes 1048608 | tf_op jit(solution)/shard_map/ppermute | solution.py:1192
  95.6 16.6 %project.1 = (bf16[3,1024,1024]{2,1,0:T(8,128)(2,1)}, bf16[1024,1024]{1,0:T(8,128)(2,1)}, bf16[512,1024]{1,0:T(8,128)(2,1)}, bf16[1536,1024]{1,0:T(8,128)(2,1)},...) custom-call(s32[1]{0:T(128)} %bitcast.2.device_ref, bf16[512,1024]{1,0:T(8,128)(2,1)} %collective-permute-done.7.refs_0_, ...), custom_call_target="tpu_custom_call" | custom-call | flops 7516192768 | bytes 16777216 | tf_op jit(solution)/shard_map/project/pallas_call | solution.py:391
  117.2 4.3 convert_reduce_fusion
  122.8 14.5 %attend.2 = (bf16[512,512]{1,0:T(8,128)(2,1)}, f32[4,2,512]{2,1,0:T(2,128)}) custom-call(s32[1,512]{1,0:T(1,128)} %bitcast.156, s32[1536,1]{1,0:T(8,128)} %reshape.400.key_labels, bf16[512,1024]{1,0:T(8,128)(2,1)} %get-tuple-element.312.q_ref, bf16[1536,1024]{1,0:T(8,128)(2,1)} %get-tuple-element.304.k_ref, bf16[1536,1024]{1,0:T(8,128)(2,1)} %get-tuple-element.305.v_ref), custom_call_target="tpu_custom_call" | custom-call | flops 2684354560 | bytes 4194304 | tf_op jit(solution)/shard_map/attend/pallas_call | solution.py:714
  140.1 2.8 pad_maximum_fusion.2
  149.5 15.1 %attend.3 = (bf16[512,512]{1,0:T(8,128)(2,1)}, f32[4,2,512]{2,1,0:T(2,128)}) custom-call(s32[1,512]{1,0:T(1,128)} %bitcast.157, s32[1536,1]{1,0:T(8,128)} %reshape.400.key_labels, bf16[512,1024]{1,0:T(8,128)(2,1)} %get-tuple-element.312.q_ref, bf16[1536,1024]{1,0:T(8,128)(2,1)} %get-tuple-element.304.k_ref, bf16[1536,1024]{1,0:T(8,128)(2,1)} %get-tuple-element.305.v_ref), custom_call_target="tpu_custom_call" | custom-call | flops 2684354560 | bytes 4194304 | tf_op jit(solution)/shard_map/attend/pallas_call | solution.py:714
  175.9 26.1 %hidden_layer.2 = (f32[512,1024]{1,0:T(8,128)}, f32[512,1024]{1,0:T(8,128)}, bf16[4,2,2112,128]{3,2,1,0:T(8,128)(2,1)}, bf16[4,2,2112,128]{3,2,1,0:T(8,128)(2,1)}) custom-call(s32[1]{0:T(128)} %bitcast.2.device_ref, bf16[512,1024]{1,0:T(8,128)(2,1)} %multiply_convert_fusion.normed_ref, bf16[512,1024]{1,0:T(8,128)(2,1)} %fusion.11.grads_ref, ...), custom_call_target="tpu_custom_call" | custom-call | flops 13287555072 | bytes 17301504 | tf_op jit(solution)/shard_map/hidden_layer/pallas_call | solution.py:506
  208.4 9.7 %collective-permute-done.25 = bf16[1,2144,128]{2,1,0:T(8,128)(2,1)S(1)} collective-permute-done((bf16[1,2144,128]{2,1,0:T(8,128)(2,1)S(1)}, bf16[1,2144,128]{2,1,0:T(8,128)(2,1)S(1)}, u32[]{:S(2)}, u32[]{:S(2)}) %collective-permute-start.25) | collective-permute-done | bytes 548896 | tf_op jit(solution)/shard_map/ppermute | solution.py:82
  218.2 3.5 collective-permute-done.26
  226.2 26.3 %hidden_layer.3 = (f32[512,1024]{1,0:T(8,128)}, f32[512,1024]{1,0:T(8,128)}, bf16[4,2,2112,128]{3,2,1,0:T(8,128)(2,1)}, bf16[4,2,2112,128]{3,2,1,0:T(8,128)(2,1)}) custom-call(s32[1]{0:T(128)} %bitcast.2.device_ref, bf16[512,1024]{1,0:T(8,128)(2,1)} %multiply_convert_fusion.normed_ref, bf16[512,1024]{1,0:T(8,128)(2,1)} %fusion.11.grads_ref, ...), custom_call_target="tpu_custom_call" | custom-call | flops 13287555072 | bytes 17301504 | tf_op jit(solution)/shard_map/hidden_layer/pallas_call | solution.py:506
  254.7 3.0 add_corner.4
  260.6 3.0 multiply_reduce_fusion
  273.5 3.8 add_sides.4
  279.2 16.7 %attend_back.2 = (bf16[512,512]{1,0:T(8,128)(2,1)}, bf16[1536,512]{1,0:T(8,128)(2,1)}, bf16[1536,512]{1,0:T(8,128)(2,1)}) custom-call(s32[1,512]{1,0:T(1,128)} %bitcast.158, s32[1536,1]{1,0:T(8,128)} %reshape.400.key_labels, bf16[512,1024]{1,0:T(8,128)(2,1)} %get-tuple-element.312.q_ref, bf16[1536,1024]{1,0:T(8,128)(2,1)} %get-tuple-element.304.k_ref, ...), custom_call_target="tpu_custom_call" | custom-call | flops 6710886400 | bytes 8388608 | tf_op jit(solution)/shard_map/attend_back/pallas_call | solution.py:739
  295.9 5.2 convolution_convert_fusion.3.key
  302.7 3.9 add_own.4
  306.5 3.2 add_corner.5
  312.6 3.1 convolution_convert_fusion.8.query
  315.7 4.7 convolution_convert_fusion.2.value
  320.4 4.1 cut_attend.2
  324.5 3.9 add_sides.5
  328.4 3.5 convolution_convert_fusion.5.output
  335.1 16.8 %attend_back.3 = (bf16[512,512]{1,0:T(8,128)(2,1)}, bf16[1536,512]{1,0:T(8,128)(2,1)}, bf16[1536,512]{1,0:T(8,128)(2,1)}) custom-call(s32[1,512]{1,0:T(1,128)} %bitcast.159, s32[1536,1]{1,0:T(8,128)} %reshape.400.key_labels, bf16[512,1024]{1,0:T(8,128)(2,1)} %get-tuple-element.312.q_ref, bf16[1536,1024]{1,0:T(8,128)(2,1)} %get-tuple-element.304.k_ref, ...), custom_call_target="tpu_custom_call" | custom-call | flops 6710886400 | bytes 8388608 | tf_op jit(solution)/shard_map/attend_back/pallas_call | solution.py:739
  351.8 5.1 convolution_convert_fusion.1.key
  357.0 3.1 collective-permute-done.40.from_x
  360.5 3.9 add_own.5
  368.8 5.1 convolution_convert_fusion.value
  374.0 2.9 convolution_convert_fusion.6.query
  376.9 4.3 cut_attend.3
  390.1 15.8 %project_back.1 = (bf16[512,1024]{1,0:T(8,128)(2,1)}, f32[512,1024]{1,0:T(8,128)}, f32[512,1024]{1,0:T(8,128)}, f32[1,1024]{1,0:T(1,128)}) custom-call(bf16[512,512]{1,0:T(8,128)(2,1)} %get-tuple-element.378.refs_0_, bf16[512,512]{1,0:T(8,128)(2,1)} %get-tuple-element.433.refs_1_, bf16[1536,512]{1,0:T(8,128)(2,1)} %get-tuple-element.434.refs_2_, ...), custom_call_target="tpu_custom_call" | custom-call | flops 7516192768 | bytes 18874368 | tf_op jit(solution)/shard_map/project_back/pallas_call | solution.py:810
  405.9 3.7 add_convert_fusion.1
  409.6 5.7 %collective-permute-done.50.two = bf16[2112,128]{1,0:T(8,128)(2,1)} collective-permute-done((bf16[2112,128]{1,0:T(8,128)(2,1)}, bf16[2112,128]{1,0:T(8,128)(2,1)}, u32[]{:S(2)}, u32[]{:S(2)}) %collective-permute-start.50) | collective-permute-done | bytes 540704 | tf_op jit(solution)/shard_map/ppermute | solution.py:82
  436.3 9.4 %shampoo_rows.5 = (f32[1,8,64,176]{3,2,1,0:T(8,128)}, f32[1,8,64,176]{3,2,1,0:T(8,128)}, f32[1,8,64,64]{3,2,1,0:T(8,128)}, f32[1,8,176,176]{3,2,1,0:T(8,128)}) custom-call(f32[1]{0:T(128)} %bitcast.46.scale_ref, f32[1,2112,128]{2,1,0:T(8,128)} %get-tuple-element.452.own, bf16[2112,128]{1,0:T(8,128)(2,1)} %collective-permute-done.43.one, ...), custom_call_target="tpu_custom_call" | custom-call | flops 6978273280 | bytes 3686400 | tf_op jit(solution)/shard_map/shampoo_rows/pallas_call | solution.py:1008
  458.8 9.3 %shampoo_rows.6 = (f32[2,8,64,176]{3,2,1,0:T(8,128)}, f32[2,8,64,176]{3,2,1,0:T(8,128)}, f32[2,8,64,64]{3,2,1,0:T(8,128)}, f32[2,8,176,176]{3,2,1,0:T(8,128)}) custom-call(f32[1]{0:T(128)} %bitcast.46.scale_ref, f32[1,2112,128]{2,1,0:T(8,128)} %get-tuple-element.452.own, bf16[2112,128]{1,0:T(8,128)(2,1)} %collective-permute-done.43.one, ...), custom_call_target="tpu_custom_call" | custom-call | flops 6978273280 | bytes 3686400 | tf_op jit(solution)/shard_map/shampoo_rows/pallas_call | solution.py:1008
  473.2 9.4 %shampoo_rows.7 = (f32[2,8,64,176]{3,2,1,0:T(8,128)}, f32[2,8,64,176]{3,2,1,0:T(8,128)}, f32[2,8,64,64]{3,2,1,0:T(8,128)}, f32[2,8,176,176]{3,2,1,0:T(8,128)}) custom-call(f32[1]{0:T(128)} %bitcast.46.scale_ref, f32[1,2112,128]{2,1,0:T(8,128)} %get-tuple-element.452.own, ...), custom_call_target="tpu_custom_call", output_to_operand_aliasing={{0}: (7, {}), {1}: (8, {}), {2}: (9, {}), {3}: (10, {})} | custom-call | flops 6978273280 | bytes 3686400 | tf_op jit(solution)/shard_map/shampoo_rows/pallas_call | solution.py:1008
  482.6 9.9 %collective-permute-done.62 = bf16[512,1024]{1,0:T(8,128)(2,1)} collective-permute-done((bf16[512,1024]{1,0:T(8,128)(2,1)}, bf16[512,1024]{1,0:T(8,128)(2,1)}, u32[]{:S(2)}, u32[]{:S(2)}) %collective-permute-start.62) | collective-permute-done | bytes 1048608 | tf_op jit(solution)/shard_map/ppermute | solution.py:1393
  494.4 3.3 fusion.8
  497.7 5.9 %collective-permute-done.60.two = bf16[1024,128]{1,0:T(8,128)(2,1)} collective-permute-done((bf16[1024,128]{1,0:T(8,128)(2,1)}, bf16[1024,128]{1,0:T(8,128)(2,1)}, u32[]{:S(2)}, u32[]{:S(2)}) %collective-permute-start.60) | collective-permute-done | bytes 262176 | tf_op jit(solution)/shard_map/ppermute | solution.py:82
  503.6 4.4 collective-permute-start.65
  508.0 13.9 %shampoo_rows.8 = (f32[3,8,64,64]{3,2,1,0:T(8,128)}, f32[3,8,64,64]{3,2,1,0:T(8,128)}, f32[3,8,64,64]{3,2,1,0:T(8,128)}, f32[3,8,64,64]{3,2,1,0:T(8,128)}) custom-call(f32[1]{0:T(128)} %bitcast.46.scale_ref, f32[1,1024,128]{2,1,0:T(8,128)} %get-tuple-element.525.own, bf16[1024,128]{1,0:T(8,128)(2,1)} %copy-done.27, ...), custom_call_target="tpu_custom_call" | custom-call | flops 1006632960 | bytes 3145728 | tf_op jit(solution)/shard_map/shampoo_rows/pallas_call | solution.py:1008
  524.5 5.8 %shampoo_rows.9 = (f32[1,8,64,64]{3,2,1,0:T(8,128)}, f32[1,8,64,64]{3,2,1,0:T(8,128)}, f32[1,8,64,64]{3,2,1,0:T(8,128)}, f32[1,8,64,64]{3,2,1,0:T(8,128)}) custom-call(f32[1]{0:T(128)} %bitcast.46.scale_ref, f32[1,1024,128]{2,1,0:T(8,128)} %get-tuple-element.525.own, bf16[1024,128]{1,0:T(8,128)(2,1)} %copy-done.27, ...), custom_call_target="tpu_custom_call" | custom-call | flops 335544320 | bytes 1048576 | tf_op jit(solution)/shard_map/shampoo_rows/pallas_call | solution.py:1008
  (305 shorter events, 152.5 us)
Async XLA Ops:
  4.6 18.2 %collective-permute-start.2 = (bf16[1056,128]{1,0:T(8,128)(2,1)S(1)}, bf16[1056,128]{1,0:T(8,128)(2,1)S(1)}, u32[]{:S(2)}, u32[]{:S(2)}) collective-permute-start(bf16[1056,128]{1,0:T(8,128)(2,1)S(1)} %get-tuple-element.563), channel_id=1, source_target_pairs={{0,1},{1,0},{2,3},{3,2},{4,5},{5,4},{6,7},{7,6},{8,9},{9,8},{10,11... | collective-permute-start | bytes 811016 | tf_op jit(solution)/shard_map/ppermute | solution.py:82
  7.7 14.7 %collective-permute-start = (bf16[1056,128]{1,0:T(8,128)(2,1)S(1)}, bf16[1056,128]{1,0:T(8,128)(2,1)S(1)}, u32[]{:S(2)}, u32[]{:S(2)}) collective-permute-start(bf16[1056,128]{1,0:T(8,128)(2,1)S(1)} %get-tuple-element.563), channel_id=1, source_target_pairs={{0,2},{1,3},{2,0},{3,1},{4,6},{5,7},{6,4},{7,5},{8,10},{9,11},{10,... | collective-permute-start | bytes 811016 | tf_op jit(solution)/shard_map/ppermute | solution.py:82
  30.0 29.0 %collective-permute-start.6 = (bf16[4,1056,128]{2,1,0:T(8,128)(2,1)}, bf16[4,1056,128]{2,1,0:T(8,128)(2,1)}, u32[]{:S(2)}, u32[]{:S(2)}) collective-permute-start(bf16[4,1056,128]{2,1,0:T(8,128)(2,1)} %pad_maximum_fusion.3.refs_3_), channel_id=1, source_target_pairs={{0,4},{4,0},{8,12},{12,8},{16,20},{20,16},{24,28},{28,24},{1,5},{5... | collective-permute-start | bytes 3244040 | tf_op jit(solution)/shard_map/ppermute | solution.py:82
  30.0 29.0 %collective-permute-start.5 = (bf16[4,1056,128]{2,1,0:T(8,128)(2,1)}, bf16[4,1056,128]{2,1,0:T(8,128)(2,1)S(1)}, u32[]{:S(2)}, u32[]{:S(2)}) collective-permute-start(bf16[4,1056,128]{2,1,0:T(8,128)(2,1)} %pad_maximum_fusion.3.refs_3_), channel_id=1, source_target_pairs={{0,16},{4,20},{8,24},{12,28},{16,0},{20,4},{24,8},{28,12},{1,17},{... | collective-permute-start | bytes 3244040 | tf_op jit(solution)/shard_map/ppermute | solution.py:82
  31.5 27.5 %collective-permute-start.4 = (bf16[4,1056,128]{2,1,0:T(8,128)(2,1)}, bf16[4,1056,128]{2,1,0:T(8,128)(2,1)S(1)}, u32[]{:S(2)}, u32[]{:S(2)}) collective-permute-start(bf16[4,1056,128]{2,1,0:T(8,128)(2,1)} %pad_maximum_fusion.3.refs_3_), channel_id=1, source_target_pairs={{0,8},{4,12},{8,0},{12,4},{16,24},{20,28},{24,16},{28,20},{1,9},{5... | collective-permute-start | bytes 3244040 | tf_op jit(solution)/shard_map/ppermute | solution.py:82
  33.0 26.0 %collective-permute-start.1 = (bf16[512,1024]{1,0:T(8,128)(2,1)}, bf16[512,1024]{1,0:T(8,128)(2,1)}, u32[]{:S(2)}, u32[]{:S(2)}) collective-permute-start(bf16[512,1024]{1,0:T(8,128)(2,1)} %fusion.3.refs_2_), channel_id=1, source_target_pairs={{0,1},{1,2},{2,3},{4,5},{5,6},{6,7},{8,9},{9,10},{10,11},{12,13},{... | collective-permute-start | bytes 3145736 | tf_op jit(solution)/shard_map/ppermute | solution.py:1192
  60.7 31.1 %collective-permute-start.10 = (bf16[8,1056,128]{2,1,0:T(8,128)(2,1)}, bf16[8,1056,128]{2,1,0:T(8,128)(2,1)}, u32[]{:S(2)}, u32[]{:S(2)}) collective-permute-start(bf16[8,1056,128]{2,1,0:T(8,128)(2,1)} %pad_maximum_fusion.1), channel_id=1, source_target_pairs={{0,4},{4,0},{8,12},{12,8},{16,20},{20,16},{24,28},{28,24},{1,5},{5... | collective-permute-start | bytes 6488072 | tf_op jit(solution)/shard_map/ppermute | solution.py:82
  64.0 27.8 %collective-permute-start.7 = (bf16[512,1024]{1,0:T(8,128)(2,1)}, bf16[512,1024]{1,0:T(8,128)(2,1)}, u32[]{:S(2)}, u32[]{:S(2)}) collective-permute-start(bf16[512,1024]{1,0:T(8,128)(2,1)} %collective-permute-done.1.refs_1_), channel_id=1, source_target_pairs={{0,1},{1,2},{2,3},{4,5},{5,6},{6,7},{8,9},{9,10},{10,11},{12,13},{... | collective-permute-start | bytes 3145736 | tf_op jit(solution)/shard_map/ppermute | solution.py:1192
  70.4 14.7 %collective-permute-start.9 = (bf16[2,1056,128]{2,1,0:T(8,128)(2,1)}, bf16[2,1056,128]{2,1,0:T(8,128)(2,1)S(1)}, u32[]{:S(2)}, u32[]{:S(2)}) collective-permute-start(bf16[2,1056,128]{2,1,0:T(8,128)(2,1)} %slice.179), channel_id=1, source_target_pairs={{0,16},{4,20},{8,24},{12,28},{16,0},{20,4},{24,8},{28,12},{1,17},{... | collective-permute-start | bytes 1622024 | tf_op jit(solution)/shard_map/ppermute | solution.py:82
  92.9 19.3 %collective-permute-start.12 = (bf16[2112,128]{1,0:T(8,128)(2,1)}, bf16[2112,128]{1,0:T(8,128)(2,1)S(1)}, u32[]{:S(2)}, u32[]{:S(2)}) collective-permute-start(bf16[2112,128]{1,0:T(8,128)(2,1)} %pad_maximum_fusion.5), channel_id=1, source_target_pairs={{0,1},{1,0},{2,3},{3,2},{4,5},{5,4},{6,7},{7,6},{8,9},{9,8},{10,11... | collective-permute-start | bytes 1622024 | tf_op jit(solution)/shard_map/ppermute | solution.py:82
  113.3 24.0 %collective-permute-start.15 = (bf16[2,2112,128]{2,1,0:T(8,128)(2,1)}, bf16[2,2112,128]{2,1,0:T(8,128)(2,1)}, u32[]{:S(2)}, u32[]{:S(2)}) collective-permute-start(bf16[2,2112,128]{2,1,0:T(8,128)(2,1)} %pad_maximum_fusion.4.refs_0_.refs_1_.refs_2_), channel_id=1, source_target_pairs={{0,4},{4,0},{8,12},{12,8},{16,20},{20,16},{24,28},{28,24},{1,5},{5... | collective-permute-start | bytes 3244040 | tf_op jit(solution)/shard_map/ppermute | solution.py:82
  113.5 26.3 %collective-permute-start.14 = (bf16[2,2112,128]{2,1,0:T(8,128)(2,1)}, bf16[2,2112,128]{2,1,0:T(8,128)(2,1)S(1)}, u32[]{:S(2)}, u32[]{:S(2)}) collective-permute-start(bf16[2,2112,128]{2,1,0:T(8,128)(2,1)} %pad_maximum_fusion.4.refs_0_.refs_1_.refs_2_), channel_id=1, source_target_pairs={{0,16},{4,20},{8,24},{12,28},{16,0},{20,4},{24,8},{28,12},{1,17},{... | collective-permute-start | bytes 3244040 | tf_op jit(solution)/shard_map/ppermute | solution.py:82
  114.0 26.1 %collective-permute-start.13 = (bf16[2,2112,128]{2,1,0:T(8,128)(2,1)}, bf16[2,2112,128]{2,1,0:T(8,128)(2,1)}, u32[]{:S(2)}, u32[]{:S(2)}) collective-permute-start(bf16[2,2112,128]{2,1,0:T(8,128)(2,1)} %pad_maximum_fusion.4.refs_0_.refs_1_.refs_2_), channel_id=1, source_target_pairs={{0,8},{4,12},{8,0},{12,4},{16,24},{20,28},{24,16},{28,20},{1,9},{5... | collective-permute-start | bytes 3244040 | tf_op jit(solution)/shard_map/ppermute | solution.py:82
  115.3 27.7 %collective-permute-start.16 = (bf16[2112,128]{1,0:T(8,128)(2,1)}, bf16[2112,128]{1,0:T(8,128)(2,1)}, u32[]{:S(2)}, u32[]{:S(2)}) collective-permute-start(bf16[2112,128]{1,0:T(8,128)(2,1)} %pad_maximum_fusion.5), channel_id=1, source_target_pairs={{0,2},{1,3},{2,0},{3,1},{4,6},{5,7},{6,4},{7,5},{8,10},{9,11},{10,... | collective-permute-start | bytes 1622024 | tf_op jit(solution)/shard_map/ppermute | solution.py:82
  143.0 23.5 %collective-permute-start.19 = (bf16[4,2112,128]{2,1,0:T(8,128)(2,1)}, bf16[4,2112,128]{2,1,0:T(8,128)(2,1)}, u32[]{:S(2)}, u32[]{:S(2)}) collective-permute-start(bf16[4,2112,128]{2,1,0:T(8,128)(2,1)} %pad_maximum_fusion.2), channel_id=1, source_target_pairs={{0,4},{4,0},{8,12},{12,8},{16,20},{20,16},{24,28},{28,24},{1,5},{5... | collective-permute-start | bytes 6488072 | tf_op jit(solution)/shard_map/ppermute | solution.py:82
  145.7 20.7 %collective-permute-start.17 = (bf16[1,2112,128]{2,1,0:T(8,128)(2,1)}, bf16[1,2112,128]{2,1,0:T(8,128)(2,1)}, u32[]{:S(2)}, u32[]{:S(2)}) collective-permute-start(bf16[1,2112,128]{2,1,0:T(8,128)(2,1)} %slice.209), channel_id=1, source_target_pairs={{0,8},{4,12},{8,0},{12,4},{16,24},{20,28},{24,16},{28,20},{1,9},{5... | collective-permute-start | bytes 1622024 | tf_op jit(solution)/shard_map/ppermute | solution.py:82
  146.3 20.1 %collective-permute-start.18 = (bf16[1,2112,128]{2,1,0:T(8,128)(2,1)}, bf16[1,2112,128]{2,1,0:T(8,128)(2,1)}, u32[]{:S(2)}, u32[]{:S(2)}) collective-permute-start(bf16[1,2112,128]{2,1,0:T(8,128)(2,1)} %slice.210), channel_id=1, source_target_pairs={{0,16},{4,20},{8,24},{12,28},{16,0},{20,4},{24,8},{28,12},{1,17},{... | collective-permute-start | bytes 1622024 | tf_op jit(solution)/shard_map/ppermute | solution.py:82
  147.9 18.6 %collective-permute-start.20 = (bf16[2112,128]{1,0:T(8,128)(2,1)}, bf16[2112,128]{1,0:T(8,128)(2,1)}, u32[]{:S(2)}, u32[]{:S(2)}) collective-permute-start(bf16[2112,128]{1,0:T(8,128)(2,1)} %collective-permute-done.16), channel_id=1, source_target_pairs={{0,1},{1,0},{2,3},{3,2},{4,5},{5,4},{6,7},{7,6},{8,9},{9,8},{10,11... | collective-permute-start | bytes 1622024 | tf_op jit(solution)/shard_map/ppermute | solution.py:82
  171.5 30.5 %collective-permute-start.24 = (bf16[2,2144,128]{2,1,0:T(8,128)(2,1)}, bf16[2,2144,128]{2,1,0:T(8,128)(2,1)}, u32[]{:S(2)}, u32[]{:S(2)}) collective-permute-start(bf16[2,2144,128]{2,1,0:T(8,128)(2,1)} %maximum_maximum_fusion.refs_0_.refs_1_.refs_2_), channel_id=1, source_target_pairs={{0,4},{4,0},{8,12},{12,8},{16,20},{20,16},{24,28},{28,24},{1,5},{5... | collective-permute-start | bytes 3293192 | tf_op jit(solution)/shard_map/ppermute | solution.py:82
  171.7 30.3 %collective-permute-start.23 = (bf16[2,2144,128]{2,1,0:T(8,128)(2,1)}, bf16[2,2144,128]{2,1,0:T(8,128)(2,1)}, u32[]{:S(2)}, u32[]{:S(2)}) collective-permute-start(bf16[2,2144,128]{2,1,0:T(8,128)(2,1)} %maximum_maximum_fusion.refs_0_.refs_1_.refs_2_), channel_id=1, source_target_pairs={{0,16},{4,20},{8,24},{12,28},{16,0},{20,4},{24,8},{28,12},{1,17},{... | collective-permute-start | bytes 3293192 | tf_op jit(solution)/shard_map/ppermute | solution.py:82
  172.3 29.8 %collective-permute-start.22 = (bf16[2,2144,128]{2,1,0:T(8,128)(2,1)}, bf16[2,2144,128]{2,1,0:T(8,128)(2,1)}, u32[]{:S(2)}, u32[]{:S(2)}) collective-permute-start(bf16[2,2144,128]{2,1,0:T(8,128)(2,1)} %maximum_maximum_fusion.refs_0_.refs_1_.refs_2_), channel_id=1, source_target_pairs={{0,8},{4,12},{8,0},{12,4},{16,24},{20,28},{24,16},{28,20},{1,9},{5... | collective-permute-start | bytes 3293192 | tf_op jit(solution)/shard_map/ppermute | solution.py:82
  202.1 50.5 %collective-permute-start.29 = (bf16[4,2,2112,128]{3,2,1,0:T(8,128)(2,1)}, bf16[4,2,2112,128]{3,2,1,0:T(8,128)(2,1)}, u32[]{:S(2)}, u32[]{:S(2)}) collective-permute-start(bf16[4,2,2112,128]{3,2,1,0:T(8,128)(2,1)} %get-tuple-element.347), channel_id=1, source_target_pairs={{0,4},{4,0},{8,12},{12,8},{16,20},{20,16},{24,28},{28,24},{1,5},{5... | collective-permute-start | bytes 12976136 | tf_op jit(solution)/shard_map/ppermute | solution.py:82
  203.2 14.9 %collective-permute-start.25 = (bf16[1,2144,128]{2,1,0:T(8,128)(2,1)S(1)}, bf16[1,2144,128]{2,1,0:T(8,128)(2,1)S(1)}, u32[]{:S(2)}, u32[]{:S(2)}) collective-permute-start(bf16[1,2144,128]{2,1,0:T(8,128)(2,1)S(1)} %slice.213), channel_id=1, source_target_pairs={{0,8},{4,12},{8,0},{12,4},{16,24},{20,28},{24,16},{28,20},{1,9},{5... | collective-permute-start | bytes 1646600 | tf_op jit(solution)/shard_map/ppermute | solution.py:82
  205.6 19.0 %collective-permute-start.27 = (bf16[4,2144,128]{2,1,0:T(8,128)(2,1)S(1)}, bf16[4,2144,128]{2,1,0:T(8,128)(2,1)S(1)}, u32[]{:S(2)}, u32[]{:S(2)}) collective-permute-start(bf16[4,2144,128]{2,1,0:T(8,128)(2,1)S(1)} %pad_maximum_fusion), channel_id=1, source_target_pairs={{0,4},{4,0},{8,12},{12,8},{16,20},{20,16},{24,28},{28,24},{1,5},{5... | collective-permute-start | bytes 6586376 | tf_op jit(solution)/shard_map/ppermute | solution.py:82
  206.9 14.7 %collective-permute-start.26 = (bf16[1,2144,128]{2,1,0:T(8,128)(2,1)S(1)}, bf16[1,2144,128]{2,1,0:T(8,128)(2,1)S(1)}, u32[]{:S(2)}, u32[]{:S(2)}) collective-permute-start(bf16[1,2144,128]{2,1,0:T(8,128)(2,1)S(1)} %slice.214), channel_id=1, source_target_pairs={{0,16},{4,20},{8,24},{12,28},{16,0},{20,4},{24,8},{28,12},{1,17},{... | collective-permute-start | bytes 1646600 | tf_op jit(solution)/shard_map/ppermute | solution.py:82
  252.6 50.1 %collective-permute-start.37 = (bf16[4,2,2112,128]{3,2,1,0:T(8,128)(2,1)}, bf16[4,2,2112,128]{3,2,1,0:T(8,128)(2,1)}, u32[]{:S(2)}, u32[]{:S(2)}) collective-permute-start(bf16[4,2,2112,128]{3,2,1,0:T(8,128)(2,1)} %get-tuple-element.367), channel_id=1, source_target_pairs={{0,4},{4,0},{8,12},{12,8},{16,20},{20,16},{24,28},{28,24},{1,5},{5... | collective-permute-start | bytes 12976136 | tf_op jit(solution)/shard_map/ppermute | solution.py:82
  252.8 14.8 %collective-permute-start.34 = (f32[1,128]{1,0:T(1,128)S(1)}, f32[1,128]{1,0:T(1,128)S(1)}, u32[]{:S(2)}, u32[]{:S(2)}) collective-permute-start(f32[1,128]{1,0:T(1,128)S(1)} %add_bitcast_fusion), channel_id=1, source_target_pairs={{0,3},{1,2},{2,1},{3,0},{4,7},{5,6},{6,5},{7,4},{8,11},{9,10},{10,... | collective-permute-start | bytes 1544 | tf_op jit(solution)/shard_map/ppermute | solution.py:82
  254.4 17.4 %collective-permute-start.33 = (f32[1,128]{1,0:T(1,128)S(1)}, f32[1,128]{1,0:T(1,128)S(1)}, u32[]{:S(2)}, u32[]{:S(2)}) collective-permute-start(f32[1,128]{1,0:T(1,128)S(1)} %add_bitcast_fusion), channel_id=1, source_target_pairs={{0,2},{1,3},{2,0},{3,1},{4,6},{5,7},{6,4},{7,5},{8,10},{9,11},{10,... | collective-permute-start | bytes 1544 | tf_op jit(solution)/shard_map/ppermute | solution.py:82
  257.6 14.6 %collective-permute-start.30 = (bf16[1,2112,128]{2,1,0:T(8,128)(2,1)}, bf16[1,2112,128]{2,1,0:T(8,128)(2,1)}, u32[]{:S(2)}, u32[]{:S(2)}) collective-permute-start(bf16[1,2112,128]{2,1,0:T(8,128)(2,1)} %get-tuple-element.351), channel_id=1, source_target_pairs={{0,8},{4,12},{8,0},{12,4},{16,24},{20,28},{24,16},{28,20},{1,9},{5... | collective-permute-start | bytes 1622024 | tf_op jit(solution)/shard_map/ppermute | solution.py:82
  277.3 25.0 %collective-permute-start.35 = (bf16[2,2112,128]{2,1,0:T(8,128)(2,1)}, bf16[2,2112,128]{2,1,0:T(8,128)(2,1)}, u32[]{:S(2)}, u32[]{:S(2)}) collective-permute-start(bf16[2,2112,128]{2,1,0:T(8,128)(2,1)} %get-tuple-element.365), channel_id=1, source_target_pairs={{0,8},{4,12},{8,0},{12,4},{16,24},{20,28},{24,16},{28,20},{1,9},{5... | collective-permute-start | bytes 3244040 | tf_op jit(solution)/shard_map/ppermute | solution.py:82
  277.8 24.8 %collective-permute-start.36 = (bf16[2,2112,128]{2,1,0:T(8,128)(2,1)}, bf16[2,2112,128]{2,1,0:T(8,128)(2,1)}, u32[]{:S(2)}, u32[]{:S(2)}) collective-permute-start(bf16[2,2112,128]{2,1,0:T(8,128)(2,1)} %get-tuple-element.366), channel_id=1, source_target_pairs={{0,16},{4,20},{8,24},{12,28},{16,0},{20,4},{24,8},{28,12},{1,17},{... | collective-permute-start | bytes 3244040 | tf_op jit(solution)/shard_map/ppermute | solution.py:82
  309.7 14.8 %collective-permute-start.38 = (bf16[1,2112,128]{2,1,0:T(8,128)(2,1)}, bf16[1,2112,128]{2,1,0:T(8,128)(2,1)}, u32[]{:S(2)}, u32[]{:S(2)}) collective-permute-start(bf16[1,2112,128]{2,1,0:T(8,128)(2,1)} %get-tuple-element.383), channel_id=1, source_target_pairs={{0,8},{4,12},{8,0},{12,4},{16,24},{20,28},{24,16},{28,20},{1,9},{5... | collective-permute-start | bytes 1622024 | tf_op jit(solution)/shard_map/ppermute | solution.py:82
  328.4 32.0 %collective-permute-start.42 = (bf16[4,2,1024,128]{3,2,1,0:T(8,128)(2,1)}, bf16[4,2,1024,128]{3,2,1,0:T(8,128)(2,1)}, u32[]{:S(2)}, u32[]{:S(2)}) collective-permute-start(bf16[4,2,1024,128]{3,2,1,0:T(8,128)(2,1)} %get-tuple-element.399), channel_id=1, source_target_pairs={{0,4},{4,0},{8,12},{12,8},{16,20},{20,16},{24,28},{28,24},{1,5},{5... | collective-permute-start | bytes 6291464 | tf_op jit(solution)/shard_map/ppermute | solution.py:82
  331.9 25.1 %collective-permute-start.43 = (bf16[2112,128]{1,0:T(8,128)(2,1)}, bf16[2112,128]{1,0:T(8,128)(2,1)}, u32[]{:S(2)}, u32[]{:S(2)}) collective-permute-start(bf16[2112,128]{1,0:T(8,128)(2,1)} %bitcast.43), channel_id=1, source_target_pairs={{0,1},{1,0},{2,3},{3,2},{4,5},{5,4},{6,7},{7,6},{8,9},{9,8},{10,11... | collective-permute-start | bytes 1622024 | tf_op jit(solution)/shard_map/ppermute | solution.py:82
  333.8 26.3 %collective-permute-start.40 = (bf16[2,2112,128]{2,1,0:T(8,128)(2,1)}, bf16[2,2112,128]{2,1,0:T(8,128)(2,1)}, u32[]{:S(2)}, u32[]{:S(2)}) collective-permute-start(bf16[2,2112,128]{2,1,0:T(8,128)(2,1)} %get-tuple-element.397), channel_id=1, source_target_pairs={{0,8},{4,12},{8,0},{12,4},{16,24},{20,28},{24,16},{28,20},{1,9},{5... | collective-permute-start | bytes 3244040 | tf_op jit(solution)/shard_map/ppermute | solution.py:82
  334.4 26.0 %collective-permute-start.41 = (bf16[2,2112,128]{2,1,0:T(8,128)(2,1)}, bf16[2,2112,128]{2,1,0:T(8,128)(2,1)}, u32[]{:S(2)}, u32[]{:S(2)}) collective-permute-start(bf16[2,2112,128]{2,1,0:T(8,128)(2,1)} %get-tuple-element.398), channel_id=1, source_target_pairs={{0,16},{4,20},{8,24},{12,28},{16,0},{20,4},{24,8},{28,12},{1,17},{... | collective-permute-start | bytes 3244040 | tf_op jit(solution)/shard_map/ppermute | solution.py:82
  366.5 14.7 %collective-permute-start.44 = (bf16[1,1024,128]{2,1,0:T(8,128)(2,1)}, bf16[1,1024,128]{2,1,0:T(8,128)(2,1)S(1)}, u32[]{:S(2)}, u32[]{:S(2)}) collective-permute-start(bf16[1,1024,128]{2,1,0:T(8,128)(2,1)} %get-tuple-element.417), channel_id=1, source_target_pairs={{0,8},{4,12},{8,0},{12,4},{16,24},{20,28},{24,16},{28,20},{1,9},{5... | collective-permute-start | bytes 786440 | tf_op jit(solution)/shard_map/ppermute | solution.py:82
  386.5 28.9 %collective-permute-start.47 = (bf16[4,2,1024,128]{3,2,1,0:T(8,128)(2,1)}, bf16[4,2,1024,128]{3,2,1,0:T(8,128)(2,1)}, u32[]{:S(2)}, u32[]{:S(2)}) collective-permute-start(bf16[4,2,1024,128]{3,2,1,0:T(8,128)(2,1)} %get-tuple-element.441), channel_id=1, source_target_pairs={{0,4},{4,0},{8,12},{12,8},{16,20},{20,16},{24,28},{28,24},{1,5},{5... | collective-permute-start | bytes 6291464 | tf_op jit(solution)/shard_map/ppermute | solution.py:82
  386.5 23.2 %collective-permute-start.48 = (bf16[2,1024,128]{2,1,0:T(8,128)(2,1)}, bf16[2,1024,128]{2,1,0:T(8,128)(2,1)}, u32[]{:S(2)}, u32[]{:S(2)}) collective-permute-start(bf16[2,1024,128]{2,1,0:T(8,128)(2,1)} %get-tuple-element.442), channel_id=1, source_target_pairs={{0,8},{4,12},{8,0},{12,4},{16,24},{20,28},{24,16},{28,20},{1,9},{5... | collective-permute-start | bytes 1572872 | tf_op jit(solution)/shard_map/ppermute | solution.py:82
  387.1 22.5 %collective-permute-start.49 = (bf16[2,1024,128]{2,1,0:T(8,128)(2,1)}, bf16[2,1024,128]{2,1,0:T(8,128)(2,1)}, u32[]{:S(2)}, u32[]{:S(2)}) collective-permute-start(bf16[2,1024,128]{2,1,0:T(8,128)(2,1)} %get-tuple-element.443), channel_id=1, source_target_pairs={{0,16},{4,20},{8,24},{12,28},{16,0},{20,4},{24,8},{28,12},{1,17},{... | collective-permute-start | bytes 1572872 | tf_op jit(solution)/shard_map/ppermute | solution.py:82
  388.5 26.9 %collective-permute-start.50 = (bf16[2112,128]{1,0:T(8,128)(2,1)}, bf16[2112,128]{1,0:T(8,128)(2,1)}, u32[]{:S(2)}, u32[]{:S(2)}) collective-permute-start(bf16[2112,128]{1,0:T(8,128)(2,1)} %fusion.12), channel_id=1, source_target_pairs={{0,2},{1,3},{2,0},{3,1},{4,6},{5,7},{6,4},{7,5},{8,10},{9,11},{10,... | collective-permute-start | bytes 1622024 | tf_op jit(solution)/shard_map/ppermute | solution.py:82
  420.1 28.3 %collective-permute-start.55 = (bf16[512,1024]{1,0:T(8,128)(2,1)}, bf16[512,1024]{1,0:T(8,128)(2,1)}, u32[]{:S(2)}, u32[]{:S(2)}) collective-permute-start(bf16[512,1024]{1,0:T(8,128)(2,1)} %get-tuple-element.480), channel_id=1, source_target_pairs={{1,0},{2,1},{3,2},{5,4},{6,5},{7,6},{9,8},{10,9},{11,10},{13,12},{... | collective-permute-start | bytes 3145736 | tf_op jit(solution)/shard_map/ppermute | solution.py:1393
  424.9 72.8 %collective-permute-start.61 = (bf16[1024,128]{1,0:T(8,128)(2,1)}, bf16[1024,128]{1,0:T(8,128)(2,1)S(1)}, u32[]{:S(2)}, u32[]{:S(2)}) collective-permute-start(bf16[1024,128]{1,0:T(8,128)(2,1)} %bitcast.47), channel_id=1, source_target_pairs={{0,1},{1,0},{2,3},{3,2},{4,5},{5,4},{6,7},{7,6},{8,9},{9,8},{10,11... | collective-permute-start | bytes 786440 | tf_op jit(solution)/shard_map/ppermute | solution.py:82
  468.1 24.4 %collective-permute-start.62 = (bf16[512,1024]{1,0:T(8,128)(2,1)}, bf16[512,1024]{1,0:T(8,128)(2,1)}, u32[]{:S(2)}, u32[]{:S(2)}) collective-permute-start(bf16[512,1024]{1,0:T(8,128)(2,1)} %add_convert_fusion), channel_id=1, source_target_pairs={{1,0},{2,1},{3,2},{5,4},{6,5},{7,6},{9,8},{10,9},{11,10},{13,12},{... | collective-permute-start | bytes 3145736 | tf_op jit(solution)/shard_map/ppermute | solution.py:1393
  470.5 27.2 %collective-permute-start.63 = (f32[2,1024]{1,0:T(2,128)S(1)}, f32[2,1024]{1,0:T(2,128)S(1)}, u32[]{:S(2)}, u32[]{:S(2)}) collective-permute-start(f32[2,1024]{1,0:T(2,128)S(1)} %add_add_fusion), channel_id=1, source_target_pairs={{0,4},{4,0},{8,12},{12,8},{16,20},{20,16},{24,28},{28,24},{1,5},{5... | collective-permute-start | bytes 24584 | tf_op jit(solution)/shard_map/ppermute | solution.py:82
  470.5 33.0 %collective-permute-start.60 = (bf16[1024,128]{1,0:T(8,128)(2,1)}, bf16[1024,128]{1,0:T(8,128)(2,1)}, u32[]{:S(2)}, u32[]{:S(2)}) collective-permute-start(bf16[1024,128]{1,0:T(8,128)(2,1)} %fusion.20), channel_id=1, source_target_pairs={{0,2},{1,3},{2,0},{3,1},{4,6},{5,7},{6,4},{7,5},{8,10},{9,11},{10,... | collective-permute-start | bytes 786440 | tf_op jit(solution)/shard_map/ppermute | solution.py:82
  503.6 18.3 %collective-permute-start.66 = (f32[2,1024]{1,0:T(2,128)S(1)}, f32[2,1024]{1,0:T(2,128)S(1)}, u32[]{:S(2)}, u32[]{:S(2)}) collective-permute-start(f32[2,1024]{1,0:T(2,128)S(1)} %add.254), channel_id=1, source_target_pairs={{0,3},{1,2},{2,1},{3,0},{4,7},{5,6},{6,5},{7,4},{8,11},{9,10},{10,... | collective-permute-start | bytes 24584 | tf_op jit(solution)/shard_map/ppermute | solution.py:82
  503.6 18.3 %collective-permute-start.65 = (f32[2,1024]{1,0:T(2,128)S(1)}, f32[2,1024]{1,0:T(2,128)S(1)}, u32[]{:S(2)}, u32[]{:S(2)}) collective-permute-start(f32[2,1024]{1,0:T(2,128)S(1)} %add.254), channel_id=1, source_target_pairs={{0,2},{1,3},{2,0},{3,1},{4,6},{5,7},{6,4},{7,5},{8,10},{9,11},{10,... | collective-permute-start | bytes 24584 | tf_op jit(solution)/shard_map/ppermute | solution.py:82
  (59 other events, 505.6 us)
